TPU v7x, 256 devices: a whole 4x4x8 slice. The times are simulated.
256 devices in a mesh: pipe: 2 (over z_lo), tensor: 8 (over x, core), dp: 16 (over z_hi, y).
Axes of the slice: x: 4, y: 4, z: 8 (z_hi: 4, z_lo: 2; z = z_hi * 2 + z_lo), core: 2. Of those that a mesh axis runs over, the one named last changes fastest.
Arguments:
- attn_out: bfloat16 [2, 4, 2048, 4096], P('pipe', None, 'dp', 'tensor'), may hold values from -6 to 6
- grad_top: bfloat16 [4, 2048, 4096], P(None, 'dp', 'tensor'), may hold values from -6 to 6
- branch_grad: bfloat16 [2, 4, 2048, 4096], P('pipe', None, 'dp', 'tensor'), may hold values from -6 to 6
- error_prev: bfloat16 [2, 16, 4096, 4096], P('pipe', 'dp', 'tensor'), may hold values from -0.3984375 to 0.3984375
- q_prev: float32 [2, 4096, 64], P('pipe', 'tensor'), may hold values from -6 to 6
Outputs:
- grad_input: bfloat16 [2, 4, 2048, 4096], P('pipe', None, 'dp', 'tensor')
- error_next: bfloat16 [2, 16, 4096, 4096], P('pipe', 'dp', 'tensor')
- p_factor: float32 [2, 4096, 64], P('pipe', 'tensor')
- q_factor: float32 [2, 4096, 64], P('pipe', 'tensor')
All inputs are finite; a program needn't handle non-finite values.
Results may differ from a plain program's by a relative error of at most 0.012.
Values may be sent and summed in bfloat16 or wider, within the bound.
No kernel may reach another device: no remote copies, remote signals or barrier semaphores. Data moves between devices by JAX's collectives and lax.ppermute only.
A program may use at most 128 MiB of HBM per device.

v0:
```python
import jax
import jax.numpy as jnp
from jax import lax
from jax.sharding import PartitionSpec as P


def copy_for_each(value, axis):
    devices = lax.axis_size(axis)
    return lax.all_to_all(
        jnp.broadcast_to(value[None], (devices, *value.shape)), axis, 0, 0, tiled=True
    )


def in_order(tiles, dim):
    shape = list(tiles.shape[1:])
    shape[dim] *= tiles.shape[0]
    return jnp.moveaxis(tiles, 0, dim).reshape(shape)


def collect(value, axis, dim):
    tiles = copy_for_each(value, axis)
    return in_order(tiles, dim)


def from_behind(value, axis, by):
    devices = lax.axis_size(axis)
    pairs = [(i, i + by) for i in range(devices) if 0 <= i + by < devices]
    return lax.ppermute(value, axis, pairs)


def of_everyone(value, axis):
    everything = copy_for_each(value, axis)
    return jnp.sum(everything, axis=0)


def split_up(value, dim, devices):
    before, after = (value.shape[:dim], value.shape[dim + 1 :])
    return jnp.moveaxis(value.reshape(*before, devices, -1, *after), dim, 0)


def summed_on_arrival(value, axis, dim):
    devices = lax.axis_size(axis)
    tiles = lax.all_to_all(split_up(value, dim, devices), axis, 0, 0, tiled=True)
    return jnp.sum(tiles.astype(jnp.float32), axis=0)


def of_everyone_2(value, axis):
    return copy_for_each(value, axis).astype(jnp.float32).sum(axis=0)


def on_device(attn_out, grad_top, branch_grad, error_prev, q_prev):
    high = lax.Precision.HIGHEST
    section = lax.axis_index("pipe")
    sections = lax.axis_size("pipe")
    last = sections - 1
    micro_count = attn_out.shape[1]
    tok_rows = attn_out.shape[2]
    head_rows = attn_out.shape[3]
    width = error_prev.shape[3]
    replicas = lax.axis_size("dp")
    grads = jnp.zeros((head_rows, width), jnp.float32)
    received = jnp.zeros(grad_top.shape[1:], jnp.bfloat16)
    grad_all = jnp.zeros(grad_top.shape, jnp.bfloat16)
    for tick in range(micro_count + sections - 1):
        micro = tick - (last - section)
        valid = jnp.logical_and(micro >= 0, micro < micro_count)
        index = jnp.clip(micro, 0, micro_count - 1)
        top_slab = lax.dynamic_index_in_dim(grad_top, index, 0, keepdims=False)
        out_grad = jnp.where(section == last, top_slab, received)
        branch = lax.dynamic_index_in_dim(branch_grad[0], index, 0, keepdims=False)
        grad_in = (out_grad.astype(jnp.float32) + branch.astype(jnp.float32)).astype(jnp.bfloat16)
        updated = lax.dynamic_update_index_in_dim(grad_all, grad_in, index, 0)
        grad_all = jnp.where(valid, updated, grad_all)
        acts = lax.dynamic_index_in_dim(attn_out[0], index, 0, keepdims=False)
        contrib = lax.dot_general(
            acts,
            collect(out_grad, "tensor", 1),
            (((0,), (0,)), ((), ())),
            preferred_element_type=jnp.float32,
        )
        grads = grads + jnp.where(valid, contrib, 0.0)
        received = from_behind(grad_in, "pipe", -1)
    matrix = grads / (micro_count * tok_rows) + error_prev[0, 0].astype(jnp.float32)
    p_local = jnp.dot(matrix, collect(q_prev[0], "tensor", 0), precision=high)
    praw = of_everyone(p_local, "dp") / replicas
    gram = of_everyone(jnp.dot(praw.T, praw, precision=high), "tensor")
    lower = jnp.linalg.cholesky(gram)
    phat = lax.linalg.triangular_solve(lower, praw, left_side=False, lower=True, transpose_a=True)
    q_local = lax.dot_general(matrix, phat, (((0,), (0,)), ((), ())), precision=high)
    q_part = summed_on_arrival(q_local.astype(jnp.bfloat16), "tensor", 0)
    q_own = of_everyone_2(q_part.astype(jnp.bfloat16), "dp").astype(jnp.float32) / replicas
    q_full = collect(q_own.astype(jnp.bfloat16), "tensor", 0).astype(q_own.dtype)
    error_next = (matrix - jnp.dot(phat, q_full.T, precision=high)).astype(jnp.bfloat16)
    return (grad_all[None], error_next[None, None], phat[None], q_own[None])


def solution(mesh):
    return jax.shard_map(
        on_device,
        mesh=mesh,
        in_specs=(
            P("pipe", None, "dp", "tensor"),
            P(None, "dp", "tensor"),
            P("pipe", None, "dp", "tensor"),
            P("pipe", "dp", "tensor", None),
            P("pipe", "tensor", None),
        ),
        out_specs=(
            P("pipe", None, "dp", "tensor"),
            P("pipe", "dp", "tensor", None),
            P("pipe", "tensor", None),
            P("pipe", "tensor", None),
        ),
        check_vma=False,
    )
```

profile of v0, /device:TPU:1, one launch (start us, length us, event | category | flops | bytes accessed | tf_op | source)
XLA Modules:
  0.0 314.9 jit_solution(4728397418898245322)
XLA Ops:
  2.0 20.7 %all_to_all.55 = bf16[8,128,512]{1,2,0:T(8,128)(2,1)S(1)} all-to-all(bf16[8,128,512]{1,2,0:T(8,128)(2,1)S(1)} %broadcast_in_dim.111), channel_id=1, replica_groups=mesh['pipe'=2,'tensor'=8,'dp'=16] {'tensor'}, dimensions={0} | all-to-all | bytes 2097152 | tf_op jit(solution)/shard_map/all_to_all | solution.py:9
  22.7 2.0 broadcast_in_dim.118
  24.7 4.5 %all-to-all-start.5 = ((f32[8,512,64]{1,2,0:T(8,128)}), f32[8,512,64]{1,2,0:T(8,128)S(1)}, u32[]{:S(2)}, u32[]{:S(2)}) async-start(f32[8,512,64]{1,2,0:T(8,128)} %broadcast_in_dim.118), calls=%async_computation.5 | async-start | bytes 2097152 | tf_op jit(solution)/shard_map/all_to_all | solution.py:9
  31.6 4.6 %collective-permute-done = bf16[128,512]{1,0:T(8,128)(2,1)} collective-permute-done((bf16[128,512]{1,0:T(8,128)(2,1)S(1)}, bf16[128,512]{1,0:T(8,128)(2,1)}, u32[]{:S(2)}, u32[]{:S(2)}) %collective-permute-start) | collective-permute-done | bytes 131104 | tf_op jit(solution)/shard_map/ppermute | solution.py:28
  37.4 6.9 %all-to-all-done.5 = f32[8,512,64]{1,2,0:T(8,128)S(1)} async-done(((f32[8,512,64]{1,2,0:T(8,128)}), f32[8,512,64]{1,2,0:T(8,128)S(1)}, u32[]{:S(2)}, u32[]{:S(2)}) %all-to-all-start.5) | async-done | bytes 1048608 | tf_op jit(solution)/shard_map/all_to_all | solution.py:9
  45.7 4.3 %all-to-all-start.1 = ((bf16[8,128,512]{1,2,0:T(8,128)(2,1)}), bf16[8,128,512]{1,2,0:T(8,128)(2,1)S(1)}, u32[]{:S(2)}, u32[]{:S(2)}) async-start(bf16[8,128,512]{1,2,0:T(8,128)(2,1)} %broadcast_in_dim.113), calls=%async_computation.1 | async-start | bytes 2097152 | tf_op jit(solution)/shard_map/all_to_all | solution.py:9
  51.3 5.6 %collective-permute-done.1 = bf16[128,512]{1,0:T(8,128)(2,1)S(1)} collective-permute-done((bf16[128,512]{1,0:T(8,128)(2,1)S(1)}, bf16[128,512]{1,0:T(8,128)(2,1)S(1)}, u32[]{:S(2)}, u32[]{:S(2)}) %collective-permute-start.1) | collective-permute-done | bytes 131104 | tf_op jit(solution)/shard_map/ppermute | solution.py:28
  58.0 7.1 %all-to-all-done.1 = bf16[8,128,512]{1,2,0:T(8,128)(2,1)S(1)} async-done(((bf16[8,128,512]{1,2,0:T(8,128)(2,1)}), bf16[8,128,512]{1,2,0:T(8,128)(2,1)S(1)}, u32[]{:S(2)}, u32[]{:S(2)}) %all-to-all-start.1) | async-done | bytes 1048608 | tf_op jit(solution)/shard_map/all_to_all | solution.py:9
  66.2 5.0 %all-to-all-start.2 = ((bf16[8,128,512]{1,2,0:T(8,128)(2,1)}), bf16[8,128,512]{1,2,0:T(8,128)(2,1)}, u32[]{:S(2)}, u32[]{:S(2)}) async-start(bf16[8,128,512]{1,2,0:T(8,128)(2,1)} %broadcast_in_dim.114), calls=%async_computation.2 | async-start | bytes 2097152 | tf_op jit(solution)/shard_map/all_to_all | solution.py:9
  72.5 5.6 %collective-permute-done.2 = bf16[128,512]{1,0:T(8,128)(2,1)S(1)} collective-permute-done((bf16[128,512]{1,0:T(8,128)(2,1)S(1)}, bf16[128,512]{1,0:T(8,128)(2,1)S(1)}, u32[]{:S(2)}, u32[]{:S(2)}) %collective-permute-start.2) | collective-permute-done | bytes 131104 | tf_op jit(solution)/shard_map/ppermute | solution.py:28
  78.1 1.7 fusion.24
  81.3 4.9 %collective-permute-done.3 = bf16[128,512]{1,0:T(8,128)(2,1)S(1)} collective-permute-done((bf16[128,512]{1,0:T(8,128)(2,1)}, bf16[128,512]{1,0:T(8,128)(2,1)S(1)}, u32[]{:S(2)}, u32[]{:S(2)}) %collective-permute-start.3) | collective-permute-done | bytes 131104 | tf_op jit(solution)/shard_map/ppermute | solution.py:28
  88.1 2.3 copy.52
  91.5 6.0 %all-to-all-start.3 = ((bf16[8,128,512]{1,2,0:T(8,128)(2,1)}), bf16[8,128,512]{1,2,0:T(8,128)(2,1)}, u32[]{:S(2)}, u32[]{:S(2)}) async-start(bf16[8,128,512]{1,2,0:T(8,128)(2,1)} %broadcast_in_dim.115), calls=%async_computation.3 | async-start | bytes 2097152 | tf_op jit(solution)/shard_map/all_to_all | solution.py:9
  97.6 4.5 %fusion.22 = f32[512,4096]{1,0:T(8,128)} fusion(bf16[128,4096]{0,1:T(8,128)(2,1)S(1)} %bitcast.139, bf16[1,4,128,512]{3,2,1,0:T(8,128)(2,1)S(1)} %copy-done, s32[]{:T(128)S(6)} %min.16), kind=kOutput, calls=%fused_computation.33 | convolution fusion | flops 536870912 | bytes 9568260 | tf_op jit(solution)/shard_map/dot_general | solution.py:75
  102.1 4.5 %fusion.20 = f32[512,4096]{1,0:T(8,128)} fusion(bf16[128,4096]{0,1:T(8,128)(2,1)S(1)} %bitcast.140, bf16[1,4,128,512]{3,2,1,0:T(8,128)(2,1)S(1)} %copy-done, s32[]{:T(128)S(6)} %min.17), kind=kOutput, calls=%fused_computation.31 | convolution fusion | flops 536870912 | bytes 9568260 | tf_op jit(solution)/shard_map/dot_general | solution.py:75
  106.6 6.2 %all-to-all-done.3 = bf16[8,128,512]{1,2,0:T(8,128)(2,1)} async-done(((bf16[8,128,512]{1,2,0:T(8,128)(2,1)}), bf16[8,128,512]{1,2,0:T(8,128)(2,1)}, u32[]{:S(2)}, u32[]{:S(2)}) %all-to-all-start.3) | async-done | bytes 1048608 | tf_op jit(solution)/shard_map/all_to_all | solution.py:9
  113.9 4.3 %all-to-all-start.4 = ((bf16[8,128,512]{1,2,0:T(8,128)(2,1)}), bf16[8,128,512]{1,2,0:T(8,128)(2,1)S(1)}, u32[]{:S(2)}, u32[]{:S(2)}) async-start(bf16[8,128,512]{1,2,0:T(8,128)(2,1)} %broadcast_in_dim.116), calls=%async_computation.4 | async-start | bytes 2097152 | tf_op jit(solution)/shard_map/all_to_all | solution.py:9
  118.2 5.7 %fusion.18 = f32[512,4096]{1,0:T(8,128)} fusion(bf16[128,4096]{0,1:T(8,128)(2,1)} %bitcast.25, bf16[1,4,128,512]{3,2,1,0:T(8,128)(2,1)S(1)} %copy-done, s32[]{:T(128)S(6)} %min.18), kind=kOutput, calls=%fused_computation.29 | convolution fusion | flops 536870912 | bytes 9568260 | tf_op jit(solution)/shard_map/dot_general | solution.py:75
  123.9 5.7 %fusion.16 = f32[512,4096]{1,0:T(8,128)} fusion(bf16[128,4096]{0,1:T(8,128)(2,1)} %bitcast.28, bf16[1,4,128,512]{3,2,1,0:T(8,128)(2,1)S(1)} %copy-done, s32[]{:T(128)S(6)} %min.19), kind=kOutput, calls=%fused_computation.27 | convolution fusion | flops 536870912 | bytes 9568260 | tf_op jit(solution)/shard_map/dot_general | solution.py:75
  129.7 3.7 %all-to-all-done.4 = bf16[8,128,512]{1,2,0:T(8,128)(2,1)S(1)} async-done(((bf16[8,128,512]{1,2,0:T(8,128)(2,1)}), bf16[8,128,512]{1,2,0:T(8,128)(2,1)S(1)}, u32[]{:S(2)}, u32[]{:S(2)}) %all-to-all-start.4) | async-done | bytes 1048608 | tf_op jit(solution)/shard_map/all_to_all | solution.py:9
  133.3 14.8 %convert_add_fusion = f32[512,4096]{1,0:T(8,128)} fusion(f32[512,4096]{1,0:T(8,128)} %fusion.16, f32[512,4096]{1,0:T(8,128)} %fusion.18, f32[512,4096]{1,0:T(8,128)} %fusion.20, f32[512,4096]{1,0:T(8,128)} %fusion.22, bf16[128,4096]{0,1:T(8,128)(2,1)S(1)} %bitcast.143, bf16[1,1,512,4096]{3,2,1,0:T(8,128)(2,1)} %param.8, pred[]{:T(512)S(6)} %and.20, ...), kind=kOutput, calls=%fused_computation | convolution fusion | flops 562036736 | bytes 47317000 | tf_op jit(solution)/shard_map/dot_general | solution.py:75
  148.1 10.1 %fusion.53 = f32[512,64]{0,1:T(8,128)S(1)} fusion(f32[512,4096]{1,0:T(8,128)} %convert_add_fusion, f32[4096,64]{0,1:T(8,128)S(1)} %bitcast.141), kind=kOutput, calls=%fused_computation.76 | convolution fusion | flops 1610612736 | bytes 9568256 | tf_op jit(solution)/shard_map/dot_general | solution.py:84
  158.5 49.1 %all_to_all.56 = f32[16,512,64]{1,2,0:T(8,128)S(1)} all-to-all(f32[16,512,64]{1,2,0:T(8,128)S(1)} %broadcast_in_dim.119), channel_id=1, replica_groups=mesh['pipe'=2,'tensor'=8,'dp'=16] {'dp'}, dimensions={0} | all-to-all | bytes 4194304 | tf_op jit(solution)/shard_map/all_to_all | solution.py:9
  208.3 11.3 %all_to_all.57 = f32[8,1,4096]{2,1,0:T(1,128)S(1)} all-to-all(f32[8,1,4096]{2,1,0:T(1,128)S(1)} %reshape.126), channel_id=1, replica_groups=mesh['pipe'=2,'tensor'=8,'dp'=16] {'tensor'}, dimensions={0} | all-to-all | bytes 262144 | tf_op jit(solution)/shard_map/all_to_all | solution.py:9
  221.3 5.8 %cholesky.16 = f32[64,64]{1,0:T(8,128)S(1)} custom-call(f32[64,64]{1,0:T(8,128)S(1)} %fusion.41), custom_call_target="Cholesky" | custom-call | tf_op jit(solution)/shard_map/jit(cholesky)/cholesky | solution.py:87
  228.5 4.9 %custom-call.6 = f32[1,64,64]{1,2,0:T(8,128)S(1)} custom-call(f32[1,64,64]{2,1,0:T(8,128)S(1)} %fusion.39), custom_call_target="InvertDiagBlocksLowerTriangular" | custom-call | tf_op jit(solution)/shard_map/triangular_solve | solution.py:88
  233.7 8.0 %convolution_convert_fusion = bf16[4096,64]{0,1:T(8,128)(2,1)S(1)} fusion(f32[512,4096]{1,0:T(8,128)} %convert_add_fusion, f32[512,64]{0,1:T(8,128)S(1)} %fusion.32), kind=kOutput, calls=%fused_computation.3 | convolution fusion | flops 1610874880 | bytes 9043968 | tf_op jit(solution)/shard_map/dot_general | solution.py:89
  241.8 12.6 %all_to_all.58 = bf16[8,512,64]{1,2,0:T(8,128)(2,1)S(1)} all-to-all(bf16[8,512,64]{1,2,0:T(8,128)(2,1)S(1)} %bitcast.146), channel_id=1, replica_groups=mesh['pipe'=2,'tensor'=8,'dp'=16] {'tensor'}, dimensions={0} | all-to-all | bytes 1048576 | tf_op jit(solution)/shard_map/all_to_all | solution.py:43
  254.6 36.3 %all_to_all.59 = bf16[16,512,64]{1,2,0:T(8,128)(2,1)S(1)} all-to-all(bf16[16,512,64]{1,2,0:T(8,128)(2,1)S(1)} %broadcast_in_dim.121), channel_id=1, replica_groups=mesh['pipe'=2,'tensor'=8,'dp'=16] {'dp'}, dimensions={0} | all-to-all | bytes 2097152 | tf_op jit(solution)/shard_map/all_to_all | solution.py:9
  291.8 15.7 %all_to_all.60 = bf16[8,512,64]{1,2,0:T(8,128)(2,1)S(1)} all-to-all(bf16[8,512,64]{1,2,0:T(8,128)(2,1)S(1)} %broadcast_in_dim.122), channel_id=1, replica_groups=mesh['pipe'=2,'tensor'=8,'dp'=16] {'tensor'}, dimensions={0} | all-to-all | bytes 1048576 | tf_op jit(solution)/shard_map/all_to_all | solution.py:9
  307.5 7.4 %fusion = bf16[1,1,512,4096]{3,2,1,0:T(8,128)(2,1)} fusion(f32[512,4096]{1,0:T(8,128)} %convert_add_fusion, f32[512,64]{0,1:T(8,128)S(1)} %fusion.32, bf16[4096,64]{0,1:T(8,128)(2,1)S(1)} %bitcast.144), kind=kOutput, calls=%fused_computation.2 | convolution fusion | flops 1614807040 | bytes 13238272 | tf_op jit(solution)/shard_map/dot_general | solution.py:93
  (56 shorter events, 22.0 us)
Async XLA Ops:
  0.6 96.9 %copy-start = (bf16[1,4,128,512]{3,2,1,0:T(8,128)(2,1)S(1)}, bf16[1,4,128,512]{3,2,1,0:T(8,128)(2,1)}, u32[]{:S(2)}) copy-start(bf16[1,4,128,512]{3,2,1,0:T(8,128)(2,1)} %param.5) | copy-start | bytes 1572868
  24.7 19.6 %all-to-all-start.5 = ((f32[8,512,64]{1,2,0:T(8,128)}), f32[8,512,64]{1,2,0:T(8,128)S(1)}, u32[]{:S(2)}, u32[]{:S(2)}) async-start(f32[8,512,64]{1,2,0:T(8,128)} %broadcast_in_dim.118), calls=%async_computation.5 | async-start | bytes 2097152 | tf_op jit(solution)/shard_map/all_to_all | solution.py:9
  29.2 7.0 %collective-permute-start = (bf16[128,512]{1,0:T(8,128)(2,1)S(1)}, bf16[128,512]{1,0:T(8,128)(2,1)}, u32[]{:S(2)}, u32[]{:S(2)}) collective-permute-start(bf16[128,512]{1,0:T(8,128)(2,1)S(1)} %get-tuple-element.15), channel_id=1, source_target_pairs={{128,0},{129,1},{130,2},{131,3},{132,4},{133,5},{134,6},{135,7},{1... | collective-permute-start | bytes 393224 | tf_op jit(solution)/shard_map/ppermute | solution.py:28
  44.3 1.3 copy-start.3
  45.7 19.5 %all-to-all-start.1 = ((bf16[8,128,512]{1,2,0:T(8,128)(2,1)}), bf16[8,128,512]{1,2,0:T(8,128)(2,1)S(1)}, u32[]{:S(2)}, u32[]{:S(2)}) async-start(bf16[8,128,512]{1,2,0:T(8,128)(2,1)} %broadcast_in_dim.113), calls=%async_computation.1 | async-start | bytes 2097152 | tf_op jit(solution)/shard_map/all_to_all | solution.py:9
  50.0 6.8 %collective-permute-start.1 = (bf16[128,512]{1,0:T(8,128)(2,1)S(1)}, bf16[128,512]{1,0:T(8,128)(2,1)S(1)}, u32[]{:S(2)}, u32[]{:S(2)}) collective-permute-start(bf16[128,512]{1,0:T(8,128)(2,1)S(1)} %get-tuple-element.13), channel_id=1, source_target_pairs={{128,0},{129,1},{130,2},{131,3},{132,4},{133,5},{134,6},{135,7},{1... | collective-permute-start | bytes 393224 | tf_op jit(solution)/shard_map/ppermute | solution.py:28
  66.2 24.2 %all-to-all-start.2 = ((bf16[8,128,512]{1,2,0:T(8,128)(2,1)}), bf16[8,128,512]{1,2,0:T(8,128)(2,1)}, u32[]{:S(2)}, u32[]{:S(2)}) async-start(bf16[8,128,512]{1,2,0:T(8,128)(2,1)} %broadcast_in_dim.114), calls=%async_computation.2 | async-start | bytes 2097152 | tf_op jit(solution)/shard_map/all_to_all | solution.py:9
  71.2 6.9 %collective-permute-start.2 = (bf16[128,512]{1,0:T(8,128)(2,1)S(1)}, bf16[128,512]{1,0:T(8,128)(2,1)S(1)}, u32[]{:S(2)}, u32[]{:S(2)}) collective-permute-start(bf16[128,512]{1,0:T(8,128)(2,1)S(1)} %get-tuple-element.10), channel_id=1, source_target_pairs={{128,0},{129,1},{130,2},{131,3},{132,4},{133,5},{134,6},{135,7},{1... | collective-permute-start | bytes 393224 | tf_op jit(solution)/shard_map/ppermute | solution.py:28
  79.8 6.3 %collective-permute-start.3 = (bf16[128,512]{1,0:T(8,128)(2,1)}, bf16[128,512]{1,0:T(8,128)(2,1)S(1)}, u32[]{:S(2)}, u32[]{:S(2)}) collective-permute-start(bf16[128,512]{1,0:T(8,128)(2,1)} %get-tuple-element.7), channel_id=1, source_target_pairs={{128,0},{129,1},{130,2},{131,3},{132,4},{133,5},{134,6},{135,7},{1... | collective-permute-start | bytes 393224 | tf_op jit(solution)/shard_map/ppermute | solution.py:28
  87.2 0.8 copy-start.5
  91.5 21.2 %all-to-all-start.3 = ((bf16[8,128,512]{1,2,0:T(8,128)(2,1)}), bf16[8,128,512]{1,2,0:T(8,128)(2,1)}, u32[]{:S(2)}, u32[]{:S(2)}) async-start(bf16[8,128,512]{1,2,0:T(8,128)(2,1)} %broadcast_in_dim.115), calls=%async_computation.3 | async-start | bytes 2097152 | tf_op jit(solution)/shard_map/all_to_all | solution.py:9
  113.9 19.5 %all-to-all-start.4 = ((bf16[8,128,512]{1,2,0:T(8,128)(2,1)}), bf16[8,128,512]{1,2,0:T(8,128)(2,1)S(1)}, u32[]{:S(2)}, u32[]{:S(2)}) async-start(bf16[8,128,512]{1,2,0:T(8,128)(2,1)} %broadcast_in_dim.116), calls=%async_computation.4 | async-start | bytes 2097152 | tf_op jit(solution)/shard_map/all_to_all | solution.py:9
  133.3 14.8 %copy-start.2 = (f32[8,8,8,512]{3,2,0,1:T(8,128)S(1)}, f32[8,8,8,512]{3,2,0,1:T(8,128)}, u32[]{:S(2)}) copy-start(f32[8,8,8,512]{3,2,0,1:T(8,128)} %copy.52) | copy-start | bytes 3145732
  233.7 73.7 %copy-start.4 = (f32[512,64]{0,1:T(8,128)}, f32[512,64]{0,1:T(8,128)S(1)}, u32[]{:S(2)}) copy-start(f32[512,64]{0,1:T(8,128)S(1)} %fusion.32) | copy-start | bytes 393220
  290.9 24.0 %copy-start.1 = (bf16[1,4,128,512]{3,2,1,0:T(8,128)(2,1)S(1)}, bf16[1,4,128,512]{3,2,1,0:T(8,128)(2,1)}, u32[]{:S(2)}) copy-start(bf16[1,4,128,512]{3,2,1,0:T(8,128)(2,1)} %param.5) | copy-start | bytes 1572868
where the time goes:
time: 319 us; the launch traced here: 315 us
  blocking collectives  146 us (46%)
  matrix products  61.3 us (19%)
  waiting for transfers between devices  44.6 us (14%)
  starting transfers between devices  29.3 us (9%)
  other arithmetic  21.1 us (7%)
  local copies, waits for them, and re-layouts  11.9 us (4%)
    all_to_all x5, blocking collectives, copy_for_each(): lax.all_to_all(jnp.broadcast_to(value[None], (devices, *value.shape)), ax...  133 us
    dot_general x5, matrix products, on_device(): lax.dot_general(acts, collect(out_grad, 'tensor', 1), (((0,), (0,)), ((),...  35.3 us
    all_to_all x5, starting transfers between devices, copy_for_each(): lax.all_to_all(jnp.broadcast_to(value[None], (devices, *value.shape)), ax...  24.2 us
    all_to_all x5, waiting for transfers between devices, copy_for_each(): lax.all_to_all(jnp.broadcast_to(value[None], (devices, *value.shape)), ax...  23.9 us
    ppermute x4, waiting for transfers between devices, from_behind(): return lax.ppermute(value, axis, pairs)  20.7 us
    all_to_all x1, blocking collectives, summed_on_arrival(): lax.all_to_all(split_up(value, dim, devices), axis, 0, 0, tiled=True)  12.6 us
    dot_general x1, matrix products, on_device(): p_local = jnp.dot(matrix, collect(q_prev[0], 'tensor', 0), precision=high)  10.1 us
    dot_general x1, matrix products, on_device(): lax.dot_general(matrix, phat, (((0,), (0,)), ((), ())), precision=high)  7.98 us
  transfers between devices with their start and end apart: 9, of which 8 were waited for; matrix products, arithmetic and copies ran while one was open for 9% of the time, Pallas kernels for 0%

commit v1 on v0

v1 whole, which is shorter than its diff:
```python
import jax
import jax.numpy as jnp
from jax import lax
from jax.experimental import pallas as pl
from jax.experimental.pallas import tpu as pltpu
from jax.sharding import Mesh, PartitionSpec as P

BF = jnp.bfloat16
F32 = jnp.float32
HIGH = lax.Precision.HIGHEST
MIB = 1024 * 1024
ANY = pl.BlockSpec(memory_space=pl.ANY)
VMEM = pl.BlockSpec(memory_space=pltpu.VMEM)
SMEM = pl.BlockSpec(memory_space=pltpu.SMEM)


def sds(shape, dtype):
    return jax.ShapeDtypeStruct(shape, dtype)


def params(mib):
    return pltpu.CompilerParams(vmem_limit_bytes=mib * MIB)


def split3(v):
    h = v.astype(BF)
    r = v - h.astype(F32)
    m = r.astype(BF)
    l = (r - m.astype(F32)).astype(BF)
    return jnp.concatenate([h, m, l], axis=0)


def fold3(v):
    n = v.shape[0] // 3
    return v[:n] + (v[n : 2 * n] + v[2 * n :])


def dot(a, b, ca, cb):
    return lax.dot_general(a, b, (((ca,), (cb,)), ((), ())), preferred_element_type=F32)


def grad_kernel(last_ref, top_ref, recv_ref, br_ref, q_ref, g_ref, gin_ref, u_ref):
    last = last_ref[0]

    @pl.when(last == 1)
    def _():
        g_ref[...] = top_ref[...]

    @pl.when(last == 0)
    def _():
        g_ref[...] = recv_ref[...]

    g = g_ref[...]
    gin_ref[...] = (g.astype(F32) + br_ref[...].astype(F32)).astype(BF)
    u_ref[...] = fold3(dot(split3(q_ref[...]), g, 1, 1))


def eq_kernel(idx_ref, qa_ref, qb_ref, act_ref, e_hbm, out_ref, at_ref, e_buf, sems):
    w = e_buf.shape[2]
    cps = []
    for j in range(8):
        cp = pltpu.make_async_copy(
            e_hbm.at[:, pl.ds(pl.multiple_of(idx_ref[j] * w, w), w)], e_buf.at[j], sems.at[j]
        )
        cp.start()
        cps.append(cp)
    at_ref[...] = act_ref[...].T
    acc = None
    for j in range(8):
        q3 = split3(qa_ref[j] if j < 4 else qb_ref[j - 4])
        cps[j].wait()
        part = dot(q3, e_buf[j], 1, 1)
        acc = part if acc is None else acc + part
    out_ref[...] = fold3(acc)


def p_kernel(u0, u1, u2, u3, act_ref, eq_ref, out_ref):
    u = (u0[...] + u2[...]) + (u1[...] + u3[...])
    p = fold3(dot(split3(u), act_ref[...], 1, 0)) * (1.0 / 512.0) + eq_ref[...]
    for k in range(4):
        out_ref[k] = p


def sum_kernel(in_ref, out_ref):
    s = (in_ref[0] + in_ref[2]) + (in_ref[1] + in_ref[3])
    for k in range(4):
        out_ref[k] = s


def put_chunks(out_ref, slot, r, gram):
    for y in range(4):
        out_ref[slot, y, 0:64, :] = r[:, y * 128 : (y + 1) * 128]
        out_ref[slot, y, 64:96, :] = gram


def q_blocks(idx_ref, p3, v3, gram, gs, e_hbm, out_ref, e_buf, g_buf, sems, base):
    w = e_buf.shape[2]
    cps = []
    for k in range(4):
        a = pltpu.make_async_copy(
            e_hbm.at[:, pl.ds(pl.multiple_of(idx_ref[base + k] * w, w), w)], e_buf.at[k], sems.at[k]
        )
        b = pltpu.make_async_copy(gs[k], g_buf.at[k], sems.at[4 + k])
        a.start()
        b.start()
        cps.append((a, b))
    p3, v3, gram = p3(), v3(), gram()
    for k in range(4):
        cps[k][0].wait()
        cps[k][1].wait()
        r = dot(p3, e_buf[k], 1, 0) + dot(v3, g_buf[k], 1, 0) * (1.0 / 512.0)
        put_chunks(out_ref, idx_ref[base + k] // 2, fold3(r), gram)


def q_send_kernel(
    idx_ref, pz_ref, act_ref, g0, g1, g2, g3, e_hbm, out_ref, p_ref, p3_ref, v3_ref, gram_ref, e_buf, g_buf, sems
):
    def get_p3():
        p = ((pz_ref[0] + pz_ref[2]) + (pz_ref[1] + pz_ref[3])) * (1.0 / 16.0)
        p_ref[...] = p
        p3_ref[...] = split3(p)
        return p3_ref[...]

    def get_v3():
        v3_ref[...] = split3(fold3(dot(p3_ref[...], act_ref[...], 1, 1)))
        return v3_ref[...]

    def get_gram():
        p3 = p3_ref[...]
        g = dot(p3, p3[0:64], 1, 1) + (dot(p3, p3[64:128], 1, 1) + dot(p3, p3[128:192], 1, 1))
        g = fold3(g)
        gram_ref[...] = jnp.concatenate([g[0:32], g[32:64]], axis=1)
        return gram_ref[...]

    q_blocks(idx_ref, get_p3, get_v3, get_gram, (g0, g1, g2, g3), e_hbm, out_ref, e_buf, g_buf, sems, 4)


def q_keep_kernel(idx_ref, p3_ref, v3_ref, gram_ref, g0, g1, g2, g3, e_hbm, out_ref, e_buf, g_buf, sems):
    q_blocks(
        idx_ref,
        lambda: p3_ref[...],
        lambda: v3_ref[...],
        lambda: gram_ref[...],
        (g0, g1, g2, g3),
        e_hbm,
        out_ref,
        e_buf,
        g_buf,
        sems,
        0,
    )


def chunk_sum_kernel(in_ref, q_ref, gram_ref):
    s = in_ref[0]
    for k in range(1, 16):
        s = s + in_ref[k]
    q_ref[...] = s[0:64]
    gram_ref[...] = s[64:96]


def factor_kernel(gram_ref, p_ref, phat_ref, ph2_ref, linv_ref):
    gp = gram_ref[...] * 0.25
    n = 64
    left = jnp.concatenate([gp, pltpu.roll(gp, 64, 1)], axis=0)
    row = lax.broadcasted_iota(jnp.int32, (n, 2 * n), 0)
    lane = lax.broadcasted_iota(jnp.int32, (n, 2 * n), 1)
    a = jnp.where(lane < n, left, jnp.where(lane == row + n, 1.0, 0.0))
    for k in range(n):
        d = a[k : k + 1, k : k + 1]
        r = lax.rsqrt(d)
        r = r * (1.5 - 0.5 * d * r * r)
        rowk = a[k : k + 1, :] * r
        f = jnp.where(row > k, a[:, k : k + 1] * r, 0.0)
        a = jnp.where(row == k, rowk, a - f * rowk)
    linv = pltpu.roll(a, 64, 1)[:, 0:n]
    linv_ref[...] = linv
    phat = jnp.dot(linv, p_ref[...], precision=HIGH, preferred_element_type=F32)
    phat_ref[...] = phat
    hi = phat.astype(BF)
    ph2_ref[0:64] = hi
    ph2_ref[64:128] = (phat - hi.astype(F32)).astype(BF)


def q_scale_kernel(q0, q1, q2, q3, linv_ref, out_ref):
    s = ((q0[...] + q2[...]) + (q1[...] + q3[...])) * (1.0 / 16.0)
    q = jnp.dot(linv_ref[...], s, precision=HIGH, preferred_element_type=F32).astype(BF)
    for k in range(16):
        out_ref[k] = q


def error_kernel(
    idx_ref, at_ref, ph2_ref, qa_ref, qb_ref, ga0, ga1, ga2, ga3, gb0, gb1, gb2, gb3, e_hbm, err_hbm, qf_ref,
    e_buf, g_buf, o_buf, sems
):
    w = e_buf.shape[2]
    gs = (ga0, ga1, ga2, ga3, gb0, gb1, gb2, gb3)

    def cols(j):
        return pl.ds(pl.multiple_of(idx_ref[j] * w, w), w)

    cps = []
    for j in range(8):
        a = pltpu.make_async_copy(e_hbm.at[:, cols(j)], e_buf.at[j], sems.at[j])
        b = pltpu.make_async_copy(gs[j], g_buf.at[j], sems.at[8 + j])
        a.start()
        b.start()
        cps.append((a, b))
    at = at_ref[...]
    ph = -(ph2_ref[...].T)
    outs = []
    for j in range(8):
        src = qa_ref if j < 4 else qb_ref
        base = (idx_ref[j] // 2) * 4
        q = jnp.concatenate([src[base + y] for y in range(4)], axis=1)
        if j == 0:
            qf_ref[...] = q.astype(F32)
        q2 = jnp.concatenate([q, q], axis=0)
        cps[j][0].wait()
        cps[j][1].wait()
        m = dot(at, g_buf[j], 1, 0) * (1.0 / 512.0) + e_buf[j].astype(F32)
        o_buf[j] = (m + dot(ph, q2, 1, 0)).astype(BF)
        o = pltpu.make_async_copy(o_buf.at[j], err_hbm.at[:, cols(j)], sems.at[16 + j])
        o.start()
        outs.append(o)
    for o in outs:
        o.wait()


def shift(v, axis, k):
    n = lax.axis_size(axis)
    return lax.ppermute(v, axis, [(i, (i + k) % n) for i in range(n)])


def swap(v):
    return lax.ppermute(v, "core", [(0, 1), (1, 0)])


def exchange(v, axes):
    return lax.all_to_all(v, axes, 0, 0, tiled=True)


def on_device(attn_out, grad_top, branch_grad, error_prev, q_prev):
    x = lax.axis_index("x")
    c = lax.axis_index("core")
    last = (lax.axis_index("pipe") == 1).astype(jnp.int32).reshape(1)
    act = attn_out.reshape(512, 512)
    top = grad_top.reshape(512, 512)
    br = branch_grad.reshape(512, 512)
    err = error_prev.reshape(512, 4096)
    qt = q_prev[0].T
    ks = jnp.arange(4, dtype=jnp.int32)
    xs = (x - ks) % 4
    idx = jnp.concatenate([xs * 2 + c, xs * 2 + (1 - c)]).astype(jnp.int32)

    sent = (top.astype(F32) + br.astype(F32)).astype(BF)
    recv = lax.ppermute(sent, "pipe", [(1, 0)])

    qa = jnp.stack([qt] + [shift(qt, "x", k) for k in (1, 2, 3)])
    qb = swap(qa)

    grad, grad_in, u = pl.pallas_call(
        grad_kernel,
        out_shape=(sds((512, 512), BF), sds((512, 512), BF), sds((64, 512), F32)),
        in_specs=[SMEM, VMEM, VMEM, VMEM, VMEM],
        out_specs=(VMEM, VMEM, VMEM),
        compiler_params=params(16),
        name="grad_kernel",
    )(last, top, recv, br, qt)

    u = u + swap(u)
    us = [u] + [shift(u, "x", k) for k in (1, 2, 3)]

    ga = [grad] + [shift(grad, "x", k) for k in (1, 2, 3)]
    gb = [swap(g) for g in ga]

    eq, act_t = pl.pallas_call(
        eq_kernel,
        out_shape=(sds((64, 512), F32), sds((512, 512), BF)),
        in_specs=[SMEM, VMEM, VMEM, VMEM, ANY],
        out_specs=(VMEM, VMEM),
        scratch_shapes=[pltpu.VMEM((8, 512, 512), BF), pltpu.SemaphoreType.DMA((8,))],
        compiler_params=params(24),
        name="eq_kernel",
    )(idx, qa, qb, act, err)

    p4 = pl.pallas_call(
        p_kernel,
        out_shape=sds((4, 64, 512), F32),
        in_specs=[VMEM] * 6,
        out_specs=VMEM,
        compiler_params=params(16),
        name="p_kernel",
    )(*us, act, eq)
    p4 = exchange(p4, "y")
    p4 = pl.pallas_call(
        sum_kernel, out_shape=sds((4, 64, 512), F32), in_specs=[VMEM], out_specs=VMEM, name="sum_kernel"
    )(p4)
    p4 = exchange(p4, "zhi")

    scratch = [pltpu.VMEM((4, 512, 512), BF), pltpu.VMEM((4, 512, 512), BF), pltpu.SemaphoreType.DMA((8,))]
    send, p, p3, v3, gram = pl.pallas_call(
        q_send_kernel,
        out_shape=(
            sds((4, 4, 96, 128), F32),
            sds((64, 512), F32),
            sds((192, 512), BF),
            sds((192, 512), BF),
            sds((32, 128), F32),
        ),
        in_specs=[SMEM, VMEM, VMEM] + [ANY] * 5,
        out_specs=(VMEM,) * 5,
        scratch_shapes=scratch,
        compiler_params=params(24),
        name="q_send_kernel",
    )(idx, p4, act, *gb, err)
    arrived = swap(send)
    keep = pl.pallas_call(
        q_keep_kernel,
        out_shape=sds((4, 4, 96, 128), F32),
        in_specs=[SMEM, VMEM, VMEM, VMEM] + [ANY] * 5,
        out_specs=VMEM,
        scratch_shapes=scratch,
        compiler_params=params(24),
        name="q_keep_kernel",
    )(idx, p3, v3, gram, *ga, err)
    chunks = exchange((keep + arrived).reshape(16, 96, 128), ("x", "y"))

    q_part, gram = pl.pallas_call(
        chunk_sum_kernel,
        out_shape=(sds((64, 128), F32), sds((32, 128), F32)),
        in_specs=[VMEM],
        out_specs=(VMEM, VMEM),
        name="chunk_sum_kernel",
    )(chunks)
    qs = [q_part] + [shift(q_part, "zhi", k) for k in (1, 2, 3)]
    phat, ph2, linv = pl.pallas_call(
        factor_kernel,
        out_shape=(sds((64, 512), F32), sds((128, 512), BF), sds((64, 64), F32)),
        in_specs=[VMEM, VMEM],
        out_specs=(VMEM, VMEM, VMEM),
        name="factor_kernel",
    )(gram, p)
    q16 = pl.pallas_call(
        q_scale_kernel,
        out_shape=sds((16, 64, 128), BF),
        in_specs=[VMEM] * 5,
        out_specs=VMEM,
        name="q_scale_kernel",
    )(*qs, linv)
    qfa = exchange(q16, ("x", "y"))
    qfb = swap(qfa)

    error_next, q_own = pl.pallas_call(
        error_kernel,
        out_shape=(sds((512, 4096), BF), sds((64, 512), F32)),
        in_specs=[SMEM, VMEM, VMEM, VMEM, VMEM] + [ANY] * 9,
        out_specs=(ANY, VMEM),
        scratch_shapes=[
            pltpu.VMEM((8, 512, 512), BF),
            pltpu.VMEM((8, 512, 512), BF),
            pltpu.VMEM((8, 512, 512), BF),
            pltpu.SemaphoreType.DMA((24,)),
        ],
        compiler_params=params(32),
        name="error_kernel",
    )(idx, act_t, ph2, qfa, qfb, *ga, *gb, err)
    return (
        grad_in.reshape(branch_grad.shape),
        error_next.reshape(error_prev.shape),
        phat.T[None],
        q_own.T[None],
    )


def solution(mesh):
    fine = Mesh(mesh.devices.reshape(2, 4, 2, 4, 4), ("pipe", "x", "core", "zhi", "y"))
    tensor = ("x", "core")
    dp = ("zhi", "y")
    return jax.shard_map(
        on_device,
        mesh=fine,
        in_specs=(
            P("pipe", None, dp, tensor),
            P(None, dp, tensor),
            P("pipe", None, dp, tensor),
            P("pipe", dp, tensor, None),
            P("pipe", tensor, None),
        ),
        out_specs=(
            P("pipe", None, dp, tensor),
            P("pipe", dp, tensor, None),
            P("pipe", tensor, None),
            P("pipe", tensor, None),
        ),
        check_vma=False,
    )
```

time: 319 us -> 155 us (0.49); the launches traced: 315 us -> 154 us
  blocking collectives: 146 us -> 28.2 us
  matrix products: 61.3 us -> 0 us
  Pallas kernels: 0 us -> 33.1 us
  waiting for transfers between devices: 44.6 us -> 25.2 us
  other arithmetic: 21.1 us -> 2.55 us
  starting transfers between devices: 29.3 us -> 42.7 us
  local copies, waits for them, and re-layouts: 11.9 us -> 21.3 us
    all_to_all x6 -> x2, blocking collectives: 146 us -> 28.2 us  [exchange(): return lax.all_to_all(v, axes, 0, 0, tiled=True)]
    dot_general x9 -> x0, matrix products: 61 us -> none  [the longest x5 35.3 us: on_device(): lax.dot_general(acts, collect(out_grad, 'tensor', 1), (((0,), (0,)), ((),...]
    pallas_call x0 -> x10, Pallas kernels: none -> 33.1 us  [the longest x1 8.08 us: on_device(): pl.pallas_call(error_kernel, out_shape=(sds((512, 4096), BF), sds((64, 51...]
    ppermute x4 -> x21, starting transfers between devices: 5.12 us -> 30.3 us  [the longest x12 17.5 us: shift(): return lax.ppermute(v, axis, [(i, (i + k) % n) for i in range(n)])]
    unnamed x15 -> x48, local copies, waits for them, and re-layouts: 1.22 us -> 21.3 us
    all_to_all x5 -> x2, waiting for transfers between devices: 23.9 us -> 11.6 us  [exchange(): return lax.all_to_all(v, axes, 0, 0, tiled=True)]
    all_to_all x5 -> x2, starting transfers between devices: 24.2 us -> 12.4 us  [exchange(): return lax.all_to_all(v, axes, 0, 0, tiled=True)]
    another operation x5 -> x1, other arithmetic: 12.1 us -> 0.96 us  [on_device(): qa = jnp.stack([qt] + [shift(qt, 'x', k) for k in (1, 2, 3)])]
  transfers between devices with their start and end apart: 9 -> 23, of which waited for: 8 -> 7; matrix products, arithmetic and copies ran while one was open for 9% -> 1% of each run, Pallas kernels for 0% -> 11%
where the time goes in v1:
time: 155 us; the launch traced here: 154 us
  starting transfers between devices  42.7 us (28%)
  Pallas kernels  33.1 us (21%)
  blocking collectives  28.2 us (18%)
  waiting for transfers between devices  25.2 us (16%)
  local copies, waits for them, and re-layouts  21.3 us (14%)
  other arithmetic  2.55 us (2%)
    all_to_all x2, blocking collectives, exchange(): return lax.all_to_all(v, axes, 0, 0, tiled=True)  28.2 us
    unnamed x48, local copies, waits for them, and re-layouts  21.3 us
    ppermute x12, starting transfers between devices, shift(): return lax.ppermute(v, axis, [(i, (i + k) % n) for i in range(n)])  17.5 us
    all_to_all x2, starting transfers between devices, exchange(): return lax.all_to_all(v, axes, 0, 0, tiled=True)  12.4 us
    all_to_all x2, waiting for transfers between devices, exchange(): return lax.all_to_all(v, axes, 0, 0, tiled=True)  11.6 us
    ppermute x8, starting transfers between devices, swap(): return lax.ppermute(v, 'core', [(0, 1), (1, 0)])  11.6 us
    ppermute x12, waiting for transfers between devices, shift(): return lax.ppermute(v, axis, [(i, (i + k) % n) for i in range(n)])  11.5 us
    pallas_call x1, Pallas kernels, on_device(): pl.pallas_call(error_kernel, out_shape=(sds((512, 4096), BF), sds((64, 51...  8.08 us
  transfers between devices with their start and end apart: 23, of which 7 were waited for; matrix products, arithmetic and copies ran while one was open for 1% of the time, Pallas kernels for 11%

profile of v1, /device:TPU:1, one launch (start us, length us, event | category | flops | bytes accessed | tf_op | source)
XLA Modules:
  0.0 154.1 jit_solution(1047308347620032732)
XLA Ops:
  0.6 1.4 add_convert_fusion
  2.0 1.3 collective-permute-start
  3.3 3.7 %collective-permute-start.2 = (f32[64,512]{1,0:T(8,128)}, f32[64,512]{1,0:T(8,128)S(1)}, u32[]{:S(2)}, u32[]{:S(2)}) collective-permute-start(f32[64,512]{1,0:T(8,128)} %bitcast.33), channel_id=1, source_target_pairs={{0,64},{32,96},{64,0},{96,32},{1,65},{33,97},{65,1},{97,33},{2,66}... | collective-permute-start | bytes 393224 | tf_op jit(solution)/shard_map/ppermute | solution.py:232
  7.3 2.4 %collective-permute-start.3 = (f32[64,512]{1,0:T(8,128)}, f32[64,512]{1,0:T(8,128)S(1)}, u32[]{:S(2)}, u32[]{:S(2)}) collective-permute-start(f32[64,512]{1,0:T(8,128)} %bitcast.35), channel_id=1, source_target_pairs={{0,96},{32,0},{64,32},{96,64},{1,97},{33,1},{65,33},{97,65},{2,98}... | collective-permute-start | bytes 393224 | tf_op jit(solution)/shard_map/ppermute | solution.py:232
  9.7 4.7 %collective-permute-done.1 = f32[64,512]{1,0:T(8,128)S(1)} collective-permute-done((f32[64,512]{1,0:T(8,128)}, f32[64,512]{1,0:T(8,128)S(1)}, u32[]{:S(2)}, u32[]{:S(2)}) %collective-permute-start.1) | collective-permute-done | bytes 131104 | tf_op jit(solution)/shard_map/ppermute | solution.py:232
  15.4 1.4 collective-permute-start.4
  20.8 1.9 %collective-permute-start.5 = (f32[64,512]{1,0:T(8,128)S(1)}, f32[64,512]{1,0:T(8,128)S(1)}, u32[]{:S(2)}, u32[]{:S(2)}) collective-permute-start(f32[64,512]{1,0:T(8,128)S(1)} %get-tuple-element.23), channel_id=1, source_target_pairs={{0,16},{16,0},{1,17},{17,1},{2,18},{18,2},{3,19},{19,3},{4,20},{20... | collective-permute-start | bytes 393224 | tf_op jit(solution)/shard_map/ppermute | solution.py:236
  23.6 3.0 %collective-permute-start.8 = (f32[64,512]{1,0:T(8,128)S(1)}, f32[64,512]{1,0:T(8,128)S(1)}, u32[]{:S(2)}, u32[]{:S(2)}) collective-permute-start(f32[64,512]{1,0:T(8,128)S(1)} %add.33.u0), channel_id=1, source_target_pairs={{0,96},{32,0},{64,32},{96,64},{1,97},{33,1},{65,33},{97,65},{2,98}... | collective-permute-start | bytes 393224 | tf_op jit(solution)/shard_map/ppermute | solution.py:232
  27.9 2.2 %copy-done = bf16[1,1,512,4096]{3,2,1,0:T(8,128)(2,1)S(1)} copy-done((bf16[1,1,512,4096]{3,2,1,0:T(8,128)(2,1)S(1)}, bf16[1,1,512,4096]{3,2,1,0:T(8,128)(2,1)}, u32[]{:S(2)}) %copy-start) | copy-done | bytes 4194328
  30.1 3.3 %eq_kernel.1 = (f32[64,512]{1,0:T(8,128)S(1)}, bf16[512,512]{1,0:T(8,128)(2,1)S(1)}) custom-call(s32[8]{0:T(128)S(1)} %pad_add_fusion.idx_ref, f32[4,64,512]{2,1,0:T(8,128)S(1)} %pad_maximum_fusion.qa_ref, f32[4,64,512]{2,1,0:T(8,128)S(1)} %collective-permute-done.4.qb_ref, bf16[512,512]{1,0:T(8,128)(2,1)S(1)} %bitcast.28, bf16[512,4096]{1,0:T(8,128)(2,1)S(1)} %bitcast.24), custom_call_target="tpu_custom_call" | custom-call | tf_op jit(solution)/shard_map/eq_kernel/pallas_call | solution.py:277
  34.2 2.2 %collective-permute-done.6.u1 = f32[64,512]{1,0:T(8,128)S(1)} collective-permute-done((f32[64,512]{1,0:T(8,128)S(1)}, f32[64,512]{1,0:T(8,128)S(1)}, u32[]{:S(2)}, u32[]{:S(2)}) %collective-permute-start.6) | collective-permute-done | bytes 131104 | tf_op jit(solution)/shard_map/ppermute | solution.py:232
  37.5 4.2 %all-to-all-start = ((f32[4,64,512]{2,1,0:T(8,128)}), f32[4,64,512]{2,1,0:T(8,128)S(1)}, u32[]{:S(2)}, u32[]{:S(2)}) async-start(f32[4,64,512]{2,1,0:T(8,128)} %p_kernel.1), calls=%async_computation | async-start | bytes 1048576 | tf_op jit(solution)/shard_map/all_to_all | solution.py:240
  43.1 7.3 %all-to-all-done.in_ref = f32[4,64,512]{2,1,0:T(8,128)S(1)} async-done(((f32[4,64,512]{2,1,0:T(8,128)}), f32[4,64,512]{2,1,0:T(8,128)S(1)}, u32[]{:S(2)}, u32[]{:S(2)}) %all-to-all-start) | async-done | bytes 524320 | tf_op jit(solution)/shard_map/all_to_all | solution.py:240
  51.2 1.9 %sum_kernel.1 = f32[4,64,512]{2,1,0:T(8,128)} custom-call(f32[4,64,512]{2,1,0:T(8,128)} %copy-done.20), custom_call_target="tpu_custom_call" | custom-call | tf_op jit(solution)/shard_map/sum_kernel/pallas_call | solution.py:296
  53.1 8.2 %all-to-all-start.1 = ((f32[4,64,512]{2,1,0:T(8,128)}), f32[4,64,512]{2,1,0:T(8,128)}, u32[]{:S(2)}, u32[]{:S(2)}) async-start(f32[4,64,512]{2,1,0:T(8,128)} %sum_kernel.1), calls=%async_computation.1 | async-start | bytes 1048576 | tf_op jit(solution)/shard_map/all_to_all | solution.py:240
  61.3 1.9 %collective-permute-start.9 = (bf16[512,512]{1,0:T(8,128)(2,1)S(1)}, bf16[512,512]{1,0:T(8,128)(2,1)S(1)}, u32[]{:S(2)}, u32[]{:S(2)}) collective-permute-start(bf16[512,512]{1,0:T(8,128)(2,1)S(1)} %get-tuple-element.25.g0.ga0), channel_id=1, source_target_pairs={{0,16},{16,0},{1,17},{17,1},{2,18},{18,2},{3,19},{19,3},{4,20},{20... | collective-permute-start | bytes 1572872 | tf_op jit(solution)/shard_map/ppermute | solution.py:236
  63.7 4.5 %collective-permute-done.10.g1.ga1 = bf16[512,512]{1,0:T(8,128)(2,1)S(1)} collective-permute-done((bf16[512,512]{1,0:T(8,128)(2,1)S(1)}, bf16[512,512]{1,0:T(8,128)(2,1)S(1)}, u32[]{:S(2)}, u32[]{:S(2)}) %collective-permute-start.10) | collective-permute-done | bytes 524320 | tf_op jit(solution)/shard_map/ppermute | solution.py:232
  71.2 4.3 %all-to-all-done.1.pz_ref = f32[4,64,512]{2,1,0:T(8,128)} async-done(((f32[4,64,512]{2,1,0:T(8,128)}), f32[4,64,512]{2,1,0:T(8,128)}, u32[]{:S(2)}, u32[]{:S(2)}) %all-to-all-start.1) | async-done | bytes 524320 | tf_op jit(solution)/shard_map/all_to_all | solution.py:240
  75.5 2.2 %copy-done.1 = bf16[1,1,512,4096]{3,2,1,0:T(8,128)(2,1)S(1)} copy-done((bf16[1,1,512,4096]{3,2,1,0:T(8,128)(2,1)S(1)}, bf16[1,1,512,4096]{3,2,1,0:T(8,128)(2,1)}, u32[]{:S(2)}) %copy-start.1) | copy-done | bytes 4194328
  80.8 3.8 %q_send_kernel.1 = (f32[4,4,96,128]{3,2,1,0:T(8,128)S(1)}, f32[64,512]{1,0:T(8,128)S(1)}, bf16[192,512]{1,0:T(8,128)(2,1)S(1)}, bf16[192,512]{1,0:T(8,128)(2,1)S(1)}, f32[32,128]{1,0:T(8,128)S(1)}) custom-call(s32[8]{0:T(128)S(1)} %pad_add_fusion.idx_ref, f32[4,64,512]{2,1,0:T(8,128)} %all-to-all-done.1.pz_ref, bf16[512,512]{1,0:T(8,128)(2,1)S(1)} %bitcast.30, ...), custom_call_target="tpu_custom_call" | custom-call | tf_op jit(solution)/shard_map/q_send_kernel/pallas_call | solution.py:302
  84.6 2.1 %collective-permute-start.16 = (f32[4,4,96,128]{3,2,1,0:T(8,128)S(1)}, f32[4,4,96,128]{3,2,1,0:T(8,128)S(1)}, u32[]{:S(2)}, u32[]{:S(2)}) collective-permute-start(f32[4,4,96,128]{3,2,1,0:T(8,128)S(1)} %get-tuple-element.29), channel_id=1, source_target_pairs={{0,16},{16,0},{1,17},{17,1},{2,18},{18,2},{3,19},{19,3},{4,20},{20... | collective-permute-start | bytes 2359304 | tf_op jit(solution)/shard_map/ppermute | solution.py:236
  86.8 2.6 %q_keep_kernel.1 = f32[4,4,96,128]{3,2,1,0:T(8,128)S(1)} custom-call(s32[8]{0:T(128)S(1)} %pad_add_fusion.idx_ref, bf16[192,512]{1,0:T(8,128)(2,1)S(1)} %get-tuple-element.26.p3_ref, bf16[192,512]{1,0:T(8,128)(2,1)S(1)} %get-tuple-element.27.v3_ref, f32[32,128]{1,0:T(8,128)S(1)} %get-tuple-element.28.gram_ref, ...), custom_call_target="tpu_custom_call" | custom-call | tf_op jit(solution)/shard_map/q_keep_kernel/pallas_call | solution.py:318
  89.6 17.0 %all_to_all.20.in_ref = f32[16,96,128]{2,1,0:T(8,128)} all-to-all(f32[16,96,128]{2,1,0:T(8,128)S(1)} %bitcast.38), channel_id=1, replica_groups=mesh['pipe'=2,'x'=4,'core'=2,'zhi'=4,'y'=4] {'x','y'}, dimensions={0} | all-to-all | bytes 1572864 | tf_op jit(solution)/shard_map/all_to_all | solution.py:240
  106.6 1.8 %chunk_sum_kernel.1 = (f32[64,128]{1,0:T(8,128)}, f32[32,128]{1,0:T(8,128)}) custom-call(f32[16,96,128]{2,1,0:T(8,128)} %all_to_all.20.in_ref), custom_call_target="tpu_custom_call" | custom-call | tf_op jit(solution)/shard_map/chunk_sum_kernel/pallas_call | solution.py:329
  108.3 2.3 %collective-permute-start.19 = (f32[64,128]{1,0:T(8,128)}, f32[64,128]{1,0:T(8,128)S(1)}, u32[]{:S(2)}, u32[]{:S(2)}) collective-permute-start(f32[64,128]{1,0:T(8,128)} %get-tuple-element.33.q0), channel_id=1, source_target_pairs={{0,12},{4,0},{8,4},{12,8},{1,13},{5,1},{9,5},{13,9},{2,14},{6,2},{... | collective-permute-start | bytes 98312 | tf_op jit(solution)/shard_map/ppermute | solution.py:232
  110.6 3.3 %collective-permute-start.18 = (f32[64,128]{1,0:T(8,128)}, f32[64,128]{1,0:T(8,128)S(1)}, u32[]{:S(2)}, u32[]{:S(2)}) collective-permute-start(f32[64,128]{1,0:T(8,128)} %get-tuple-element.33.q0), channel_id=1, source_target_pairs={{0,8},{4,12},{8,0},{12,4},{1,9},{5,13},{9,1},{13,5},{2,10},{6,14},... | collective-permute-start | bytes 98312 | tf_op jit(solution)/shard_map/ppermute | solution.py:232
  113.9 7.7 %factor_kernel.1 = (f32[64,512]{1,0:T(8,128)}, bf16[128,512]{1,0:T(8,128)(2,1)}, f32[64,64]{1,0:T(8,128)}) custom-call(f32[32,128]{1,0:T(8,128)} %get-tuple-element.30.gram_ref, f32[64,512]{1,0:T(8,128)} %copy-done.19), custom_call_target="tpu_custom_call" | custom-call | tf_op jit(solution)/shard_map/factor_kernel/pallas_call | solution.py:337
  122.2 1.7 %q_scale_kernel.1 = bf16[16,64,128]{2,1,0:T(8,128)(2,1)} custom-call(f32[64,128]{1,0:T(8,128)} %get-tuple-element.33.q0, f32[64,128]{1,0:T(8,128)} %copy-done.23, f32[64,128]{1,0:T(8,128)} %copy-done.22, f32[64,128]{1,0:T(8,128)} %copy-done.21, f32[64,64]{1,0:T(8,128)} %get-tuple-element.34.linv_ref), custom_call_target="tpu_custom_call" | custom-call | tf_op jit(solution)/shard_map/q_scale_kernel/pallas_call | solution.py:344
  124.0 11.2 %all_to_all.21.qa_ref = bf16[16,64,128]{2,1,0:T(8,128)(2,1)S(1)} all-to-all(bf16[16,64,128]{2,1,0:T(8,128)(2,1)} %q_scale_kernel.1), channel_id=1, replica_groups=mesh['pipe'=2,'x'=4,'core'=2,'zhi'=4,'y'=4] {'x','y'}, dimensions={0} | all-to-all | bytes 524288 | tf_op jit(solution)/shard_map/all_to_all | solution.py:240
  135.2 3.2 %collective-permute-start.20 = (bf16[16,64,128]{2,1,0:T(8,128)(2,1)S(1)}, bf16[16,64,128]{2,1,0:T(8,128)(2,1)S(1)}, u32[]{:S(2)}, u32[]{:S(2)}) collective-permute-start(bf16[16,64,128]{2,1,0:T(8,128)(2,1)S(1)} %all_to_all.21.qa_ref), channel_id=1, source_target_pairs={{0,16},{16,0},{1,17},{17,1},{2,18},{18,2},{3,19},{19,3},{4,20},{20... | collective-permute-start | bytes 786440 | tf_op jit(solution)/shard_map/ppermute | solution.py:236
  139.6 2.2 %copy-done.2 = bf16[1,1,512,4096]{3,2,1,0:T(8,128)(2,1)S(1)} copy-done((bf16[1,1,512,4096]{3,2,1,0:T(8,128)(2,1)S(1)}, bf16[1,1,512,4096]{3,2,1,0:T(8,128)(2,1)}, u32[]{:S(2)}) %copy-start.2) | copy-done | bytes 4194328
  145.8 8.1 %error_kernel.1 = (bf16[512,4096]{1,0:T(8,128)(2,1)}, f32[64,512]{1,0:T(8,128)}) custom-call(s32[8]{0:T(128)S(1)} %pad_add_fusion.idx_ref, bf16[512,512]{1,0:T(8,128)(2,1)S(1)} %copy-done.16, bf16[128,512]{1,0:T(8,128)(2,1)S(1)} %copy-done.18, bf16[16,64,128]{2,1,0:T(8,128)(2,1)S(1)} %all_to_all.21.qa_ref, ...), custom_call_target="tpu_custom_call" | custom-call | tf_op jit(solution)/shard_map/error_kernel/pallas_call | solution.py:354
  (80 shorter events, 24.1 us)
Async XLA Ops:
  0.6 27.2 %copy-start.3 = (bf16[1,4,128,512]{3,2,1,0:T(8,128)(2,1)S(1)}, bf16[1,4,128,512]{3,2,1,0:T(8,128)(2,1)}, u32[]{:S(2)}) copy-start(bf16[1,4,128,512]{3,2,1,0:T(8,128)(2,1)} %param.5) | copy-start | bytes 1572868
  2.0 14.8 %collective-permute-start = (bf16[512,512]{1,0:T(8,128)(2,1)S(1)}, bf16[512,512]{1,0:T(8,128)(2,1)S(1)}, u32[]{:S(2)}, u32[]{:S(2)}) collective-permute-start(bf16[512,512]{1,0:T(8,128)(2,1)S(1)} %add_convert_fusion), channel_id=1, source_target_pairs={{128,0},{129,1},{130,2},{131,3},{132,4},{133,5},{134,6},{135,7},{1... | collective-permute-start | bytes 1572872 | tf_op jit(solution)/shard_map/ppermute | solution.py:257
  3.3 6.3 %collective-permute-start.2 = (f32[64,512]{1,0:T(8,128)}, f32[64,512]{1,0:T(8,128)S(1)}, u32[]{:S(2)}, u32[]{:S(2)}) collective-permute-start(f32[64,512]{1,0:T(8,128)} %bitcast.33), channel_id=1, source_target_pairs={{0,64},{32,96},{64,0},{96,32},{1,65},{33,97},{65,1},{97,33},{2,66}... | collective-permute-start | bytes 393224 | tf_op jit(solution)/shard_map/ppermute | solution.py:232
  7.0 7.4 %collective-permute-start.1 = (f32[64,512]{1,0:T(8,128)}, f32[64,512]{1,0:T(8,128)S(1)}, u32[]{:S(2)}, u32[]{:S(2)}) collective-permute-start(f32[64,512]{1,0:T(8,128)} %bitcast.34), channel_id=1, source_target_pairs={{0,32},{32,64},{64,96},{96,0},{1,33},{33,65},{65,97},{97,1},{2,34}... | collective-permute-start | bytes 393224 | tf_op jit(solution)/shard_map/ppermute | solution.py:232
  7.3 7.1 %collective-permute-start.3 = (f32[64,512]{1,0:T(8,128)}, f32[64,512]{1,0:T(8,128)S(1)}, u32[]{:S(2)}, u32[]{:S(2)}) collective-permute-start(f32[64,512]{1,0:T(8,128)} %bitcast.35), channel_id=1, source_target_pairs={{0,96},{32,0},{64,32},{96,64},{1,97},{33,1},{65,33},{97,65},{2,98}... | collective-permute-start | bytes 393224 | tf_op jit(solution)/shard_map/ppermute | solution.py:232
  15.4 12.5 %collective-permute-start.4 = (f32[4,64,512]{2,1,0:T(8,128)S(1)}, f32[4,64,512]{2,1,0:T(8,128)S(1)}, u32[]{:S(2)}, u32[]{:S(2)}) collective-permute-start(f32[4,64,512]{2,1,0:T(8,128)S(1)} %pad_maximum_fusion.qa_ref), channel_id=1, source_target_pairs={{0,16},{16,0},{1,17},{17,1},{2,18},{18,2},{3,19},{19,3},{4,20},{20... | collective-permute-start | bytes 1572872 | tf_op jit(solution)/shard_map/ppermute | solution.py:236
  16.8 1.0 copy-start.4
  17.8 1.0 copy-start.5
  20.8 2.9 %collective-permute-start.5 = (f32[64,512]{1,0:T(8,128)S(1)}, f32[64,512]{1,0:T(8,128)S(1)}, u32[]{:S(2)}, u32[]{:S(2)}) collective-permute-start(f32[64,512]{1,0:T(8,128)S(1)} %get-tuple-element.23), channel_id=1, source_target_pairs={{0,16},{16,0},{1,17},{17,1},{2,18},{18,2},{3,19},{19,3},{4,20},{20... | collective-permute-start | bytes 393224 | tf_op jit(solution)/shard_map/ppermute | solution.py:236
  23.6 10.6 %collective-permute-start.8 = (f32[64,512]{1,0:T(8,128)S(1)}, f32[64,512]{1,0:T(8,128)S(1)}, u32[]{:S(2)}, u32[]{:S(2)}) collective-permute-start(f32[64,512]{1,0:T(8,128)S(1)} %add.33.u0), channel_id=1, source_target_pairs={{0,96},{32,0},{64,32},{96,64},{1,97},{33,1},{65,33},{97,65},{2,98}... | collective-permute-start | bytes 393224 | tf_op jit(solution)/shard_map/ppermute | solution.py:232
  26.6 7.5 %collective-permute-start.7 = (f32[64,512]{1,0:T(8,128)S(1)}, f32[64,512]{1,0:T(8,128)S(1)}, u32[]{:S(2)}, u32[]{:S(2)}) collective-permute-start(f32[64,512]{1,0:T(8,128)S(1)} %add.33.u0), channel_id=1, source_target_pairs={{0,64},{32,96},{64,0},{96,32},{1,65},{33,97},{65,1},{97,33},{2,66}... | collective-permute-start | bytes 393224 | tf_op jit(solution)/shard_map/ppermute | solution.py:232
  27.2 9.2 %collective-permute-start.6 = (f32[64,512]{1,0:T(8,128)S(1)}, f32[64,512]{1,0:T(8,128)S(1)}, u32[]{:S(2)}, u32[]{:S(2)}) collective-permute-start(f32[64,512]{1,0:T(8,128)S(1)} %add.33.u0), channel_id=1, source_target_pairs={{0,32},{32,64},{64,96},{96,0},{1,33},{33,65},{65,97},{97,1},{2,34}... | collective-permute-start | bytes 393224 | tf_op jit(solution)/shard_map/ppermute | solution.py:232
  27.9 2.2 %copy-start = (bf16[1,1,512,4096]{3,2,1,0:T(8,128)(2,1)S(1)}, bf16[1,1,512,4096]{3,2,1,0:T(8,128)(2,1)}, u32[]{:S(2)}) copy-start(bf16[1,1,512,4096]{3,2,1,0:T(8,128)(2,1)} %param.8) | copy-start | bytes 12582916
  37.5 13.0 %all-to-all-start = ((f32[4,64,512]{2,1,0:T(8,128)}), f32[4,64,512]{2,1,0:T(8,128)S(1)}, u32[]{:S(2)}, u32[]{:S(2)}) async-start(f32[4,64,512]{2,1,0:T(8,128)} %p_kernel.1), calls=%async_computation | async-start | bytes 1048576 | tf_op jit(solution)/shard_map/all_to_all | solution.py:240
  41.7 21.5 %collective-permute-start.14 = (bf16[512,512]{1,0:T(8,128)(2,1)S(1)}, bf16[512,512]{1,0:T(8,128)(2,1)S(1)}, u32[]{:S(2)}, u32[]{:S(2)}) collective-permute-start(bf16[512,512]{1,0:T(8,128)(2,1)S(1)} %get-tuple-element.25.g0.ga0), channel_id=1, source_target_pairs={{0,96},{32,0},{64,32},{96,64},{1,97},{33,1},{65,33},{97,65},{2,98}... | collective-permute-start | bytes 1572872 | tf_op jit(solution)/shard_map/ppermute | solution.py:232
  41.7 21.6 %collective-permute-start.12 = (bf16[512,512]{1,0:T(8,128)(2,1)S(1)}, bf16[512,512]{1,0:T(8,128)(2,1)S(1)}, u32[]{:S(2)}, u32[]{:S(2)}) collective-permute-start(bf16[512,512]{1,0:T(8,128)(2,1)S(1)} %get-tuple-element.25.g0.ga0), channel_id=1, source_target_pairs={{0,64},{32,96},{64,0},{96,32},{1,65},{33,97},{65,1},{97,33},{2,66}... | collective-permute-start | bytes 1572872 | tf_op jit(solution)/shard_map/ppermute | solution.py:232
  42.8 25.4 %collective-permute-start.10 = (bf16[512,512]{1,0:T(8,128)(2,1)S(1)}, bf16[512,512]{1,0:T(8,128)(2,1)S(1)}, u32[]{:S(2)}, u32[]{:S(2)}) collective-permute-start(bf16[512,512]{1,0:T(8,128)(2,1)S(1)} %get-tuple-element.25.g0.ga0), channel_id=1, source_target_pairs={{0,32},{32,64},{64,96},{96,0},{1,33},{33,65},{65,97},{97,1},{2,34}... | collective-permute-start | bytes 1572872 | tf_op jit(solution)/shard_map/ppermute | solution.py:232
  53.1 22.4 %all-to-all-start.1 = ((f32[4,64,512]{2,1,0:T(8,128)}), f32[4,64,512]{2,1,0:T(8,128)}, u32[]{:S(2)}, u32[]{:S(2)}) async-start(f32[4,64,512]{2,1,0:T(8,128)} %sum_kernel.1), calls=%async_computation.1 | async-start | bytes 1048576 | tf_op jit(solution)/shard_map/all_to_all | solution.py:240
  61.3 7.5 %collective-permute-start.9 = (bf16[512,512]{1,0:T(8,128)(2,1)S(1)}, bf16[512,512]{1,0:T(8,128)(2,1)S(1)}, u32[]{:S(2)}, u32[]{:S(2)}) collective-permute-start(bf16[512,512]{1,0:T(8,128)(2,1)S(1)} %get-tuple-element.25.g0.ga0), channel_id=1, source_target_pairs={{0,16},{16,0},{1,17},{17,1},{2,18},{18,2},{3,19},{19,3},{4,20},{20... | collective-permute-start | bytes 1572872 | tf_op jit(solution)/shard_map/ppermute | solution.py:236
  63.2 5.5 %collective-permute-start.15 = (bf16[512,512]{1,0:T(8,128)(2,1)S(1)}, bf16[512,512]{1,0:T(8,128)(2,1)S(1)}, u32[]{:S(2)}, u32[]{:S(2)}) collective-permute-start(bf16[512,512]{1,0:T(8,128)(2,1)S(1)} %collective-permute-done.14.g3.ga3), channel_id=1, source_target_pairs={{0,16},{16,0},{1,17},{17,1},{2,18},{18,2},{3,19},{19,3},{4,20},{20... | collective-permute-start | bytes 1572872 | tf_op jit(solution)/shard_map/ppermute | solution.py:236
  63.3 6.3 %collective-permute-start.13 = (bf16[512,512]{1,0:T(8,128)(2,1)S(1)}, bf16[512,512]{1,0:T(8,128)(2,1)S(1)}, u32[]{:S(2)}, u32[]{:S(2)}) collective-permute-start(bf16[512,512]{1,0:T(8,128)(2,1)S(1)} %collective-permute-done.12.g2.ga2), channel_id=1, source_target_pairs={{0,16},{16,0},{1,17},{17,1},{2,18},{18,2},{3,19},{19,3},{4,20},{20... | collective-permute-start | bytes 1572872 | tf_op jit(solution)/shard_map/ppermute | solution.py:236
  68.2 2.1 %collective-permute-start.11 = (bf16[512,512]{1,0:T(8,128)(2,1)S(1)}, bf16[512,512]{1,0:T(8,128)(2,1)S(1)}, u32[]{:S(2)}, u32[]{:S(2)}) collective-permute-start(bf16[512,512]{1,0:T(8,128)(2,1)S(1)} %collective-permute-done.10.g1.ga1), channel_id=1, source_target_pairs={{0,16},{16,0},{1,17},{17,1},{2,18},{18,2},{3,19},{19,3},{4,20},{20... | collective-permute-start | bytes 1572872 | tf_op jit(solution)/shard_map/ppermute | solution.py:236
  75.5 2.2 %copy-start.1 = (bf16[1,1,512,4096]{3,2,1,0:T(8,128)(2,1)S(1)}, bf16[1,1,512,4096]{3,2,1,0:T(8,128)(2,1)}, u32[]{:S(2)}) copy-start(bf16[1,1,512,4096]{3,2,1,0:T(8,128)(2,1)} %param.8) | copy-start | bytes 12582916
  77.7 1.0 copy-start.7
  84.6 4.9 %copy-start.19 = (f32[64,512]{1,0:T(8,128)}, f32[64,512]{1,0:T(8,128)S(1)}, u32[]{:S(2)}) copy-start(f32[64,512]{1,0:T(8,128)S(1)} %get-tuple-element.31.p_ref) | copy-start | bytes 393220
  84.6 4.8 %collective-permute-start.16 = (f32[4,4,96,128]{3,2,1,0:T(8,128)S(1)}, f32[4,4,96,128]{3,2,1,0:T(8,128)S(1)}, u32[]{:S(2)}, u32[]{:S(2)}) collective-permute-start(f32[4,4,96,128]{3,2,1,0:T(8,128)S(1)} %get-tuple-element.29), channel_id=1, source_target_pairs={{0,16},{16,0},{1,17},{17,1},{2,18},{18,2},{3,19},{19,3},{4,20},{20... | collective-permute-start | bytes 2359304 | tf_op jit(solution)/shard_map/ppermute | solution.py:236
  89.4 50.2 %copy-start.8 = (bf16[512,512]{1,0:T(8,128)(2,1)S(1)}, bf16[512,512]{1,0:T(8,128)(2,1)}, u32[]{:S(2)}) copy-start(bf16[512,512]{1,0:T(8,128)(2,1)} %copy-done.6) | copy-start | bytes 1572868
  108.3 13.3 %collective-permute-start.19 = (f32[64,128]{1,0:T(8,128)}, f32[64,128]{1,0:T(8,128)S(1)}, u32[]{:S(2)}, u32[]{:S(2)}) collective-permute-start(f32[64,128]{1,0:T(8,128)} %get-tuple-element.33.q0), channel_id=1, source_target_pairs={{0,12},{4,0},{8,4},{12,8},{1,13},{5,1},{9,5},{13,9},{2,14},{6,2},{... | collective-permute-start | bytes 98312 | tf_op jit(solution)/shard_map/ppermute | solution.py:232
  110.6 11.0 %collective-permute-start.18 = (f32[64,128]{1,0:T(8,128)}, f32[64,128]{1,0:T(8,128)S(1)}, u32[]{:S(2)}, u32[]{:S(2)}) collective-permute-start(f32[64,128]{1,0:T(8,128)} %get-tuple-element.33.q0), channel_id=1, source_target_pairs={{0,8},{4,12},{8,0},{12,4},{1,9},{5,13},{9,1},{13,5},{2,10},{6,14},... | collective-permute-start | bytes 98312 | tf_op jit(solution)/shard_map/ppermute | solution.py:232
  113.8 7.8 %collective-permute-start.17 = (f32[64,128]{1,0:T(8,128)}, f32[64,128]{1,0:T(8,128)S(1)}, u32[]{:S(2)}, u32[]{:S(2)}) collective-permute-start(f32[64,128]{1,0:T(8,128)} %get-tuple-element.33.q0), channel_id=1, source_target_pairs={{0,4},{4,8},{8,12},{12,0},{1,5},{5,9},{9,13},{13,1},{2,6},{6,10},{... | collective-permute-start | bytes 98312 | tf_op jit(solution)/shard_map/ppermute | solution.py:232
  135.2 4.4 %collective-permute-start.20 = (bf16[16,64,128]{2,1,0:T(8,128)(2,1)S(1)}, bf16[16,64,128]{2,1,0:T(8,128)(2,1)S(1)}, u32[]{:S(2)}, u32[]{:S(2)}) collective-permute-start(bf16[16,64,128]{2,1,0:T(8,128)(2,1)S(1)} %all_to_all.21.qa_ref), channel_id=1, source_target_pairs={{0,16},{16,0},{1,17},{17,1},{2,18},{18,2},{3,19},{19,3},{4,20},{20... | collective-permute-start | bytes 786440 | tf_op jit(solution)/shard_map/ppermute | solution.py:236
  139.6 2.2 %copy-start.2 = (bf16[1,1,512,4096]{3,2,1,0:T(8,128)(2,1)S(1)}, bf16[1,1,512,4096]{3,2,1,0:T(8,128)(2,1)}, u32[]{:S(2)}) copy-start(bf16[1,1,512,4096]{3,2,1,0:T(8,128)(2,1)} %param.8) | copy-start | bytes 12582916
  (15 other events, 12.8 us)

commit v2 on v1

v2 whole, which is shorter than its diff:
```python
import jax
import jax.numpy as jnp
from jax import lax
from jax.experimental import pallas as pl
from jax.experimental.pallas import tpu as pltpu
from jax.sharding import Mesh, PartitionSpec as P

BF = jnp.bfloat16
F32 = jnp.float32
HIGH = lax.Precision.HIGHEST
MIB = 1024 * 1024
ANY = pl.BlockSpec(memory_space=pl.ANY)
VMEM = pl.BlockSpec(memory_space=pltpu.VMEM)
SMEM = pl.BlockSpec(memory_space=pltpu.SMEM)


def sds(shape, dtype):
    return jax.ShapeDtypeStruct(shape, dtype)


def params(mib):
    return pltpu.CompilerParams(vmem_limit_bytes=mib * MIB)


def split3(v):
    h = v.astype(BF)
    r = v - h.astype(F32)
    m = r.astype(BF)
    l = (r - m.astype(F32)).astype(BF)
    return jnp.concatenate([h, m, l], axis=0)


def fold3(v):
    n = v.shape[0] // 3
    return v[:n] + (v[n : 2 * n] + v[2 * n :])


def dot(a, b, ca, cb):
    return lax.dot_general(a, b, (((ca,), (cb,)), ((), ())), preferred_element_type=F32)


def first_kernel(top_ref, br_ref, q_ref, qr_ref, s_ref, ua_ref, ub_ref):
    top = top_ref[...]
    s = (top.astype(F32) + br_ref[...].astype(F32)).astype(BF)
    s_ref[...] = s
    ub_ref[...] = fold3(dot(split3(qr_ref[...]), s, 1, 1))
    ua = fold3(dot(split3(q_ref[...]), top, 1, 1))
    ua_ref[...] = jnp.where(lax.axis_index("pipe") == 1, ua, 0.0)


def grad_kernel(top_ref, recv_ref, s_ref, br_ref, g_ref, gin_ref):
    last = lax.axis_index("pipe")

    @pl.when(last == 1)
    def _():
        g_ref[...] = top_ref[...]
        gin_ref[...] = s_ref[...]

    @pl.when(last == 0)
    def _():
        g = recv_ref[...]
        g_ref[...] = g
        gin_ref[...] = (g.astype(F32) + br_ref[...].astype(F32)).astype(BF)


def block_row(j):
    return lax.rem(lax.axis_index("x") + 4 - j % 4, 4)


def cols(j, w=512):
    c = lax.axis_index("core")
    owner = block_row(j) * 2 + (c if j < 4 else 1 - c)
    return pl.ds(pl.multiple_of(owner * w, w), w)


def eq_kernel(qa_ref, qb_ref, act_ref, e_ref, out_ref, at_ref):
    at_ref[...] = act_ref[...].T
    acc = None
    for j in range(8):
        q3 = split3(qa_ref[j] if j < 4 else qb_ref[j - 4])
        part = dot(q3, e_ref[:, cols(j)], 1, 1)
        acc = part if acc is None else acc + part
    out_ref[...] = fold3(acc)


def p_kernel(u0, u1, u2, u3, act_ref, eq_ref, out_ref):
    u = sum_of((u0, u1, u2, u3))
    p = fold3(dot(split3(u), act_ref[...], 1, 0)) * (1.0 / 512.0) + eq_ref[...]
    out_ref[...] = p


def sum_of(refs):
    a, b, c, d = refs
    return (a[...] + c[...]) + (b[...] + d[...])


def sum_kernel(a, b, c, d, out_ref):
    out_ref[...] = sum_of((a, b, c, d))


def put_chunks(out_ref, slot, r, gram):
    for y in range(4):
        out_ref[slot, y, 0:64, :] = r[:, y * 128 : (y + 1) * 128]
        out_ref[slot, y, 64:96, :] = gram


def half_kernel(e_ref, out_ref):
    for k in range(4):
        out_ref[k] = e_ref[:, cols(4 + k)]


def pv_kernel(z0, z1, z2, z3, act_ref, out_ref):
    p = sum_of((z0, z1, z2, z3)) * (1.0 / 16.0)
    out_ref[0] = p
    out_ref[1] = fold3(dot(split3(p), act_ref[...], 1, 1))


def q_own_kernel(pv_ref, e_ref, out_ref):
    p3 = split3(pv_ref[0])
    for k in range(4):
        out_ref[k] = fold3(dot(p3, e_ref[:, cols(k)], 1, 0))


def q_kernel(pv_ref, pvs_ref, r_ref, es_ref, g0, g1, g2a, g2b, g3, out_ref, gs_ref):
    v3 = split3(pv_ref[1] + pvs_ref[1])
    q3 = split3(pvs_ref[0])

    def gram_of(p3):
        return dot(p3, p3[0:64], 1, 1) + (dot(p3, p3[64:128], 1, 1) + dot(p3, p3[128:192], 1, 1))

    g = fold3(gram_of(split3(pv_ref[0])) + gram_of(q3))
    gram = jnp.concatenate([g[0:32], g[32:64]], axis=1)
    for k, gr in enumerate((g0, g1, None, g3)):
        if k == 2:
            vg = dot(v3[:, 0:256], g2a[...], 1, 0) + dot(v3[:, 256:512], g2b[...], 1, 0)
            gs_ref[k, 0:256] = g2a[...]
            gs_ref[k, 256:512] = g2b[...]
        else:
            vg = dot(v3, gr[...], 1, 0)
            gs_ref[k] = gr[...]
        r = fold3(dot(q3, es_ref[k], 1, 0) + vg * (1.0 / 512.0)) + r_ref[k]
        put_chunks(out_ref, block_row(k), r, gram)


def chunk_sum_kernel(in_ref, q_ref, gram_ref):
    s = in_ref[0]
    for k in range(1, 16):
        s = s + in_ref[k]
    q_ref[...] = s[0:64]
    gram_ref[...] = s[64:96]


def factor_kernel(gram_ref, p_ref, phat_ref, ph2_ref, linv_ref):
    gp = gram_ref[...] * 0.25
    n = 64
    left = jnp.concatenate([gp, pltpu.roll(gp, 64, 1)], axis=0)
    row = lax.broadcasted_iota(jnp.int32, (n, 2 * n), 0)
    lane = lax.broadcasted_iota(jnp.int32, (n, 2 * n), 1)
    a = jnp.where(lane < n, left, jnp.where(lane == row + n, 1.0, 0.0))
    for k in range(n):
        d = a[k : k + 1, k : k + 1]
        r = lax.rsqrt(d)
        r = r * (1.5 - 0.5 * d * r * r)
        rowk = a[k : k + 1, :] * r
        f = jnp.where(row > k, a[:, k : k + 1] * r, 0.0)
        a = jnp.where(row == k, rowk, a - f * rowk)
    linv = pltpu.roll(a, 64, 1)[:, 0:n]
    linv_ref[...] = linv
    phat = jnp.dot(linv, p_ref[0], precision=HIGH, preferred_element_type=F32)
    phat_ref[...] = phat
    hi = phat.astype(BF)
    ph2_ref[0:64] = hi
    ph2_ref[64:128] = (phat - hi.astype(F32)).astype(BF)


def q_scale_kernel(q0, q1, q2, q3, linv_ref, out_ref):
    s = sum_of((q0, q1, q2, q3)) * (1.0 / 16.0)
    q = jnp.dot(linv_ref[...], s, precision=HIGH, preferred_element_type=F32).astype(BF)
    for k in range(16):
        out_ref[k] = q


def matrix_kernel(at_ref, ga_ref, gb_ref, e_ref, m_ref):
    at = at_ref[...]
    for j in range(8):
        g = ga_ref[j] if j < 4 else gb_ref[j - 4]
        m_ref[j] = dot(at, g, 1, 0) * (1.0 / 512.0) + e_ref[:, cols(j)].astype(F32)


def error_kernel(ph2_ref, qa_ref, qb_ref, m_ref, err_hbm, qf_ref, o_buf, sems):
    ph = -(ph2_ref[...].T)
    outs = []
    for j in range(8):
        src = qa_ref if j < 4 else qb_ref
        base = block_row(j) * 4
        q = jnp.concatenate([src[base + y] for y in range(4)], axis=1)
        if j == 0:
            qf_ref[...] = q.astype(F32)
        q2 = jnp.concatenate([q, q], axis=0)
        o_buf[j] = (m_ref[j] + dot(ph, q2, 1, 0)).astype(BF)
        o = pltpu.make_async_copy(o_buf.at[j], err_hbm.at[:, cols(j)], sems.at[j])
        o.start()
        outs.append(o)
    for o in outs:
        o.wait()


def shift(v, axis, k):
    n = lax.axis_size(axis)
    return lax.ppermute(v, axis, [(i, (i + k) % n) for i in range(n)])


def swap(v):
    return lax.ppermute(v, "core", [(0, 1), (1, 0)])


def ring(v, axis):
    return [v] + [shift(v, axis, k) for k in (1, 2, 3)]


def exchange(v, axes):
    return lax.all_to_all(v, axes, 0, 0, tiled=True)


def on_device(attn_out, grad_top, branch_grad, error_prev, q_prev):
    act = attn_out.reshape(512, 512)
    top = grad_top.reshape(512, 512)
    br = branch_grad.reshape(512, 512)
    err = error_prev.reshape(512, 4096)
    qt = q_prev[0].T

    qr = lax.ppermute(qt, "pipe", [(0, 1)])
    qa = jnp.stack(ring(qt, "x"))
    qb = swap(qa)

    sent, ua, ub = pl.pallas_call(
        first_kernel,
        out_shape=(sds((512, 512), BF), sds((64, 512), F32), sds((64, 512), F32)),
        in_specs=[VMEM] * 4,
        out_specs=(VMEM,) * 3,
        compiler_params=params(6),
        name="first_kernel",
    )(top, br, qt, qr)
    err, ua = lax.optimization_barrier((err, ua))
    eh = pl.pallas_call(
        half_kernel,
        out_shape=sds((4, 512, 512), BF),
        in_specs=[VMEM],
        out_specs=VMEM,
        compiler_params=params(10),
        name="half_kernel",
    )(err)
    eh_s = swap(eh)
    u = ua + lax.ppermute(ub, "pipe", [(1, 0)])
    sent, u = lax.optimization_barrier((sent, u))
    recv = lax.ppermute(sent, "pipe", [(1, 0)])
    u = u + swap(u)
    us = ring(u, "x")

    grad, grad_in = pl.pallas_call(
        grad_kernel,
        out_shape=(sds((512, 512), BF), sds((512, 512), BF)),
        in_specs=[VMEM] * 4,
        out_specs=(VMEM,) * 2,
        compiler_params=params(6),
        name="grad_kernel",
    )(top, recv, sent, br)
    grad, eh_s, *us = lax.optimization_barrier((grad, eh_s, *us))
    g1 = shift(grad, "x", 1)
    g3 = shift(grad, "x", 3)

    eq, act_t = pl.pallas_call(
        eq_kernel,
        out_shape=(sds((64, 512), F32), sds((512, 512), BF)),
        in_specs=[VMEM] * 4,
        out_specs=(VMEM, VMEM),
        compiler_params=params(12),
        name="eq_kernel",
    )(qa, qb, act, err)

    part = pl.pallas_call(
        p_kernel,
        out_shape=sds((64, 512), F32),
        in_specs=[VMEM] * 6,
        out_specs=VMEM,
        compiler_params=params(6),
        name="p_kernel",
    )(*us, act, eq)
    part = pl.pallas_call(
        sum_kernel,
        out_shape=sds((64, 512), F32),
        in_specs=[VMEM] * 4,
        out_specs=VMEM,
        compiler_params=params(4),
        name="sum_kernel",
    )(*ring(part, "y"))

    part, g1, g3 = lax.optimization_barrier((part, g1, g3))
    g2a = shift(g1[:256], "x", 1)
    g2b = shift(g3[256:], "x", 3)
    pv = pl.pallas_call(
        pv_kernel,
        out_shape=sds((2, 64, 512), F32),
        in_specs=[VMEM] * 5,
        out_specs=VMEM,
        compiler_params=params(4),
        name="pv_kernel",
    )(*ring(part, "zhi"), act)
    pvs = swap(pv)
    q_own_part = pl.pallas_call(
        q_own_kernel,
        out_shape=sds((4, 64, 512), F32),
        in_specs=[VMEM] * 2,
        out_specs=VMEM,
        compiler_params=params(8),
        name="q_own_kernel",
    )(pv, err)
    chunks, gs = pl.pallas_call(
        q_kernel,
        out_shape=(sds((4, 4, 96, 128), F32), sds((4, 512, 512), BF)),
        in_specs=[VMEM] * 9,
        out_specs=(VMEM, VMEM),
        compiler_params=params(12),
        name="q_kernel",
    )(pv, pvs, q_own_part, eh_s, grad, g1, g2a, g2b, g3)
    gb = swap(gs)
    chunks = exchange(chunks.reshape(16, 96, 128), ("x", "y"))

    q_part, gram = pl.pallas_call(
        chunk_sum_kernel,
        out_shape=(sds((64, 128), F32), sds((32, 128), F32)),
        in_specs=[VMEM],
        out_specs=(VMEM, VMEM),
        compiler_params=params(4),
        name="chunk_sum_kernel",
    )(chunks)
    qs = ring(q_part, "zhi")
    phat, ph2, linv = pl.pallas_call(
        factor_kernel,
        out_shape=(sds((64, 512), F32), sds((128, 512), BF), sds((64, 64), F32)),
        in_specs=[VMEM, VMEM],
        out_specs=(VMEM, VMEM, VMEM),
        compiler_params=params(4),
        name="factor_kernel",
    )(gram, pv)
    act_t, gram = lax.optimization_barrier((act_t, gram))
    matrix = pl.pallas_call(
        matrix_kernel,
        out_shape=sds((8, 512, 512), F32),
        in_specs=[VMEM] * 4,
        out_specs=VMEM,
        compiler_params=params(20),
        name="matrix_kernel",
    )(act_t, gs, gb, err)
    matrix, linv = lax.optimization_barrier((matrix, linv))
    q16 = pl.pallas_call(
        q_scale_kernel,
        out_shape=sds((16, 64, 128), BF),
        in_specs=[VMEM] * 5,
        out_specs=VMEM,
        compiler_params=params(4),
        name="q_scale_kernel",
    )(*qs, linv)
    qfa = exchange(q16, ("x", "y"))
    qfb = swap(qfa)

    error_next, q_own = pl.pallas_call(
        error_kernel,
        out_shape=(sds((512, 4096), BF), sds((64, 512), F32)),
        in_specs=[VMEM] * 4,
        out_specs=(ANY, VMEM),
        scratch_shapes=[pltpu.VMEM((8, 512, 512), BF), pltpu.SemaphoreType.DMA((8,))],
        compiler_params=params(18),
        name="error_kernel",
    )(ph2, qfa, qfb, matrix)
    return (
        grad_in.reshape(branch_grad.shape),
        error_next.reshape(error_prev.shape),
        phat.T[None],
        q_own.T[None],
    )


def solution(mesh):
    fine = Mesh(mesh.devices.reshape(2, 4, 2, 4, 4), ("pipe", "x", "core", "zhi", "y"))
    tensor = ("x", "core")
    dp = ("zhi", "y")
    return jax.shard_map(
        on_device,
        mesh=fine,
        in_specs=(
            P("pipe", None, dp, tensor),
            P(None, dp, tensor),
            P("pipe", None, dp, tensor),
            P("pipe", dp, tensor, None),
            P("pipe", tensor, None),
        ),
        out_specs=(
            P("pipe", None, dp, tensor),
            P("pipe", dp, tensor, None),
            P("pipe", tensor, None),
            P("pipe", tensor, None),
        ),
        check_vma=False,
    )
```

time: 155 us -> 138 us (0.89)
  starting transfers between devices: 42.7 us -> 58.8 us
  local copies, waits for them, and re-layouts: 21.3 us -> 5.23 us
  Pallas kernels: 33.1 us -> 18.1 us
  other arithmetic: 2.55 us -> 0.07 us
  blocking collectives: 28.2 us -> 30.2 us
  waiting for transfers between devices: 25.2 us -> 23.4 us
    unnamed x48 -> x18, local copies, waits for them, and re-layouts: 21.3 us -> 5.2 us
    ppermute x12 -> x19, starting transfers between devices: 17.5 us -> 33 us  [shift(): return lax.ppermute(v, axis, [(i, (i + k) % n) for i in range(n)])]
    all_to_all x2 -> x0, starting transfers between devices: 12.4 us -> none  [exchange(): return lax.all_to_all(v, axes, 0, 0, tiled=True)]
    all_to_all x2 -> x0, waiting for transfers between devices: 11.6 us -> none  [exchange(): return lax.all_to_all(v, axes, 0, 0, tiled=True)]
    ppermute x0 -> x2, waiting for transfers between devices: none -> 7.74 us  [the longest x1 5.28 us: on_device(): u = ua + lax.ppermute(ub, 'pipe', [(1, 0)])]
    ppermute x8 -> x6, starting transfers between devices: 11.6 us -> 18.8 us  [swap(): return lax.ppermute(v, 'core', [(0, 1), (1, 0)])]
    ppermute x0 -> x2, starting transfers between devices: none -> 5.66 us  [the longest x1 4.38 us: on_device(): qr = lax.ppermute(qt, 'pipe', [(0, 1)])]
    pallas_call x1, Pallas kernels: 8.08 us -> 3.04 us  [on_device(): pl.pallas_call(error_kernel, out_shape=(sds((512, 4096), BF), sds((64, 51...]
  transfers between devices with their start and end apart: 23 -> 28, of which waited for: 7 -> 14; matrix products, arithmetic and copies ran while one was open for 1% -> 0% of each run, Pallas kernels for 11% -> 9%
where the time goes in v2:
time: 138 us; the launch traced here: 137 us
  starting transfers between devices  58.8 us (43%)
  blocking collectives  30.2 us (22%)
  waiting for transfers between devices  23.4 us (17%)
  Pallas kernels  18.1 us (13%)
  local copies, waits for them, and re-layouts  5.23 us (4%)
    ppermute x19, starting transfers between devices, shift(): return lax.ppermute(v, axis, [(i, (i + k) % n) for i in range(n)])  33 us
    all_to_all x2, blocking collectives, exchange(): return lax.all_to_all(v, axes, 0, 0, tiled=True)  30.2 us
    ppermute x6, starting transfers between devices, swap(): return lax.ppermute(v, 'core', [(0, 1), (1, 0)])  18.8 us
    ppermute x19, waiting for transfers between devices, shift(): return lax.ppermute(v, axis, [(i, (i + k) % n) for i in range(n)])  13.9 us
    pallas_call x1, Pallas kernels, on_device(): pl.pallas_call(factor_kernel, out_shape=(sds((64, 512), F32), sds((128, 5...  6.77 us
    ppermute x1, waiting for transfers between devices, on_device(): u = ua + lax.ppermute(ub, 'pipe', [(1, 0)])  5.28 us
    unnamed x18, local copies, waits for them, and re-layouts  5.2 us
    ppermute x1, starting transfers between devices, on_device(): qr = lax.ppermute(qt, 'pipe', [(0, 1)])  4.38 us
  transfers between devices with their start and end apart: 28, of which 14 were waited for; matrix products, arithmetic and copies ran while one was open for 0% of the time, Pallas kernels for 9%

profile of v2, /device:TPU:1, one launch (start us, length us, event | category | flops | bytes accessed | tf_op | source)
XLA Modules:
  0.0 136.8 jit_solution(7091253873621872229)
XLA Ops:
  0.6 4.4 %collective-permute-start = (f32[64,512]{1,0:T(8,128)}, f32[64,512]{1,0:T(8,128)S(1)}, u32[]{:S(2)}, u32[]{:S(2)}) collective-permute-start(f32[64,512]{1,0:T(8,128)} %bitcast.33), channel_id=1, source_target_pairs={{0,128},{1,129},{2,130},{3,131},{4,132},{5,133},{6,134},{7,135},{8... | collective-permute-start | bytes 393224 | tf_op jit(solution)/shard_map/ppermute | solution.py:232
  5.0 2.5 %collective-permute-done.qr_ref = f32[64,512]{1,0:T(8,128)S(1)} collective-permute-done((f32[64,512]{1,0:T(8,128)}, f32[64,512]{1,0:T(8,128)S(1)}, u32[]{:S(2)}, u32[]{:S(2)}) %collective-permute-start) | collective-permute-done | bytes 131104 | tf_op jit(solution)/shard_map/ppermute | solution.py:232
  11.0 2.2 %copy-done = bf16[1,1,512,4096]{3,2,1,0:T(8,128)(2,1)S(1)} copy-done((bf16[1,1,512,4096]{3,2,1,0:T(8,128)(2,1)S(1)}, bf16[1,1,512,4096]{3,2,1,0:T(8,128)(2,1)}, u32[]{:S(2)}) %copy-start) | copy-done | bytes 4194328
  13.4 1.6 %collective-permute-start.3 = (bf16[4,512,512]{2,1,0:T(8,128)(2,1)S(1)}, bf16[4,512,512]{2,1,0:T(8,128)(2,1)S(1)}, u32[]{:S(2)}, u32[]{:S(2)}) collective-permute-start(bf16[4,512,512]{2,1,0:T(8,128)(2,1)S(1)} %half_kernel.1), channel_id=1, source_target_pairs={{0,16},{16,0},{1,17},{17,1},{2,18},{18,2},{3,19},{19,3},{4,20},{20... | collective-permute-start | bytes 6291464 | tf_op jit(solution)/shard_map/ppermute | solution.py:214
  15.0 1.3 collective-permute-start.1
  16.3 5.3 %collective-permute-done.1 = f32[64,512]{1,0:T(8,128)S(1)} collective-permute-done((f32[64,512]{1,0:T(8,128)S(1)}, f32[64,512]{1,0:T(8,128)S(1)}, u32[]{:S(2)}, u32[]{:S(2)}) %collective-permute-start.1) | collective-permute-done | bytes 131104 | tf_op jit(solution)/shard_map/ppermute | solution.py:254
  21.6 1.3 collective-permute-start.2
  22.9 2.8 %collective-permute-start.9 = (f32[64,512]{1,0:T(8,128)S(1)}, f32[64,512]{1,0:T(8,128)S(1)}, u32[]{:S(2)}, u32[]{:S(2)}) collective-permute-start(f32[64,512]{1,0:T(8,128)S(1)} %bitcast.35), channel_id=1, source_target_pairs={{0,64},{32,96},{64,0},{96,32},{1,65},{33,97},{65,1},{97,33},{2,66}... | collective-permute-start | bytes 393224 | tf_op jit(solution)/shard_map/ppermute | solution.py:210
  28.3 3.6 %collective-permute-start.4 = (f32[64,512]{1,0:T(8,128)S(1)}, f32[64,512]{1,0:T(8,128)S(1)}, u32[]{:S(2)}, u32[]{:S(2)}) collective-permute-start(f32[64,512]{1,0:T(8,128)S(1)} %add.6), channel_id=1, source_target_pairs={{0,16},{16,0},{1,17},{17,1},{2,18},{18,2},{3,19},{19,3},{4,20},{20... | collective-permute-start | bytes 393224 | tf_op jit(solution)/shard_map/ppermute | solution.py:214
  32.2 2.5 %collective-permute-start.11 = (f32[4,64,512]{2,1,0:T(8,128)S(1)}, f32[4,64,512]{2,1,0:T(8,128)S(1)}, u32[]{:S(2)}, u32[]{:S(2)}) collective-permute-start(f32[4,64,512]{2,1,0:T(8,128)S(1)} %pad_maximum_fusion.qa_ref), channel_id=1, source_target_pairs={{0,16},{16,0},{1,17},{17,1},{2,18},{18,2},{3,19},{19,3},{4,20},{20... | collective-permute-start | bytes 1572872 | tf_op jit(solution)/shard_map/ppermute | solution.py:214
  34.8 2.3 %collective-permute-start.6 = (f32[64,512]{1,0:T(8,128)S(1)}, f32[64,512]{1,0:T(8,128)S(1)}, u32[]{:S(2)}, u32[]{:S(2)}) collective-permute-start(f32[64,512]{1,0:T(8,128)S(1)} %add.7.u0), channel_id=1, source_target_pairs={{0,64},{32,96},{64,0},{96,32},{1,65},{33,97},{65,1},{97,33},{2,66}... | collective-permute-start | bytes 393224 | tf_op jit(solution)/shard_map/ppermute | solution.py:210
  39.2 2.3 %collective-permute-done.5.u1 = f32[64,512]{1,0:T(8,128)S(1)} collective-permute-done((f32[64,512]{1,0:T(8,128)S(1)}, f32[64,512]{1,0:T(8,128)S(1)}, u32[]{:S(2)}, u32[]{:S(2)}) %collective-permute-start.5) | collective-permute-done | bytes 131104 | tf_op jit(solution)/shard_map/ppermute | solution.py:210
  41.5 2.1 %collective-permute-done.6.u2 = f32[64,512]{1,0:T(8,128)S(1)} collective-permute-done((f32[64,512]{1,0:T(8,128)S(1)}, f32[64,512]{1,0:T(8,128)S(1)}, u32[]{:S(2)}, u32[]{:S(2)}) %collective-permute-start.6) | collective-permute-done | bytes 131104 | tf_op jit(solution)/shard_map/ppermute | solution.py:210
  44.2 1.4 %collective-permute-start.15 = (bf16[512,512]{1,0:T(8,128)(2,1)S(1)}, bf16[512,512]{1,0:T(8,128)(2,1)S(1)}, u32[]{:S(2)}, u32[]{:S(2)}) collective-permute-start(bf16[512,512]{1,0:T(8,128)(2,1)S(1)} %get-tuple-element.50.g0), channel_id=1, source_target_pairs={{0,32},{32,64},{64,96},{96,0},{1,33},{33,65},{65,97},{97,1},{2,34}... | collective-permute-start | bytes 1572872 | tf_op jit(solution)/shard_map/ppermute | solution.py:210
  46.9 1.6 %eq_kernel.1 = (f32[64,512]{1,0:T(8,128)S(1)}, bf16[512,512]{1,0:T(8,128)(2,1)S(1)}) custom-call(f32[4,64,512]{2,1,0:T(8,128)S(1)} %pad_maximum_fusion.qa_ref, f32[4,64,512]{2,1,0:T(8,128)S(1)} %collective-permute-done.11.qb_ref, bf16[512,512]{1,0:T(8,128)(2,1)S(1)} %bitcast.25, bf16[512,4096]{1,0:T(8,128)(2,1)S(1)} %bitcast.22), custom_call_target="tpu_custom_call" | custom-call | tf_op jit(solution)/shard_map/eq_kernel/pallas_call | solution.py:272
  48.7 1.4 %collective-permute-start.12 = (f32[64,512]{1,0:T(8,128)S(1)}, f32[64,512]{1,0:T(8,128)S(1)}, u32[]{:S(2)}, u32[]{:S(2)}) collective-permute-start(f32[64,512]{1,0:T(8,128)S(1)} %p_kernel.1.a), channel_id=1, source_target_pairs={{0,1},{1,2},{2,3},{3,0},{4,5},{5,6},{6,7},{7,4},{8,9},{9,10},{10,1... | collective-permute-start | bytes 393224 | tf_op jit(solution)/shard_map/ppermute | solution.py:210
  50.1 2.6 %collective-permute-start.13 = (f32[64,512]{1,0:T(8,128)S(1)}, f32[64,512]{1,0:T(8,128)S(1)}, u32[]{:S(2)}, u32[]{:S(2)}) collective-permute-start(f32[64,512]{1,0:T(8,128)S(1)} %p_kernel.1.a), channel_id=1, source_target_pairs={{0,2},{1,3},{2,0},{3,1},{4,6},{5,7},{6,4},{7,5},{8,10},{9,11},{10,... | collective-permute-start | bytes 393224 | tf_op jit(solution)/shard_map/ppermute | solution.py:210
  54.2 2.9 %collective-permute-done.13.c = f32[64,512]{1,0:T(8,128)S(1)} collective-permute-done((f32[64,512]{1,0:T(8,128)S(1)}, f32[64,512]{1,0:T(8,128)S(1)}, u32[]{:S(2)}, u32[]{:S(2)}) %collective-permute-start.13) | collective-permute-done | bytes 131104 | tf_op jit(solution)/shard_map/ppermute | solution.py:210
  58.3 3.0 %collective-permute-start.17 = (f32[64,512]{1,0:T(8,128)S(1)}, f32[64,512]{1,0:T(8,128)S(1)}, u32[]{:S(2)}, u32[]{:S(2)}) collective-permute-start(f32[64,512]{1,0:T(8,128)S(1)} %sum_kernel.1.z0), channel_id=1, source_target_pairs={{0,4},{4,8},{8,12},{12,0},{1,5},{5,9},{9,13},{13,1},{2,6},{6,10},{... | collective-permute-start | bytes 393224 | tf_op jit(solution)/shard_map/ppermute | solution.py:210
  61.3 4.2 %collective-permute-start.18 = (f32[64,512]{1,0:T(8,128)S(1)}, f32[64,512]{1,0:T(8,128)S(1)}, u32[]{:S(2)}, u32[]{:S(2)}) collective-permute-start(f32[64,512]{1,0:T(8,128)S(1)} %sum_kernel.1.z0), channel_id=1, source_target_pairs={{0,8},{4,12},{8,0},{12,4},{1,9},{5,13},{9,1},{13,5},{2,10},{6,14},... | collective-permute-start | bytes 393224 | tf_op jit(solution)/shard_map/ppermute | solution.py:210
  65.5 2.4 %collective-permute-start.19 = (f32[64,512]{1,0:T(8,128)S(1)}, f32[64,512]{1,0:T(8,128)S(1)}, u32[]{:S(2)}, u32[]{:S(2)}) collective-permute-start(f32[64,512]{1,0:T(8,128)S(1)} %sum_kernel.1.z0), channel_id=1, source_target_pairs={{0,12},{4,0},{8,4},{12,8},{1,13},{5,1},{9,5},{13,9},{2,14},{6,2},{... | collective-permute-start | bytes 393224 | tf_op jit(solution)/shard_map/ppermute | solution.py:210
  68.5 2.3 %collective-permute-start.22 = (bf16[256,512]{1,0:T(8,128)(2,1)S(1)}, bf16[256,512]{1,0:T(8,128)(2,1)S(1)}, u32[]{:S(2)}, u32[]{:S(2)}) collective-permute-start(bf16[256,512]{1,0:T(8,128)(2,1)S(1)} %slice.7), channel_id=1, source_target_pairs={{0,96},{32,0},{64,32},{96,64},{1,97},{33,1},{65,33},{97,65},{2,98}... | collective-permute-start | bytes 786440 | tf_op jit(solution)/shard_map/ppermute | solution.py:210
  70.8 3.2 %collective-permute-done.19.z3 = f32[64,512]{1,0:T(8,128)S(1)} collective-permute-done((f32[64,512]{1,0:T(8,128)S(1)}, f32[64,512]{1,0:T(8,128)S(1)}, u32[]{:S(2)}, u32[]{:S(2)}) %collective-permute-start.19) | collective-permute-done | bytes 131104 | tf_op jit(solution)/shard_map/ppermute | solution.py:210
  74.3 7.3 %collective-permute-start.20 = (f32[2,64,512]{2,1,0:T(8,128)S(1)}, f32[2,64,512]{2,1,0:T(8,128)S(1)}, u32[]{:S(2)}, u32[]{:S(2)}) collective-permute-start(f32[2,64,512]{2,1,0:T(8,128)S(1)} %pv_kernel.1.pv_ref.p_ref), channel_id=1, source_target_pairs={{0,16},{16,0},{1,17},{17,1},{2,18},{18,2},{3,19},{19,3},{4,20},{20... | collective-permute-start | bytes 786440 | tf_op jit(solution)/shard_map/ppermute | solution.py:214
  82.8 1.3 q_kernel.1
  84.5 19.4 %all_to_all.10.in_ref = f32[16,96,128]{2,1,0:T(8,128)S(1)} all-to-all(f32[16,96,128]{2,1,0:T(8,128)S(1)} %bitcast.32), channel_id=1, replica_groups=mesh['pipe'=2,'x'=4,'core'=2,'zhi'=4,'y'=4] {'x','y'}, dimensions={0} | all-to-all | bytes 1572864 | tf_op jit(solution)/shard_map/all_to_all | solution.py:222
  104.1 5.0 %collective-permute-start.24 = (f32[64,128]{1,0:T(8,128)S(1)}, f32[64,128]{1,0:T(8,128)S(1)}, u32[]{:S(2)}, u32[]{:S(2)}) collective-permute-start(f32[64,128]{1,0:T(8,128)S(1)} %get-tuple-element.58.q0), channel_id=1, source_target_pairs={{0,8},{4,12},{8,0},{12,4},{1,9},{5,13},{9,1},{13,5},{2,10},{6,14},... | collective-permute-start | bytes 98312 | tf_op jit(solution)/shard_map/ppermute | solution.py:210
  109.1 6.8 %factor_kernel.1 = (f32[64,512]{1,0:T(8,128)}, bf16[128,512]{1,0:T(8,128)(2,1)S(1)}, f32[64,64]{1,0:T(8,128)S(1)}) custom-call(f32[32,128]{1,0:T(8,128)S(1)} %get-tuple-element.56.gram_ref, f32[2,64,512]{2,1,0:T(8,128)S(1)} %pv_kernel.1.pv_ref.p_ref), custom_call_target="tpu_custom_call" | custom-call | tf_op jit(solution)/shard_map/factor_kernel/pallas_call | solution.py:338
  115.9 2.3 %matrix_kernel.1.m_ref = f32[8,512,512]{2,1,0:T(8,128)S(1)} custom-call(bf16[512,512]{1,0:T(8,128)(2,1)S(1)} %get-tuple-element.60.at_ref, bf16[4,512,512]{2,1,0:T(8,128)(2,1)S(1)} %get-tuple-element.61.ga_ref, bf16[4,512,512]{2,1,0:T(8,128)(2,1)S(1)} %collective-permute-done.26.gb_ref, bf16[512,4096]{1,0:T(8,128)(2,1)S(1)} %bitcast.24), custom_call_target="tpu_custom_call" | custom-call | tf_op jit(solution)/shard_map/matrix_kernel/pallas_call | solution.py:347
  118.5 10.8 %all_to_all.11.qa_ref = bf16[16,64,128]{2,1,0:T(8,128)(2,1)S(1)} all-to-all(bf16[16,64,128]{2,1,0:T(8,128)(2,1)S(1)} %q_scale_kernel.1), channel_id=1, replica_groups=mesh['pipe'=2,'x'=4,'core'=2,'zhi'=4,'y'=4] {'x','y'}, dimensions={0} | all-to-all | bytes 524288 | tf_op jit(solution)/shard_map/all_to_all | solution.py:222
  129.2 3.2 %collective-permute-start.27 = (bf16[16,64,128]{2,1,0:T(8,128)(2,1)S(1)}, bf16[16,64,128]{2,1,0:T(8,128)(2,1)S(1)}, u32[]{:S(2)}, u32[]{:S(2)}) collective-permute-start(bf16[16,64,128]{2,1,0:T(8,128)(2,1)S(1)} %all_to_all.11.qa_ref), channel_id=1, source_target_pairs={{0,16},{16,0},{1,17},{17,1},{2,18},{18,2},{3,19},{19,3},{4,20},{20... | collective-permute-start | bytes 786440 | tf_op jit(solution)/shard_map/ppermute | solution.py:214
  133.6 3.0 %error_kernel.1 = (bf16[512,4096]{1,0:T(8,128)(2,1)}, f32[64,512]{1,0:T(8,128)}) custom-call(bf16[128,512]{1,0:T(8,128)(2,1)S(1)} %get-tuple-element.57.ph2_ref, bf16[16,64,128]{2,1,0:T(8,128)(2,1)S(1)} %all_to_all.11.qa_ref, bf16[16,64,128]{2,1,0:T(8,128)(2,1)S(1)} %collective-permute-done.27.qb_ref, f32[8,512,512]{2,1,0:T(8,128)S(1)} %matrix_kernel.1.m_ref), custom_call_target="tpu_custom_call" | custom-call | tf_op jit(solution)/shard_map/error_kernel/pallas_call | solution.py:367
  (63 shorter events, 17.5 us)
Async XLA Ops:
  0.6 6.8 %collective-permute-start = (f32[64,512]{1,0:T(8,128)}, f32[64,512]{1,0:T(8,128)S(1)}, u32[]{:S(2)}, u32[]{:S(2)}) collective-permute-start(f32[64,512]{1,0:T(8,128)} %bitcast.33), channel_id=1, source_target_pairs={{0,128},{1,129},{2,130},{3,131},{4,132},{5,133},{6,134},{7,135},{8... | collective-permute-start | bytes 393224 | tf_op jit(solution)/shard_map/ppermute | solution.py:232
  13.2 33.7 %copy-start.1 = (bf16[1,1,512,4096]{3,2,1,0:T(8,128)(2,1)S(1)}, bf16[1,1,512,4096]{3,2,1,0:T(8,128)(2,1)}, u32[]{:S(2)}) copy-start(bf16[1,1,512,4096]{3,2,1,0:T(8,128)(2,1)} %param.8) | copy-start | bytes 12582916
  13.3 24.9 %copy-start.4 = (bf16[4,128,512]{2,1,0:T(8,128)(2,1)S(1)}, bf16[4,128,512]{2,1,0:T(8,128)(2,1)}, u32[]{:S(2)}) copy-start(bf16[4,128,512]{2,1,0:T(8,128)(2,1)} %param.6) | copy-start | bytes 1572868
  13.3 24.9 %copy-start.6 = (bf16[1,4,128,512]{3,2,1,0:T(8,128)(2,1)S(1)}, bf16[1,4,128,512]{3,2,1,0:T(8,128)(2,1)}, u32[]{:S(2)}) copy-start(bf16[1,4,128,512]{3,2,1,0:T(8,128)(2,1)} %param.7) | copy-start | bytes 1572868
  13.4 33.5 %copy-start.2 = (bf16[1,4,128,512]{3,2,1,0:T(8,128)(2,1)S(1)}, bf16[1,4,128,512]{3,2,1,0:T(8,128)(2,1)}, u32[]{:S(2)}) copy-start(bf16[1,4,128,512]{3,2,1,0:T(8,128)(2,1)} %param.5) | copy-start | bytes 1572868
  13.4 30.8 %collective-permute-start.3 = (bf16[4,512,512]{2,1,0:T(8,128)(2,1)S(1)}, bf16[4,512,512]{2,1,0:T(8,128)(2,1)S(1)}, u32[]{:S(2)}, u32[]{:S(2)}) collective-permute-start(bf16[4,512,512]{2,1,0:T(8,128)(2,1)S(1)} %half_kernel.1), channel_id=1, source_target_pairs={{0,16},{16,0},{1,17},{17,1},{2,18},{18,2},{3,19},{19,3},{4,20},{20... | collective-permute-start | bytes 6291464 | tf_op jit(solution)/shard_map/ppermute | solution.py:214
  15.0 6.6 %collective-permute-start.1 = (f32[64,512]{1,0:T(8,128)S(1)}, f32[64,512]{1,0:T(8,128)S(1)}, u32[]{:S(2)}, u32[]{:S(2)}) collective-permute-start(f32[64,512]{1,0:T(8,128)S(1)} %get-tuple-element.39), channel_id=1, source_target_pairs={{128,0},{129,1},{130,2},{131,3},{132,4},{133,5},{134,6},{135,7},{1... | collective-permute-start | bytes 393224 | tf_op jit(solution)/shard_map/ppermute | solution.py:254
  21.6 15.5 %collective-permute-start.2 = (bf16[512,512]{1,0:T(8,128)(2,1)S(1)}, bf16[512,512]{1,0:T(8,128)(2,1)S(1)}, u32[]{:S(2)}, u32[]{:S(2)}) collective-permute-start(bf16[512,512]{1,0:T(8,128)(2,1)S(1)} %get-tuple-element.40.s_ref), channel_id=1, source_target_pairs={{128,0},{129,1},{130,2},{131,3},{132,4},{133,5},{134,6},{135,7},{1... | collective-permute-start | bytes 1572872 | tf_op jit(solution)/shard_map/ppermute | solution.py:256
  22.9 5.4 %collective-permute-start.9 = (f32[64,512]{1,0:T(8,128)S(1)}, f32[64,512]{1,0:T(8,128)S(1)}, u32[]{:S(2)}, u32[]{:S(2)}) collective-permute-start(f32[64,512]{1,0:T(8,128)S(1)} %bitcast.35), channel_id=1, source_target_pairs={{0,64},{32,96},{64,0},{96,32},{1,65},{33,97},{65,1},{97,33},{2,66}... | collective-permute-start | bytes 393224 | tf_op jit(solution)/shard_map/ppermute | solution.py:210
  25.7 6.2 %collective-permute-start.10 = (f32[64,512]{1,0:T(8,128)S(1)}, f32[64,512]{1,0:T(8,128)S(1)}, u32[]{:S(2)}, u32[]{:S(2)}) collective-permute-start(f32[64,512]{1,0:T(8,128)S(1)} %bitcast.36), channel_id=1, source_target_pairs={{0,96},{32,0},{64,32},{96,64},{1,97},{33,1},{65,33},{97,65},{2,98}... | collective-permute-start | bytes 393224 | tf_op jit(solution)/shard_map/ppermute | solution.py:210
  26.6 5.5 %collective-permute-start.8 = (f32[64,512]{1,0:T(8,128)S(1)}, f32[64,512]{1,0:T(8,128)S(1)}, u32[]{:S(2)}, u32[]{:S(2)}) collective-permute-start(f32[64,512]{1,0:T(8,128)S(1)} %bitcast.37), channel_id=1, source_target_pairs={{0,32},{32,64},{64,96},{96,0},{1,33},{33,65},{65,97},{97,1},{2,34}... | collective-permute-start | bytes 393224 | tf_op jit(solution)/shard_map/ppermute | solution.py:210
  28.3 6.4 %collective-permute-start.4 = (f32[64,512]{1,0:T(8,128)S(1)}, f32[64,512]{1,0:T(8,128)S(1)}, u32[]{:S(2)}, u32[]{:S(2)}) collective-permute-start(f32[64,512]{1,0:T(8,128)S(1)} %add.6), channel_id=1, source_target_pairs={{0,16},{16,0},{1,17},{17,1},{2,18},{18,2},{3,19},{19,3},{4,20},{20... | collective-permute-start | bytes 393224 | tf_op jit(solution)/shard_map/ppermute | solution.py:214
  32.2 14.7 %collective-permute-start.11 = (f32[4,64,512]{2,1,0:T(8,128)S(1)}, f32[4,64,512]{2,1,0:T(8,128)S(1)}, u32[]{:S(2)}, u32[]{:S(2)}) collective-permute-start(f32[4,64,512]{2,1,0:T(8,128)S(1)} %pad_maximum_fusion.qa_ref), channel_id=1, source_target_pairs={{0,16},{16,0},{1,17},{17,1},{2,18},{18,2},{3,19},{19,3},{4,20},{20... | collective-permute-start | bytes 1572872 | tf_op jit(solution)/shard_map/ppermute | solution.py:214
  34.7 6.8 %collective-permute-start.5 = (f32[64,512]{1,0:T(8,128)S(1)}, f32[64,512]{1,0:T(8,128)S(1)}, u32[]{:S(2)}, u32[]{:S(2)}) collective-permute-start(f32[64,512]{1,0:T(8,128)S(1)} %add.7.u0), channel_id=1, source_target_pairs={{0,32},{32,64},{64,96},{96,0},{1,33},{33,65},{65,97},{97,1},{2,34}... | collective-permute-start | bytes 393224 | tf_op jit(solution)/shard_map/ppermute | solution.py:210
  34.8 8.8 %collective-permute-start.6 = (f32[64,512]{1,0:T(8,128)S(1)}, f32[64,512]{1,0:T(8,128)S(1)}, u32[]{:S(2)}, u32[]{:S(2)}) collective-permute-start(f32[64,512]{1,0:T(8,128)S(1)} %add.7.u0), channel_id=1, source_target_pairs={{0,64},{32,96},{64,0},{96,32},{1,65},{33,97},{65,1},{97,33},{2,66}... | collective-permute-start | bytes 393224 | tf_op jit(solution)/shard_map/ppermute | solution.py:210
  37.1 7.1 %collective-permute-start.7 = (f32[64,512]{1,0:T(8,128)S(1)}, f32[64,512]{1,0:T(8,128)S(1)}, u32[]{:S(2)}, u32[]{:S(2)}) collective-permute-start(f32[64,512]{1,0:T(8,128)S(1)} %add.7.u0), channel_id=1, source_target_pairs={{0,96},{32,0},{64,32},{96,64},{1,97},{33,1},{65,33},{97,65},{2,98}... | collective-permute-start | bytes 393224 | tf_op jit(solution)/shard_map/ppermute | solution.py:210
  44.2 13.8 %collective-permute-start.15 = (bf16[512,512]{1,0:T(8,128)(2,1)S(1)}, bf16[512,512]{1,0:T(8,128)(2,1)S(1)}, u32[]{:S(2)}, u32[]{:S(2)}) collective-permute-start(bf16[512,512]{1,0:T(8,128)(2,1)S(1)} %get-tuple-element.50.g0), channel_id=1, source_target_pairs={{0,32},{32,64},{64,96},{96,0},{1,33},{33,65},{65,97},{97,1},{2,34}... | collective-permute-start | bytes 1572872 | tf_op jit(solution)/shard_map/ppermute | solution.py:210
  45.6 12.7 %collective-permute-start.16 = (bf16[512,512]{1,0:T(8,128)(2,1)S(1)}, bf16[512,512]{1,0:T(8,128)(2,1)S(1)}, u32[]{:S(2)}, u32[]{:S(2)}) collective-permute-start(bf16[512,512]{1,0:T(8,128)(2,1)S(1)} %get-tuple-element.50.g0), channel_id=1, source_target_pairs={{0,96},{32,0},{64,32},{96,64},{1,97},{33,1},{65,33},{97,65},{2,98}... | collective-permute-start | bytes 1572872 | tf_op jit(solution)/shard_map/ppermute | solution.py:210
  48.7 5.5 %collective-permute-start.12 = (f32[64,512]{1,0:T(8,128)S(1)}, f32[64,512]{1,0:T(8,128)S(1)}, u32[]{:S(2)}, u32[]{:S(2)}) collective-permute-start(f32[64,512]{1,0:T(8,128)S(1)} %p_kernel.1.a), channel_id=1, source_target_pairs={{0,1},{1,2},{2,3},{3,0},{4,5},{5,6},{6,7},{7,4},{8,9},{9,10},{10,1... | collective-permute-start | bytes 393224 | tf_op jit(solution)/shard_map/ppermute | solution.py:210
  50.1 7.0 %collective-permute-start.13 = (f32[64,512]{1,0:T(8,128)S(1)}, f32[64,512]{1,0:T(8,128)S(1)}, u32[]{:S(2)}, u32[]{:S(2)}) collective-permute-start(f32[64,512]{1,0:T(8,128)S(1)} %p_kernel.1.a), channel_id=1, source_target_pairs={{0,2},{1,3},{2,0},{3,1},{4,6},{5,7},{6,4},{7,5},{8,10},{9,11},{10,... | collective-permute-start | bytes 393224 | tf_op jit(solution)/shard_map/ppermute | solution.py:210
  52.7 5.2 %collective-permute-start.14 = (f32[64,512]{1,0:T(8,128)S(1)}, f32[64,512]{1,0:T(8,128)S(1)}, u32[]{:S(2)}, u32[]{:S(2)}) collective-permute-start(f32[64,512]{1,0:T(8,128)S(1)} %p_kernel.1.a), channel_id=1, source_target_pairs={{0,3},{1,0},{2,1},{3,2},{4,7},{5,4},{6,5},{7,6},{8,11},{9,8},{10,9... | collective-permute-start | bytes 393224 | tf_op jit(solution)/shard_map/ppermute | solution.py:210
  58.3 12.5 %collective-permute-start.17 = (f32[64,512]{1,0:T(8,128)S(1)}, f32[64,512]{1,0:T(8,128)S(1)}, u32[]{:S(2)}, u32[]{:S(2)}) collective-permute-start(f32[64,512]{1,0:T(8,128)S(1)} %sum_kernel.1.z0), channel_id=1, source_target_pairs={{0,4},{4,8},{8,12},{12,0},{1,5},{5,9},{9,13},{13,1},{2,6},{6,10},{... | collective-permute-start | bytes 393224 | tf_op jit(solution)/shard_map/ppermute | solution.py:210
  61.3 9.5 %collective-permute-start.18 = (f32[64,512]{1,0:T(8,128)S(1)}, f32[64,512]{1,0:T(8,128)S(1)}, u32[]{:S(2)}, u32[]{:S(2)}) collective-permute-start(f32[64,512]{1,0:T(8,128)S(1)} %sum_kernel.1.z0), channel_id=1, source_target_pairs={{0,8},{4,12},{8,0},{12,4},{1,9},{5,13},{9,1},{13,5},{2,10},{6,14},... | collective-permute-start | bytes 393224 | tf_op jit(solution)/shard_map/ppermute | solution.py:210
  65.5 8.4 %collective-permute-start.19 = (f32[64,512]{1,0:T(8,128)S(1)}, f32[64,512]{1,0:T(8,128)S(1)}, u32[]{:S(2)}, u32[]{:S(2)}) collective-permute-start(f32[64,512]{1,0:T(8,128)S(1)} %sum_kernel.1.z0), channel_id=1, source_target_pairs={{0,12},{4,0},{8,4},{12,8},{1,13},{5,1},{9,5},{13,9},{2,14},{6,2},{... | collective-permute-start | bytes 393224 | tf_op jit(solution)/shard_map/ppermute | solution.py:210
  67.9 14.3 %collective-permute-start.21 = (bf16[256,512]{1,0:T(8,128)(2,1)S(1)}, bf16[256,512]{1,0:T(8,128)(2,1)S(1)}, u32[]{:S(2)}, u32[]{:S(2)}) collective-permute-start(bf16[256,512]{1,0:T(8,128)(2,1)S(1)} %slice.6), channel_id=1, source_target_pairs={{0,32},{32,64},{64,96},{96,0},{1,33},{33,65},{65,97},{97,1},{2,34}... | collective-permute-start | bytes 786440 | tf_op jit(solution)/shard_map/ppermute | solution.py:210
  68.5 13.8 %collective-permute-start.22 = (bf16[256,512]{1,0:T(8,128)(2,1)S(1)}, bf16[256,512]{1,0:T(8,128)(2,1)S(1)}, u32[]{:S(2)}, u32[]{:S(2)}) collective-permute-start(bf16[256,512]{1,0:T(8,128)(2,1)S(1)} %slice.7), channel_id=1, source_target_pairs={{0,96},{32,0},{64,32},{96,64},{1,97},{33,1},{65,33},{97,65},{2,98}... | collective-permute-start | bytes 786440 | tf_op jit(solution)/shard_map/ppermute | solution.py:210
  74.3 8.5 %collective-permute-start.20 = (f32[2,64,512]{2,1,0:T(8,128)S(1)}, f32[2,64,512]{2,1,0:T(8,128)S(1)}, u32[]{:S(2)}, u32[]{:S(2)}) collective-permute-start(f32[2,64,512]{2,1,0:T(8,128)S(1)} %pv_kernel.1.pv_ref.p_ref), channel_id=1, source_target_pairs={{0,16},{16,0},{1,17},{17,1},{2,18},{18,2},{3,19},{19,3},{4,20},{20... | collective-permute-start | bytes 786440 | tf_op jit(solution)/shard_map/ppermute | solution.py:214
  84.1 31.8 %collective-permute-start.26 = (bf16[4,512,512]{2,1,0:T(8,128)(2,1)S(1)}, bf16[4,512,512]{2,1,0:T(8,128)(2,1)S(1)}, u32[]{:S(2)}, u32[]{:S(2)}) collective-permute-start(bf16[4,512,512]{2,1,0:T(8,128)(2,1)S(1)} %get-tuple-element.61.ga_ref), channel_id=1, source_target_pairs={{0,16},{16,0},{1,17},{17,1},{2,18},{18,2},{3,19},{19,3},{4,20},{20... | collective-permute-start | bytes 6291464 | tf_op jit(solution)/shard_map/ppermute | solution.py:214
  104.0 14.2 %collective-permute-start.23 = (f32[64,128]{1,0:T(8,128)S(1)}, f32[64,128]{1,0:T(8,128)S(1)}, u32[]{:S(2)}, u32[]{:S(2)}) collective-permute-start(f32[64,128]{1,0:T(8,128)S(1)} %get-tuple-element.58.q0), channel_id=1, source_target_pairs={{0,4},{4,8},{8,12},{12,0},{1,5},{5,9},{9,13},{13,1},{2,6},{6,10},{... | collective-permute-start | bytes 98312 | tf_op jit(solution)/shard_map/ppermute | solution.py:210
  104.1 14.1 %collective-permute-start.24 = (f32[64,128]{1,0:T(8,128)S(1)}, f32[64,128]{1,0:T(8,128)S(1)}, u32[]{:S(2)}, u32[]{:S(2)}) collective-permute-start(f32[64,128]{1,0:T(8,128)S(1)} %get-tuple-element.58.q0), channel_id=1, source_target_pairs={{0,8},{4,12},{8,0},{12,4},{1,9},{5,13},{9,1},{13,5},{2,10},{6,14},... | collective-permute-start | bytes 98312 | tf_op jit(solution)/shard_map/ppermute | solution.py:210
  109.1 9.2 %collective-permute-start.25 = (f32[64,128]{1,0:T(8,128)S(1)}, f32[64,128]{1,0:T(8,128)S(1)}, u32[]{:S(2)}, u32[]{:S(2)}) collective-permute-start(f32[64,128]{1,0:T(8,128)S(1)} %get-tuple-element.58.q0), channel_id=1, source_target_pairs={{0,12},{4,0},{8,4},{12,8},{1,13},{5,1},{9,5},{13,9},{2,14},{6,2},{... | collective-permute-start | bytes 98312 | tf_op jit(solution)/shard_map/ppermute | solution.py:210
  129.2 4.4 %collective-permute-start.27 = (bf16[16,64,128]{2,1,0:T(8,128)(2,1)S(1)}, bf16[16,64,128]{2,1,0:T(8,128)(2,1)S(1)}, u32[]{:S(2)}, u32[]{:S(2)}) collective-permute-start(bf16[16,64,128]{2,1,0:T(8,128)(2,1)S(1)} %all_to_all.11.qa_ref), channel_id=1, source_target_pairs={{0,16},{16,0},{1,17},{17,1},{2,18},{18,2},{3,19},{19,3},{4,20},{20... | collective-permute-start | bytes 786440 | tf_op jit(solution)/shard_map/ppermute | solution.py:214
  (5 other events, 14.9 us)

commit v3 on v2

--- a/solution.py
+++ b/solution.py
@@ -10,6 +10,7 @@
 HIGH = lax.Precision.HIGHEST
 MIB = 1024 * 1024
 ANY = pl.BlockSpec(memory_space=pl.ANY)
+HBM = pl.BlockSpec(memory_space=pltpu.HBM)
 VMEM = pl.BlockSpec(memory_space=pltpu.VMEM)
 SMEM = pl.BlockSpec(memory_space=pltpu.SMEM)
 
@@ -73,19 +74,22 @@
     return pl.ds(pl.multiple_of(owner * w, w), w)
 
 
-def eq_kernel(qa_ref, qb_ref, act_ref, e_ref, out_ref, at_ref):
+def eq_kernel(q0, q1, q2, q3, act_ref, e_ref, es_ref, own_ref, sib_ref, at_ref):
     at_ref[...] = act_ref[...].T
-    acc = None
-    for j in range(8):
-        q3 = split3(qa_ref[j] if j < 4 else qb_ref[j - 4])
-        part = dot(q3, e_ref[:, cols(j)], 1, 1)
-        acc = part if acc is None else acc + part
-    out_ref[...] = fold3(acc)
-
-
-def p_kernel(u0, u1, u2, u3, act_ref, eq_ref, out_ref):
+    own = sib = None
+    for k, q in enumerate((q0, q1, q2, q3)):
+        q3 = split3(q[...])
+        a = dot(q3, e_ref[:, cols(k)], 1, 1)
+        b = dot(q3, es_ref[k], 1, 1)
+        own = a if own is None else own + a
+        sib = b if sib is None else sib + b
+    own_ref[...] = fold3(own)
+    sib_ref[...] = fold3(sib)
+
+
+def p_kernel(u0, u1, u2, u3, act_ref, eq_ref, eqs_ref, out_ref):
     u = sum_of((u0, u1, u2, u3))
-    p = fold3(dot(split3(u), act_ref[...], 1, 0)) * (1.0 / 512.0) + eq_ref[...]
+    p = fold3(dot(split3(u), act_ref[...], 1, 0)) * (1.0 / 512.0) + (eq_ref[...] + eqs_ref[...])
     out_ref[...] = p
 
 
@@ -104,9 +108,21 @@
         out_ref[slot, y, 64:96, :] = gram
 
 
-def half_kernel(e_ref, out_ref):
-    for k in range(4):
-        out_ref[k] = e_ref[:, cols(4 + k)]
+def run_copies(pairs, sems):
+    cps = [pltpu.make_async_copy(s, d, sems.at[i]) for i, (s, d) in enumerate(pairs)]
+    for cp in cps:
+        cp.start()
+    for cp in cps:
+        cp.wait()
+
+
+def load_kernel(q, top, br, q_v, top_v, br_v, sems):
+    run_copies(((q, q_v), (top, top_v), (br, br_v)), sems)
+
+
+def load_error_kernel(e, act, eh_v, e_v, act_v, sems):
+    pairs = [(e.at[:, cols(4 + k)], eh_v.at[k]) for k in range(4)]
+    run_copies(pairs + [(act, act_v), (e, e_v)], sems)
 
 
 def pv_kernel(z0, z1, z2, z3, act_ref, out_ref):
@@ -157,13 +173,28 @@
     row = lax.broadcasted_iota(jnp.int32, (n, 2 * n), 0)
     lane = lax.broadcasted_iota(jnp.int32, (n, 2 * n), 1)
     a = jnp.where(lane < n, left, jnp.where(lane == row + n, 1.0, 0.0))
-    for k in range(n):
-        d = a[k : k + 1, k : k + 1]
-        r = lax.rsqrt(d)
-        r = r * (1.5 - 0.5 * d * r * r)
-        rowk = a[k : k + 1, :] * r
-        f = jnp.where(row > k, a[:, k : k + 1] * r, 0.0)
-        a = jnp.where(row == k, rowk, a - f * rowk)
+    for k in range(0, n, 8):
+        rows = [a[k + i : k + i + 1, :] for i in range(8)]
+        fs = [jnp.broadcast_to(a[:, k + i : k + i + 1], (n, 2 * n)) for i in range(8)]
+        for i in range(8):
+            d = fs[i][k + i : k + i + 1, :]
+            r = lax.rsqrt(d)
+            r = r * (1.5 - 0.5 * d * r * r)
+            rows[i] = rows[i] * r
+            fs[i] = fs[i] * r
+            for j in range(i + 1, 8):
+                m = fs[i][k + j : k + j + 1, :]
+                rows[j] = rows[j] - m * rows[i]
+                fs[j] = fs[j] - m * fs[i]
+        upd = fs[0] * rows[0]
+        for i in range(1, 8):
+            upd = upd + fs[i] * rows[i]
+        block = jnp.concatenate(rows, axis=0)
+        parts = [a[:k]] if k else []
+        parts.append(block)
+        if k + 8 < n:
+            parts.append(a[k + 8 :] - upd[k + 8 :])
+        a = jnp.concatenate(parts, axis=0) if len(parts) > 1 else block
     linv = pltpu.roll(a, 64, 1)[:, 0:n]
     linv_ref[...] = linv
     phat = jnp.dot(linv, p_ref[0], precision=HIGH, preferred_element_type=F32)
@@ -187,22 +218,35 @@
         m_ref[j] = dot(at, g, 1, 0) * (1.0 / 512.0) + e_ref[:, cols(j)].astype(F32)
 
 
-def error_kernel(ph2_ref, qa_ref, qb_ref, m_ref, err_hbm, qf_ref, o_buf, sems):
+def error_half(ph2_ref, q_ref, m_ref, err_hbm, o_buf, sems, base):
     ph = -(ph2_ref[...].T)
     outs = []
-    for j in range(8):
-        src = qa_ref if j < 4 else qb_ref
-        base = block_row(j) * 4
-        q = jnp.concatenate([src[base + y] for y in range(4)], axis=1)
-        if j == 0:
-            qf_ref[...] = q.astype(F32)
+    for k in range(4):
+        row = block_row(base + k) * 4
+        q = jnp.concatenate([q_ref[row + y] for y in range(4)], axis=1)
         q2 = jnp.concatenate([q, q], axis=0)
-        o_buf[j] = (m_ref[j] + dot(ph, q2, 1, 0)).astype(BF)
-        o = pltpu.make_async_copy(o_buf.at[j], err_hbm.at[:, cols(j)], sems.at[j])
+        o_buf[k] = (m_ref[base + k] + dot(ph, q2, 1, 0)).astype(BF)
+        o = pltpu.make_async_copy(o_buf.at[k], err_hbm.at[:, cols(base + k)], sems.at[k])
         o.start()
         outs.append(o)
+    return outs
+
+
+def error_own_kernel(ph2_ref, q_ref, m_ref, err_hbm, qf_ref, o_buf, sems):
+    outs = error_half(ph2_ref, q_ref, m_ref, err_hbm, o_buf, sems, 0)
+    row = lax.axis_index("x") * 4
+    qf_ref[...] = jnp.concatenate([q_ref[row + y] for y in range(4)], axis=1).astype(F32)
     for o in outs:
         o.wait()
+
+
+def error_sib_kernel(ph2_ref, q_ref, m_ref, _, err_hbm, o_buf, sems):
+    for o in error_half(ph2_ref, q_ref, m_ref, err_hbm, o_buf, sems, 4):
+        o.wait()
+
+
+def in_hbm(v):
+    return pltpu.with_memory_space_constraint(v, pltpu.HBM)
 
 
 def shift(v, axis, k):
@@ -230,9 +274,26 @@
     qt = q_prev[0].T
 
     qr = lax.ppermute(qt, "pipe", [(0, 1)])
-    qa = jnp.stack(ring(qt, "x"))
-    qb = swap(qa)
-
+    qx = ring(qt, "x")
+    qv, top, br = pl.pallas_call(
+        load_kernel,
+        out_shape=(sds((64, 512), F32), sds((512, 512), BF), sds((512, 512), BF)),
+        in_specs=[HBM] * 3,
+        out_specs=(VMEM,) * 3,
+        scratch_shapes=[pltpu.SemaphoreType.DMA((3,))],
+        compiler_params=params(4),
+        name="load_kernel",
+    )(*(in_hbm(v) for v in (qt, top, br)))
+
+    eh, err, act = pl.pallas_call(
+        load_error_kernel,
+        out_shape=(sds((4, 512, 512), BF), sds((512, 4096), BF), sds((512, 512), BF)),
+        in_specs=[HBM] * 2,
+        out_specs=(VMEM,) * 3,
+        scratch_shapes=[pltpu.SemaphoreType.DMA((6,))],
+        compiler_params=params(12),
+        name="load_error_kernel",
+    )(in_hbm(err), in_hbm(act))
     sent, ua, ub = pl.pallas_call(
         first_kernel,
         out_shape=(sds((512, 512), BF), sds((64, 512), F32), sds((64, 512), F32)),
@@ -240,22 +301,27 @@
         out_specs=(VMEM,) * 3,
         compiler_params=params(6),
         name="first_kernel",
-    )(top, br, qt, qr)
-    err, ua = lax.optimization_barrier((err, ua))
-    eh = pl.pallas_call(
-        half_kernel,
-        out_shape=sds((4, 512, 512), BF),
-        in_specs=[VMEM],
-        out_specs=VMEM,
-        compiler_params=params(10),
-        name="half_kernel",
-    )(err)
+    )(top, br, qv, qr)
+    ub, *qx = lax.optimization_barrier((ub, *qx))
+    ubr = lax.ppermute(ub, "pipe", [(1, 0)])
+    sent, _ = lax.optimization_barrier((sent, eh))
+    recv = lax.ppermute(sent, "pipe", [(1, 0)])
+    u = ua + ubr
+    eh, _ = lax.optimization_barrier((eh, u))
     eh_s = swap(eh)
-    u = ua + lax.ppermute(ub, "pipe", [(1, 0)])
-    sent, u = lax.optimization_barrier((sent, u))
-    recv = lax.ppermute(sent, "pipe", [(1, 0)])
     u = u + swap(u)
     us = ring(u, "x")
+    q0, _ = lax.optimization_barrier((qv, u))
+    eq, eq_sib, act_t = pl.pallas_call(
+        eq_kernel,
+        out_shape=(sds((64, 512), F32), sds((64, 512), F32), sds((512, 512), BF)),
+        in_specs=[VMEM] * 7,
+        out_specs=(VMEM,) * 3,
+        compiler_params=params(12),
+        name="eq_kernel",
+    )(q0, *qx[1:], act, err, eh_s)
+    eqs = swap(eq_sib)
+    recv, _ = lax.optimization_barrier((recv, eq))
 
     grad, grad_in = pl.pallas_call(
         grad_kernel,
@@ -265,27 +331,18 @@
         compiler_params=params(6),
         name="grad_kernel",
     )(top, recv, sent, br)
-    grad, eh_s, *us = lax.optimization_barrier((grad, eh_s, *us))
+    grad, eqs, *us = lax.optimization_barrier((grad, eqs, *us))
     g1 = shift(grad, "x", 1)
     g3 = shift(grad, "x", 3)
-
-    eq, act_t = pl.pallas_call(
-        eq_kernel,
-        out_shape=(sds((64, 512), F32), sds((512, 512), BF)),
-        in_specs=[VMEM] * 4,
-        out_specs=(VMEM, VMEM),
-        compiler_params=params(12),
-        name="eq_kernel",
-    )(qa, qb, act, err)
 
     part = pl.pallas_call(
         p_kernel,
         out_shape=sds((64, 512), F32),
-        in_specs=[VMEM] * 6,
+        in_specs=[VMEM] * 7,
         out_specs=VMEM,
         compiler_params=params(6),
         name="p_kernel",
-    )(*us, act, eq)
+    )(*us, act, eq, eqs)
     part = pl.pallas_call(
         sum_kernel,
         out_shape=sds((64, 512), F32),
@@ -364,15 +421,26 @@
     qfa = exchange(q16, ("x", "y"))
     qfb = swap(qfa)
 
+    scratch = [pltpu.VMEM((4, 512, 512), BF), pltpu.SemaphoreType.DMA((4,))]
     error_next, q_own = pl.pallas_call(
-        error_kernel,
+        error_own_kernel,
         out_shape=(sds((512, 4096), BF), sds((64, 512), F32)),
-        in_specs=[VMEM] * 4,
-        out_specs=(ANY, VMEM),
-        scratch_shapes=[pltpu.VMEM((8, 512, 512), BF), pltpu.SemaphoreType.DMA((8,))],
-        compiler_params=params(18),
-        name="error_kernel",
-    )(ph2, qfa, qfb, matrix)
+        in_specs=[VMEM] * 3,
+        out_specs=(HBM, VMEM),
+        scratch_shapes=scratch,
+        compiler_params=params(14),
+        name="error_own_kernel",
+    )(ph2, qfa, matrix)
+    error_next = pl.pallas_call(
+        error_sib_kernel,
+        out_shape=sds((512, 4096), BF),
+        in_specs=[VMEM] * 3 + [HBM],
+        out_specs=HBM,
+        scratch_shapes=scratch,
+        input_output_aliases={3: 0},
+        compiler_params=params(14),
+        name="error_sib_kernel",
+    )(ph2, qfb, matrix, error_next)
     return (
         grad_in.reshape(branch_grad.shape),
         error_next.reshape(error_prev.shape),

time: 138 us -> 128 us (0.928)
  starting transfers between devices: 58.8 us -> 53 us
  local copies, waits for them, and re-layouts: 5.23 us -> 0.04 us
    ppermute x6, starting transfers between devices: 18.8 us -> 8.88 us  [swap(): return lax.ppermute(v, 'core', [(0, 1), (1, 0)])]
    unnamed x18 -> x0, local copies, waits for them, and re-layouts: 5.2 us -> none
    pallas_call x3 -> x5, Pallas kernels: 4.75 us -> 9.89 us  [the longest x1 3.1 us: on_device(): pl.pallas_call(load_error_kernel, out_shape=(sds((4, 512, 512), BF), sds(...]
    ppermute x1, waiting for transfers between devices: 0.01 us -> 4.65 us  [on_device(): recv = lax.ppermute(sent, 'pipe', [(1, 0)])]
    ppermute x19, starting transfers between devices: 33 us -> 37.2 us  [shift(): return lax.ppermute(v, axis, [(i, (i + k) % n) for i in range(n)])]
    pallas_call x1, Pallas kernels: 6.77 us -> 2.76 us  [on_device(): pl.pallas_call(factor_kernel, out_shape=(sds((64, 512), F32), sds((128, 5...]
    ppermute x1, waiting for transfers between devices: 5.28 us -> 1.3 us  [on_device(): ubr = lax.ppermute(ub, 'pipe', [(1, 0)])]
    ppermute x1, waiting for transfers between devices: 2.46 us -> 0.01 us  [on_device(): qr = lax.ppermute(qt, 'pipe', [(0, 1)])]
  transfers between devices with their start and end apart: 28 -> 28, of which waited for: 14 -> 12; matrix products, arithmetic and copies ran while one was open for 0% -> 0% of each run, Pallas kernels for 9% -> 13%
where the time goes in v3:
time: 128 us
  starting transfers between devices  53 us (41%)
  blocking collectives  30.5 us (24%)
  waiting for transfers between devices  23.7 us (19%)
  Pallas kernels  19.2 us (15%)
    ppermute x19, starting transfers between devices, shift(): return lax.ppermute(v, axis, [(i, (i + k) % n) for i in range(n)])  37.2 us
    all_to_all x2, blocking collectives, exchange(): return lax.all_to_all(v, axes, 0, 0, tiled=True)  30.5 us
    ppermute x19, waiting for transfers between devices, shift(): return lax.ppermute(v, axis, [(i, (i + k) % n) for i in range(n)])  14.6 us
    ppermute x6, starting transfers between devices, swap(): return lax.ppermute(v, 'core', [(0, 1), (1, 0)])  8.88 us
    ppermute x1, waiting for transfers between devices, on_device(): recv = lax.ppermute(sent, 'pipe', [(1, 0)])  4.65 us
    ppermute x1, starting transfers between devices, on_device(): qr = lax.ppermute(qt, 'pipe', [(0, 1)])  4.38 us
    ppermute x6, waiting for transfers between devices, swap(): return lax.ppermute(v, 'core', [(0, 1), (1, 0)])  3.13 us
    pallas_call x1, Pallas kernels, on_device(): pl.pallas_call(load_error_kernel, out_shape=(sds((4, 512, 512), BF), sds(...  3.1 us
  transfers between devices with their start and end apart: 28, of which 12 were waited for; matrix products, arithmetic and copies ran while one was open for 0% of the time, Pallas kernels for 13%

profile of v3, /device:TPU:1, one launch (start us, length us, event | category | flops | bytes accessed | tf_op | source)
XLA Modules:
  0.0 127.5 jit_solution(9891592053744655319)
XLA Ops:
  0.6 4.4 %collective-permute-start = (f32[64,512]{1,0:T(8,128)}, f32[64,512]{1,0:T(8,128)S(1)}, u32[]{:S(2)}, u32[]{:S(2)}) collective-permute-start(f32[64,512]{1,0:T(8,128)} %bitcast.22), channel_id=1, source_target_pairs={{0,128},{1,129},{2,130},{3,131},{4,132},{5,133},{6,134},{7,135},{8... | collective-permute-start | bytes 393224 | tf_op jit(solution)/shard_map/ppermute | solution.py:276
  6.3 2.5 %collective-permute-start.3 = (f32[64,512]{1,0:T(8,128)}, f32[64,512]{1,0:T(8,128)S(1)}, u32[]{:S(2)}, u32[]{:S(2)}) collective-permute-start(f32[64,512]{1,0:T(8,128)} %bitcast.24), channel_id=1, source_target_pairs={{0,64},{32,96},{64,0},{96,32},{1,65},{33,97},{65,1},{97,33},{2,66}... | collective-permute-start | bytes 393224 | tf_op jit(solution)/shard_map/ppermute | solution.py:254
  11.7 2.3 %collective-permute-done.3.q2 = f32[64,512]{1,0:T(8,128)S(1)} collective-permute-done((f32[64,512]{1,0:T(8,128)}, f32[64,512]{1,0:T(8,128)S(1)}, u32[]{:S(2)}, u32[]{:S(2)}) %collective-permute-start.3) | collective-permute-done | bytes 131104 | tf_op jit(solution)/shard_map/ppermute | solution.py:254
  15.8 3.1 %load_error_kernel.1 = (bf16[4,512,512]{2,1,0:T(8,128)(2,1)S(1)}, bf16[512,4096]{1,0:T(8,128)(2,1)S(1)}, bf16[512,512]{1,0:T(8,128)(2,1)S(1)}) custom-call(bf16[512,4096]{1,0:T(8,128)(2,1)} %bitcast.17, bf16[512,512]{1,0:T(8,128)(2,1)} %bitcast.19), custom_call_target="tpu_custom_call" | custom-call | tf_op jit(solution)/shard_map/load_error_kernel/pallas_call | solution.py:288
  18.9 1.3 %collective-permute-done.5 = f32[64,512]{1,0:T(8,128)S(1)} collective-permute-done((f32[64,512]{1,0:T(8,128)S(1)}, f32[64,512]{1,0:T(8,128)S(1)}, u32[]{:S(2)}, u32[]{:S(2)}) %collective-permute-start.5) | collective-permute-done | bytes 131104 | tf_op jit(solution)/shard_map/ppermute | solution.py:306
  20.2 3.0 %collective-permute-start.7 = (bf16[4,512,512]{2,1,0:T(8,128)(2,1)S(1)}, bf16[4,512,512]{2,1,0:T(8,128)(2,1)S(1)}, u32[]{:S(2)}, u32[]{:S(2)}) collective-permute-start(bf16[4,512,512]{2,1,0:T(8,128)(2,1)S(1)} %get-tuple-element.62), channel_id=1, source_target_pairs={{0,16},{16,0},{1,17},{17,1},{2,18},{18,2},{3,19},{19,3},{4,20},{20... | collective-permute-start | bytes 6291464 | tf_op jit(solution)/shard_map/ppermute | solution.py:258
  24.6 2.6 %collective-permute-done.6 = f32[64,512]{1,0:T(8,128)S(1)} collective-permute-done((f32[64,512]{1,0:T(8,128)S(1)}, f32[64,512]{1,0:T(8,128)S(1)}, u32[]{:S(2)}, u32[]{:S(2)}) %collective-permute-start.6) | collective-permute-done | bytes 131104 | tf_op jit(solution)/shard_map/ppermute | solution.py:258
  27.2 2.5 %collective-permute-start.10 = (f32[64,512]{1,0:T(8,128)S(1)}, f32[64,512]{1,0:T(8,128)S(1)}, u32[]{:S(2)}, u32[]{:S(2)}) collective-permute-start(f32[64,512]{1,0:T(8,128)S(1)} %add.7.u0), channel_id=1, source_target_pairs={{0,64},{32,96},{64,0},{96,32},{1,65},{33,97},{65,1},{97,33},{2,66}... | collective-permute-start | bytes 393224 | tf_op jit(solution)/shard_map/ppermute | solution.py:254
  31.1 1.5 %eq_kernel.1 = (f32[64,512]{1,0:T(8,128)S(1)}, f32[64,512]{1,0:T(8,128)S(1)}, bf16[512,512]{1,0:T(8,128)(2,1)S(1)}) custom-call(f32[64,512]{1,0:T(8,128)S(1)} %get-tuple-element.56.q_ref.q0, f32[64,512]{1,0:T(8,128)S(1)} %collective-permute-done.2.q1, f32[64,512]{1,0:T(8,128)S(1)} %collective-permute-done.3.q2, f32[64,512]{1,0:T(8,128)S(1)} %collective-permute-done.4.q3, ...), custom_call_target="tpu_custom_call" | custom-call | tf_op jit(solution)/shard_map/eq_kernel/pallas_call | solution.py:315
  32.6 1.3 %collective-permute-start.8 = (f32[64,512]{1,0:T(8,128)S(1)}, f32[64,512]{1,0:T(8,128)S(1)}, u32[]{:S(2)}, u32[]{:S(2)}) collective-permute-start(f32[64,512]{1,0:T(8,128)S(1)} %get-tuple-element.67), channel_id=1, source_target_pairs={{0,16},{16,0},{1,17},{17,1},{2,18},{18,2},{3,19},{19,3},{4,20},{20... | collective-permute-start | bytes 393224 | tf_op jit(solution)/shard_map/ppermute | solution.py:258
  33.9 4.7 %collective-permute-done.1.recv_ref = bf16[512,512]{1,0:T(8,128)(2,1)S(1)} collective-permute-done((bf16[512,512]{1,0:T(8,128)(2,1)S(1)}, bf16[512,512]{1,0:T(8,128)(2,1)S(1)}, u32[]{:S(2)}, u32[]{:S(2)}) %collective-permute-start.1) | collective-permute-done | bytes 524320 | tf_op jit(solution)/shard_map/ppermute | solution.py:308
  40.7 1.6 %collective-permute-start.16 = (bf16[512,512]{1,0:T(8,128)(2,1)S(1)}, bf16[512,512]{1,0:T(8,128)(2,1)S(1)}, u32[]{:S(2)}, u32[]{:S(2)}) collective-permute-start(bf16[512,512]{1,0:T(8,128)(2,1)S(1)} %get-tuple-element.73.g0), channel_id=1, source_target_pairs={{0,96},{32,0},{64,32},{96,64},{1,97},{33,1},{65,33},{97,65},{2,98}... | collective-permute-start | bytes 1572872 | tf_op jit(solution)/shard_map/ppermute | solution.py:254
  42.6 1.4 %collective-permute-start.12 = (f32[64,512]{1,0:T(8,128)S(1)}, f32[64,512]{1,0:T(8,128)S(1)}, u32[]{:S(2)}, u32[]{:S(2)}) collective-permute-start(f32[64,512]{1,0:T(8,128)S(1)} %p_kernel.1.a), channel_id=1, source_target_pairs={{0,1},{1,2},{2,3},{3,0},{4,5},{5,6},{6,7},{7,4},{8,9},{9,10},{10,1... | collective-permute-start | bytes 393224 | tf_op jit(solution)/shard_map/ppermute | solution.py:254
  44.0 2.6 %collective-permute-start.13 = (f32[64,512]{1,0:T(8,128)S(1)}, f32[64,512]{1,0:T(8,128)S(1)}, u32[]{:S(2)}, u32[]{:S(2)}) collective-permute-start(f32[64,512]{1,0:T(8,128)S(1)} %p_kernel.1.a), channel_id=1, source_target_pairs={{0,2},{1,3},{2,0},{3,1},{4,6},{5,7},{6,4},{7,5},{8,10},{9,11},{10,... | collective-permute-start | bytes 393224 | tf_op jit(solution)/shard_map/ppermute | solution.py:254
  48.1 3.2 %collective-permute-done.13.c = f32[64,512]{1,0:T(8,128)S(1)} collective-permute-done((f32[64,512]{1,0:T(8,128)S(1)}, f32[64,512]{1,0:T(8,128)S(1)}, u32[]{:S(2)}, u32[]{:S(2)}) %collective-permute-start.13) | collective-permute-done | bytes 131104 | tf_op jit(solution)/shard_map/ppermute | solution.py:254
  52.2 1.4 %collective-permute-done.15.g1 = bf16[512,512]{1,0:T(8,128)(2,1)S(1)} collective-permute-done((bf16[512,512]{1,0:T(8,128)(2,1)S(1)}, bf16[512,512]{1,0:T(8,128)(2,1)S(1)}, u32[]{:S(2)}, u32[]{:S(2)}) %collective-permute-start.15) | collective-permute-done | bytes 524320 | tf_op jit(solution)/shard_map/ppermute | solution.py:254
  53.5 3.0 %collective-permute-start.17 = (f32[64,512]{1,0:T(8,128)S(1)}, f32[64,512]{1,0:T(8,128)S(1)}, u32[]{:S(2)}, u32[]{:S(2)}) collective-permute-start(f32[64,512]{1,0:T(8,128)S(1)} %sum_kernel.1.z0), channel_id=1, source_target_pairs={{0,4},{4,8},{8,12},{12,0},{1,5},{5,9},{9,13},{13,1},{2,6},{6,10},{... | collective-permute-start | bytes 393224 | tf_op jit(solution)/shard_map/ppermute | solution.py:254
  56.5 4.2 %collective-permute-start.18 = (f32[64,512]{1,0:T(8,128)S(1)}, f32[64,512]{1,0:T(8,128)S(1)}, u32[]{:S(2)}, u32[]{:S(2)}) collective-permute-start(f32[64,512]{1,0:T(8,128)S(1)} %sum_kernel.1.z0), channel_id=1, source_target_pairs={{0,8},{4,12},{8,0},{12,4},{1,9},{5,13},{9,1},{13,5},{2,10},{6,14},... | collective-permute-start | bytes 393224 | tf_op jit(solution)/shard_map/ppermute | solution.py:254
  60.7 2.4 %collective-permute-start.19 = (f32[64,512]{1,0:T(8,128)S(1)}, f32[64,512]{1,0:T(8,128)S(1)}, u32[]{:S(2)}, u32[]{:S(2)}) collective-permute-start(f32[64,512]{1,0:T(8,128)S(1)} %sum_kernel.1.z0), channel_id=1, source_target_pairs={{0,12},{4,0},{8,4},{12,8},{1,13},{5,1},{9,5},{13,9},{2,14},{6,2},{... | collective-permute-start | bytes 393224 | tf_op jit(solution)/shard_map/ppermute | solution.py:254
  63.8 2.2 %collective-permute-start.22 = (bf16[256,512]{1,0:T(8,128)(2,1)S(1)}, bf16[256,512]{1,0:T(8,128)(2,1)S(1)}, u32[]{:S(2)}, u32[]{:S(2)}) collective-permute-start(bf16[256,512]{1,0:T(8,128)(2,1)S(1)} %slice.7), channel_id=1, source_target_pairs={{0,96},{32,0},{64,32},{96,64},{1,97},{33,1},{65,33},{97,65},{2,98}... | collective-permute-start | bytes 786440 | tf_op jit(solution)/shard_map/ppermute | solution.py:254
  66.0 3.9 %collective-permute-done.18.z2 = f32[64,512]{1,0:T(8,128)S(1)} collective-permute-done((f32[64,512]{1,0:T(8,128)S(1)}, f32[64,512]{1,0:T(8,128)S(1)}, u32[]{:S(2)}, u32[]{:S(2)}) %collective-permute-start.18) | collective-permute-done | bytes 131104 | tf_op jit(solution)/shard_map/ppermute | solution.py:254
  69.9 2.1 %collective-permute-done.19.z3 = f32[64,512]{1,0:T(8,128)S(1)} collective-permute-done((f32[64,512]{1,0:T(8,128)S(1)}, f32[64,512]{1,0:T(8,128)S(1)}, u32[]{:S(2)}, u32[]{:S(2)}) %collective-permute-start.19) | collective-permute-done | bytes 131104 | tf_op jit(solution)/shard_map/ppermute | solution.py:254
  75.8 19.7 %all_to_all.10.in_ref = f32[16,96,128]{2,1,0:T(8,128)S(1)} all-to-all(f32[16,96,128]{2,1,0:T(8,128)S(1)} %bitcast.16), channel_id=1, replica_groups=mesh['pipe'=2,'x'=4,'core'=2,'zhi'=4,'y'=4] {'x','y'}, dimensions={0} | all-to-all | bytes 1572864 | tf_op jit(solution)/shard_map/all_to_all | solution.py:266
  95.6 2.3 %collective-permute-start.23 = (f32[64,128]{1,0:T(8,128)S(1)}, f32[64,128]{1,0:T(8,128)S(1)}, u32[]{:S(2)}, u32[]{:S(2)}) collective-permute-start(f32[64,128]{1,0:T(8,128)S(1)} %get-tuple-element.80.q0), channel_id=1, source_target_pairs={{0,4},{4,8},{8,12},{12,0},{1,5},{5,9},{9,13},{13,1},{2,6},{6,10},{... | collective-permute-start | bytes 98312 | tf_op jit(solution)/shard_map/ppermute | solution.py:254
  97.8 3.2 %collective-permute-start.24 = (f32[64,128]{1,0:T(8,128)S(1)}, f32[64,128]{1,0:T(8,128)S(1)}, u32[]{:S(2)}, u32[]{:S(2)}) collective-permute-start(f32[64,128]{1,0:T(8,128)S(1)} %get-tuple-element.80.q0), channel_id=1, source_target_pairs={{0,8},{4,12},{8,0},{12,4},{1,9},{5,13},{9,1},{13,5},{2,10},{6,14},... | collective-permute-start | bytes 98312 | tf_op jit(solution)/shard_map/ppermute | solution.py:254
  101.1 2.7 %collective-permute-start.25 = (f32[64,128]{1,0:T(8,128)S(1)}, f32[64,128]{1,0:T(8,128)S(1)}, u32[]{:S(2)}, u32[]{:S(2)}) collective-permute-start(f32[64,128]{1,0:T(8,128)S(1)} %get-tuple-element.80.q0), channel_id=1, source_target_pairs={{0,12},{4,0},{8,4},{12,8},{1,13},{5,1},{9,5},{13,9},{2,14},{6,2},{... | collective-permute-start | bytes 98312 | tf_op jit(solution)/shard_map/ppermute | solution.py:254
  103.7 2.8 %factor_kernel.1 = (f32[64,512]{1,0:T(8,128)}, bf16[128,512]{1,0:T(8,128)(2,1)S(1)}, f32[64,64]{1,0:T(8,128)S(1)}) custom-call(f32[32,128]{1,0:T(8,128)S(1)} %get-tuple-element.78.gram_ref, f32[2,64,512]{2,1,0:T(8,128)S(1)} %pv_kernel.1.pv_ref.p_ref), custom_call_target="tpu_custom_call" | custom-call | tf_op jit(solution)/shard_map/factor_kernel/pallas_call | solution.py:395
  106.5 2.3 %matrix_kernel.1.m_ref = f32[8,512,512]{2,1,0:T(8,128)S(1)} custom-call(bf16[512,512]{1,0:T(8,128)(2,1)S(1)} %get-tuple-element.82.at_ref, bf16[4,512,512]{2,1,0:T(8,128)(2,1)S(1)} %get-tuple-element.83.ga_ref, bf16[4,512,512]{2,1,0:T(8,128)(2,1)S(1)} %collective-permute-done.26.gb_ref, bf16[512,4096]{1,0:T(8,128)(2,1)S(1)} %get-tuple-element.61.e_ref), custom_call_target="tpu_custom_call" | custom-call | tf_op jit(solution)/shard_map/matrix_kernel/pallas_call | solution.py:404
  109.1 10.9 %all_to_all.11.q_ref = bf16[16,64,128]{2,1,0:T(8,128)(2,1)S(1)} all-to-all(bf16[16,64,128]{2,1,0:T(8,128)(2,1)S(1)} %q_scale_kernel.1), channel_id=1, replica_groups=mesh['pipe'=2,'x'=4,'core'=2,'zhi'=4,'y'=4] {'x','y'}, dimensions={0} | all-to-all | bytes 524288 | tf_op jit(solution)/shard_map/all_to_all | solution.py:266
  119.9 3.4 %collective-permute-start.27 = (bf16[16,64,128]{2,1,0:T(8,128)(2,1)S(1)}, bf16[16,64,128]{2,1,0:T(8,128)(2,1)S(1)}, u32[]{:S(2)}, u32[]{:S(2)}) collective-permute-start(bf16[16,64,128]{2,1,0:T(8,128)(2,1)S(1)} %all_to_all.11.q_ref), channel_id=1, source_target_pairs={{0,16},{16,0},{1,17},{17,1},{2,18},{18,2},{3,19},{19,3},{4,20},{20... | collective-permute-start | bytes 786440 | tf_op jit(solution)/shard_map/ppermute | solution.py:258
  123.4 2.3 %error_own_kernel.1 = (bf16[512,4096]{1,0:T(8,128)(2,1)}, f32[64,512]{1,0:T(8,128)}) custom-call(bf16[128,512]{1,0:T(8,128)(2,1)S(1)} %get-tuple-element.79.ph2_ref, bf16[16,64,128]{2,1,0:T(8,128)(2,1)S(1)} %all_to_all.11.q_ref, f32[8,512,512]{2,1,0:T(8,128)S(1)} %matrix_kernel.1.m_ref), custom_call_target="tpu_custom_call" | custom-call | tf_op jit(solution)/shard_map/error_own_kernel/pallas_call | solution.py:425
  125.7 1.7 %error_sib_kernel.1 = bf16[512,4096]{1,0:T(8,128)(2,1)} custom-call(bf16[128,512]{1,0:T(8,128)(2,1)S(1)} %get-tuple-element.79.ph2_ref, bf16[16,64,128]{2,1,0:T(8,128)(2,1)S(1)} %collective-permute-done.27.q_ref, f32[8,512,512]{2,1,0:T(8,128)S(1)} %matrix_kernel.1.m_ref, bf16[512,4096]{1,0:T(8,128)(2,1)} %get-tuple-element.87._), custom_call_target="tpu_custom_call", output_to_operand_aliasing={{}: (3, {})} | custom-call | tf_op jit(solution)/shard_map/error_sib_kernel/pallas_call | solution.py:434
  (46 shorter events, 18.3 us)
Async XLA Ops:
  0.6 10.6 %collective-permute-start = (f32[64,512]{1,0:T(8,128)}, f32[64,512]{1,0:T(8,128)S(1)}, u32[]{:S(2)}, u32[]{:S(2)}) collective-permute-start(f32[64,512]{1,0:T(8,128)} %bitcast.22), channel_id=1, source_target_pairs={{0,128},{1,129},{2,130},{3,131},{4,132},{5,133},{6,134},{7,135},{8... | collective-permute-start | bytes 393224 | tf_op jit(solution)/shard_map/ppermute | solution.py:276
  5.0 6.7 %collective-permute-start.2 = (f32[64,512]{1,0:T(8,128)}, f32[64,512]{1,0:T(8,128)S(1)}, u32[]{:S(2)}, u32[]{:S(2)}) collective-permute-start(f32[64,512]{1,0:T(8,128)} %bitcast.23), channel_id=1, source_target_pairs={{0,32},{32,64},{64,96},{96,0},{1,33},{33,65},{65,97},{97,1},{2,34}... | collective-permute-start | bytes 393224 | tf_op jit(solution)/shard_map/ppermute | solution.py:254
  6.3 7.8 %collective-permute-start.3 = (f32[64,512]{1,0:T(8,128)}, f32[64,512]{1,0:T(8,128)S(1)}, u32[]{:S(2)}, u32[]{:S(2)}) collective-permute-start(f32[64,512]{1,0:T(8,128)} %bitcast.24), channel_id=1, source_target_pairs={{0,64},{32,96},{64,0},{96,32},{1,65},{33,97},{65,1},{97,33},{2,66}... | collective-permute-start | bytes 393224 | tf_op jit(solution)/shard_map/ppermute | solution.py:254
  8.8 5.7 %collective-permute-start.4 = (f32[64,512]{1,0:T(8,128)}, f32[64,512]{1,0:T(8,128)S(1)}, u32[]{:S(2)}, u32[]{:S(2)}) collective-permute-start(f32[64,512]{1,0:T(8,128)} %bitcast.25), channel_id=1, source_target_pairs={{0,96},{32,0},{64,32},{96,64},{1,97},{33,1},{65,33},{97,65},{2,98}... | collective-permute-start | bytes 393224 | tf_op jit(solution)/shard_map/ppermute | solution.py:254
  14.5 5.7 %collective-permute-start.5 = (f32[64,512]{1,0:T(8,128)S(1)}, f32[64,512]{1,0:T(8,128)S(1)}, u32[]{:S(2)}, u32[]{:S(2)}) collective-permute-start(f32[64,512]{1,0:T(8,128)S(1)} %get-tuple-element.55), channel_id=1, source_target_pairs={{128,0},{129,1},{130,2},{131,3},{132,4},{133,5},{134,6},{135,7},{1... | collective-permute-start | bytes 393224 | tf_op jit(solution)/shard_map/ppermute | solution.py:306
  20.2 10.9 %collective-permute-start.7 = (bf16[4,512,512]{2,1,0:T(8,128)(2,1)S(1)}, bf16[4,512,512]{2,1,0:T(8,128)(2,1)S(1)}, u32[]{:S(2)}, u32[]{:S(2)}) collective-permute-start(bf16[4,512,512]{2,1,0:T(8,128)(2,1)S(1)} %get-tuple-element.62), channel_id=1, source_target_pairs={{0,16},{16,0},{1,17},{17,1},{2,18},{18,2},{3,19},{19,3},{4,20},{20... | collective-permute-start | bytes 6291464 | tf_op jit(solution)/shard_map/ppermute | solution.py:258
  23.2 15.4 %collective-permute-start.1 = (bf16[512,512]{1,0:T(8,128)(2,1)S(1)}, bf16[512,512]{1,0:T(8,128)(2,1)S(1)}, u32[]{:S(2)}, u32[]{:S(2)}) collective-permute-start(bf16[512,512]{1,0:T(8,128)(2,1)S(1)} %get-tuple-element.52.s_ref), channel_id=1, source_target_pairs={{128,0},{129,1},{130,2},{131,3},{132,4},{133,5},{134,6},{135,7},{1... | collective-permute-start | bytes 1572872 | tf_op jit(solution)/shard_map/ppermute | solution.py:308
  24.5 2.7 %collective-permute-start.6 = (f32[64,512]{1,0:T(8,128)S(1)}, f32[64,512]{1,0:T(8,128)S(1)}, u32[]{:S(2)}, u32[]{:S(2)}) collective-permute-start(f32[64,512]{1,0:T(8,128)S(1)} %add.6), channel_id=1, source_target_pairs={{0,16},{16,0},{1,17},{17,1},{2,18},{18,2},{3,19},{19,3},{4,20},{20... | collective-permute-start | bytes 393224 | tf_op jit(solution)/shard_map/ppermute | solution.py:258
  27.2 12.4 %collective-permute-start.10 = (f32[64,512]{1,0:T(8,128)S(1)}, f32[64,512]{1,0:T(8,128)S(1)}, u32[]{:S(2)}, u32[]{:S(2)}) collective-permute-start(f32[64,512]{1,0:T(8,128)S(1)} %add.7.u0), channel_id=1, source_target_pairs={{0,64},{32,96},{64,0},{96,32},{1,65},{33,97},{65,1},{97,33},{2,66}... | collective-permute-start | bytes 393224 | tf_op jit(solution)/shard_map/ppermute | solution.py:254
  29.6 9.9 %collective-permute-start.11 = (f32[64,512]{1,0:T(8,128)S(1)}, f32[64,512]{1,0:T(8,128)S(1)}, u32[]{:S(2)}, u32[]{:S(2)}) collective-permute-start(f32[64,512]{1,0:T(8,128)S(1)} %add.7.u0), channel_id=1, source_target_pairs={{0,96},{32,0},{64,32},{96,64},{1,97},{33,1},{65,33},{97,65},{2,98}... | collective-permute-start | bytes 393224 | tf_op jit(solution)/shard_map/ppermute | solution.py:254
  30.7 8.8 %collective-permute-start.9 = (f32[64,512]{1,0:T(8,128)S(1)}, f32[64,512]{1,0:T(8,128)S(1)}, u32[]{:S(2)}, u32[]{:S(2)}) collective-permute-start(f32[64,512]{1,0:T(8,128)S(1)} %add.7.u0), channel_id=1, source_target_pairs={{0,32},{32,64},{64,96},{96,0},{1,33},{33,65},{65,97},{97,1},{2,34}... | collective-permute-start | bytes 393224 | tf_op jit(solution)/shard_map/ppermute | solution.py:254
  32.6 6.9 %collective-permute-start.8 = (f32[64,512]{1,0:T(8,128)S(1)}, f32[64,512]{1,0:T(8,128)S(1)}, u32[]{:S(2)}, u32[]{:S(2)}) collective-permute-start(f32[64,512]{1,0:T(8,128)S(1)} %get-tuple-element.67), channel_id=1, source_target_pairs={{0,16},{16,0},{1,17},{17,1},{2,18},{18,2},{3,19},{19,3},{4,20},{20... | collective-permute-start | bytes 393224 | tf_op jit(solution)/shard_map/ppermute | solution.py:258
  39.6 13.9 %collective-permute-start.15 = (bf16[512,512]{1,0:T(8,128)(2,1)S(1)}, bf16[512,512]{1,0:T(8,128)(2,1)S(1)}, u32[]{:S(2)}, u32[]{:S(2)}) collective-permute-start(bf16[512,512]{1,0:T(8,128)(2,1)S(1)} %get-tuple-element.73.g0), channel_id=1, source_target_pairs={{0,32},{32,64},{64,96},{96,0},{1,33},{33,65},{65,97},{97,1},{2,34}... | collective-permute-start | bytes 1572872 | tf_op jit(solution)/shard_map/ppermute | solution.py:254
  40.7 12.8 %collective-permute-start.16 = (bf16[512,512]{1,0:T(8,128)(2,1)S(1)}, bf16[512,512]{1,0:T(8,128)(2,1)S(1)}, u32[]{:S(2)}, u32[]{:S(2)}) collective-permute-start(bf16[512,512]{1,0:T(8,128)(2,1)S(1)} %get-tuple-element.73.g0), channel_id=1, source_target_pairs={{0,96},{32,0},{64,32},{96,64},{1,97},{33,1},{65,33},{97,65},{2,98}... | collective-permute-start | bytes 1572872 | tf_op jit(solution)/shard_map/ppermute | solution.py:254
  42.6 5.5 %collective-permute-start.12 = (f32[64,512]{1,0:T(8,128)S(1)}, f32[64,512]{1,0:T(8,128)S(1)}, u32[]{:S(2)}, u32[]{:S(2)}) collective-permute-start(f32[64,512]{1,0:T(8,128)S(1)} %p_kernel.1.a), channel_id=1, source_target_pairs={{0,1},{1,2},{2,3},{3,0},{4,5},{5,6},{6,7},{7,4},{8,9},{9,10},{10,1... | collective-permute-start | bytes 393224 | tf_op jit(solution)/shard_map/ppermute | solution.py:254
  44.0 7.3 %collective-permute-start.13 = (f32[64,512]{1,0:T(8,128)S(1)}, f32[64,512]{1,0:T(8,128)S(1)}, u32[]{:S(2)}, u32[]{:S(2)}) collective-permute-start(f32[64,512]{1,0:T(8,128)S(1)} %p_kernel.1.a), channel_id=1, source_target_pairs={{0,2},{1,3},{2,0},{3,1},{4,6},{5,7},{6,4},{7,5},{8,10},{9,11},{10,... | collective-permute-start | bytes 393224 | tf_op jit(solution)/shard_map/ppermute | solution.py:254
  46.6 5.5 %collective-permute-start.14 = (f32[64,512]{1,0:T(8,128)S(1)}, f32[64,512]{1,0:T(8,128)S(1)}, u32[]{:S(2)}, u32[]{:S(2)}) collective-permute-start(f32[64,512]{1,0:T(8,128)S(1)} %p_kernel.1.a), channel_id=1, source_target_pairs={{0,3},{1,0},{2,1},{3,2},{4,7},{5,4},{6,5},{7,6},{8,11},{9,8},{10,9... | collective-permute-start | bytes 393224 | tf_op jit(solution)/shard_map/ppermute | solution.py:254
  53.5 12.5 %collective-permute-start.17 = (f32[64,512]{1,0:T(8,128)S(1)}, f32[64,512]{1,0:T(8,128)S(1)}, u32[]{:S(2)}, u32[]{:S(2)}) collective-permute-start(f32[64,512]{1,0:T(8,128)S(1)} %sum_kernel.1.z0), channel_id=1, source_target_pairs={{0,4},{4,8},{8,12},{12,0},{1,5},{5,9},{9,13},{13,1},{2,6},{6,10},{... | collective-permute-start | bytes 393224 | tf_op jit(solution)/shard_map/ppermute | solution.py:254
  56.5 13.3 %collective-permute-start.18 = (f32[64,512]{1,0:T(8,128)S(1)}, f32[64,512]{1,0:T(8,128)S(1)}, u32[]{:S(2)}, u32[]{:S(2)}) collective-permute-start(f32[64,512]{1,0:T(8,128)S(1)} %sum_kernel.1.z0), channel_id=1, source_target_pairs={{0,8},{4,12},{8,0},{12,4},{1,9},{5,13},{9,1},{13,5},{2,10},{6,14},... | collective-permute-start | bytes 393224 | tf_op jit(solution)/shard_map/ppermute | solution.py:254
  60.7 11.3 %collective-permute-start.19 = (f32[64,512]{1,0:T(8,128)S(1)}, f32[64,512]{1,0:T(8,128)S(1)}, u32[]{:S(2)}, u32[]{:S(2)}) collective-permute-start(f32[64,512]{1,0:T(8,128)S(1)} %sum_kernel.1.z0), channel_id=1, source_target_pairs={{0,12},{4,0},{8,4},{12,8},{1,13},{5,1},{9,5},{13,9},{2,14},{6,2},{... | collective-permute-start | bytes 393224 | tf_op jit(solution)/shard_map/ppermute | solution.py:254
  63.1 10.4 %collective-permute-start.21 = (bf16[256,512]{1,0:T(8,128)(2,1)S(1)}, bf16[256,512]{1,0:T(8,128)(2,1)S(1)}, u32[]{:S(2)}, u32[]{:S(2)}) collective-permute-start(bf16[256,512]{1,0:T(8,128)(2,1)S(1)} %slice.6), channel_id=1, source_target_pairs={{0,32},{32,64},{64,96},{96,0},{1,33},{33,65},{65,97},{97,1},{2,34}... | collective-permute-start | bytes 786440 | tf_op jit(solution)/shard_map/ppermute | solution.py:254
  63.8 9.8 %collective-permute-start.22 = (bf16[256,512]{1,0:T(8,128)(2,1)S(1)}, bf16[256,512]{1,0:T(8,128)(2,1)S(1)}, u32[]{:S(2)}, u32[]{:S(2)}) collective-permute-start(bf16[256,512]{1,0:T(8,128)(2,1)S(1)} %slice.7), channel_id=1, source_target_pairs={{0,96},{32,0},{64,32},{96,64},{1,97},{33,1},{65,33},{97,65},{2,98}... | collective-permute-start | bytes 786440 | tf_op jit(solution)/shard_map/ppermute | solution.py:254
  72.3 1.7 %collective-permute-start.20 = (f32[2,64,512]{2,1,0:T(8,128)S(1)}, f32[2,64,512]{2,1,0:T(8,128)S(1)}, u32[]{:S(2)}, u32[]{:S(2)}) collective-permute-start(f32[2,64,512]{2,1,0:T(8,128)S(1)} %pv_kernel.1.pv_ref.p_ref), channel_id=1, source_target_pairs={{0,16},{16,0},{1,17},{17,1},{2,18},{18,2},{3,19},{19,3},{4,20},{20... | collective-permute-start | bytes 786440 | tf_op jit(solution)/shard_map/ppermute | solution.py:258
  75.4 31.1 %collective-permute-start.26 = (bf16[4,512,512]{2,1,0:T(8,128)(2,1)S(1)}, bf16[4,512,512]{2,1,0:T(8,128)(2,1)S(1)}, u32[]{:S(2)}, u32[]{:S(2)}) collective-permute-start(bf16[4,512,512]{2,1,0:T(8,128)(2,1)S(1)} %get-tuple-element.83.ga_ref), channel_id=1, source_target_pairs={{0,16},{16,0},{1,17},{17,1},{2,18},{18,2},{3,19},{19,3},{4,20},{20... | collective-permute-start | bytes 6291464 | tf_op jit(solution)/shard_map/ppermute | solution.py:258
  95.6 13.3 %collective-permute-start.23 = (f32[64,128]{1,0:T(8,128)S(1)}, f32[64,128]{1,0:T(8,128)S(1)}, u32[]{:S(2)}, u32[]{:S(2)}) collective-permute-start(f32[64,128]{1,0:T(8,128)S(1)} %get-tuple-element.80.q0), channel_id=1, source_target_pairs={{0,4},{4,8},{8,12},{12,0},{1,5},{5,9},{9,13},{13,1},{2,6},{6,10},{... | collective-permute-start | bytes 98312 | tf_op jit(solution)/shard_map/ppermute | solution.py:254
  97.8 11.0 %collective-permute-start.24 = (f32[64,128]{1,0:T(8,128)S(1)}, f32[64,128]{1,0:T(8,128)S(1)}, u32[]{:S(2)}, u32[]{:S(2)}) collective-permute-start(f32[64,128]{1,0:T(8,128)S(1)} %get-tuple-element.80.q0), channel_id=1, source_target_pairs={{0,8},{4,12},{8,0},{12,4},{1,9},{5,13},{9,1},{13,5},{2,10},{6,14},... | collective-permute-start | bytes 98312 | tf_op jit(solution)/shard_map/ppermute | solution.py:254
  101.1 7.8 %collective-permute-start.25 = (f32[64,128]{1,0:T(8,128)S(1)}, f32[64,128]{1,0:T(8,128)S(1)}, u32[]{:S(2)}, u32[]{:S(2)}) collective-permute-start(f32[64,128]{1,0:T(8,128)S(1)} %get-tuple-element.80.q0), channel_id=1, source_target_pairs={{0,12},{4,0},{8,4},{12,8},{1,13},{5,1},{9,5},{13,9},{2,14},{6,2},{... | collective-permute-start | bytes 98312 | tf_op jit(solution)/shard_map/ppermute | solution.py:254
  119.9 5.8 %collective-permute-start.27 = (bf16[16,64,128]{2,1,0:T(8,128)(2,1)S(1)}, bf16[16,64,128]{2,1,0:T(8,128)(2,1)S(1)}, u32[]{:S(2)}, u32[]{:S(2)}) collective-permute-start(bf16[16,64,128]{2,1,0:T(8,128)(2,1)S(1)} %all_to_all.11.q_ref), channel_id=1, source_target_pairs={{0,16},{16,0},{1,17},{17,1},{2,18},{18,2},{3,19},{19,3},{4,20},{20... | collective-permute-start | bytes 786440 | tf_op jit(solution)/shard_map/ppermute | solution.py:258

commit v4 on v3

--- a/solution.py
+++ b/solution.py
@@ -15,6 +15,9 @@
 SMEM = pl.BlockSpec(memory_space=pltpu.SMEM)
 
 
+LIGHT = pl.CostEstimate(flops=0, transcendentals=0, bytes_accessed=0)
+
+
 def sds(shape, dtype):
     return jax.ShapeDtypeStruct(shape, dtype)
 
@@ -40,28 +43,22 @@
     return lax.dot_general(a, b, (((ca,), (cb,)), ((), ())), preferred_element_type=F32)
 
 
-def first_kernel(top_ref, br_ref, q_ref, qr_ref, s_ref, ua_ref, ub_ref):
-    top = top_ref[...]
-    s = (top.astype(F32) + br_ref[...].astype(F32)).astype(BF)
-    s_ref[...] = s
-    ub_ref[...] = fold3(dot(split3(qr_ref[...]), s, 1, 1))
-    ua = fold3(dot(split3(q_ref[...]), top, 1, 1))
-    ua_ref[...] = jnp.where(lax.axis_index("pipe") == 1, ua, 0.0)
-
-
-def grad_kernel(top_ref, recv_ref, s_ref, br_ref, g_ref, gin_ref):
+def u_kernel(top_ref, recv_ref, q_ref, g_ref, u_ref):
     last = lax.axis_index("pipe")
 
     @pl.when(last == 1)
     def _():
         g_ref[...] = top_ref[...]
-        gin_ref[...] = s_ref[...]
 
     @pl.when(last == 0)
     def _():
-        g = recv_ref[...]
-        g_ref[...] = g
-        gin_ref[...] = (g.astype(F32) + br_ref[...].astype(F32)).astype(BF)
+        g_ref[...] = recv_ref[...]
+
+    u_ref[...] = fold3(dot(split3(q_ref[...]), g_ref[...], 1, 1))
+
+
+def grad_in_kernel(g_ref, br_ref, gin_ref):
+    gin_ref[...] = (g_ref[...].astype(F32) + br_ref[...].astype(F32)).astype(BF)
 
 
 def block_row(j):
@@ -79,7 +76,7 @@
     own = sib = None
     for k, q in enumerate((q0, q1, q2, q3)):
         q3 = split3(q[...])
-        a = dot(q3, e_ref[:, cols(k)], 1, 1)
+        a = dot(q3, e_ref[k], 1, 1)
         b = dot(q3, es_ref[k], 1, 1)
         own = a if own is None else own + a
         sib = b if sib is None else sib + b
@@ -105,7 +102,7 @@
 def put_chunks(out_ref, slot, r, gram):
     for y in range(4):
         out_ref[slot, y, 0:64, :] = r[:, y * 128 : (y + 1) * 128]
-        out_ref[slot, y, 64:96, :] = gram
+        out_ref[slot, y, 64:72, :] = gram
 
 
 def run_copies(pairs, sems):
@@ -116,13 +113,15 @@
         cp.wait()
 
 
-def load_kernel(q, top, br, q_v, top_v, br_v, sems):
+def load_kernel(q, top, br, q_v, top_v, br_v, s_v, sems):
     run_copies(((q, q_v), (top, top_v), (br, br_v)), sems)
+    s_v[...] = (top_v[...].astype(F32) + br_v[...].astype(F32)).astype(BF)
 
 
 def load_error_kernel(e, act, eh_v, e_v, act_v, sems):
     pairs = [(e.at[:, cols(4 + k)], eh_v.at[k]) for k in range(4)]
-    run_copies(pairs + [(act, act_v), (e, e_v)], sems)
+    pairs += [(e.at[:, cols(k)], e_v.at[k]) for k in range(4)]
+    run_copies(pairs + [(act, act_v)], sems)
 
 
 def pv_kernel(z0, z1, z2, z3, act_ref, out_ref):
@@ -134,10 +133,10 @@
 def q_own_kernel(pv_ref, e_ref, out_ref):
     p3 = split3(pv_ref[0])
     for k in range(4):
-        out_ref[k] = fold3(dot(p3, e_ref[:, cols(k)], 1, 0))
-
-
-def q_kernel(pv_ref, pvs_ref, r_ref, es_ref, g0, g1, g2a, g2b, g3, out_ref, gs_ref):
+        out_ref[k] = fold3(dot(p3, e_ref[k], 1, 0))
+
+
+def q_kernel(pv_ref, pvs_ref, r_ref, es_ref, g0, g1, g2a, g2b, g3, out_ref, gs_ref, gram_scr):
     v3 = split3(pv_ref[1] + pvs_ref[1])
     q3 = split3(pvs_ref[0])
 
@@ -145,7 +144,8 @@
         return dot(p3, p3[0:64], 1, 1) + (dot(p3, p3[64:128], 1, 1) + dot(p3, p3[128:192], 1, 1))
 
     g = fold3(gram_of(split3(pv_ref[0])) + gram_of(q3))
-    gram = jnp.concatenate([g[0:32], g[32:64]], axis=1)
+    gram_scr[...] = jnp.concatenate([g[0:32], g[32:64]], axis=1)
+    gram = gram_scr[pl.ds(pl.multiple_of(lax.axis_index("y") * 8, 8), 8), :]
     for k, gr in enumerate((g0, g1, None, g3)):
         if k == 2:
             vg = dot(v3[:, 0:256], g2a[...], 1, 0) + dot(v3[:, 256:512], g2b[...], 1, 0)
@@ -159,15 +159,17 @@
 
 
 def chunk_sum_kernel(in_ref, q_ref, gram_ref):
-    s = in_ref[0]
+    s = in_ref[0, 0:64]
     for k in range(1, 16):
-        s = s + in_ref[k]
-    q_ref[...] = s[0:64]
-    gram_ref[...] = s[64:96]
+        s = s + in_ref[k, 0:64]
+    q_ref[...] = s
+    for y in range(4):
+        g = (in_ref[y, 64:72] + in_ref[4 + y, 64:72]) + (in_ref[8 + y, 64:72] + in_ref[12 + y, 64:72])
+        gram_ref[8 * y : 8 * y + 8] = g
 
 
 def factor_kernel(gram_ref, p_ref, phat_ref, ph2_ref, linv_ref):
-    gp = gram_ref[...] * 0.25
+    gp = gram_ref[...]
     n = 64
     left = jnp.concatenate([gp, pltpu.roll(gp, 64, 1)], axis=0)
     row = lax.broadcasted_iota(jnp.int32, (n, 2 * n), 0)
@@ -211,11 +213,11 @@
         out_ref[k] = q
 
 
-def matrix_kernel(at_ref, ga_ref, gb_ref, e_ref, m_ref):
+def matrix_kernel(at_ref, ga_ref, gb_ref, ea_ref, eb_ref, m_ref):
     at = at_ref[...]
     for j in range(8):
-        g = ga_ref[j] if j < 4 else gb_ref[j - 4]
-        m_ref[j] = dot(at, g, 1, 0) * (1.0 / 512.0) + e_ref[:, cols(j)].astype(F32)
+        g, e = (ga_ref[j], ea_ref[j]) if j < 4 else (gb_ref[j - 4], eb_ref[j - 4])
+        m_ref[j] = dot(at, g, 1, 0) * (1.0 / 512.0) + e.astype(F32)
 
 
 def error_half(ph2_ref, q_ref, m_ref, err_hbm, o_buf, sems, base):
@@ -273,121 +275,131 @@
     err = error_prev.reshape(512, 4096)
     qt = q_prev[0].T
 
-    qr = lax.ppermute(qt, "pipe", [(0, 1)])
-    qx = ring(qt, "x")
-    qv, top, br = pl.pallas_call(
+    qv, top, br, sent = pl.pallas_call(
         load_kernel,
-        out_shape=(sds((64, 512), F32), sds((512, 512), BF), sds((512, 512), BF)),
+        out_shape=(sds((64, 512), F32), sds((512, 512), BF), sds((512, 512), BF), sds((512, 512), BF)),
         in_specs=[HBM] * 3,
-        out_specs=(VMEM,) * 3,
+        out_specs=(VMEM,) * 4,
         scratch_shapes=[pltpu.SemaphoreType.DMA((3,))],
+        cost_estimate=LIGHT,
         compiler_params=params(4),
         name="load_kernel",
     )(*(in_hbm(v) for v in (qt, top, br)))
 
+    recv = lax.ppermute(sent, "pipe", [(1, 0)])
+    qx = ring(qt, "x")
+    err, *_ = lax.optimization_barrier((in_hbm(err), *qx[1:]))
     eh, err, act = pl.pallas_call(
         load_error_kernel,
-        out_shape=(sds((4, 512, 512), BF), sds((512, 4096), BF), sds((512, 512), BF)),
+        out_shape=(sds((4, 512, 512), BF), sds((4, 512, 512), BF), sds((512, 512), BF)),
         in_specs=[HBM] * 2,
         out_specs=(VMEM,) * 3,
-        scratch_shapes=[pltpu.SemaphoreType.DMA((6,))],
+        scratch_shapes=[pltpu.SemaphoreType.DMA((9,))],
+        cost_estimate=LIGHT,
         compiler_params=params(12),
         name="load_error_kernel",
-    )(in_hbm(err), in_hbm(act))
-    sent, ua, ub = pl.pallas_call(
-        first_kernel,
-        out_shape=(sds((512, 512), BF), sds((64, 512), F32), sds((64, 512), F32)),
-        in_specs=[VMEM] * 4,
-        out_specs=(VMEM,) * 3,
+    )(err, in_hbm(act))
+    recv, err = lax.optimization_barrier((recv, err))
+
+    grad, u = pl.pallas_call(
+        u_kernel,
+        out_shape=(sds((512, 512), BF), sds((64, 512), F32)),
+        in_specs=[VMEM] * 3,
+        out_specs=(VMEM,) * 2,
+        cost_estimate=LIGHT,
         compiler_params=params(6),
-        name="first_kernel",
-    )(top, br, qv, qr)
-    ub, *qx = lax.optimization_barrier((ub, *qx))
-    ubr = lax.ppermute(ub, "pipe", [(1, 0)])
-    sent, _ = lax.optimization_barrier((sent, eh))
-    recv = lax.ppermute(sent, "pipe", [(1, 0)])
-    u = ua + ubr
+        name="u_kernel",
+    )(top, recv, qv)
+    grad_in = pl.pallas_call(
+        grad_in_kernel,
+        out_shape=sds((512, 512), BF),
+        in_specs=[VMEM] * 2,
+        out_specs=VMEM,
+        cost_estimate=LIGHT,
+        compiler_params=params(6),
+        name="grad_in_kernel",
+    )(grad, br)
+    other, grad_in = lax.optimization_barrier((swap(u), grad_in))
+    u = u + other
     eh, _ = lax.optimization_barrier((eh, u))
     eh_s = swap(eh)
-    u = u + swap(u)
     us = ring(u, "x")
-    q0, _ = lax.optimization_barrier((qv, u))
     eq, eq_sib, act_t = pl.pallas_call(
         eq_kernel,
         out_shape=(sds((64, 512), F32), sds((64, 512), F32), sds((512, 512), BF)),
         in_specs=[VMEM] * 7,
         out_specs=(VMEM,) * 3,
+        cost_estimate=LIGHT,
         compiler_params=params(12),
         name="eq_kernel",
-    )(q0, *qx[1:], act, err, eh_s)
+    )(qv, *qx[1:], act, err, eh_s)
     eqs = swap(eq_sib)
-    recv, _ = lax.optimization_barrier((recv, eq))
-
-    grad, grad_in = pl.pallas_call(
-        grad_kernel,
-        out_shape=(sds((512, 512), BF), sds((512, 512), BF)),
-        in_specs=[VMEM] * 4,
-        out_specs=(VMEM,) * 2,
-        compiler_params=params(6),
-        name="grad_kernel",
-    )(top, recv, sent, br)
-    grad, eqs, *us = lax.optimization_barrier((grad, eqs, *us))
-    g1 = shift(grad, "x", 1)
-    g3 = shift(grad, "x", 3)
 
     part = pl.pallas_call(
         p_kernel,
         out_shape=sds((64, 512), F32),
         in_specs=[VMEM] * 7,
         out_specs=VMEM,
+        cost_estimate=LIGHT,
         compiler_params=params(6),
         name="p_kernel",
     )(*us, act, eq, eqs)
+    grad, *_ = lax.optimization_barrier((grad, eqs, *us))
+    g1 = shift(grad, "x", 1)
+    g3 = shift(grad, "x", 3)
     part = pl.pallas_call(
         sum_kernel,
         out_shape=sds((64, 512), F32),
         in_specs=[VMEM] * 4,
         out_specs=VMEM,
+        cost_estimate=LIGHT,
         compiler_params=params(4),
         name="sum_kernel",
     )(*ring(part, "y"))
 
-    part, g1, g3 = lax.optimization_barrier((part, g1, g3))
-    g2a = shift(g1[:256], "x", 1)
-    g2b = shift(g3[256:], "x", 3)
+    h1, h3, _ = lax.optimization_barrier((g1, g3, part))
+    g2a = shift(h1[:256], "x", 1)
+    g2b = shift(h3[256:], "x", 3)
+    zs = ring(part, "zhi")
+    g2a, g2b, *zs = lax.optimization_barrier((g2a, g2b, *zs))
     pv = pl.pallas_call(
         pv_kernel,
         out_shape=sds((2, 64, 512), F32),
         in_specs=[VMEM] * 5,
         out_specs=VMEM,
+        cost_estimate=LIGHT,
         compiler_params=params(4),
         name="pv_kernel",
-    )(*ring(part, "zhi"), act)
+    )(*zs, act)
     pvs = swap(pv)
     q_own_part = pl.pallas_call(
         q_own_kernel,
         out_shape=sds((4, 64, 512), F32),
         in_specs=[VMEM] * 2,
         out_specs=VMEM,
+        cost_estimate=LIGHT,
         compiler_params=params(8),
         name="q_own_kernel",
     )(pv, err)
     chunks, gs = pl.pallas_call(
         q_kernel,
-        out_shape=(sds((4, 4, 96, 128), F32), sds((4, 512, 512), BF)),
+        out_shape=(sds((4, 4, 72, 128), F32), sds((4, 512, 512), BF)),
         in_specs=[VMEM] * 9,
         out_specs=(VMEM, VMEM),
+        scratch_shapes=[pltpu.VMEM((32, 128), F32)],
+        cost_estimate=LIGHT,
         compiler_params=params(12),
         name="q_kernel",
     )(pv, pvs, q_own_part, eh_s, grad, g1, g2a, g2b, g3)
     gb = swap(gs)
-    chunks = exchange(chunks.reshape(16, 96, 128), ("x", "y"))
+    chunks = exchange(chunks.reshape(16, 72, 128), ("x", "y"))
 
     q_part, gram = pl.pallas_call(
         chunk_sum_kernel,
         out_shape=(sds((64, 128), F32), sds((32, 128), F32)),
         in_specs=[VMEM],
         out_specs=(VMEM, VMEM),
+        cost_estimate=LIGHT,
         compiler_params=params(4),
         name="chunk_sum_kernel",
     )(chunks)
@@ -397,6 +409,7 @@
         out_shape=(sds((64, 512), F32), sds((128, 512), BF), sds((64, 64), F32)),
         in_specs=[VMEM, VMEM],
         out_specs=(VMEM, VMEM, VMEM),
+        cost_estimate=LIGHT,
         compiler_params=params(4),
         name="factor_kernel",
     )(gram, pv)
@@ -404,17 +417,19 @@
     matrix = pl.pallas_call(
         matrix_kernel,
         out_shape=sds((8, 512, 512), F32),
-        in_specs=[VMEM] * 4,
-        out_specs=VMEM,
+        in_specs=[VMEM] * 5,
+        out_specs=VMEM,
+        cost_estimate=LIGHT,
         compiler_params=params(20),
         name="matrix_kernel",
-    )(act_t, gs, gb, err)
+    )(act_t, gs, gb, err, eh)
     matrix, linv = lax.optimization_barrier((matrix, linv))
     q16 = pl.pallas_call(
         q_scale_kernel,
         out_shape=sds((16, 64, 128), BF),
         in_specs=[VMEM] * 5,
         out_specs=VMEM,
+        cost_estimate=LIGHT,
         compiler_params=params(4),
         name="q_scale_kernel",
     )(*qs, linv)
@@ -428,6 +443,7 @@
         in_specs=[VMEM] * 3,
         out_specs=(HBM, VMEM),
         scratch_shapes=scratch,
+        cost_estimate=LIGHT,
         compiler_params=params(14),
         name="error_own_kernel",
     )(ph2, qfa, matrix)
@@ -438,6 +454,7 @@
         out_specs=HBM,
         scratch_shapes=scratch,
         input_output_aliases={3: 0},
+        cost_estimate=LIGHT,
         compiler_params=params(14),
         name="error_sib_kernel",
     )(ph2, qfb, matrix, error_next)

time: 128 us -> 121 us (0.945)
  blocking collectives: 30.5 us -> 27.2 us
  starting transfers between devices: 53 us -> 50.7 us
    ppermute x19, waiting for transfers between devices: 14.6 us -> 22.5 us  [shift(): return lax.ppermute(v, axis, [(i, (i + k) % n) for i in range(n)])]
    ppermute x2 -> x0, starting transfers between devices: 5.66 us -> none  [the longest x1 4.38 us: on_device(): qr = lax.ppermute(qt, 'pipe', [(0, 1)])]
    ppermute x1, waiting for transfers between devices: 4.65 us -> 0.01 us  [on_device(): recv = lax.ppermute(sent, 'pipe', [(1, 0)])]
    all_to_all x2, blocking collectives: 30.5 us -> 27.2 us  [exchange(): return lax.all_to_all(v, axes, 0, 0, tiled=True)]
    ppermute x19, starting transfers between devices: 37.2 us -> 40 us  [shift(): return lax.ppermute(v, axis, [(i, (i + k) % n) for i in range(n)])]
    ppermute x6, waiting for transfers between devices: 3.13 us -> 0.66 us  [swap(): return lax.ppermute(v, 'core', [(0, 1), (1, 0)])]
    ppermute x2 -> x0, waiting for transfers between devices: 1.31 us -> none  [the longest x1 1.3 us: on_device(): ubr = lax.ppermute(ub, 'pipe', [(1, 0)])]
  transfers between devices with their start and end apart: 28 -> 26, of which waited for: 12 -> 11; matrix products, arithmetic and copies ran while one was open for 0% -> 0% of each run, Pallas kernels for 13% -> 11%
where the time goes in v4:
time: 121 us; the launch traced here: 120 us
  starting transfers between devices  50.7 us (42%)
  blocking collectives  27.2 us (22%)
  waiting for transfers between devices  23.1 us (19%)
  Pallas kernels  18.4 us (15%)
    ppermute x19, starting transfers between devices, shift(): return lax.ppermute(v, axis, [(i, (i + k) % n) for i in range(n)])  40 us
    all_to_all x2, blocking collectives, exchange(): return lax.all_to_all(v, axes, 0, 0, tiled=True)  27.2 us
    ppermute x19, waiting for transfers between devices, shift(): return lax.ppermute(v, axis, [(i, (i + k) % n) for i in range(n)])  22.5 us
    ppermute x6, starting transfers between devices, swap(): return lax.ppermute(v, 'core', [(0, 1), (1, 0)])  9.34 us
    pallas_call x1, Pallas kernels, on_device(): pl.pallas_call(factor_kernel, out_shape=(sds((64, 512), F32), sds((128, 5...  2.75 us
  transfers between devices with their start and end apart: 26, of which 11 were waited for; matrix products, arithmetic and copies ran while one was open for 0% of the time, Pallas kernels for 11%

profile of v4, /device:TPU:1, one launch (start us, length us, event | category | flops | bytes accessed | tf_op | source)
XLA Modules:
  0.0 120.4 jit_solution(4134073626484613530)
XLA Ops:
  0.6 1.4 %load_kernel.1 = (f32[64,512]{1,0:T(8,128)S(1)}, bf16[512,512]{1,0:T(8,128)(2,1)S(1)}, bf16[512,512]{1,0:T(8,128)(2,1)S(1)}, bf16[512,512]{1,0:T(8,128)(2,1)S(1)}) custom-call(f32[64,512]{1,0:T(8,128)} %bitcast.23, bf16[512,512]{1,0:T(8,128)(2,1)} %bitcast.21, bf16[512,512]{1,0:T(8,128)(2,1)} %bitcast.22), custom_call_target="tpu_custom_call" | custom-call | tf_op jit(solution)/shard_map/load_kernel/pallas_call | solution.py:278
  3.4 2.1 %collective-permute-start.1 = (f32[64,512]{1,0:T(8,128)}, f32[64,512]{1,0:T(8,128)S(1)}, u32[]{:S(2)}, u32[]{:S(2)}) collective-permute-start(f32[64,512]{1,0:T(8,128)} %bitcast.24), channel_id=1, source_target_pairs={{0,32},{32,64},{64,96},{96,0},{1,33},{33,65},{65,97},{97,1},{2,34}... | collective-permute-start | bytes 393224 | tf_op jit(solution)/shard_map/ppermute | solution.py:256
  5.5 2.5 %collective-permute-start.2 = (f32[64,512]{1,0:T(8,128)}, f32[64,512]{1,0:T(8,128)S(1)}, u32[]{:S(2)}, u32[]{:S(2)}) collective-permute-start(f32[64,512]{1,0:T(8,128)} %bitcast.25), channel_id=1, source_target_pairs={{0,64},{32,96},{64,0},{96,32},{1,65},{33,97},{65,1},{97,33},{2,66}... | collective-permute-start | bytes 393224 | tf_op jit(solution)/shard_map/ppermute | solution.py:256
  9.3 4.5 %collective-permute-done.2.q2 = f32[64,512]{1,0:T(8,128)S(1)} collective-permute-done((f32[64,512]{1,0:T(8,128)}, f32[64,512]{1,0:T(8,128)S(1)}, u32[]{:S(2)}, u32[]{:S(2)}) %collective-permute-start.2) | collective-permute-done | bytes 131104 | tf_op jit(solution)/shard_map/ppermute | solution.py:256
  13.9 2.4 %load_error_kernel.1 = (bf16[4,512,512]{2,1,0:T(8,128)(2,1)S(1)}, bf16[4,512,512]{2,1,0:T(8,128)(2,1)S(1)}, bf16[512,512]{1,0:T(8,128)(2,1)S(1)}) custom-call(bf16[512,4096]{1,0:T(8,128)(2,1)} %bitcast.17, bf16[512,512]{1,0:T(8,128)(2,1)} %bitcast.19), custom_call_target="tpu_custom_call" | custom-call | tf_op jit(solution)/shard_map/load_error_kernel/pallas_call | solution.py:292
  16.7 2.5 %collective-permute-start.4 = (f32[64,512]{1,0:T(8,128)S(1)}, f32[64,512]{1,0:T(8,128)S(1)}, u32[]{:S(2)}, u32[]{:S(2)}) collective-permute-start(f32[64,512]{1,0:T(8,128)S(1)} %get-tuple-element.49), channel_id=1, source_target_pairs={{0,16},{16,0},{1,17},{17,1},{2,18},{18,2},{3,19},{19,3},{4,20},{20... | collective-permute-start | bytes 393224 | tf_op jit(solution)/shard_map/ppermute | solution.py:260
  20.6 1.7 %collective-permute-start.7 = (f32[64,512]{1,0:T(8,128)S(1)}, f32[64,512]{1,0:T(8,128)S(1)}, u32[]{:S(2)}, u32[]{:S(2)}) collective-permute-start(f32[64,512]{1,0:T(8,128)S(1)} %add.3.u0), channel_id=1, source_target_pairs={{0,32},{32,64},{64,96},{96,0},{1,33},{33,65},{65,97},{97,1},{2,34}... | collective-permute-start | bytes 393224 | tf_op jit(solution)/shard_map/ppermute | solution.py:256
  22.2 2.4 %collective-permute-start.8 = (f32[64,512]{1,0:T(8,128)S(1)}, f32[64,512]{1,0:T(8,128)S(1)}, u32[]{:S(2)}, u32[]{:S(2)}) collective-permute-start(f32[64,512]{1,0:T(8,128)S(1)} %add.3.u0), channel_id=1, source_target_pairs={{0,64},{32,96},{64,0},{96,32},{1,65},{33,97},{65,1},{97,33},{2,66}... | collective-permute-start | bytes 393224 | tf_op jit(solution)/shard_map/ppermute | solution.py:256
  25.9 1.5 %eq_kernel.1 = (f32[64,512]{1,0:T(8,128)S(1)}, f32[64,512]{1,0:T(8,128)S(1)}, bf16[512,512]{1,0:T(8,128)(2,1)S(1)}) custom-call(f32[64,512]{1,0:T(8,128)S(1)} %get-tuple-element.48.q_ref.q0, f32[64,512]{1,0:T(8,128)S(1)} %collective-permute-done.1.q1, f32[64,512]{1,0:T(8,128)S(1)} %collective-permute-done.2.q2, f32[64,512]{1,0:T(8,128)S(1)} %collective-permute-done.3.q3, ...), custom_call_target="tpu_custom_call" | custom-call | tf_op jit(solution)/shard_map/eq_kernel/pallas_call | solution.py:327
  28.5 2.5 %collective-permute-done.8.u2 = f32[64,512]{1,0:T(8,128)S(1)} collective-permute-done((f32[64,512]{1,0:T(8,128)S(1)}, f32[64,512]{1,0:T(8,128)S(1)}, u32[]{:S(2)}, u32[]{:S(2)}) %collective-permute-start.8) | collective-permute-done | bytes 131104 | tf_op jit(solution)/shard_map/ppermute | solution.py:256
  31.5 2.2 %collective-permute-start.11 = (bf16[512,512]{1,0:T(8,128)(2,1)S(1)}, bf16[512,512]{1,0:T(8,128)(2,1)S(1)}, u32[]{:S(2)}, u32[]{:S(2)}) collective-permute-start(bf16[512,512]{1,0:T(8,128)(2,1)S(1)} %get-tuple-element.59.g_ref.g0), channel_id=1, source_target_pairs={{0,96},{32,0},{64,32},{96,64},{1,97},{33,1},{65,33},{97,65},{2,98}... | collective-permute-start | bytes 1572872 | tf_op jit(solution)/shard_map/ppermute | solution.py:256
  33.9 1.4 %collective-permute-start.12 = (f32[64,512]{1,0:T(8,128)S(1)}, f32[64,512]{1,0:T(8,128)S(1)}, u32[]{:S(2)}, u32[]{:S(2)}) collective-permute-start(f32[64,512]{1,0:T(8,128)S(1)} %p_kernel.1.a), channel_id=1, source_target_pairs={{0,1},{1,2},{2,3},{3,0},{4,5},{5,6},{6,7},{7,4},{8,9},{9,10},{10,1... | collective-permute-start | bytes 393224 | tf_op jit(solution)/shard_map/ppermute | solution.py:256
  35.3 2.6 %collective-permute-start.13 = (f32[64,512]{1,0:T(8,128)S(1)}, f32[64,512]{1,0:T(8,128)S(1)}, u32[]{:S(2)}, u32[]{:S(2)}) collective-permute-start(f32[64,512]{1,0:T(8,128)S(1)} %p_kernel.1.a), channel_id=1, source_target_pairs={{0,2},{1,3},{2,0},{3,1},{4,6},{5,7},{6,4},{7,5},{8,10},{9,11},{10,... | collective-permute-start | bytes 393224 | tf_op jit(solution)/shard_map/ppermute | solution.py:256
  39.4 3.0 %collective-permute-done.13.c = f32[64,512]{1,0:T(8,128)S(1)} collective-permute-done((f32[64,512]{1,0:T(8,128)S(1)}, f32[64,512]{1,0:T(8,128)S(1)}, u32[]{:S(2)}, u32[]{:S(2)}) %collective-permute-start.13) | collective-permute-done | bytes 131104 | tf_op jit(solution)/shard_map/ppermute | solution.py:256
  43.4 1.3 %collective-permute-done.10.g1 = bf16[512,512]{1,0:T(8,128)(2,1)S(1)} collective-permute-done((bf16[512,512]{1,0:T(8,128)(2,1)S(1)}, bf16[512,512]{1,0:T(8,128)(2,1)S(1)}, u32[]{:S(2)}, u32[]{:S(2)}) %collective-permute-start.10) | collective-permute-done | bytes 524320 | tf_op jit(solution)/shard_map/ppermute | solution.py:256
  44.8 2.9 %collective-permute-start.16 = (bf16[256,512]{1,0:T(8,128)(2,1)S(1)}, bf16[256,512]{1,0:T(8,128)(2,1)S(1)}, u32[]{:S(2)}, u32[]{:S(2)}) collective-permute-start(bf16[256,512]{1,0:T(8,128)(2,1)S(1)} %slice.7), channel_id=1, source_target_pairs={{0,96},{32,0},{64,32},{96,64},{1,97},{33,1},{65,33},{97,65},{2,98}... | collective-permute-start | bytes 786440 | tf_op jit(solution)/shard_map/ppermute | solution.py:256
  47.7 3.0 %collective-permute-start.17 = (f32[64,512]{1,0:T(8,128)S(1)}, f32[64,512]{1,0:T(8,128)S(1)}, u32[]{:S(2)}, u32[]{:S(2)}) collective-permute-start(f32[64,512]{1,0:T(8,128)S(1)} %sum_kernel.1.z0), channel_id=1, source_target_pairs={{0,4},{4,8},{8,12},{12,0},{1,5},{5,9},{9,13},{13,1},{2,6},{6,10},{... | collective-permute-start | bytes 393224 | tf_op jit(solution)/shard_map/ppermute | solution.py:256
  50.7 5.1 %collective-permute-start.18 = (f32[64,512]{1,0:T(8,128)S(1)}, f32[64,512]{1,0:T(8,128)S(1)}, u32[]{:S(2)}, u32[]{:S(2)}) collective-permute-start(f32[64,512]{1,0:T(8,128)S(1)} %sum_kernel.1.z0), channel_id=1, source_target_pairs={{0,8},{4,12},{8,0},{12,4},{1,9},{5,13},{9,1},{13,5},{2,10},{6,14},... | collective-permute-start | bytes 393224 | tf_op jit(solution)/shard_map/ppermute | solution.py:256
  55.8 2.4 %collective-permute-start.19 = (f32[64,512]{1,0:T(8,128)S(1)}, f32[64,512]{1,0:T(8,128)S(1)}, u32[]{:S(2)}, u32[]{:S(2)}) collective-permute-start(f32[64,512]{1,0:T(8,128)S(1)} %sum_kernel.1.z0), channel_id=1, source_target_pairs={{0,12},{4,0},{8,4},{12,8},{1,13},{5,1},{9,5},{13,9},{2,14},{6,2},{... | collective-permute-start | bytes 393224 | tf_op jit(solution)/shard_map/ppermute | solution.py:256
  58.2 5.0 %collective-permute-done.18.z2 = f32[64,512]{1,0:T(8,128)S(1)} collective-permute-done((f32[64,512]{1,0:T(8,128)S(1)}, f32[64,512]{1,0:T(8,128)S(1)}, u32[]{:S(2)}, u32[]{:S(2)}) %collective-permute-start.18) | collective-permute-done | bytes 131104 | tf_op jit(solution)/shard_map/ppermute | solution.py:256
  63.2 4.6 %collective-permute-done.19.z3 = f32[64,512]{1,0:T(8,128)S(1)} collective-permute-done((f32[64,512]{1,0:T(8,128)S(1)}, f32[64,512]{1,0:T(8,128)S(1)}, u32[]{:S(2)}, u32[]{:S(2)}) %collective-permute-start.19) | collective-permute-done | bytes 131104 | tf_op jit(solution)/shard_map/ppermute | solution.py:256
  68.1 1.4 %collective-permute-start.20 = (f32[2,64,512]{2,1,0:T(8,128)S(1)}, f32[2,64,512]{2,1,0:T(8,128)S(1)}, u32[]{:S(2)}, u32[]{:S(2)}) collective-permute-start(f32[2,64,512]{2,1,0:T(8,128)S(1)} %pv_kernel.1.pv_ref.p_ref), channel_id=1, source_target_pairs={{0,16},{16,0},{1,17},{17,1},{2,18},{18,2},{3,19},{19,3},{4,20},{20... | collective-permute-start | bytes 786440 | tf_op jit(solution)/shard_map/ppermute | solution.py:260
  72.4 16.6 %all_to_all.10.in_ref = f32[16,72,128]{2,1,0:T(8,128)S(1)} all-to-all(f32[16,72,128]{2,1,0:T(8,128)S(1)} %bitcast.16), channel_id=1, replica_groups=mesh['pipe'=2,'x'=4,'core'=2,'zhi'=4,'y'=4] {'x','y'}, dimensions={0} | all-to-all | bytes 1179648 | tf_op jit(solution)/shard_map/all_to_all | solution.py:268
  89.1 1.9 %collective-permute-start.21 = (f32[64,128]{1,0:T(8,128)S(1)}, f32[64,128]{1,0:T(8,128)S(1)}, u32[]{:S(2)}, u32[]{:S(2)}) collective-permute-start(f32[64,128]{1,0:T(8,128)S(1)} %get-tuple-element.72.q0), channel_id=1, source_target_pairs={{0,4},{4,8},{8,12},{12,0},{1,5},{5,9},{9,13},{13,1},{2,6},{6,10},{... | collective-permute-start | bytes 98312 | tf_op jit(solution)/shard_map/ppermute | solution.py:256
  91.0 3.6 %collective-permute-start.22 = (f32[64,128]{1,0:T(8,128)S(1)}, f32[64,128]{1,0:T(8,128)S(1)}, u32[]{:S(2)}, u32[]{:S(2)}) collective-permute-start(f32[64,128]{1,0:T(8,128)S(1)} %get-tuple-element.72.q0), channel_id=1, source_target_pairs={{0,8},{4,12},{8,0},{12,4},{1,9},{5,13},{9,1},{13,5},{2,10},{6,14},... | collective-permute-start | bytes 98312 | tf_op jit(solution)/shard_map/ppermute | solution.py:256
  94.6 2.3 %collective-permute-start.23 = (f32[64,128]{1,0:T(8,128)S(1)}, f32[64,128]{1,0:T(8,128)S(1)}, u32[]{:S(2)}, u32[]{:S(2)}) collective-permute-start(f32[64,128]{1,0:T(8,128)S(1)} %get-tuple-element.72.q0), channel_id=1, source_target_pairs={{0,12},{4,0},{8,4},{12,8},{1,13},{5,1},{9,5},{13,9},{2,14},{6,2},{... | collective-permute-start | bytes 98312 | tf_op jit(solution)/shard_map/ppermute | solution.py:256
  96.9 2.8 %factor_kernel.1 = (f32[64,512]{1,0:T(8,128)}, bf16[128,512]{1,0:T(8,128)(2,1)S(1)}, f32[64,64]{1,0:T(8,128)S(1)}) custom-call(f32[32,128]{1,0:T(8,128)S(1)} %get-tuple-element.70.gram_ref, f32[2,64,512]{2,1,0:T(8,128)S(1)} %pv_kernel.1.pv_ref.p_ref), custom_call_target="tpu_custom_call" | custom-call | tf_op jit(solution)/shard_map/factor_kernel/pallas_call | solution.py:407
  99.7 2.3 %matrix_kernel.1.m_ref = f32[8,512,512]{2,1,0:T(8,128)S(1)} custom-call(bf16[512,512]{1,0:T(8,128)(2,1)S(1)} %get-tuple-element.74.at_ref, bf16[4,512,512]{2,1,0:T(8,128)(2,1)S(1)} %get-tuple-element.75.ga_ref, bf16[4,512,512]{2,1,0:T(8,128)(2,1)S(1)} %collective-permute-done.24.gb_ref, bf16[4,512,512]{2,1,0:T(8,128)(2,1)S(1)} %get-tuple-element.54.e_ref.ea_ref, ...), custom_call_target="tpu_custom_call" | custom-call | tf_op jit(solution)/shard_map/matrix_kernel/pallas_call | solution.py:417
  102.3 10.6 %all_to_all.11.q_ref = bf16[16,64,128]{2,1,0:T(8,128)(2,1)S(1)} all-to-all(bf16[16,64,128]{2,1,0:T(8,128)(2,1)S(1)} %q_scale_kernel.1), channel_id=1, replica_groups=mesh['pipe'=2,'x'=4,'core'=2,'zhi'=4,'y'=4] {'x','y'}, dimensions={0} | all-to-all | bytes 524288 | tf_op jit(solution)/shard_map/all_to_all | solution.py:268
  112.8 3.4 %collective-permute-start.25 = (bf16[16,64,128]{2,1,0:T(8,128)(2,1)S(1)}, bf16[16,64,128]{2,1,0:T(8,128)(2,1)S(1)}, u32[]{:S(2)}, u32[]{:S(2)}) collective-permute-start(bf16[16,64,128]{2,1,0:T(8,128)(2,1)S(1)} %all_to_all.11.q_ref), channel_id=1, source_target_pairs={{0,16},{16,0},{1,17},{17,1},{2,18},{18,2},{3,19},{19,3},{4,20},{20... | collective-permute-start | bytes 786440 | tf_op jit(solution)/shard_map/ppermute | solution.py:260
  116.3 2.3 %error_own_kernel.1 = (bf16[512,4096]{1,0:T(8,128)(2,1)}, f32[64,512]{1,0:T(8,128)}) custom-call(bf16[128,512]{1,0:T(8,128)(2,1)S(1)} %get-tuple-element.71.ph2_ref, bf16[16,64,128]{2,1,0:T(8,128)(2,1)S(1)} %all_to_all.11.q_ref, f32[8,512,512]{2,1,0:T(8,128)S(1)} %matrix_kernel.1.m_ref), custom_call_target="tpu_custom_call" | custom-call | tf_op jit(solution)/shard_map/error_own_kernel/pallas_call | solution.py:440
  118.6 1.7 %error_sib_kernel.1 = bf16[512,4096]{1,0:T(8,128)(2,1)} custom-call(bf16[128,512]{1,0:T(8,128)(2,1)S(1)} %get-tuple-element.71.ph2_ref, bf16[16,64,128]{2,1,0:T(8,128)(2,1)S(1)} %collective-permute-done.25.q_ref, f32[8,512,512]{2,1,0:T(8,128)S(1)} %matrix_kernel.1.m_ref, bf16[512,4096]{1,0:T(8,128)(2,1)} %get-tuple-element.79._), custom_call_target="tpu_custom_call", output_to_operand_aliasing={{}: (3, {})} | custom-call | tf_op jit(solution)/shard_map/error_sib_kernel/pallas_call | solution.py:450
  (41 shorter events, 13.5 us)
Async XLA Ops:
  2.1 14.2 %collective-permute-start = (bf16[512,512]{1,0:T(8,128)(2,1)S(1)}, bf16[512,512]{1,0:T(8,128)(2,1)S(1)}, u32[]{:S(2)}, u32[]{:S(2)}) collective-permute-start(bf16[512,512]{1,0:T(8,128)(2,1)S(1)} %get-tuple-element.44), channel_id=1, source_target_pairs={{128,0},{129,1},{130,2},{131,3},{132,4},{133,5},{134,6},{135,7},{1... | collective-permute-start | bytes 1572872 | tf_op jit(solution)/shard_map/ppermute | solution.py:289
  3.4 6.0 %collective-permute-start.1 = (f32[64,512]{1,0:T(8,128)}, f32[64,512]{1,0:T(8,128)S(1)}, u32[]{:S(2)}, u32[]{:S(2)}) collective-permute-start(f32[64,512]{1,0:T(8,128)} %bitcast.24), channel_id=1, source_target_pairs={{0,32},{32,64},{64,96},{96,0},{1,33},{33,65},{65,97},{97,1},{2,34}... | collective-permute-start | bytes 393224 | tf_op jit(solution)/shard_map/ppermute | solution.py:256
  5.5 8.4 %collective-permute-start.2 = (f32[64,512]{1,0:T(8,128)}, f32[64,512]{1,0:T(8,128)S(1)}, u32[]{:S(2)}, u32[]{:S(2)}) collective-permute-start(f32[64,512]{1,0:T(8,128)} %bitcast.25), channel_id=1, source_target_pairs={{0,64},{32,96},{64,0},{96,32},{1,65},{33,97},{65,1},{97,33},{2,66}... | collective-permute-start | bytes 393224 | tf_op jit(solution)/shard_map/ppermute | solution.py:256
  7.9 5.9 %collective-permute-start.3 = (f32[64,512]{1,0:T(8,128)}, f32[64,512]{1,0:T(8,128)S(1)}, u32[]{:S(2)}, u32[]{:S(2)}) collective-permute-start(f32[64,512]{1,0:T(8,128)} %bitcast.26), channel_id=1, source_target_pairs={{0,96},{32,0},{64,32},{96,64},{1,97},{33,1},{65,33},{97,65},{2,98}... | collective-permute-start | bytes 393224 | tf_op jit(solution)/shard_map/ppermute | solution.py:256
  16.7 3.5 %collective-permute-start.4 = (f32[64,512]{1,0:T(8,128)S(1)}, f32[64,512]{1,0:T(8,128)S(1)}, u32[]{:S(2)}, u32[]{:S(2)}) collective-permute-start(f32[64,512]{1,0:T(8,128)S(1)} %get-tuple-element.49), channel_id=1, source_target_pairs={{0,16},{16,0},{1,17},{17,1},{2,18},{18,2},{3,19},{19,3},{4,20},{20... | collective-permute-start | bytes 393224 | tf_op jit(solution)/shard_map/ppermute | solution.py:260
  20.1 5.7 %collective-permute-start.5 = (bf16[4,512,512]{2,1,0:T(8,128)(2,1)S(1)}, bf16[4,512,512]{2,1,0:T(8,128)(2,1)S(1)}, u32[]{:S(2)}, u32[]{:S(2)}) collective-permute-start(bf16[4,512,512]{2,1,0:T(8,128)(2,1)S(1)} %get-tuple-element.57.eb_ref), channel_id=1, source_target_pairs={{0,16},{16,0},{1,17},{17,1},{2,18},{18,2},{3,19},{19,3},{4,20},{20... | collective-permute-start | bytes 6291464 | tf_op jit(solution)/shard_map/ppermute | solution.py:260
  20.6 7.9 %collective-permute-start.7 = (f32[64,512]{1,0:T(8,128)S(1)}, f32[64,512]{1,0:T(8,128)S(1)}, u32[]{:S(2)}, u32[]{:S(2)}) collective-permute-start(f32[64,512]{1,0:T(8,128)S(1)} %add.3.u0), channel_id=1, source_target_pairs={{0,32},{32,64},{64,96},{96,0},{1,33},{33,65},{65,97},{97,1},{2,34}... | collective-permute-start | bytes 393224 | tf_op jit(solution)/shard_map/ppermute | solution.py:256
  22.2 8.7 %collective-permute-start.8 = (f32[64,512]{1,0:T(8,128)S(1)}, f32[64,512]{1,0:T(8,128)S(1)}, u32[]{:S(2)}, u32[]{:S(2)}) collective-permute-start(f32[64,512]{1,0:T(8,128)S(1)} %add.3.u0), channel_id=1, source_target_pairs={{0,64},{32,96},{64,0},{96,32},{1,65},{33,97},{65,1},{97,33},{2,66}... | collective-permute-start | bytes 393224 | tf_op jit(solution)/shard_map/ppermute | solution.py:256
  24.7 6.3 %collective-permute-start.9 = (f32[64,512]{1,0:T(8,128)S(1)}, f32[64,512]{1,0:T(8,128)S(1)}, u32[]{:S(2)}, u32[]{:S(2)}) collective-permute-start(f32[64,512]{1,0:T(8,128)S(1)} %add.3.u0), channel_id=1, source_target_pairs={{0,96},{32,0},{64,32},{96,64},{1,97},{33,1},{65,33},{97,65},{2,98}... | collective-permute-start | bytes 393224 | tf_op jit(solution)/shard_map/ppermute | solution.py:256
  27.4 3.6 %collective-permute-start.6 = (f32[64,512]{1,0:T(8,128)S(1)}, f32[64,512]{1,0:T(8,128)S(1)}, u32[]{:S(2)}, u32[]{:S(2)}) collective-permute-start(f32[64,512]{1,0:T(8,128)S(1)} %get-tuple-element.58), channel_id=1, source_target_pairs={{0,16},{16,0},{1,17},{17,1},{2,18},{18,2},{3,19},{19,3},{4,20},{20... | collective-permute-start | bytes 393224 | tf_op jit(solution)/shard_map/ppermute | solution.py:260
  31.0 13.7 %collective-permute-start.10 = (bf16[512,512]{1,0:T(8,128)(2,1)S(1)}, bf16[512,512]{1,0:T(8,128)(2,1)S(1)}, u32[]{:S(2)}, u32[]{:S(2)}) collective-permute-start(bf16[512,512]{1,0:T(8,128)(2,1)S(1)} %get-tuple-element.59.g_ref.g0), channel_id=1, source_target_pairs={{0,32},{32,64},{64,96},{96,0},{1,33},{33,65},{65,97},{97,1},{2,34}... | collective-permute-start | bytes 1572872 | tf_op jit(solution)/shard_map/ppermute | solution.py:256
  31.5 13.2 %collective-permute-start.11 = (bf16[512,512]{1,0:T(8,128)(2,1)S(1)}, bf16[512,512]{1,0:T(8,128)(2,1)S(1)}, u32[]{:S(2)}, u32[]{:S(2)}) collective-permute-start(bf16[512,512]{1,0:T(8,128)(2,1)S(1)} %get-tuple-element.59.g_ref.g0), channel_id=1, source_target_pairs={{0,96},{32,0},{64,32},{96,64},{1,97},{33,1},{65,33},{97,65},{2,98}... | collective-permute-start | bytes 1572872 | tf_op jit(solution)/shard_map/ppermute | solution.py:256
  33.9 5.5 %collective-permute-start.12 = (f32[64,512]{1,0:T(8,128)S(1)}, f32[64,512]{1,0:T(8,128)S(1)}, u32[]{:S(2)}, u32[]{:S(2)}) collective-permute-start(f32[64,512]{1,0:T(8,128)S(1)} %p_kernel.1.a), channel_id=1, source_target_pairs={{0,1},{1,2},{2,3},{3,0},{4,5},{5,6},{6,7},{7,4},{8,9},{9,10},{10,1... | collective-permute-start | bytes 393224 | tf_op jit(solution)/shard_map/ppermute | solution.py:256
  35.3 7.1 %collective-permute-start.13 = (f32[64,512]{1,0:T(8,128)S(1)}, f32[64,512]{1,0:T(8,128)S(1)}, u32[]{:S(2)}, u32[]{:S(2)}) collective-permute-start(f32[64,512]{1,0:T(8,128)S(1)} %p_kernel.1.a), channel_id=1, source_target_pairs={{0,2},{1,3},{2,0},{3,1},{4,6},{5,7},{6,4},{7,5},{8,10},{9,11},{10,... | collective-permute-start | bytes 393224 | tf_op jit(solution)/shard_map/ppermute | solution.py:256
  37.9 5.4 %collective-permute-start.14 = (f32[64,512]{1,0:T(8,128)S(1)}, f32[64,512]{1,0:T(8,128)S(1)}, u32[]{:S(2)}, u32[]{:S(2)}) collective-permute-start(f32[64,512]{1,0:T(8,128)S(1)} %p_kernel.1.a), channel_id=1, source_target_pairs={{0,3},{1,0},{2,1},{3,2},{4,7},{5,4},{6,5},{7,6},{8,11},{9,8},{10,9... | collective-permute-start | bytes 393224 | tf_op jit(solution)/shard_map/ppermute | solution.py:256
  44.7 23.1 %collective-permute-start.15 = (bf16[256,512]{1,0:T(8,128)(2,1)S(1)}, bf16[256,512]{1,0:T(8,128)(2,1)S(1)}, u32[]{:S(2)}, u32[]{:S(2)}) collective-permute-start(bf16[256,512]{1,0:T(8,128)(2,1)S(1)} %slice.6), channel_id=1, source_target_pairs={{0,32},{32,64},{64,96},{96,0},{1,33},{33,65},{65,97},{97,1},{2,34}... | collective-permute-start | bytes 786440 | tf_op jit(solution)/shard_map/ppermute | solution.py:256
  44.8 23.0 %collective-permute-start.16 = (bf16[256,512]{1,0:T(8,128)(2,1)S(1)}, bf16[256,512]{1,0:T(8,128)(2,1)S(1)}, u32[]{:S(2)}, u32[]{:S(2)}) collective-permute-start(bf16[256,512]{1,0:T(8,128)(2,1)S(1)} %slice.7), channel_id=1, source_target_pairs={{0,96},{32,0},{64,32},{96,64},{1,97},{33,1},{65,33},{97,65},{2,98}... | collective-permute-start | bytes 786440 | tf_op jit(solution)/shard_map/ppermute | solution.py:256
  47.7 10.5 %collective-permute-start.17 = (f32[64,512]{1,0:T(8,128)S(1)}, f32[64,512]{1,0:T(8,128)S(1)}, u32[]{:S(2)}, u32[]{:S(2)}) collective-permute-start(f32[64,512]{1,0:T(8,128)S(1)} %sum_kernel.1.z0), channel_id=1, source_target_pairs={{0,4},{4,8},{8,12},{12,0},{1,5},{5,9},{9,13},{13,1},{2,6},{6,10},{... | collective-permute-start | bytes 393224 | tf_op jit(solution)/shard_map/ppermute | solution.py:256
  50.7 12.5 %collective-permute-start.18 = (f32[64,512]{1,0:T(8,128)S(1)}, f32[64,512]{1,0:T(8,128)S(1)}, u32[]{:S(2)}, u32[]{:S(2)}) collective-permute-start(f32[64,512]{1,0:T(8,128)S(1)} %sum_kernel.1.z0), channel_id=1, source_target_pairs={{0,8},{4,12},{8,0},{12,4},{1,9},{5,13},{9,1},{13,5},{2,10},{6,14},... | collective-permute-start | bytes 393224 | tf_op jit(solution)/shard_map/ppermute | solution.py:256
  55.8 11.9 %collective-permute-start.19 = (f32[64,512]{1,0:T(8,128)S(1)}, f32[64,512]{1,0:T(8,128)S(1)}, u32[]{:S(2)}, u32[]{:S(2)}) collective-permute-start(f32[64,512]{1,0:T(8,128)S(1)} %sum_kernel.1.z0), channel_id=1, source_target_pairs={{0,12},{4,0},{8,4},{12,8},{1,13},{5,1},{9,5},{13,9},{2,14},{6,2},{... | collective-permute-start | bytes 393224 | tf_op jit(solution)/shard_map/ppermute | solution.py:256
  68.1 2.6 %collective-permute-start.20 = (f32[2,64,512]{2,1,0:T(8,128)S(1)}, f32[2,64,512]{2,1,0:T(8,128)S(1)}, u32[]{:S(2)}, u32[]{:S(2)}) collective-permute-start(f32[2,64,512]{2,1,0:T(8,128)S(1)} %pv_kernel.1.pv_ref.p_ref), channel_id=1, source_target_pairs={{0,16},{16,0},{1,17},{17,1},{2,18},{18,2},{3,19},{19,3},{4,20},{20... | collective-permute-start | bytes 786440 | tf_op jit(solution)/shard_map/ppermute | solution.py:260
  72.0 27.7 %collective-permute-start.24 = (bf16[4,512,512]{2,1,0:T(8,128)(2,1)S(1)}, bf16[4,512,512]{2,1,0:T(8,128)(2,1)S(1)}, u32[]{:S(2)}, u32[]{:S(2)}) collective-permute-start(bf16[4,512,512]{2,1,0:T(8,128)(2,1)S(1)} %get-tuple-element.75.ga_ref), channel_id=1, source_target_pairs={{0,16},{16,0},{1,17},{17,1},{2,18},{18,2},{3,19},{19,3},{4,20},{20... | collective-permute-start | bytes 6291464 | tf_op jit(solution)/shard_map/ppermute | solution.py:260
  89.1 12.9 %collective-permute-start.21 = (f32[64,128]{1,0:T(8,128)S(1)}, f32[64,128]{1,0:T(8,128)S(1)}, u32[]{:S(2)}, u32[]{:S(2)}) collective-permute-start(f32[64,128]{1,0:T(8,128)S(1)} %get-tuple-element.72.q0), channel_id=1, source_target_pairs={{0,4},{4,8},{8,12},{12,0},{1,5},{5,9},{9,13},{13,1},{2,6},{6,10},{... | collective-permute-start | bytes 98312 | tf_op jit(solution)/shard_map/ppermute | solution.py:256
  91.0 11.0 %collective-permute-start.22 = (f32[64,128]{1,0:T(8,128)S(1)}, f32[64,128]{1,0:T(8,128)S(1)}, u32[]{:S(2)}, u32[]{:S(2)}) collective-permute-start(f32[64,128]{1,0:T(8,128)S(1)} %get-tuple-element.72.q0), channel_id=1, source_target_pairs={{0,8},{4,12},{8,0},{12,4},{1,9},{5,13},{9,1},{13,5},{2,10},{6,14},... | collective-permute-start | bytes 98312 | tf_op jit(solution)/shard_map/ppermute | solution.py:256
  94.6 7.5 %collective-permute-start.23 = (f32[64,128]{1,0:T(8,128)S(1)}, f32[64,128]{1,0:T(8,128)S(1)}, u32[]{:S(2)}, u32[]{:S(2)}) collective-permute-start(f32[64,128]{1,0:T(8,128)S(1)} %get-tuple-element.72.q0), channel_id=1, source_target_pairs={{0,12},{4,0},{8,4},{12,8},{1,13},{5,1},{9,5},{13,9},{2,14},{6,2},{... | collective-permute-start | bytes 98312 | tf_op jit(solution)/shard_map/ppermute | solution.py:256
  112.8 5.8 %collective-permute-start.25 = (bf16[16,64,128]{2,1,0:T(8,128)(2,1)S(1)}, bf16[16,64,128]{2,1,0:T(8,128)(2,1)S(1)}, u32[]{:S(2)}, u32[]{:S(2)}) collective-permute-start(bf16[16,64,128]{2,1,0:T(8,128)(2,1)S(1)} %all_to_all.11.q_ref), channel_id=1, source_target_pairs={{0,16},{16,0},{1,17},{17,1},{2,18},{18,2},{3,19},{19,3},{4,20},{20... | collective-permute-start | bytes 786440 | tf_op jit(solution)/shard_map/ppermute | solution.py:260

commit v5 on v4

--- a/solution.py
+++ b/solution.py
@@ -124,8 +124,9 @@
     run_copies(pairs + [(act, act_v)], sems)
 
 
-def pv_kernel(z0, z1, z2, z3, act_ref, out_ref):
-    p = sum_of((z0, z1, z2, z3)) * (1.0 / 16.0)
+def pv_kernel(z0, z1, z2a, z2b, z3, act_ref, out_ref):
+    z2 = jnp.concatenate([z2a[...], z2b[...]], axis=1)
+    p = ((z0[...] + z2) + (z1[...] + z3[...])) * (1.0 / 16.0)
     out_ref[0] = p
     out_ref[1] = fold3(dot(split3(p), act_ref[...], 1, 1))
 
@@ -344,6 +345,7 @@
         compiler_params=params(6),
         name="p_kernel",
     )(*us, act, eq, eqs)
+    ys = ring(part, "y")
     grad, *_ = lax.optimization_barrier((grad, eqs, *us))
     g1 = shift(grad, "x", 1)
     g3 = shift(grad, "x", 3)
@@ -355,22 +357,25 @@
         cost_estimate=LIGHT,
         compiler_params=params(4),
         name="sum_kernel",
-    )(*ring(part, "y"))
-
-    h1, h3, _ = lax.optimization_barrier((g1, g3, part))
+    )(*ys)
+
+    z1 = shift(part, "zhi", 1)
+    z3 = shift(part, "zhi", 3)
+    h1, h3, *_ = lax.optimization_barrier((g1, g3, z1, z3))
     g2a = shift(h1[:256], "x", 1)
     g2b = shift(h3[256:], "x", 3)
-    zs = ring(part, "zhi")
-    g2a, g2b, *zs = lax.optimization_barrier((g2a, g2b, *zs))
+    z2a = shift(z1[:, :256], "zhi", 1)
+    z2b = shift(z3[:, 256:], "zhi", 3)
+    g2a, g2b, z2a, z2b = lax.optimization_barrier((g2a, g2b, z2a, z2b))
     pv = pl.pallas_call(
         pv_kernel,
         out_shape=sds((2, 64, 512), F32),
-        in_specs=[VMEM] * 5,
+        in_specs=[VMEM] * 6,
         out_specs=VMEM,
         cost_estimate=LIGHT,
         compiler_params=params(4),
         name="pv_kernel",
-    )(*zs, act)
+    )(part, z1, z2a, z2b, z3, act)
     pvs = swap(pv)
     q_own_part = pl.pallas_call(
         q_own_kernel,

time: 121 us -> 118 us (0.975)
  waiting for transfers between devices: 23.1 us -> 21.4 us
  blocking collectives: 27.2 us -> 25.5 us
    ppermute x6, starting transfers between devices: 9.34 us -> 13.7 us  [swap(): return lax.ppermute(v, 'core', [(0, 1), (1, 0)])]
    ppermute x19 -> x20, starting transfers between devices: 40 us -> 36.5 us  [shift(): return lax.ppermute(v, axis, [(i, (i + k) % n) for i in range(n)])]
    all_to_all x2, blocking collectives: 27.2 us -> 25.5 us  [exchange(): return lax.all_to_all(v, axes, 0, 0, tiled=True)]
    ppermute x19 -> x20, waiting for transfers between devices: 22.5 us -> 20.8 us  [shift(): return lax.ppermute(v, axis, [(i, (i + k) % n) for i in range(n)])]
  transfers between devices with their start and end apart: 26 -> 27, of which waited for: 11 -> 12; matrix products, arithmetic and copies ran while one was open for 0% -> 0% of each run, Pallas kernels for 11% -> 11%
where the time goes in v5:
time: 118 us
  starting transfers between devices  51.5 us (44%)
  blocking collectives  25.5 us (22%)
  waiting for transfers between devices  21.4 us (18%)
  Pallas kernels  18.4 us (16%)
    ppermute x20, starting transfers between devices, shift(): return lax.ppermute(v, axis, [(i, (i + k) % n) for i in range(n)])  36.5 us
    all_to_all x2, blocking collectives, exchange(): return lax.all_to_all(v, axes, 0, 0, tiled=True)  25.5 us
    ppermute x20, waiting for transfers between devices, shift(): return lax.ppermute(v, axis, [(i, (i + k) % n) for i in range(n)])  20.8 us
    ppermute x6, starting transfers between devices, swap(): return lax.ppermute(v, 'core', [(0, 1), (1, 0)])  13.7 us
    pallas_call x1, Pallas kernels, on_device(): pl.pallas_call(factor_kernel, out_shape=(sds((64, 512), F32), sds((128, 5...  2.76 us
    pallas_call x1, Pallas kernels, on_device(): pl.pallas_call(load_error_kernel, out_shape=(sds((4, 512, 512), BF), sds(...  2.42 us
  transfers between devices with their start and end apart: 27, of which 12 were waited for; matrix products, arithmetic and copies ran while one was open for 0% of the time, Pallas kernels for 11%

profile of v5, /device:TPU:1, one launch (start us, length us, event | category | flops | bytes accessed | tf_op | source)
XLA Modules:
  0.0 117.9 jit_solution(13602632014226582820)
XLA Ops:
  0.6 1.4 %load_kernel.1 = (f32[64,512]{1,0:T(8,128)S(1)}, bf16[512,512]{1,0:T(8,128)(2,1)S(1)}, bf16[512,512]{1,0:T(8,128)(2,1)S(1)}, bf16[512,512]{1,0:T(8,128)(2,1)S(1)}) custom-call(f32[64,512]{1,0:T(8,128)} %bitcast.23, bf16[512,512]{1,0:T(8,128)(2,1)} %bitcast.21, bf16[512,512]{1,0:T(8,128)(2,1)} %bitcast.22), custom_call_target="tpu_custom_call" | custom-call | tf_op jit(solution)/shard_map/load_kernel/pallas_call | solution.py:279
  3.4 2.1 %collective-permute-start.1 = (f32[64,512]{1,0:T(8,128)}, f32[64,512]{1,0:T(8,128)S(1)}, u32[]{:S(2)}, u32[]{:S(2)}) collective-permute-start(f32[64,512]{1,0:T(8,128)} %bitcast.24), channel_id=1, source_target_pairs={{0,32},{32,64},{64,96},{96,0},{1,33},{33,65},{65,97},{97,1},{2,34}... | collective-permute-start | bytes 393224 | tf_op jit(solution)/shard_map/ppermute | solution.py:257
  5.5 2.5 %collective-permute-start.2 = (f32[64,512]{1,0:T(8,128)}, f32[64,512]{1,0:T(8,128)S(1)}, u32[]{:S(2)}, u32[]{:S(2)}) collective-permute-start(f32[64,512]{1,0:T(8,128)} %bitcast.25), channel_id=1, source_target_pairs={{0,64},{32,96},{64,0},{96,32},{1,65},{33,97},{65,1},{97,33},{2,66}... | collective-permute-start | bytes 393224 | tf_op jit(solution)/shard_map/ppermute | solution.py:257
  9.3 4.5 %collective-permute-done.2.q2 = f32[64,512]{1,0:T(8,128)S(1)} collective-permute-done((f32[64,512]{1,0:T(8,128)}, f32[64,512]{1,0:T(8,128)S(1)}, u32[]{:S(2)}, u32[]{:S(2)}) %collective-permute-start.2) | collective-permute-done | bytes 131104 | tf_op jit(solution)/shard_map/ppermute | solution.py:257
  13.9 2.4 %load_error_kernel.1 = (bf16[4,512,512]{2,1,0:T(8,128)(2,1)S(1)}, bf16[4,512,512]{2,1,0:T(8,128)(2,1)S(1)}, bf16[512,512]{1,0:T(8,128)(2,1)S(1)}) custom-call(bf16[512,4096]{1,0:T(8,128)(2,1)} %bitcast.17, bf16[512,512]{1,0:T(8,128)(2,1)} %bitcast.19), custom_call_target="tpu_custom_call" | custom-call | tf_op jit(solution)/shard_map/load_error_kernel/pallas_call | solution.py:293
  16.7 2.5 %collective-permute-start.4 = (f32[64,512]{1,0:T(8,128)S(1)}, f32[64,512]{1,0:T(8,128)S(1)}, u32[]{:S(2)}, u32[]{:S(2)}) collective-permute-start(f32[64,512]{1,0:T(8,128)S(1)} %get-tuple-element.47), channel_id=1, source_target_pairs={{0,16},{16,0},{1,17},{17,1},{2,18},{18,2},{3,19},{19,3},{4,20},{20... | collective-permute-start | bytes 393224 | tf_op jit(solution)/shard_map/ppermute | solution.py:261
  20.6 1.7 %collective-permute-start.5 = (f32[64,512]{1,0:T(8,128)S(1)}, f32[64,512]{1,0:T(8,128)S(1)}, u32[]{:S(2)}, u32[]{:S(2)}) collective-permute-start(f32[64,512]{1,0:T(8,128)S(1)} %add.3.u0), channel_id=1, source_target_pairs={{0,32},{32,64},{64,96},{96,0},{1,33},{33,65},{65,97},{97,1},{2,34}... | collective-permute-start | bytes 393224 | tf_op jit(solution)/shard_map/ppermute | solution.py:257
  22.2 2.4 %collective-permute-start.6 = (f32[64,512]{1,0:T(8,128)S(1)}, f32[64,512]{1,0:T(8,128)S(1)}, u32[]{:S(2)}, u32[]{:S(2)}) collective-permute-start(f32[64,512]{1,0:T(8,128)S(1)} %add.3.u0), channel_id=1, source_target_pairs={{0,64},{32,96},{64,0},{96,32},{1,65},{33,97},{65,1},{97,33},{2,66}... | collective-permute-start | bytes 393224 | tf_op jit(solution)/shard_map/ppermute | solution.py:257
  25.9 1.5 %eq_kernel.1 = (f32[64,512]{1,0:T(8,128)S(1)}, f32[64,512]{1,0:T(8,128)S(1)}, bf16[512,512]{1,0:T(8,128)(2,1)S(1)}) custom-call(f32[64,512]{1,0:T(8,128)S(1)} %get-tuple-element.46.q_ref.q0, f32[64,512]{1,0:T(8,128)S(1)} %collective-permute-done.1.q1, f32[64,512]{1,0:T(8,128)S(1)} %collective-permute-done.2.q2, f32[64,512]{1,0:T(8,128)S(1)} %collective-permute-done.3.q3, ...), custom_call_target="tpu_custom_call" | custom-call | tf_op jit(solution)/shard_map/eq_kernel/pallas_call | solution.py:328
  28.5 2.5 %collective-permute-done.6.u2 = f32[64,512]{1,0:T(8,128)S(1)} collective-permute-done((f32[64,512]{1,0:T(8,128)S(1)}, f32[64,512]{1,0:T(8,128)S(1)}, u32[]{:S(2)}, u32[]{:S(2)}) %collective-permute-start.6) | collective-permute-done | bytes 131104 | tf_op jit(solution)/shard_map/ppermute | solution.py:257
  31.5 2.2 %collective-permute-start.15 = (bf16[512,512]{1,0:T(8,128)(2,1)S(1)}, bf16[512,512]{1,0:T(8,128)(2,1)S(1)}, u32[]{:S(2)}, u32[]{:S(2)}) collective-permute-start(bf16[512,512]{1,0:T(8,128)(2,1)S(1)} %get-tuple-element.58.g_ref.g0), channel_id=1, source_target_pairs={{0,96},{32,0},{64,32},{96,64},{1,97},{33,1},{65,33},{97,65},{2,98}... | collective-permute-start | bytes 1572872 | tf_op jit(solution)/shard_map/ppermute | solution.py:257
  35.3 2.6 %collective-permute-start.11 = (f32[64,512]{1,0:T(8,128)S(1)}, f32[64,512]{1,0:T(8,128)S(1)}, u32[]{:S(2)}, u32[]{:S(2)}) collective-permute-start(f32[64,512]{1,0:T(8,128)S(1)} %p_kernel.1.a), channel_id=1, source_target_pairs={{0,2},{1,3},{2,0},{3,1},{4,6},{5,7},{6,4},{7,5},{8,10},{9,11},{10,... | collective-permute-start | bytes 393224 | tf_op jit(solution)/shard_map/ppermute | solution.py:257
  39.4 3.0 %collective-permute-done.11.c = f32[64,512]{1,0:T(8,128)S(1)} collective-permute-done((f32[64,512]{1,0:T(8,128)S(1)}, f32[64,512]{1,0:T(8,128)S(1)}, u32[]{:S(2)}, u32[]{:S(2)}) %collective-permute-start.11) | collective-permute-done | bytes 131104 | tf_op jit(solution)/shard_map/ppermute | solution.py:257
  43.4 3.1 %collective-permute-start.13 = (f32[64,512]{1,0:T(8,128)S(1)}, f32[64,512]{1,0:T(8,128)S(1)}, u32[]{:S(2)}, u32[]{:S(2)}) collective-permute-start(f32[64,512]{1,0:T(8,128)S(1)} %sum_kernel.1.z0), channel_id=1, source_target_pairs={{0,4},{4,8},{8,12},{12,0},{1,5},{5,9},{9,13},{13,1},{2,6},{6,10},{... | collective-permute-start | bytes 393224 | tf_op jit(solution)/shard_map/ppermute | solution.py:257
  46.4 3.3 %collective-permute-start.16 = (f32[64,512]{1,0:T(8,128)S(1)}, f32[64,512]{1,0:T(8,128)S(1)}, u32[]{:S(2)}, u32[]{:S(2)}) collective-permute-start(f32[64,512]{1,0:T(8,128)S(1)} %sum_kernel.1.z0), channel_id=1, source_target_pairs={{0,12},{4,0},{8,4},{12,8},{1,13},{5,1},{9,5},{13,9},{2,14},{6,2},{... | collective-permute-start | bytes 393224 | tf_op jit(solution)/shard_map/ppermute | solution.py:257
  49.7 2.2 %collective-permute-done.13.z1 = f32[64,512]{1,0:T(8,128)S(1)} collective-permute-done((f32[64,512]{1,0:T(8,128)S(1)}, f32[64,512]{1,0:T(8,128)S(1)}, u32[]{:S(2)}, u32[]{:S(2)}) %collective-permute-start.13) | collective-permute-done | bytes 131104 | tf_op jit(solution)/shard_map/ppermute | solution.py:257
  51.9 3.7 %collective-permute-done.16.z3 = f32[64,512]{1,0:T(8,128)S(1)} collective-permute-done((f32[64,512]{1,0:T(8,128)S(1)}, f32[64,512]{1,0:T(8,128)S(1)}, u32[]{:S(2)}, u32[]{:S(2)}) %collective-permute-start.16) | collective-permute-done | bytes 131104 | tf_op jit(solution)/shard_map/ppermute | solution.py:257
  55.8 2.7 %collective-permute-start.18 = (bf16[256,512]{1,0:T(8,128)(2,1)S(1)}, bf16[256,512]{1,0:T(8,128)(2,1)S(1)}, u32[]{:S(2)}, u32[]{:S(2)}) collective-permute-start(bf16[256,512]{1,0:T(8,128)(2,1)S(1)} %slice.13), channel_id=1, source_target_pairs={{0,96},{32,0},{64,32},{96,64},{1,97},{33,1},{65,33},{97,65},{2,98}... | collective-permute-start | bytes 786440 | tf_op jit(solution)/shard_map/ppermute | solution.py:257
  58.5 2.1 %collective-permute-start.19 = (f32[64,256]{1,0:T(8,128)S(1)}, f32[64,256]{1,0:T(8,128)S(1)}, u32[]{:S(2)}, u32[]{:S(2)}) collective-permute-start(f32[64,256]{1,0:T(8,128)S(1)} %slice.16), channel_id=1, source_target_pairs={{0,4},{4,8},{8,12},{12,0},{1,5},{5,9},{9,13},{13,1},{2,6},{6,10},{... | collective-permute-start | bytes 196616 | tf_op jit(solution)/shard_map/ppermute | solution.py:257
  60.6 1.5 %collective-permute-start.20 = (f32[64,256]{1,0:T(8,128)S(1)}, f32[64,256]{1,0:T(8,128)S(1)}, u32[]{:S(2)}, u32[]{:S(2)}) collective-permute-start(f32[64,256]{1,0:T(8,128)S(1)} %slice.17), channel_id=1, source_target_pairs={{0,12},{4,0},{8,4},{12,8},{1,13},{5,1},{9,5},{13,9},{2,14},{6,2},{... | collective-permute-start | bytes 196616 | tf_op jit(solution)/shard_map/ppermute | solution.py:257
  62.1 1.7 %collective-permute-done.19.z2a = f32[64,256]{1,0:T(8,128)S(1)} collective-permute-done((f32[64,256]{1,0:T(8,128)S(1)}, f32[64,256]{1,0:T(8,128)S(1)}, u32[]{:S(2)}, u32[]{:S(2)}) %collective-permute-start.19) | collective-permute-done | bytes 65568 | tf_op jit(solution)/shard_map/ppermute | solution.py:257
  63.8 1.6 %collective-permute-done.20.z2b = f32[64,256]{1,0:T(8,128)S(1)} collective-permute-done((f32[64,256]{1,0:T(8,128)S(1)}, f32[64,256]{1,0:T(8,128)S(1)}, u32[]{:S(2)}, u32[]{:S(2)}) %collective-permute-start.20) | collective-permute-done | bytes 65568 | tf_op jit(solution)/shard_map/ppermute | solution.py:257
  65.7 5.8 %collective-permute-start.21 = (f32[2,64,512]{2,1,0:T(8,128)S(1)}, f32[2,64,512]{2,1,0:T(8,128)S(1)}, u32[]{:S(2)}, u32[]{:S(2)}) collective-permute-start(f32[2,64,512]{2,1,0:T(8,128)S(1)} %pv_kernel.1.pv_ref.p_ref), channel_id=1, source_target_pairs={{0,16},{16,0},{1,17},{17,1},{2,18},{18,2},{3,19},{19,3},{4,20},{20... | collective-permute-start | bytes 786440 | tf_op jit(solution)/shard_map/ppermute | solution.py:261
  74.4 14.9 %all_to_all.10.in_ref = f32[16,72,128]{2,1,0:T(8,128)S(1)} all-to-all(f32[16,72,128]{2,1,0:T(8,128)S(1)} %bitcast.16), channel_id=1, replica_groups=mesh['pipe'=2,'x'=4,'core'=2,'zhi'=4,'y'=4] {'x','y'}, dimensions={0} | all-to-all | bytes 1179648 | tf_op jit(solution)/shard_map/all_to_all | solution.py:269
  90.6 1.9 %collective-permute-start.23 = (f32[64,128]{1,0:T(8,128)S(1)}, f32[64,128]{1,0:T(8,128)S(1)}, u32[]{:S(2)}, u32[]{:S(2)}) collective-permute-start(f32[64,128]{1,0:T(8,128)S(1)} %get-tuple-element.68.q0), channel_id=1, source_target_pairs={{0,8},{4,12},{8,0},{12,4},{1,9},{5,13},{9,1},{13,5},{2,10},{6,14},... | collective-permute-start | bytes 98312 | tf_op jit(solution)/shard_map/ppermute | solution.py:257
  92.5 1.9 %collective-permute-start.24 = (f32[64,128]{1,0:T(8,128)S(1)}, f32[64,128]{1,0:T(8,128)S(1)}, u32[]{:S(2)}, u32[]{:S(2)}) collective-permute-start(f32[64,128]{1,0:T(8,128)S(1)} %get-tuple-element.68.q0), channel_id=1, source_target_pairs={{0,12},{4,0},{8,4},{12,8},{1,13},{5,1},{9,5},{13,9},{2,14},{6,2},{... | collective-permute-start | bytes 98312 | tf_op jit(solution)/shard_map/ppermute | solution.py:257
  94.4 2.8 %factor_kernel.1 = (f32[64,512]{1,0:T(8,128)}, bf16[128,512]{1,0:T(8,128)(2,1)S(1)}, f32[64,64]{1,0:T(8,128)S(1)}) custom-call(f32[32,128]{1,0:T(8,128)S(1)} %get-tuple-element.66.gram_ref, f32[2,64,512]{2,1,0:T(8,128)S(1)} %pv_kernel.1.pv_ref.p_ref), custom_call_target="tpu_custom_call" | custom-call | tf_op jit(solution)/shard_map/factor_kernel/pallas_call | solution.py:412
  97.1 2.3 %matrix_kernel.1.m_ref = f32[8,512,512]{2,1,0:T(8,128)S(1)} custom-call(bf16[512,512]{1,0:T(8,128)(2,1)S(1)} %get-tuple-element.70.at_ref, bf16[4,512,512]{2,1,0:T(8,128)(2,1)S(1)} %get-tuple-element.71.ga_ref, bf16[4,512,512]{2,1,0:T(8,128)(2,1)S(1)} %collective-permute-done.25.gb_ref, bf16[4,512,512]{2,1,0:T(8,128)(2,1)S(1)} %get-tuple-element.53.e_ref.ea_ref, ...), custom_call_target="tpu_custom_call" | custom-call | tf_op jit(solution)/shard_map/matrix_kernel/pallas_call | solution.py:422
  99.7 10.6 %all_to_all.11.q_ref = bf16[16,64,128]{2,1,0:T(8,128)(2,1)S(1)} all-to-all(bf16[16,64,128]{2,1,0:T(8,128)(2,1)S(1)} %q_scale_kernel.1), channel_id=1, replica_groups=mesh['pipe'=2,'x'=4,'core'=2,'zhi'=4,'y'=4] {'x','y'}, dimensions={0} | all-to-all | bytes 524288 | tf_op jit(solution)/shard_map/all_to_all | solution.py:269
  110.3 3.4 %collective-permute-start.26 = (bf16[16,64,128]{2,1,0:T(8,128)(2,1)S(1)}, bf16[16,64,128]{2,1,0:T(8,128)(2,1)S(1)}, u32[]{:S(2)}, u32[]{:S(2)}) collective-permute-start(bf16[16,64,128]{2,1,0:T(8,128)(2,1)S(1)} %all_to_all.11.q_ref), channel_id=1, source_target_pairs={{0,16},{16,0},{1,17},{17,1},{2,18},{18,2},{3,19},{19,3},{4,20},{20... | collective-permute-start | bytes 786440 | tf_op jit(solution)/shard_map/ppermute | solution.py:261
  113.7 2.3 %error_own_kernel.1 = (bf16[512,4096]{1,0:T(8,128)(2,1)}, f32[64,512]{1,0:T(8,128)}) custom-call(bf16[128,512]{1,0:T(8,128)(2,1)S(1)} %get-tuple-element.67.ph2_ref, bf16[16,64,128]{2,1,0:T(8,128)(2,1)S(1)} %all_to_all.11.q_ref, f32[8,512,512]{2,1,0:T(8,128)S(1)} %matrix_kernel.1.m_ref), custom_call_target="tpu_custom_call" | custom-call | tf_op jit(solution)/shard_map/error_own_kernel/pallas_call | solution.py:445
  116.1 1.7 %error_sib_kernel.1 = bf16[512,4096]{1,0:T(8,128)(2,1)} custom-call(bf16[128,512]{1,0:T(8,128)(2,1)S(1)} %get-tuple-element.67.ph2_ref, bf16[16,64,128]{2,1,0:T(8,128)(2,1)S(1)} %collective-permute-done.26.q_ref, f32[8,512,512]{2,1,0:T(8,128)S(1)} %matrix_kernel.1.m_ref, bf16[512,4096]{1,0:T(8,128)(2,1)} %get-tuple-element.75._), custom_call_target="tpu_custom_call", output_to_operand_aliasing={{}: (3, {})} | custom-call | tf_op jit(solution)/shard_map/error_sib_kernel/pallas_call | solution.py:455
  (45 shorter events, 16.1 us)
Async XLA Ops:
  2.1 14.2 %collective-permute-start = (bf16[512,512]{1,0:T(8,128)(2,1)S(1)}, bf16[512,512]{1,0:T(8,128)(2,1)S(1)}, u32[]{:S(2)}, u32[]{:S(2)}) collective-permute-start(bf16[512,512]{1,0:T(8,128)(2,1)S(1)} %get-tuple-element.42), channel_id=1, source_target_pairs={{128,0},{129,1},{130,2},{131,3},{132,4},{133,5},{134,6},{135,7},{1... | collective-permute-start | bytes 1572872 | tf_op jit(solution)/shard_map/ppermute | solution.py:290
  3.4 6.0 %collective-permute-start.1 = (f32[64,512]{1,0:T(8,128)}, f32[64,512]{1,0:T(8,128)S(1)}, u32[]{:S(2)}, u32[]{:S(2)}) collective-permute-start(f32[64,512]{1,0:T(8,128)} %bitcast.24), channel_id=1, source_target_pairs={{0,32},{32,64},{64,96},{96,0},{1,33},{33,65},{65,97},{97,1},{2,34}... | collective-permute-start | bytes 393224 | tf_op jit(solution)/shard_map/ppermute | solution.py:257
  5.5 8.4 %collective-permute-start.2 = (f32[64,512]{1,0:T(8,128)}, f32[64,512]{1,0:T(8,128)S(1)}, u32[]{:S(2)}, u32[]{:S(2)}) collective-permute-start(f32[64,512]{1,0:T(8,128)} %bitcast.25), channel_id=1, source_target_pairs={{0,64},{32,96},{64,0},{96,32},{1,65},{33,97},{65,1},{97,33},{2,66}... | collective-permute-start | bytes 393224 | tf_op jit(solution)/shard_map/ppermute | solution.py:257
  7.9 5.9 %collective-permute-start.3 = (f32[64,512]{1,0:T(8,128)}, f32[64,512]{1,0:T(8,128)S(1)}, u32[]{:S(2)}, u32[]{:S(2)}) collective-permute-start(f32[64,512]{1,0:T(8,128)} %bitcast.26), channel_id=1, source_target_pairs={{0,96},{32,0},{64,32},{96,64},{1,97},{33,1},{65,33},{97,65},{2,98}... | collective-permute-start | bytes 393224 | tf_op jit(solution)/shard_map/ppermute | solution.py:257
  16.7 3.5 %collective-permute-start.4 = (f32[64,512]{1,0:T(8,128)S(1)}, f32[64,512]{1,0:T(8,128)S(1)}, u32[]{:S(2)}, u32[]{:S(2)}) collective-permute-start(f32[64,512]{1,0:T(8,128)S(1)} %get-tuple-element.47), channel_id=1, source_target_pairs={{0,16},{16,0},{1,17},{17,1},{2,18},{18,2},{3,19},{19,3},{4,20},{20... | collective-permute-start | bytes 393224 | tf_op jit(solution)/shard_map/ppermute | solution.py:261
  20.1 5.7 %collective-permute-start.8 = (bf16[4,512,512]{2,1,0:T(8,128)(2,1)S(1)}, bf16[4,512,512]{2,1,0:T(8,128)(2,1)S(1)}, u32[]{:S(2)}, u32[]{:S(2)}) collective-permute-start(bf16[4,512,512]{2,1,0:T(8,128)(2,1)S(1)} %get-tuple-element.55.eb_ref), channel_id=1, source_target_pairs={{0,16},{16,0},{1,17},{17,1},{2,18},{18,2},{3,19},{19,3},{4,20},{20... | collective-permute-start | bytes 6291464 | tf_op jit(solution)/shard_map/ppermute | solution.py:261
  20.6 7.9 %collective-permute-start.5 = (f32[64,512]{1,0:T(8,128)S(1)}, f32[64,512]{1,0:T(8,128)S(1)}, u32[]{:S(2)}, u32[]{:S(2)}) collective-permute-start(f32[64,512]{1,0:T(8,128)S(1)} %add.3.u0), channel_id=1, source_target_pairs={{0,32},{32,64},{64,96},{96,0},{1,33},{33,65},{65,97},{97,1},{2,34}... | collective-permute-start | bytes 393224 | tf_op jit(solution)/shard_map/ppermute | solution.py:257
  22.2 8.7 %collective-permute-start.6 = (f32[64,512]{1,0:T(8,128)S(1)}, f32[64,512]{1,0:T(8,128)S(1)}, u32[]{:S(2)}, u32[]{:S(2)}) collective-permute-start(f32[64,512]{1,0:T(8,128)S(1)} %add.3.u0), channel_id=1, source_target_pairs={{0,64},{32,96},{64,0},{96,32},{1,65},{33,97},{65,1},{97,33},{2,66}... | collective-permute-start | bytes 393224 | tf_op jit(solution)/shard_map/ppermute | solution.py:257
  24.7 6.3 %collective-permute-start.7 = (f32[64,512]{1,0:T(8,128)S(1)}, f32[64,512]{1,0:T(8,128)S(1)}, u32[]{:S(2)}, u32[]{:S(2)}) collective-permute-start(f32[64,512]{1,0:T(8,128)S(1)} %add.3.u0), channel_id=1, source_target_pairs={{0,96},{32,0},{64,32},{96,64},{1,97},{33,1},{65,33},{97,65},{2,98}... | collective-permute-start | bytes 393224 | tf_op jit(solution)/shard_map/ppermute | solution.py:257
  27.4 3.6 %collective-permute-start.9 = (f32[64,512]{1,0:T(8,128)S(1)}, f32[64,512]{1,0:T(8,128)S(1)}, u32[]{:S(2)}, u32[]{:S(2)}) collective-permute-start(f32[64,512]{1,0:T(8,128)S(1)} %get-tuple-element.57), channel_id=1, source_target_pairs={{0,16},{16,0},{1,17},{17,1},{2,18},{18,2},{3,19},{19,3},{4,20},{20... | collective-permute-start | bytes 393224 | tf_op jit(solution)/shard_map/ppermute | solution.py:261
  31.0 24.7 %collective-permute-start.14 = (bf16[512,512]{1,0:T(8,128)(2,1)S(1)}, bf16[512,512]{1,0:T(8,128)(2,1)S(1)}, u32[]{:S(2)}, u32[]{:S(2)}) collective-permute-start(bf16[512,512]{1,0:T(8,128)(2,1)S(1)} %get-tuple-element.58.g_ref.g0), channel_id=1, source_target_pairs={{0,32},{32,64},{64,96},{96,0},{1,33},{33,65},{65,97},{97,1},{2,34}... | collective-permute-start | bytes 1572872 | tf_op jit(solution)/shard_map/ppermute | solution.py:257
  31.5 24.2 %collective-permute-start.15 = (bf16[512,512]{1,0:T(8,128)(2,1)S(1)}, bf16[512,512]{1,0:T(8,128)(2,1)S(1)}, u32[]{:S(2)}, u32[]{:S(2)}) collective-permute-start(bf16[512,512]{1,0:T(8,128)(2,1)S(1)} %get-tuple-element.58.g_ref.g0), channel_id=1, source_target_pairs={{0,96},{32,0},{64,32},{96,64},{1,97},{33,1},{65,33},{97,65},{2,98}... | collective-permute-start | bytes 1572872 | tf_op jit(solution)/shard_map/ppermute | solution.py:257
  33.9 5.5 %collective-permute-start.10 = (f32[64,512]{1,0:T(8,128)S(1)}, f32[64,512]{1,0:T(8,128)S(1)}, u32[]{:S(2)}, u32[]{:S(2)}) collective-permute-start(f32[64,512]{1,0:T(8,128)S(1)} %p_kernel.1.a), channel_id=1, source_target_pairs={{0,1},{1,2},{2,3},{3,0},{4,5},{5,6},{6,7},{7,4},{8,9},{9,10},{10,1... | collective-permute-start | bytes 393224 | tf_op jit(solution)/shard_map/ppermute | solution.py:257
  35.3 7.1 %collective-permute-start.11 = (f32[64,512]{1,0:T(8,128)S(1)}, f32[64,512]{1,0:T(8,128)S(1)}, u32[]{:S(2)}, u32[]{:S(2)}) collective-permute-start(f32[64,512]{1,0:T(8,128)S(1)} %p_kernel.1.a), channel_id=1, source_target_pairs={{0,2},{1,3},{2,0},{3,1},{4,6},{5,7},{6,4},{7,5},{8,10},{9,11},{10,... | collective-permute-start | bytes 393224 | tf_op jit(solution)/shard_map/ppermute | solution.py:257
  37.9 5.4 %collective-permute-start.12 = (f32[64,512]{1,0:T(8,128)S(1)}, f32[64,512]{1,0:T(8,128)S(1)}, u32[]{:S(2)}, u32[]{:S(2)}) collective-permute-start(f32[64,512]{1,0:T(8,128)S(1)} %p_kernel.1.a), channel_id=1, source_target_pairs={{0,3},{1,0},{2,1},{3,2},{4,7},{5,4},{6,5},{7,6},{8,11},{9,8},{10,9... | collective-permute-start | bytes 393224 | tf_op jit(solution)/shard_map/ppermute | solution.py:257
  43.4 8.6 %collective-permute-start.13 = (f32[64,512]{1,0:T(8,128)S(1)}, f32[64,512]{1,0:T(8,128)S(1)}, u32[]{:S(2)}, u32[]{:S(2)}) collective-permute-start(f32[64,512]{1,0:T(8,128)S(1)} %sum_kernel.1.z0), channel_id=1, source_target_pairs={{0,4},{4,8},{8,12},{12,0},{1,5},{5,9},{9,13},{13,1},{2,6},{6,10},{... | collective-permute-start | bytes 393224 | tf_op jit(solution)/shard_map/ppermute | solution.py:257
  46.4 9.2 %collective-permute-start.16 = (f32[64,512]{1,0:T(8,128)S(1)}, f32[64,512]{1,0:T(8,128)S(1)}, u32[]{:S(2)}, u32[]{:S(2)}) collective-permute-start(f32[64,512]{1,0:T(8,128)S(1)} %sum_kernel.1.z0), channel_id=1, source_target_pairs={{0,12},{4,0},{8,4},{12,8},{1,13},{5,1},{9,5},{13,9},{2,14},{6,2},{... | collective-permute-start | bytes 393224 | tf_op jit(solution)/shard_map/ppermute | solution.py:257
  55.7 9.7 %collective-permute-start.17 = (bf16[256,512]{1,0:T(8,128)(2,1)S(1)}, bf16[256,512]{1,0:T(8,128)(2,1)S(1)}, u32[]{:S(2)}, u32[]{:S(2)}) collective-permute-start(bf16[256,512]{1,0:T(8,128)(2,1)S(1)} %slice.12), channel_id=1, source_target_pairs={{0,32},{32,64},{64,96},{96,0},{1,33},{33,65},{65,97},{97,1},{2,34}... | collective-permute-start | bytes 786440 | tf_op jit(solution)/shard_map/ppermute | solution.py:257
  55.8 9.6 %collective-permute-start.18 = (bf16[256,512]{1,0:T(8,128)(2,1)S(1)}, bf16[256,512]{1,0:T(8,128)(2,1)S(1)}, u32[]{:S(2)}, u32[]{:S(2)}) collective-permute-start(bf16[256,512]{1,0:T(8,128)(2,1)S(1)} %slice.13), channel_id=1, source_target_pairs={{0,96},{32,0},{64,32},{96,64},{1,97},{33,1},{65,33},{97,65},{2,98}... | collective-permute-start | bytes 786440 | tf_op jit(solution)/shard_map/ppermute | solution.py:257
  58.5 5.3 %collective-permute-start.19 = (f32[64,256]{1,0:T(8,128)S(1)}, f32[64,256]{1,0:T(8,128)S(1)}, u32[]{:S(2)}, u32[]{:S(2)}) collective-permute-start(f32[64,256]{1,0:T(8,128)S(1)} %slice.16), channel_id=1, source_target_pairs={{0,4},{4,8},{8,12},{12,0},{1,5},{5,9},{9,13},{13,1},{2,6},{6,10},{... | collective-permute-start | bytes 196616 | tf_op jit(solution)/shard_map/ppermute | solution.py:257
  60.6 4.7 %collective-permute-start.20 = (f32[64,256]{1,0:T(8,128)S(1)}, f32[64,256]{1,0:T(8,128)S(1)}, u32[]{:S(2)}, u32[]{:S(2)}) collective-permute-start(f32[64,256]{1,0:T(8,128)S(1)} %slice.17), channel_id=1, source_target_pairs={{0,12},{4,0},{8,4},{12,8},{1,13},{5,1},{9,5},{13,9},{2,14},{6,2},{... | collective-permute-start | bytes 196616 | tf_op jit(solution)/shard_map/ppermute | solution.py:257
  65.7 6.9 %collective-permute-start.21 = (f32[2,64,512]{2,1,0:T(8,128)S(1)}, f32[2,64,512]{2,1,0:T(8,128)S(1)}, u32[]{:S(2)}, u32[]{:S(2)}) collective-permute-start(f32[2,64,512]{2,1,0:T(8,128)S(1)} %pv_kernel.1.pv_ref.p_ref), channel_id=1, source_target_pairs={{0,16},{16,0},{1,17},{17,1},{2,18},{18,2},{3,19},{19,3},{4,20},{20... | collective-permute-start | bytes 786440 | tf_op jit(solution)/shard_map/ppermute | solution.py:261
  74.0 23.2 %collective-permute-start.25 = (bf16[4,512,512]{2,1,0:T(8,128)(2,1)S(1)}, bf16[4,512,512]{2,1,0:T(8,128)(2,1)S(1)}, u32[]{:S(2)}, u32[]{:S(2)}) collective-permute-start(bf16[4,512,512]{2,1,0:T(8,128)(2,1)S(1)} %get-tuple-element.71.ga_ref), channel_id=1, source_target_pairs={{0,16},{16,0},{1,17},{17,1},{2,18},{18,2},{3,19},{19,3},{4,20},{20... | collective-permute-start | bytes 6291464 | tf_op jit(solution)/shard_map/ppermute | solution.py:261
  89.4 10.1 %collective-permute-start.22 = (f32[64,128]{1,0:T(8,128)S(1)}, f32[64,128]{1,0:T(8,128)S(1)}, u32[]{:S(2)}, u32[]{:S(2)}) collective-permute-start(f32[64,128]{1,0:T(8,128)S(1)} %get-tuple-element.68.q0), channel_id=1, source_target_pairs={{0,4},{4,8},{8,12},{12,0},{1,5},{5,9},{9,13},{13,1},{2,6},{6,10},{... | collective-permute-start | bytes 98312 | tf_op jit(solution)/shard_map/ppermute | solution.py:257
  90.6 8.9 %collective-permute-start.23 = (f32[64,128]{1,0:T(8,128)S(1)}, f32[64,128]{1,0:T(8,128)S(1)}, u32[]{:S(2)}, u32[]{:S(2)}) collective-permute-start(f32[64,128]{1,0:T(8,128)S(1)} %get-tuple-element.68.q0), channel_id=1, source_target_pairs={{0,8},{4,12},{8,0},{12,4},{1,9},{5,13},{9,1},{13,5},{2,10},{6,14},... | collective-permute-start | bytes 98312 | tf_op jit(solution)/shard_map/ppermute | solution.py:257
  92.5 7.0 %collective-permute-start.24 = (f32[64,128]{1,0:T(8,128)S(1)}, f32[64,128]{1,0:T(8,128)S(1)}, u32[]{:S(2)}, u32[]{:S(2)}) collective-permute-start(f32[64,128]{1,0:T(8,128)S(1)} %get-tuple-element.68.q0), channel_id=1, source_target_pairs={{0,12},{4,0},{8,4},{12,8},{1,13},{5,1},{9,5},{13,9},{2,14},{6,2},{... | collective-permute-start | bytes 98312 | tf_op jit(solution)/shard_map/ppermute | solution.py:257
  110.3 5.8 %collective-permute-start.26 = (bf16[16,64,128]{2,1,0:T(8,128)(2,1)S(1)}, bf16[16,64,128]{2,1,0:T(8,128)(2,1)S(1)}, u32[]{:S(2)}, u32[]{:S(2)}) collective-permute-start(bf16[16,64,128]{2,1,0:T(8,128)(2,1)S(1)} %all_to_all.11.q_ref), channel_id=1, source_target_pairs={{0,16},{16,0},{1,17},{17,1},{2,18},{18,2},{3,19},{19,3},{4,20},{20... | collective-permute-start | bytes 786440 | tf_op jit(solution)/shard_map/ppermute | solution.py:261

commit v6 on v5

--- a/solution.py
+++ b/solution.py
@@ -124,27 +124,27 @@
     run_copies(pairs + [(act, act_v)], sems)
 
 
-def pv_kernel(z0, z1, z2a, z2b, z3, act_ref, out_ref):
+def pv_kernel(z0, z1, z2a, z2b, z3, act_ref, p_ref, v_ref):
     z2 = jnp.concatenate([z2a[...], z2b[...]], axis=1)
     p = ((z0[...] + z2) + (z1[...] + z3[...])) * (1.0 / 16.0)
-    out_ref[0] = p
-    out_ref[1] = fold3(dot(split3(p), act_ref[...], 1, 1))
-
-
-def q_own_kernel(pv_ref, e_ref, out_ref):
-    p3 = split3(pv_ref[0])
+    p_ref[...] = p
+    v_ref[...] = fold3(dot(split3(p), act_ref[...], 1, 1))
+
+
+def q_own_kernel(p_ref, e_ref, out_ref):
+    p3 = split3(p_ref[...])
     for k in range(4):
         out_ref[k] = fold3(dot(p3, e_ref[k], 1, 0))
 
 
-def q_kernel(pv_ref, pvs_ref, r_ref, es_ref, g0, g1, g2a, g2b, g3, out_ref, gs_ref, gram_scr):
-    v3 = split3(pv_ref[1] + pvs_ref[1])
-    q3 = split3(pvs_ref[0])
+def q_kernel(p_ref, v_ref, ps_ref, vs_ref, r_ref, es_ref, g0, g1, g2a, g2b, g3, out_ref, gs_ref, gram_scr):
+    v3 = split3(v_ref[...] + vs_ref[...])
+    q3 = split3(ps_ref[...])
 
     def gram_of(p3):
         return dot(p3, p3[0:64], 1, 1) + (dot(p3, p3[64:128], 1, 1) + dot(p3, p3[128:192], 1, 1))
 
-    g = fold3(gram_of(split3(pv_ref[0])) + gram_of(q3))
+    g = fold3(gram_of(split3(p_ref[...])) + gram_of(q3))
     gram_scr[...] = jnp.concatenate([g[0:32], g[32:64]], axis=1)
     gram = gram_scr[pl.ds(pl.multiple_of(lax.axis_index("y") * 8, 8), 8), :]
     for k, gr in enumerate((g0, g1, None, g3)):
@@ -200,7 +200,7 @@
         a = jnp.concatenate(parts, axis=0) if len(parts) > 1 else block
     linv = pltpu.roll(a, 64, 1)[:, 0:n]
     linv_ref[...] = linv
-    phat = jnp.dot(linv, p_ref[0], precision=HIGH, preferred_element_type=F32)
+    phat = jnp.dot(linv, p_ref[...], precision=HIGH, preferred_element_type=F32)
     phat_ref[...] = phat
     hi = phat.astype(BF)
     ph2_ref[0:64] = hi
@@ -361,22 +361,22 @@
 
     z1 = shift(part, "zhi", 1)
     z3 = shift(part, "zhi", 3)
-    h1, h3, *_ = lax.optimization_barrier((g1, g3, z1, z3))
+    h1, h3, *_ = lax.optimization_barrier((g1, g3, z3))
     g2a = shift(h1[:256], "x", 1)
     g2b = shift(h3[256:], "x", 3)
     z2a = shift(z1[:, :256], "zhi", 1)
     z2b = shift(z3[:, 256:], "zhi", 3)
-    g2a, g2b, z2a, z2b = lax.optimization_barrier((g2a, g2b, z2a, z2b))
-    pv = pl.pallas_call(
+    p, v = pl.pallas_call(
         pv_kernel,
-        out_shape=sds((2, 64, 512), F32),
+        out_shape=(sds((64, 512), F32), sds((64, 512), F32)),
         in_specs=[VMEM] * 6,
-        out_specs=VMEM,
+        out_specs=(VMEM, VMEM),
         cost_estimate=LIGHT,
         compiler_params=params(4),
         name="pv_kernel",
     )(part, z1, z2a, z2b, z3, act)
-    pvs = swap(pv)
+    ps = swap(p)
+    vs = swap(v)
     q_own_part = pl.pallas_call(
         q_own_kernel,
         out_shape=sds((4, 64, 512), F32),
@@ -385,17 +385,17 @@
         cost_estimate=LIGHT,
         compiler_params=params(8),
         name="q_own_kernel",
-    )(pv, err)
+    )(p, err)
     chunks, gs = pl.pallas_call(
         q_kernel,
         out_shape=(sds((4, 4, 72, 128), F32), sds((4, 512, 512), BF)),
-        in_specs=[VMEM] * 9,
+        in_specs=[VMEM] * 11,
         out_specs=(VMEM, VMEM),
         scratch_shapes=[pltpu.VMEM((32, 128), F32)],
         cost_estimate=LIGHT,
         compiler_params=params(12),
         name="q_kernel",
-    )(pv, pvs, q_own_part, eh_s, grad, g1, g2a, g2b, g3)
+    )(p, v, ps, vs, q_own_part, eh_s, grad, g1, g2a, g2b, g3)
     gb = swap(gs)
     chunks = exchange(chunks.reshape(16, 72, 128), ("x", "y"))
 
@@ -417,7 +417,7 @@
         cost_estimate=LIGHT,
         compiler_params=params(4),
         name="factor_kernel",
-    )(gram, pv)
+    )(gram, p)
     act_t, gram = lax.optimization_barrier((act_t, gram))
     matrix = pl.pallas_call(
         matrix_kernel,

time: 118 us -> 118 us (level)
    ppermute x20, starting transfers between devices: 36.5 us -> 39.2 us  [shift(): return lax.ppermute(v, axis, [(i, (i + k) % n) for i in range(n)])]
    ppermute x6 -> x7, starting transfers between devices: 13.7 us -> 12 us  [swap(): return lax.ppermute(v, 'core', [(0, 1), (1, 0)])]
    ppermute x20, waiting for transfers between devices: 20.8 us -> 19.5 us  [shift(): return lax.ppermute(v, axis, [(i, (i + k) % n) for i in range(n)])]
  transfers between devices with their start and end apart: 27 -> 28, of which waited for: 12 -> 13; matrix products, arithmetic and copies ran while one was open for 0% -> 0% of each run, Pallas kernels for 11% -> 11%
where the time goes in v6:
time: 118 us; the launch traced here: 117 us
  starting transfers between devices  52.4 us (44%)
  blocking collectives  25.2 us (21%)
  waiting for transfers between devices  20.3 us (17%)
  Pallas kernels  18.4 us (16%)
    ppermute x20, starting transfers between devices, shift(): return lax.ppermute(v, axis, [(i, (i + k) % n) for i in range(n)])  39.2 us
    all_to_all x2, blocking collectives, exchange(): return lax.all_to_all(v, axes, 0, 0, tiled=True)  25.2 us
    ppermute x20, waiting for transfers between devices, shift(): return lax.ppermute(v, axis, [(i, (i + k) % n) for i in range(n)])  19.5 us
    ppermute x7, starting transfers between devices, swap(): return lax.ppermute(v, 'core', [(0, 1), (1, 0)])  12 us
    pallas_call x1, Pallas kernels, on_device(): pl.pallas_call(factor_kernel, out_shape=(sds((64, 512), F32), sds((128, 5...  2.75 us
    pallas_call x1, Pallas kernels, on_device(): pl.pallas_call(load_error_kernel, out_shape=(sds((4, 512, 512), BF), sds(...  2.42 us
  transfers between devices with their start and end apart: 28, of which 13 were waited for; matrix products, arithmetic and copies ran while one was open for 0% of the time, Pallas kernels for 11%

profile of v6, /device:TPU:1, one launch (start us, length us, event | category | flops | bytes accessed | tf_op | source)
XLA Modules:
  0.0 117.4 jit_solution(13685361436188139179)
XLA Ops:
  0.6 1.4 %load_kernel.1 = (f32[64,512]{1,0:T(8,128)S(1)}, bf16[512,512]{1,0:T(8,128)(2,1)S(1)}, bf16[512,512]{1,0:T(8,128)(2,1)S(1)}, bf16[512,512]{1,0:T(8,128)(2,1)S(1)}) custom-call(f32[64,512]{1,0:T(8,128)} %bitcast.23, bf16[512,512]{1,0:T(8,128)(2,1)} %bitcast.21, bf16[512,512]{1,0:T(8,128)(2,1)} %bitcast.22), custom_call_target="tpu_custom_call" | custom-call | tf_op jit(solution)/shard_map/load_kernel/pallas_call | solution.py:279
  3.4 2.1 %collective-permute-start.1 = (f32[64,512]{1,0:T(8,128)}, f32[64,512]{1,0:T(8,128)S(1)}, u32[]{:S(2)}, u32[]{:S(2)}) collective-permute-start(f32[64,512]{1,0:T(8,128)} %bitcast.24), channel_id=1, source_target_pairs={{0,32},{32,64},{64,96},{96,0},{1,33},{33,65},{65,97},{97,1},{2,34}... | collective-permute-start | bytes 393224 | tf_op jit(solution)/shard_map/ppermute | solution.py:257
  5.5 2.5 %collective-permute-start.2 = (f32[64,512]{1,0:T(8,128)}, f32[64,512]{1,0:T(8,128)S(1)}, u32[]{:S(2)}, u32[]{:S(2)}) collective-permute-start(f32[64,512]{1,0:T(8,128)} %bitcast.25), channel_id=1, source_target_pairs={{0,64},{32,96},{64,0},{96,32},{1,65},{33,97},{65,1},{97,33},{2,66}... | collective-permute-start | bytes 393224 | tf_op jit(solution)/shard_map/ppermute | solution.py:257
  9.3 4.5 %collective-permute-done.2.q2 = f32[64,512]{1,0:T(8,128)S(1)} collective-permute-done((f32[64,512]{1,0:T(8,128)}, f32[64,512]{1,0:T(8,128)S(1)}, u32[]{:S(2)}, u32[]{:S(2)}) %collective-permute-start.2) | collective-permute-done | bytes 131104 | tf_op jit(solution)/shard_map/ppermute | solution.py:257
  13.9 2.4 %load_error_kernel.1 = (bf16[4,512,512]{2,1,0:T(8,128)(2,1)S(1)}, bf16[4,512,512]{2,1,0:T(8,128)(2,1)S(1)}, bf16[512,512]{1,0:T(8,128)(2,1)S(1)}) custom-call(bf16[512,4096]{1,0:T(8,128)(2,1)} %bitcast.17, bf16[512,512]{1,0:T(8,128)(2,1)} %bitcast.19), custom_call_target="tpu_custom_call" | custom-call | tf_op jit(solution)/shard_map/load_error_kernel/pallas_call | solution.py:293
  16.7 2.5 %collective-permute-start.4 = (f32[64,512]{1,0:T(8,128)S(1)}, f32[64,512]{1,0:T(8,128)S(1)}, u32[]{:S(2)}, u32[]{:S(2)}) collective-permute-start(f32[64,512]{1,0:T(8,128)S(1)} %get-tuple-element.45), channel_id=1, source_target_pairs={{0,16},{16,0},{1,17},{17,1},{2,18},{18,2},{3,19},{19,3},{4,20},{20... | collective-permute-start | bytes 393224 | tf_op jit(solution)/shard_map/ppermute | solution.py:261
  20.6 1.7 %collective-permute-start.5 = (f32[64,512]{1,0:T(8,128)S(1)}, f32[64,512]{1,0:T(8,128)S(1)}, u32[]{:S(2)}, u32[]{:S(2)}) collective-permute-start(f32[64,512]{1,0:T(8,128)S(1)} %add.3.u0), channel_id=1, source_target_pairs={{0,32},{32,64},{64,96},{96,0},{1,33},{33,65},{65,97},{97,1},{2,34}... | collective-permute-start | bytes 393224 | tf_op jit(solution)/shard_map/ppermute | solution.py:257
  22.2 2.4 %collective-permute-start.6 = (f32[64,512]{1,0:T(8,128)S(1)}, f32[64,512]{1,0:T(8,128)S(1)}, u32[]{:S(2)}, u32[]{:S(2)}) collective-permute-start(f32[64,512]{1,0:T(8,128)S(1)} %add.3.u0), channel_id=1, source_target_pairs={{0,64},{32,96},{64,0},{96,32},{1,65},{33,97},{65,1},{97,33},{2,66}... | collective-permute-start | bytes 393224 | tf_op jit(solution)/shard_map/ppermute | solution.py:257
  25.9 1.5 %eq_kernel.1 = (f32[64,512]{1,0:T(8,128)S(1)}, f32[64,512]{1,0:T(8,128)S(1)}, bf16[512,512]{1,0:T(8,128)(2,1)S(1)}) custom-call(f32[64,512]{1,0:T(8,128)S(1)} %get-tuple-element.44.q_ref.q0, f32[64,512]{1,0:T(8,128)S(1)} %collective-permute-done.1.q1, f32[64,512]{1,0:T(8,128)S(1)} %collective-permute-done.2.q2, f32[64,512]{1,0:T(8,128)S(1)} %collective-permute-done.3.q3, ...), custom_call_target="tpu_custom_call" | custom-call | tf_op jit(solution)/shard_map/eq_kernel/pallas_call | solution.py:328
  28.5 2.5 %collective-permute-done.6.u2 = f32[64,512]{1,0:T(8,128)S(1)} collective-permute-done((f32[64,512]{1,0:T(8,128)S(1)}, f32[64,512]{1,0:T(8,128)S(1)}, u32[]{:S(2)}, u32[]{:S(2)}) %collective-permute-start.6) | collective-permute-done | bytes 131104 | tf_op jit(solution)/shard_map/ppermute | solution.py:257
  31.5 2.2 %collective-permute-start.20 = (bf16[512,512]{1,0:T(8,128)(2,1)S(1)}, bf16[512,512]{1,0:T(8,128)(2,1)S(1)}, u32[]{:S(2)}, u32[]{:S(2)}) collective-permute-start(bf16[512,512]{1,0:T(8,128)(2,1)S(1)} %get-tuple-element.58.g_ref.g0), channel_id=1, source_target_pairs={{0,96},{32,0},{64,32},{96,64},{1,97},{33,1},{65,33},{97,65},{2,98}... | collective-permute-start | bytes 1572872 | tf_op jit(solution)/shard_map/ppermute | solution.py:257
  33.9 1.4 %collective-permute-start.10 = (f32[64,512]{1,0:T(8,128)S(1)}, f32[64,512]{1,0:T(8,128)S(1)}, u32[]{:S(2)}, u32[]{:S(2)}) collective-permute-start(f32[64,512]{1,0:T(8,128)S(1)} %p_kernel.1.a), channel_id=1, source_target_pairs={{0,1},{1,2},{2,3},{3,0},{4,5},{5,6},{6,7},{7,4},{8,9},{9,10},{10,1... | collective-permute-start | bytes 393224 | tf_op jit(solution)/shard_map/ppermute | solution.py:257
  35.3 2.6 %collective-permute-start.11 = (f32[64,512]{1,0:T(8,128)S(1)}, f32[64,512]{1,0:T(8,128)S(1)}, u32[]{:S(2)}, u32[]{:S(2)}) collective-permute-start(f32[64,512]{1,0:T(8,128)S(1)} %p_kernel.1.a), channel_id=1, source_target_pairs={{0,2},{1,3},{2,0},{3,1},{4,6},{5,7},{6,4},{7,5},{8,10},{9,11},{10,... | collective-permute-start | bytes 393224 | tf_op jit(solution)/shard_map/ppermute | solution.py:257
  39.4 3.0 %collective-permute-done.11.c = f32[64,512]{1,0:T(8,128)S(1)} collective-permute-done((f32[64,512]{1,0:T(8,128)S(1)}, f32[64,512]{1,0:T(8,128)S(1)}, u32[]{:S(2)}, u32[]{:S(2)}) %collective-permute-start.11) | collective-permute-done | bytes 131104 | tf_op jit(solution)/shard_map/ppermute | solution.py:257
  43.4 6.1 %collective-permute-start.15 = (f32[64,512]{1,0:T(8,128)S(1)}, f32[64,512]{1,0:T(8,128)S(1)}, u32[]{:S(2)}, u32[]{:S(2)}) collective-permute-start(f32[64,512]{1,0:T(8,128)S(1)} %sum_kernel.1.z0), channel_id=1, source_target_pairs={{0,12},{4,0},{8,4},{12,8},{1,13},{5,1},{9,5},{13,9},{2,14},{6,2},{... | collective-permute-start | bytes 393224 | tf_op jit(solution)/shard_map/ppermute | solution.py:257
  49.5 3.1 %collective-permute-done.15.z3 = f32[64,512]{1,0:T(8,128)S(1)} collective-permute-done((f32[64,512]{1,0:T(8,128)S(1)}, f32[64,512]{1,0:T(8,128)S(1)}, u32[]{:S(2)}, u32[]{:S(2)}) %collective-permute-start.15) | collective-permute-done | bytes 131104 | tf_op jit(solution)/shard_map/ppermute | solution.py:257
  52.7 2.7 %collective-permute-start.22 = (bf16[256,512]{1,0:T(8,128)(2,1)S(1)}, bf16[256,512]{1,0:T(8,128)(2,1)S(1)}, u32[]{:S(2)}, u32[]{:S(2)}) collective-permute-start(bf16[256,512]{1,0:T(8,128)(2,1)S(1)} %slice.15), channel_id=1, source_target_pairs={{0,96},{32,0},{64,32},{96,64},{1,97},{33,1},{65,33},{97,65},{2,98}... | collective-permute-start | bytes 786440 | tf_op jit(solution)/shard_map/ppermute | solution.py:257
  56.2 3.5 %collective-permute-start.14 = (f32[64,256]{1,0:T(8,128)S(1)}, f32[64,256]{1,0:T(8,128)S(1)}, u32[]{:S(2)}, u32[]{:S(2)}) collective-permute-start(f32[64,256]{1,0:T(8,128)S(1)} %slice.16), channel_id=1, source_target_pairs={{0,4},{4,8},{8,12},{12,0},{1,5},{5,9},{9,13},{13,1},{2,6},{6,10},{... | collective-permute-start | bytes 196616 | tf_op jit(solution)/shard_map/ppermute | solution.py:257
  59.8 1.6 %collective-permute-done.14.z2a = f32[64,256]{1,0:T(8,128)S(1)} collective-permute-done((f32[64,256]{1,0:T(8,128)S(1)}, f32[64,256]{1,0:T(8,128)S(1)}, u32[]{:S(2)}, u32[]{:S(2)}) %collective-permute-start.14) | collective-permute-done | bytes 65568 | tf_op jit(solution)/shard_map/ppermute | solution.py:257
  61.4 2.4 %collective-permute-done.16.z2b = f32[64,256]{1,0:T(8,128)S(1)} collective-permute-done((f32[64,256]{1,0:T(8,128)S(1)}, f32[64,256]{1,0:T(8,128)S(1)}, u32[]{:S(2)}, u32[]{:S(2)}) %collective-permute-start.16) | collective-permute-done | bytes 65568 | tf_op jit(solution)/shard_map/ppermute | solution.py:257
  64.2 3.9 %collective-permute-start.17 = (f32[64,512]{1,0:T(8,128)S(1)}, f32[64,512]{1,0:T(8,128)S(1)}, u32[]{:S(2)}, u32[]{:S(2)}) collective-permute-start(f32[64,512]{1,0:T(8,128)S(1)} %get-tuple-element.56.p_ref), channel_id=1, source_target_pairs={{0,16},{16,0},{1,17},{17,1},{2,18},{18,2},{3,19},{19,3},{4,20},{20... | collective-permute-start | bytes 393224 | tf_op jit(solution)/shard_map/ppermute | solution.py:261
  69.4 1.3 %q_kernel.1 = (f32[4,4,72,128]{3,2,1,0:T(8,128)S(1)}, bf16[4,512,512]{2,1,0:T(8,128)(2,1)S(1)}) custom-call(f32[64,512]{1,0:T(8,128)S(1)} %get-tuple-element.56.p_ref, f32[64,512]{1,0:T(8,128)S(1)} %get-tuple-element.57.v_ref, f32[64,512]{1,0:T(8,128)S(1)} %collective-permute-done.17.ps_ref, f32[64,512]{1,0:T(8,128)S(1)} %collective-permute-done.18.vs_ref, ...), custom_call_target="tpu_custom_call" | custom-call | tf_op jit(solution)/shard_map/q_kernel/pallas_call | solution.py:389
  71.0 14.7 %all_to_all.10.in_ref = f32[16,72,128]{2,1,0:T(8,128)S(1)} all-to-all(f32[16,72,128]{2,1,0:T(8,128)S(1)} %bitcast.16), channel_id=1, replica_groups=mesh['pipe'=2,'x'=4,'core'=2,'zhi'=4,'y'=4] {'x','y'}, dimensions={0} | all-to-all | bytes 1179648 | tf_op jit(solution)/shard_map/all_to_all | solution.py:269
  85.7 3.4 %collective-permute-start.23 = (f32[64,128]{1,0:T(8,128)S(1)}, f32[64,128]{1,0:T(8,128)S(1)}, u32[]{:S(2)}, u32[]{:S(2)}) collective-permute-start(f32[64,128]{1,0:T(8,128)S(1)} %get-tuple-element.64.q0), channel_id=1, source_target_pairs={{0,4},{4,8},{8,12},{12,0},{1,5},{5,9},{9,13},{13,1},{2,6},{6,10},{... | collective-permute-start | bytes 98312 | tf_op jit(solution)/shard_map/ppermute | solution.py:257
  89.2 2.3 %collective-permute-start.24 = (f32[64,128]{1,0:T(8,128)S(1)}, f32[64,128]{1,0:T(8,128)S(1)}, u32[]{:S(2)}, u32[]{:S(2)}) collective-permute-start(f32[64,128]{1,0:T(8,128)S(1)} %get-tuple-element.64.q0), channel_id=1, source_target_pairs={{0,8},{4,12},{8,0},{12,4},{1,9},{5,13},{9,1},{13,5},{2,10},{6,14},... | collective-permute-start | bytes 98312 | tf_op jit(solution)/shard_map/ppermute | solution.py:257
  91.5 2.2 %collective-permute-start.25 = (f32[64,128]{1,0:T(8,128)S(1)}, f32[64,128]{1,0:T(8,128)S(1)}, u32[]{:S(2)}, u32[]{:S(2)}) collective-permute-start(f32[64,128]{1,0:T(8,128)S(1)} %get-tuple-element.64.q0), channel_id=1, source_target_pairs={{0,12},{4,0},{8,4},{12,8},{1,13},{5,1},{9,5},{13,9},{2,14},{6,2},{... | collective-permute-start | bytes 98312 | tf_op jit(solution)/shard_map/ppermute | solution.py:257
  93.7 2.8 %factor_kernel.1 = (f32[64,512]{1,0:T(8,128)}, bf16[128,512]{1,0:T(8,128)(2,1)S(1)}, f32[64,64]{1,0:T(8,128)S(1)}) custom-call(f32[32,128]{1,0:T(8,128)S(1)} %get-tuple-element.62.gram_ref, f32[64,512]{1,0:T(8,128)S(1)} %get-tuple-element.56.p_ref), custom_call_target="tpu_custom_call" | custom-call | tf_op jit(solution)/shard_map/factor_kernel/pallas_call | solution.py:412
  96.5 2.3 %matrix_kernel.1.m_ref = f32[8,512,512]{2,1,0:T(8,128)S(1)} custom-call(bf16[512,512]{1,0:T(8,128)(2,1)S(1)} %get-tuple-element.66.at_ref, bf16[4,512,512]{2,1,0:T(8,128)(2,1)S(1)} %get-tuple-element.67.ga_ref, bf16[4,512,512]{2,1,0:T(8,128)(2,1)S(1)} %collective-permute-done.26.gb_ref, bf16[4,512,512]{2,1,0:T(8,128)(2,1)S(1)} %get-tuple-element.51.e_ref.ea_ref, ...), custom_call_target="tpu_custom_call" | custom-call | tf_op jit(solution)/shard_map/matrix_kernel/pallas_call | solution.py:422
  99.0 10.5 %all_to_all.11.q_ref = bf16[16,64,128]{2,1,0:T(8,128)(2,1)S(1)} all-to-all(bf16[16,64,128]{2,1,0:T(8,128)(2,1)S(1)} %q_scale_kernel.1), channel_id=1, replica_groups=mesh['pipe'=2,'x'=4,'core'=2,'zhi'=4,'y'=4] {'x','y'}, dimensions={0} | all-to-all | bytes 524288 | tf_op jit(solution)/shard_map/all_to_all | solution.py:269
  109.5 3.7 %collective-permute-start.27 = (bf16[16,64,128]{2,1,0:T(8,128)(2,1)S(1)}, bf16[16,64,128]{2,1,0:T(8,128)(2,1)S(1)}, u32[]{:S(2)}, u32[]{:S(2)}) collective-permute-start(bf16[16,64,128]{2,1,0:T(8,128)(2,1)S(1)} %all_to_all.11.q_ref), channel_id=1, source_target_pairs={{0,16},{16,0},{1,17},{17,1},{2,18},{18,2},{3,19},{19,3},{4,20},{20... | collective-permute-start | bytes 786440 | tf_op jit(solution)/shard_map/ppermute | solution.py:261
  113.2 2.3 %error_own_kernel.1 = (bf16[512,4096]{1,0:T(8,128)(2,1)}, f32[64,512]{1,0:T(8,128)}) custom-call(bf16[128,512]{1,0:T(8,128)(2,1)S(1)} %get-tuple-element.63.ph2_ref, bf16[16,64,128]{2,1,0:T(8,128)(2,1)S(1)} %all_to_all.11.q_ref, f32[8,512,512]{2,1,0:T(8,128)S(1)} %matrix_kernel.1.m_ref), custom_call_target="tpu_custom_call" | custom-call | tf_op jit(solution)/shard_map/error_own_kernel/pallas_call | solution.py:445
  115.6 1.7 %error_sib_kernel.1 = bf16[512,4096]{1,0:T(8,128)(2,1)} custom-call(bf16[128,512]{1,0:T(8,128)(2,1)S(1)} %get-tuple-element.63.ph2_ref, bf16[16,64,128]{2,1,0:T(8,128)(2,1)S(1)} %collective-permute-done.27.q_ref, f32[8,512,512]{2,1,0:T(8,128)S(1)} %matrix_kernel.1.m_ref, bf16[512,4096]{1,0:T(8,128)(2,1)} %get-tuple-element.71._), custom_call_target="tpu_custom_call", output_to_operand_aliasing={{}: (3, {})} | custom-call | tf_op jit(solution)/shard_map/error_sib_kernel/pallas_call | solution.py:455
  (47 shorter events, 13.1 us)
Async XLA Ops:
  2.1 14.2 %collective-permute-start = (bf16[512,512]{1,0:T(8,128)(2,1)S(1)}, bf16[512,512]{1,0:T(8,128)(2,1)S(1)}, u32[]{:S(2)}, u32[]{:S(2)}) collective-permute-start(bf16[512,512]{1,0:T(8,128)(2,1)S(1)} %get-tuple-element.40), channel_id=1, source_target_pairs={{128,0},{129,1},{130,2},{131,3},{132,4},{133,5},{134,6},{135,7},{1... | collective-permute-start | bytes 1572872 | tf_op jit(solution)/shard_map/ppermute | solution.py:290
  3.4 6.0 %collective-permute-start.1 = (f32[64,512]{1,0:T(8,128)}, f32[64,512]{1,0:T(8,128)S(1)}, u32[]{:S(2)}, u32[]{:S(2)}) collective-permute-start(f32[64,512]{1,0:T(8,128)} %bitcast.24), channel_id=1, source_target_pairs={{0,32},{32,64},{64,96},{96,0},{1,33},{33,65},{65,97},{97,1},{2,34}... | collective-permute-start | bytes 393224 | tf_op jit(solution)/shard_map/ppermute | solution.py:257
  5.5 8.4 %collective-permute-start.2 = (f32[64,512]{1,0:T(8,128)}, f32[64,512]{1,0:T(8,128)S(1)}, u32[]{:S(2)}, u32[]{:S(2)}) collective-permute-start(f32[64,512]{1,0:T(8,128)} %bitcast.25), channel_id=1, source_target_pairs={{0,64},{32,96},{64,0},{96,32},{1,65},{33,97},{65,1},{97,33},{2,66}... | collective-permute-start | bytes 393224 | tf_op jit(solution)/shard_map/ppermute | solution.py:257
  7.9 5.9 %collective-permute-start.3 = (f32[64,512]{1,0:T(8,128)}, f32[64,512]{1,0:T(8,128)S(1)}, u32[]{:S(2)}, u32[]{:S(2)}) collective-permute-start(f32[64,512]{1,0:T(8,128)} %bitcast.26), channel_id=1, source_target_pairs={{0,96},{32,0},{64,32},{96,64},{1,97},{33,1},{65,33},{97,65},{2,98}... | collective-permute-start | bytes 393224 | tf_op jit(solution)/shard_map/ppermute | solution.py:257
  16.7 3.5 %collective-permute-start.4 = (f32[64,512]{1,0:T(8,128)S(1)}, f32[64,512]{1,0:T(8,128)S(1)}, u32[]{:S(2)}, u32[]{:S(2)}) collective-permute-start(f32[64,512]{1,0:T(8,128)S(1)} %get-tuple-element.45), channel_id=1, source_target_pairs={{0,16},{16,0},{1,17},{17,1},{2,18},{18,2},{3,19},{19,3},{4,20},{20... | collective-permute-start | bytes 393224 | tf_op jit(solution)/shard_map/ppermute | solution.py:261
  20.1 5.7 %collective-permute-start.8 = (bf16[4,512,512]{2,1,0:T(8,128)(2,1)S(1)}, bf16[4,512,512]{2,1,0:T(8,128)(2,1)S(1)}, u32[]{:S(2)}, u32[]{:S(2)}) collective-permute-start(bf16[4,512,512]{2,1,0:T(8,128)(2,1)S(1)} %get-tuple-element.53.eb_ref), channel_id=1, source_target_pairs={{0,16},{16,0},{1,17},{17,1},{2,18},{18,2},{3,19},{19,3},{4,20},{20... | collective-permute-start | bytes 6291464 | tf_op jit(solution)/shard_map/ppermute | solution.py:261
  20.6 7.9 %collective-permute-start.5 = (f32[64,512]{1,0:T(8,128)S(1)}, f32[64,512]{1,0:T(8,128)S(1)}, u32[]{:S(2)}, u32[]{:S(2)}) collective-permute-start(f32[64,512]{1,0:T(8,128)S(1)} %add.3.u0), channel_id=1, source_target_pairs={{0,32},{32,64},{64,96},{96,0},{1,33},{33,65},{65,97},{97,1},{2,34}... | collective-permute-start | bytes 393224 | tf_op jit(solution)/shard_map/ppermute | solution.py:257
  22.2 8.7 %collective-permute-start.6 = (f32[64,512]{1,0:T(8,128)S(1)}, f32[64,512]{1,0:T(8,128)S(1)}, u32[]{:S(2)}, u32[]{:S(2)}) collective-permute-start(f32[64,512]{1,0:T(8,128)S(1)} %add.3.u0), channel_id=1, source_target_pairs={{0,64},{32,96},{64,0},{96,32},{1,65},{33,97},{65,1},{97,33},{2,66}... | collective-permute-start | bytes 393224 | tf_op jit(solution)/shard_map/ppermute | solution.py:257
  24.7 6.3 %collective-permute-start.7 = (f32[64,512]{1,0:T(8,128)S(1)}, f32[64,512]{1,0:T(8,128)S(1)}, u32[]{:S(2)}, u32[]{:S(2)}) collective-permute-start(f32[64,512]{1,0:T(8,128)S(1)} %add.3.u0), channel_id=1, source_target_pairs={{0,96},{32,0},{64,32},{96,64},{1,97},{33,1},{65,33},{97,65},{2,98}... | collective-permute-start | bytes 393224 | tf_op jit(solution)/shard_map/ppermute | solution.py:257
  27.4 3.6 %collective-permute-start.9 = (f32[64,512]{1,0:T(8,128)S(1)}, f32[64,512]{1,0:T(8,128)S(1)}, u32[]{:S(2)}, u32[]{:S(2)}) collective-permute-start(f32[64,512]{1,0:T(8,128)S(1)} %get-tuple-element.55), channel_id=1, source_target_pairs={{0,16},{16,0},{1,17},{17,1},{2,18},{18,2},{3,19},{19,3},{4,20},{20... | collective-permute-start | bytes 393224 | tf_op jit(solution)/shard_map/ppermute | solution.py:261
  31.0 21.5 %collective-permute-start.19 = (bf16[512,512]{1,0:T(8,128)(2,1)S(1)}, bf16[512,512]{1,0:T(8,128)(2,1)S(1)}, u32[]{:S(2)}, u32[]{:S(2)}) collective-permute-start(bf16[512,512]{1,0:T(8,128)(2,1)S(1)} %get-tuple-element.58.g_ref.g0), channel_id=1, source_target_pairs={{0,32},{32,64},{64,96},{96,0},{1,33},{33,65},{65,97},{97,1},{2,34}... | collective-permute-start | bytes 1572872 | tf_op jit(solution)/shard_map/ppermute | solution.py:257
  31.5 21.0 %collective-permute-start.20 = (bf16[512,512]{1,0:T(8,128)(2,1)S(1)}, bf16[512,512]{1,0:T(8,128)(2,1)S(1)}, u32[]{:S(2)}, u32[]{:S(2)}) collective-permute-start(bf16[512,512]{1,0:T(8,128)(2,1)S(1)} %get-tuple-element.58.g_ref.g0), channel_id=1, source_target_pairs={{0,96},{32,0},{64,32},{96,64},{1,97},{33,1},{65,33},{97,65},{2,98}... | collective-permute-start | bytes 1572872 | tf_op jit(solution)/shard_map/ppermute | solution.py:257
  33.9 5.5 %collective-permute-start.10 = (f32[64,512]{1,0:T(8,128)S(1)}, f32[64,512]{1,0:T(8,128)S(1)}, u32[]{:S(2)}, u32[]{:S(2)}) collective-permute-start(f32[64,512]{1,0:T(8,128)S(1)} %p_kernel.1.a), channel_id=1, source_target_pairs={{0,1},{1,2},{2,3},{3,0},{4,5},{5,6},{6,7},{7,4},{8,9},{9,10},{10,1... | collective-permute-start | bytes 393224 | tf_op jit(solution)/shard_map/ppermute | solution.py:257
  35.3 7.1 %collective-permute-start.11 = (f32[64,512]{1,0:T(8,128)S(1)}, f32[64,512]{1,0:T(8,128)S(1)}, u32[]{:S(2)}, u32[]{:S(2)}) collective-permute-start(f32[64,512]{1,0:T(8,128)S(1)} %p_kernel.1.a), channel_id=1, source_target_pairs={{0,2},{1,3},{2,0},{3,1},{4,6},{5,7},{6,4},{7,5},{8,10},{9,11},{10,... | collective-permute-start | bytes 393224 | tf_op jit(solution)/shard_map/ppermute | solution.py:257
  37.9 5.4 %collective-permute-start.12 = (f32[64,512]{1,0:T(8,128)S(1)}, f32[64,512]{1,0:T(8,128)S(1)}, u32[]{:S(2)}, u32[]{:S(2)}) collective-permute-start(f32[64,512]{1,0:T(8,128)S(1)} %p_kernel.1.a), channel_id=1, source_target_pairs={{0,3},{1,0},{2,1},{3,2},{4,7},{5,4},{6,5},{7,6},{8,11},{9,8},{10,9... | collective-permute-start | bytes 393224 | tf_op jit(solution)/shard_map/ppermute | solution.py:257
  43.4 9.2 %collective-permute-start.15 = (f32[64,512]{1,0:T(8,128)S(1)}, f32[64,512]{1,0:T(8,128)S(1)}, u32[]{:S(2)}, u32[]{:S(2)}) collective-permute-start(f32[64,512]{1,0:T(8,128)S(1)} %sum_kernel.1.z0), channel_id=1, source_target_pairs={{0,12},{4,0},{8,4},{12,8},{1,13},{5,1},{9,5},{13,9},{2,14},{6,2},{... | collective-permute-start | bytes 393224 | tf_op jit(solution)/shard_map/ppermute | solution.py:257
  49.5 6.7 %collective-permute-start.13 = (f32[64,512]{1,0:T(8,128)S(1)}, f32[64,512]{1,0:T(8,128)S(1)}, u32[]{:S(2)}, u32[]{:S(2)}) collective-permute-start(f32[64,512]{1,0:T(8,128)S(1)} %sum_kernel.1.z0), channel_id=1, source_target_pairs={{0,4},{4,8},{8,12},{12,0},{1,5},{5,9},{9,13},{13,1},{2,6},{6,10},{... | collective-permute-start | bytes 393224 | tf_op jit(solution)/shard_map/ppermute | solution.py:257
  52.5 16.8 %collective-permute-start.21 = (bf16[256,512]{1,0:T(8,128)(2,1)S(1)}, bf16[256,512]{1,0:T(8,128)(2,1)S(1)}, u32[]{:S(2)}, u32[]{:S(2)}) collective-permute-start(bf16[256,512]{1,0:T(8,128)(2,1)S(1)} %slice.14), channel_id=1, source_target_pairs={{0,32},{32,64},{64,96},{96,0},{1,33},{33,65},{65,97},{97,1},{2,34}... | collective-permute-start | bytes 786440 | tf_op jit(solution)/shard_map/ppermute | solution.py:257
  52.7 16.7 %collective-permute-start.22 = (bf16[256,512]{1,0:T(8,128)(2,1)S(1)}, bf16[256,512]{1,0:T(8,128)(2,1)S(1)}, u32[]{:S(2)}, u32[]{:S(2)}) collective-permute-start(bf16[256,512]{1,0:T(8,128)(2,1)S(1)} %slice.15), channel_id=1, source_target_pairs={{0,96},{32,0},{64,32},{96,64},{1,97},{33,1},{65,33},{97,65},{2,98}... | collective-permute-start | bytes 786440 | tf_op jit(solution)/shard_map/ppermute | solution.py:257
  56.2 5.2 %collective-permute-start.14 = (f32[64,256]{1,0:T(8,128)S(1)}, f32[64,256]{1,0:T(8,128)S(1)}, u32[]{:S(2)}, u32[]{:S(2)}) collective-permute-start(f32[64,256]{1,0:T(8,128)S(1)} %slice.16), channel_id=1, source_target_pairs={{0,4},{4,8},{8,12},{12,0},{1,5},{5,9},{9,13},{13,1},{2,6},{6,10},{... | collective-permute-start | bytes 196616 | tf_op jit(solution)/shard_map/ppermute | solution.py:257
  59.7 4.2 %collective-permute-start.16 = (f32[64,256]{1,0:T(8,128)S(1)}, f32[64,256]{1,0:T(8,128)S(1)}, u32[]{:S(2)}, u32[]{:S(2)}) collective-permute-start(f32[64,256]{1,0:T(8,128)S(1)} %slice.17), channel_id=1, source_target_pairs={{0,12},{4,0},{8,4},{12,8},{1,13},{5,1},{9,5},{13,9},{2,14},{6,2},{... | collective-permute-start | bytes 196616 | tf_op jit(solution)/shard_map/ppermute | solution.py:257
  64.2 4.9 %collective-permute-start.17 = (f32[64,512]{1,0:T(8,128)S(1)}, f32[64,512]{1,0:T(8,128)S(1)}, u32[]{:S(2)}, u32[]{:S(2)}) collective-permute-start(f32[64,512]{1,0:T(8,128)S(1)} %get-tuple-element.56.p_ref), channel_id=1, source_target_pairs={{0,16},{16,0},{1,17},{17,1},{2,18},{18,2},{3,19},{19,3},{4,20},{20... | collective-permute-start | bytes 393224 | tf_op jit(solution)/shard_map/ppermute | solution.py:261
  68.0 1.3 %collective-permute-start.18 = (f32[64,512]{1,0:T(8,128)S(1)}, f32[64,512]{1,0:T(8,128)S(1)}, u32[]{:S(2)}, u32[]{:S(2)}) collective-permute-start(f32[64,512]{1,0:T(8,128)S(1)} %get-tuple-element.57.v_ref), channel_id=1, source_target_pairs={{0,16},{16,0},{1,17},{17,1},{2,18},{18,2},{3,19},{19,3},{4,20},{20... | collective-permute-start | bytes 393224 | tf_op jit(solution)/shard_map/ppermute | solution.py:261
  70.7 25.8 %collective-permute-start.26 = (bf16[4,512,512]{2,1,0:T(8,128)(2,1)S(1)}, bf16[4,512,512]{2,1,0:T(8,128)(2,1)S(1)}, u32[]{:S(2)}, u32[]{:S(2)}) collective-permute-start(bf16[4,512,512]{2,1,0:T(8,128)(2,1)S(1)} %get-tuple-element.67.ga_ref), channel_id=1, source_target_pairs={{0,16},{16,0},{1,17},{17,1},{2,18},{18,2},{3,19},{19,3},{4,20},{20... | collective-permute-start | bytes 6291464 | tf_op jit(solution)/shard_map/ppermute | solution.py:261
  85.7 13.1 %collective-permute-start.23 = (f32[64,128]{1,0:T(8,128)S(1)}, f32[64,128]{1,0:T(8,128)S(1)}, u32[]{:S(2)}, u32[]{:S(2)}) collective-permute-start(f32[64,128]{1,0:T(8,128)S(1)} %get-tuple-element.64.q0), channel_id=1, source_target_pairs={{0,4},{4,8},{8,12},{12,0},{1,5},{5,9},{9,13},{13,1},{2,6},{6,10},{... | collective-permute-start | bytes 98312 | tf_op jit(solution)/shard_map/ppermute | solution.py:257
  89.2 9.7 %collective-permute-start.24 = (f32[64,128]{1,0:T(8,128)S(1)}, f32[64,128]{1,0:T(8,128)S(1)}, u32[]{:S(2)}, u32[]{:S(2)}) collective-permute-start(f32[64,128]{1,0:T(8,128)S(1)} %get-tuple-element.64.q0), channel_id=1, source_target_pairs={{0,8},{4,12},{8,0},{12,4},{1,9},{5,13},{9,1},{13,5},{2,10},{6,14},... | collective-permute-start | bytes 98312 | tf_op jit(solution)/shard_map/ppermute | solution.py:257
  91.5 7.4 %collective-permute-start.25 = (f32[64,128]{1,0:T(8,128)S(1)}, f32[64,128]{1,0:T(8,128)S(1)}, u32[]{:S(2)}, u32[]{:S(2)}) collective-permute-start(f32[64,128]{1,0:T(8,128)S(1)} %get-tuple-element.64.q0), channel_id=1, source_target_pairs={{0,12},{4,0},{8,4},{12,8},{1,13},{5,1},{9,5},{13,9},{2,14},{6,2},{... | collective-permute-start | bytes 98312 | tf_op jit(solution)/shard_map/ppermute | solution.py:257
  109.5 6.0 %collective-permute-start.27 = (bf16[16,64,128]{2,1,0:T(8,128)(2,1)S(1)}, bf16[16,64,128]{2,1,0:T(8,128)(2,1)S(1)}, u32[]{:S(2)}, u32[]{:S(2)}) collective-permute-start(bf16[16,64,128]{2,1,0:T(8,128)(2,1)S(1)} %all_to_all.11.q_ref), channel_id=1, source_target_pairs={{0,16},{16,0},{1,17},{17,1},{2,18},{18,2},{3,19},{19,3},{4,20},{20... | collective-permute-start | bytes 786440 | tf_op jit(solution)/shard_map/ppermute | solution.py:261

commit v7 on v6

--- a/solution.py
+++ b/solution.py
@@ -95,8 +95,15 @@
     return (a[...] + c[...]) + (b[...] + d[...])
 
 
-def sum_kernel(a, b, c, d, out_ref):
-    out_ref[...] = sum_of((a, b, c, d))
+def sum_kernel(a, b, c, d, lo_ref, hi_ref):
+    s = sum_of((a, b, c, d))
+    lo_ref[...] = s[:, 0:256]
+    hi_ref[...] = s[:, 256:512]
+
+
+def add_kernel(a, b, c, d, ab_ref, cd_ref):
+    ab_ref[...] = a[...] + b[...]
+    cd_ref[...] = c[...] + d[...]
 
 
 def put_chunks(out_ref, slot, r, gram):
@@ -124,9 +131,8 @@
     run_copies(pairs + [(act, act_v)], sems)
 
 
-def pv_kernel(z0, z1, z2a, z2b, z3, act_ref, p_ref, v_ref):
-    z2 = jnp.concatenate([z2a[...], z2b[...]], axis=1)
-    p = ((z0[...] + z2) + (z1[...] + z3[...])) * (1.0 / 16.0)
+def pv_kernel(lo, lo_far, hi, hi_far, act_ref, p_ref, v_ref):
+    p = jnp.concatenate([lo[...] + lo_far[...], hi[...] + hi_far[...]], axis=1) * (1.0 / 16.0)
     p_ref[...] = p
     v_ref[...] = fold3(dot(split3(p), act_ref[...], 1, 1))
 
@@ -207,8 +213,8 @@
     ph2_ref[64:128] = (phat - hi.astype(F32)).astype(BF)
 
 
-def q_scale_kernel(q0, q1, q2, q3, linv_ref, out_ref):
-    s = sum_of((q0, q1, q2, q3)) * (1.0 / 16.0)
+def q_scale_kernel(near, far, linv_ref, out_ref):
+    s = (near[...] + far[...]) * (1.0 / 16.0)
     q = jnp.dot(linv_ref[...], s, precision=HIGH, preferred_element_type=F32).astype(BF)
     for k in range(16):
         out_ref[k] = q
@@ -255,6 +261,10 @@
 def shift(v, axis, k):
     n = lax.axis_size(axis)
     return lax.ppermute(v, axis, [(i, (i + k) % n) for i in range(n)])
+
+
+def trade(v, axis, flip):
+    return lax.ppermute(v, axis, [(i, i ^ 1 if flip else 3 - i) for i in range(4)])
 
 
 def swap(v):
@@ -349,32 +359,41 @@
     grad, *_ = lax.optimization_barrier((grad, eqs, *us))
     g1 = shift(grad, "x", 1)
     g3 = shift(grad, "x", 3)
-    part = pl.pallas_call(
+    lo, hi = pl.pallas_call(
         sum_kernel,
-        out_shape=sds((64, 512), F32),
+        out_shape=(sds((64, 256), F32), sds((64, 256), F32)),
         in_specs=[VMEM] * 4,
-        out_specs=VMEM,
+        out_specs=(VMEM, VMEM),
         cost_estimate=LIGHT,
         compiler_params=params(4),
         name="sum_kernel",
     )(*ys)
 
-    z1 = shift(part, "zhi", 1)
-    z3 = shift(part, "zhi", 3)
-    h1, h3, *_ = lax.optimization_barrier((g1, g3, z3))
+    lo_in = trade(lo, "zhi", True)
+    hi_in = trade(hi, "zhi", False)
+    h1, h3, _ = lax.optimization_barrier((g1, g3, lo_in))
     g2a = shift(h1[:256], "x", 1)
     g2b = shift(h3[256:], "x", 3)
-    z2a = shift(z1[:, :256], "zhi", 1)
-    z2b = shift(z3[:, 256:], "zhi", 3)
+    lo, hi = pl.pallas_call(
+        add_kernel,
+        out_shape=(sds((64, 256), F32), sds((64, 256), F32)),
+        in_specs=[VMEM] * 4,
+        out_specs=(VMEM, VMEM),
+        cost_estimate=LIGHT,
+        compiler_params=params(4),
+        name="add_kernel",
+    )(lo, lo_in, hi, hi_in)
+    lo_in = trade(lo, "zhi", False)
+    hi_in = trade(hi, "zhi", True)
     p, v = pl.pallas_call(
         pv_kernel,
         out_shape=(sds((64, 512), F32), sds((64, 512), F32)),
-        in_specs=[VMEM] * 6,
+        in_specs=[VMEM] * 5,
         out_specs=(VMEM, VMEM),
         cost_estimate=LIGHT,
         compiler_params=params(4),
         name="pv_kernel",
-    )(part, z1, z2a, z2b, z3, act)
+    )(lo, lo_in, hi, hi_in, act)
     ps = swap(p)
     vs = swap(v)
     q_own_part = pl.pallas_call(
@@ -408,7 +427,7 @@
         compiler_params=params(4),
         name="chunk_sum_kernel",
     )(chunks)
-    qs = ring(q_part, "zhi")
+    q_in = trade(q_part, "zhi", True)
     phat, ph2, linv = pl.pallas_call(
         factor_kernel,
         out_shape=(sds((64, 512), F32), sds((128, 512), BF), sds((64, 64), F32)),
@@ -418,7 +437,10 @@
         compiler_params=params(4),
         name="factor_kernel",
     )(gram, p)
-    act_t, gram = lax.optimization_barrier((act_t, gram))
+    q_in, linv = lax.optimization_barrier((q_in, linv))
+    q_part = q_part + q_in
+    q_in = trade(q_part, "zhi", False)
+    act_t, _ = lax.optimization_barrier((act_t, q_part))
     matrix = pl.pallas_call(
         matrix_kernel,
         out_shape=sds((8, 512, 512), F32),
@@ -428,16 +450,16 @@
         compiler_params=params(20),
         name="matrix_kernel",
     )(act_t, gs, gb, err, eh)
-    matrix, linv = lax.optimization_barrier((matrix, linv))
+    q_in, matrix = lax.optimization_barrier((q_in, matrix))
     q16 = pl.pallas_call(
         q_scale_kernel,
         out_shape=sds((16, 64, 128), BF),
-        in_specs=[VMEM] * 5,
+        in_specs=[VMEM] * 3,
         out_specs=VMEM,
         cost_estimate=LIGHT,
         compiler_params=params(4),
         name="q_scale_kernel",
-    )(*qs, linv)
+    )(q_part, q_in, linv)
     qfa = exchange(q16, ("x", "y"))
     qfb = swap(qfa)
 

time: 118 us -> 114 us (0.966)
  waiting for transfers between devices: 20.3 us -> 16.8 us
    ppermute x20 -> x13, starting transfers between devices: 39.2 us -> 21.5 us  [shift(): return lax.ppermute(v, axis, [(i, (i + k) % n) for i in range(n)])]
    ppermute x0 -> x6, starting transfers between devices: none -> 13.6 us  [trade(): lax.ppermute(v, axis, [(i, i ^ 1 if flip else 3 - i) for i in range(4)])]
    ppermute x20 -> x13, waiting for transfers between devices: 19.5 us -> 11.6 us  [shift(): return lax.ppermute(v, axis, [(i, (i + k) % n) for i in range(n)])]
    ppermute x0 -> x6, waiting for transfers between devices: none -> 4.46 us  [trade(): lax.ppermute(v, axis, [(i, i ^ 1 if flip else 3 - i) for i in range(4)])]
    ppermute x7, starting transfers between devices: 12 us -> 15.8 us  [swap(): return lax.ppermute(v, 'core', [(0, 1), (1, 0)])]
  transfers between devices with their start and end apart: 28 -> 27, of which waited for: 13 -> 13; matrix products, arithmetic and copies ran while one was open for 0% -> 0% of each run, Pallas kernels for 11% -> 12%
where the time goes in v7:
time: 114 us
  starting transfers between devices  52.2 us (46%)
  blocking collectives  25.4 us (22%)
  Pallas kernels  18.4 us (16%)
  waiting for transfers between devices  16.8 us (15%)
    all_to_all x2, blocking collectives, exchange(): return lax.all_to_all(v, axes, 0, 0, tiled=True)  25.4 us
    ppermute x13, starting transfers between devices, shift(): return lax.ppermute(v, axis, [(i, (i + k) % n) for i in range(n)])  21.5 us
    ppermute x7, starting transfers between devices, swap(): return lax.ppermute(v, 'core', [(0, 1), (1, 0)])  15.8 us
    ppermute x6, starting transfers between devices, trade(): lax.ppermute(v, axis, [(i, i ^ 1 if flip else 3 - i) for i in range(4)])  13.6 us
    ppermute x13, waiting for transfers between devices, shift(): return lax.ppermute(v, axis, [(i, (i + k) % n) for i in range(n)])  11.6 us
    ppermute x6, waiting for transfers between devices, trade(): lax.ppermute(v, axis, [(i, i ^ 1 if flip else 3 - i) for i in range(4)])  4.46 us
    pallas_call x1, Pallas kernels, on_device(): pl.pallas_call(factor_kernel, out_shape=(sds((64, 512), F32), sds((128, 5...  2.76 us
    pallas_call x1, Pallas kernels, on_device(): pl.pallas_call(load_error_kernel, out_shape=(sds((4, 512, 512), BF), sds(...  2.42 us
  transfers between devices with their start and end apart: 27, of which 13 were waited for; matrix products, arithmetic and copies ran while one was open for 0% of the time, Pallas kernels for 12%

profile of v7, /device:TPU:1, one launch (start us, length us, event | category | flops | bytes accessed | tf_op | source)
XLA Modules:
  0.0 113.9 jit_solution(1460278699408509991)
XLA Ops:
  0.6 1.4 %load_kernel.1 = (f32[64,512]{1,0:T(8,128)S(1)}, bf16[512,512]{1,0:T(8,128)(2,1)S(1)}, bf16[512,512]{1,0:T(8,128)(2,1)S(1)}, bf16[512,512]{1,0:T(8,128)(2,1)S(1)}) custom-call(f32[64,512]{1,0:T(8,128)} %bitcast.23, bf16[512,512]{1,0:T(8,128)(2,1)} %bitcast.21, bf16[512,512]{1,0:T(8,128)(2,1)} %bitcast.22), custom_call_target="tpu_custom_call" | custom-call | tf_op jit(solution)/shard_map/load_kernel/pallas_call | solution.py:289
  2.1 1.3 %collective-permute-start = (bf16[512,512]{1,0:T(8,128)(2,1)S(1)}, bf16[512,512]{1,0:T(8,128)(2,1)S(1)}, u32[]{:S(2)}, u32[]{:S(2)}) collective-permute-start(bf16[512,512]{1,0:T(8,128)(2,1)S(1)} %get-tuple-element.46), channel_id=1, source_target_pairs={{128,0},{129,1},{130,2},{131,3},{132,4},{133,5},{134,6},{135,7},{1... | collective-permute-start | bytes 1572872 | tf_op jit(solution)/shard_map/ppermute | solution.py:300
  3.4 2.1 %collective-permute-start.1 = (f32[64,512]{1,0:T(8,128)}, f32[64,512]{1,0:T(8,128)S(1)}, u32[]{:S(2)}, u32[]{:S(2)}) collective-permute-start(f32[64,512]{1,0:T(8,128)} %bitcast.24), channel_id=1, source_target_pairs={{0,32},{32,64},{64,96},{96,0},{1,33},{33,65},{65,97},{97,1},{2,34}... | collective-permute-start | bytes 393224 | tf_op jit(solution)/shard_map/ppermute | solution.py:263
  5.5 2.5 %collective-permute-start.2 = (f32[64,512]{1,0:T(8,128)}, f32[64,512]{1,0:T(8,128)S(1)}, u32[]{:S(2)}, u32[]{:S(2)}) collective-permute-start(f32[64,512]{1,0:T(8,128)} %bitcast.25), channel_id=1, source_target_pairs={{0,64},{32,96},{64,0},{96,32},{1,65},{33,97},{65,1},{97,33},{2,66}... | collective-permute-start | bytes 393224 | tf_op jit(solution)/shard_map/ppermute | solution.py:263
  9.3 4.5 %collective-permute-done.2.q2 = f32[64,512]{1,0:T(8,128)S(1)} collective-permute-done((f32[64,512]{1,0:T(8,128)}, f32[64,512]{1,0:T(8,128)S(1)}, u32[]{:S(2)}, u32[]{:S(2)}) %collective-permute-start.2) | collective-permute-done | bytes 131104 | tf_op jit(solution)/shard_map/ppermute | solution.py:263
  13.9 2.4 %load_error_kernel.1 = (bf16[4,512,512]{2,1,0:T(8,128)(2,1)S(1)}, bf16[4,512,512]{2,1,0:T(8,128)(2,1)S(1)}, bf16[512,512]{1,0:T(8,128)(2,1)S(1)}) custom-call(bf16[512,4096]{1,0:T(8,128)(2,1)} %bitcast.17, bf16[512,512]{1,0:T(8,128)(2,1)} %bitcast.19), custom_call_target="tpu_custom_call" | custom-call | tf_op jit(solution)/shard_map/load_error_kernel/pallas_call | solution.py:303
  16.7 2.5 %collective-permute-start.4 = (f32[64,512]{1,0:T(8,128)S(1)}, f32[64,512]{1,0:T(8,128)S(1)}, u32[]{:S(2)}, u32[]{:S(2)}) collective-permute-start(f32[64,512]{1,0:T(8,128)S(1)} %get-tuple-element.51), channel_id=1, source_target_pairs={{0,16},{16,0},{1,17},{17,1},{2,18},{18,2},{3,19},{19,3},{4,20},{20... | collective-permute-start | bytes 393224 | tf_op jit(solution)/shard_map/ppermute | solution.py:271
  20.6 1.7 %collective-permute-start.5 = (f32[64,512]{1,0:T(8,128)S(1)}, f32[64,512]{1,0:T(8,128)S(1)}, u32[]{:S(2)}, u32[]{:S(2)}) collective-permute-start(f32[64,512]{1,0:T(8,128)S(1)} %add.6.u0), channel_id=1, source_target_pairs={{0,32},{32,64},{64,96},{96,0},{1,33},{33,65},{65,97},{97,1},{2,34}... | collective-permute-start | bytes 393224 | tf_op jit(solution)/shard_map/ppermute | solution.py:263
  22.2 2.4 %collective-permute-start.6 = (f32[64,512]{1,0:T(8,128)S(1)}, f32[64,512]{1,0:T(8,128)S(1)}, u32[]{:S(2)}, u32[]{:S(2)}) collective-permute-start(f32[64,512]{1,0:T(8,128)S(1)} %add.6.u0), channel_id=1, source_target_pairs={{0,64},{32,96},{64,0},{96,32},{1,65},{33,97},{65,1},{97,33},{2,66}... | collective-permute-start | bytes 393224 | tf_op jit(solution)/shard_map/ppermute | solution.py:263
  24.7 1.2 %collective-permute-start.7 = (f32[64,512]{1,0:T(8,128)S(1)}, f32[64,512]{1,0:T(8,128)S(1)}, u32[]{:S(2)}, u32[]{:S(2)}) collective-permute-start(f32[64,512]{1,0:T(8,128)S(1)} %add.6.u0), channel_id=1, source_target_pairs={{0,96},{32,0},{64,32},{96,64},{1,97},{33,1},{65,33},{97,65},{2,98}... | collective-permute-start | bytes 393224 | tf_op jit(solution)/shard_map/ppermute | solution.py:263
  25.9 1.5 %eq_kernel.1 = (f32[64,512]{1,0:T(8,128)S(1)}, f32[64,512]{1,0:T(8,128)S(1)}, bf16[512,512]{1,0:T(8,128)(2,1)S(1)}) custom-call(f32[64,512]{1,0:T(8,128)S(1)} %get-tuple-element.50.q_ref.q0, f32[64,512]{1,0:T(8,128)S(1)} %collective-permute-done.1.q1, f32[64,512]{1,0:T(8,128)S(1)} %collective-permute-done.2.q2, f32[64,512]{1,0:T(8,128)S(1)} %collective-permute-done.3.q3, ...), custom_call_target="tpu_custom_call" | custom-call | tf_op jit(solution)/shard_map/eq_kernel/pallas_call | solution.py:338
  28.5 2.5 %collective-permute-done.6.u2 = f32[64,512]{1,0:T(8,128)S(1)} collective-permute-done((f32[64,512]{1,0:T(8,128)S(1)}, f32[64,512]{1,0:T(8,128)S(1)}, u32[]{:S(2)}, u32[]{:S(2)}) %collective-permute-start.6) | collective-permute-done | bytes 131104 | tf_op jit(solution)/shard_map/ppermute | solution.py:263
  31.5 2.2 %collective-permute-start.20 = (bf16[512,512]{1,0:T(8,128)(2,1)S(1)}, bf16[512,512]{1,0:T(8,128)(2,1)S(1)}, u32[]{:S(2)}, u32[]{:S(2)}) collective-permute-start(bf16[512,512]{1,0:T(8,128)(2,1)S(1)} %get-tuple-element.68.g_ref.g0), channel_id=1, source_target_pairs={{0,96},{32,0},{64,32},{96,64},{1,97},{33,1},{65,33},{97,65},{2,98}... | collective-permute-start | bytes 1572872 | tf_op jit(solution)/shard_map/ppermute | solution.py:263
  33.9 1.4 %collective-permute-start.10 = (f32[64,512]{1,0:T(8,128)S(1)}, f32[64,512]{1,0:T(8,128)S(1)}, u32[]{:S(2)}, u32[]{:S(2)}) collective-permute-start(f32[64,512]{1,0:T(8,128)S(1)} %p_kernel.1.a), channel_id=1, source_target_pairs={{0,1},{1,2},{2,3},{3,0},{4,5},{5,6},{6,7},{7,4},{8,9},{9,10},{10,1... | collective-permute-start | bytes 393224 | tf_op jit(solution)/shard_map/ppermute | solution.py:263
  35.3 2.6 %collective-permute-start.11 = (f32[64,512]{1,0:T(8,128)S(1)}, f32[64,512]{1,0:T(8,128)S(1)}, u32[]{:S(2)}, u32[]{:S(2)}) collective-permute-start(f32[64,512]{1,0:T(8,128)S(1)} %p_kernel.1.a), channel_id=1, source_target_pairs={{0,2},{1,3},{2,0},{3,1},{4,6},{5,7},{6,4},{7,5},{8,10},{9,11},{10,... | collective-permute-start | bytes 393224 | tf_op jit(solution)/shard_map/ppermute | solution.py:263
  39.4 3.0 %collective-permute-done.11.c = f32[64,512]{1,0:T(8,128)S(1)} collective-permute-done((f32[64,512]{1,0:T(8,128)S(1)}, f32[64,512]{1,0:T(8,128)S(1)}, u32[]{:S(2)}, u32[]{:S(2)}) %collective-permute-start.11) | collective-permute-done | bytes 131104 | tf_op jit(solution)/shard_map/ppermute | solution.py:263
  43.4 3.1 %collective-permute-start.13 = (f32[64,256]{1,0:T(8,128)S(1)}, f32[64,256]{1,0:T(8,128)S(1)}, u32[]{:S(2)}, u32[]{:S(2)}) collective-permute-start(f32[64,256]{1,0:T(8,128)S(1)} %get-tuple-element.62.a), channel_id=1, source_target_pairs={{0,4},{4,0},{8,12},{12,8},{1,5},{5,1},{9,13},{13,9},{2,6},{6,2},{1... | collective-permute-start | bytes 196616 | tf_op jit(solution)/shard_map/ppermute | solution.py:267
  46.4 4.2 %collective-permute-start.14 = (f32[64,256]{1,0:T(8,128)S(1)}, f32[64,256]{1,0:T(8,128)S(1)}, u32[]{:S(2)}, u32[]{:S(2)}) collective-permute-start(f32[64,256]{1,0:T(8,128)S(1)} %get-tuple-element.63.c), channel_id=1, source_target_pairs={{0,12},{4,8},{8,4},{12,0},{1,13},{5,9},{9,5},{13,1},{2,14},{6,10},... | collective-permute-start | bytes 196616 | tf_op jit(solution)/shard_map/ppermute | solution.py:267
  50.8 2.7 %collective-permute-start.22 = (bf16[256,512]{1,0:T(8,128)(2,1)S(1)}, bf16[256,512]{1,0:T(8,128)(2,1)S(1)}, u32[]{:S(2)}, u32[]{:S(2)}) collective-permute-start(bf16[256,512]{1,0:T(8,128)(2,1)S(1)} %slice.7), channel_id=1, source_target_pairs={{0,96},{32,0},{64,32},{96,64},{1,97},{33,1},{65,33},{97,65},{2,98}... | collective-permute-start | bytes 786440 | tf_op jit(solution)/shard_map/ppermute | solution.py:263
  53.6 3.1 %collective-permute-start.15 = (f32[64,256]{1,0:T(8,128)S(1)}, f32[64,256]{1,0:T(8,128)S(1)}, u32[]{:S(2)}, u32[]{:S(2)}) collective-permute-start(f32[64,256]{1,0:T(8,128)S(1)} %get-tuple-element.64.lo), channel_id=1, source_target_pairs={{0,12},{4,8},{8,4},{12,0},{1,13},{5,9},{9,5},{13,1},{2,14},{6,10},... | collective-permute-start | bytes 196616 | tf_op jit(solution)/shard_map/ppermute | solution.py:267
  56.7 1.7 %collective-permute-start.16 = (f32[64,256]{1,0:T(8,128)S(1)}, f32[64,256]{1,0:T(8,128)S(1)}, u32[]{:S(2)}, u32[]{:S(2)}) collective-permute-start(f32[64,256]{1,0:T(8,128)S(1)} %get-tuple-element.65.hi), channel_id=1, source_target_pairs={{0,4},{4,0},{8,12},{12,8},{1,5},{5,1},{9,13},{13,9},{2,6},{6,2},{1... | collective-permute-start | bytes 196616 | tf_op jit(solution)/shard_map/ppermute | solution.py:267
  59.0 1.7 %collective-permute-done.16.hi_far = f32[64,256]{1,0:T(8,128)S(1)} collective-permute-done((f32[64,256]{1,0:T(8,128)S(1)}, f32[64,256]{1,0:T(8,128)S(1)}, u32[]{:S(2)}, u32[]{:S(2)}) %collective-permute-start.16) | collective-permute-done | bytes 65568 | tf_op jit(solution)/shard_map/ppermute | solution.py:267
  61.0 6.3 %collective-permute-start.17 = (f32[64,512]{1,0:T(8,128)S(1)}, f32[64,512]{1,0:T(8,128)S(1)}, u32[]{:S(2)}, u32[]{:S(2)}) collective-permute-start(f32[64,512]{1,0:T(8,128)S(1)} %get-tuple-element.66.p_ref), channel_id=1, source_target_pairs={{0,16},{16,0},{1,17},{17,1},{2,18},{18,2},{3,19},{19,3},{4,20},{20... | collective-permute-start | bytes 393224 | tf_op jit(solution)/shard_map/ppermute | solution.py:271
  68.7 1.3 %q_kernel.1 = (f32[4,4,72,128]{3,2,1,0:T(8,128)S(1)}, bf16[4,512,512]{2,1,0:T(8,128)(2,1)S(1)}) custom-call(f32[64,512]{1,0:T(8,128)S(1)} %get-tuple-element.66.p_ref, f32[64,512]{1,0:T(8,128)S(1)} %get-tuple-element.67.v_ref, f32[64,512]{1,0:T(8,128)S(1)} %collective-permute-done.17.ps_ref, f32[64,512]{1,0:T(8,128)S(1)} %collective-permute-done.18.vs_ref, ...), custom_call_target="tpu_custom_call" | custom-call | tf_op jit(solution)/shard_map/q_kernel/pallas_call | solution.py:408
  70.3 15.0 %all_to_all.10.in_ref = f32[16,72,128]{2,1,0:T(8,128)S(1)} all-to-all(f32[16,72,128]{2,1,0:T(8,128)S(1)} %bitcast.16), channel_id=1, replica_groups=mesh['pipe'=2,'x'=4,'core'=2,'zhi'=4,'y'=4] {'x','y'}, dimensions={0} | all-to-all | bytes 1179648 | tf_op jit(solution)/shard_map/all_to_all | solution.py:279
  85.8 2.8 %factor_kernel.1 = (f32[64,512]{1,0:T(8,128)}, bf16[128,512]{1,0:T(8,128)(2,1)S(1)}, f32[64,64]{1,0:T(8,128)S(1)}) custom-call(f32[32,128]{1,0:T(8,128)S(1)} %get-tuple-element.72.gram_ref, f32[64,512]{1,0:T(8,128)S(1)} %get-tuple-element.66.p_ref), custom_call_target="tpu_custom_call" | custom-call | tf_op jit(solution)/shard_map/factor_kernel/pallas_call | solution.py:431
  90.0 2.3 %matrix_kernel.1.m_ref = f32[8,512,512]{2,1,0:T(8,128)S(1)} custom-call(bf16[512,512]{1,0:T(8,128)(2,1)S(1)} %get-tuple-element.78.at_ref, bf16[4,512,512]{2,1,0:T(8,128)(2,1)S(1)} %get-tuple-element.79.ga_ref, bf16[4,512,512]{2,1,0:T(8,128)(2,1)S(1)} %collective-permute-done.25.gb_ref, bf16[4,512,512]{2,1,0:T(8,128)(2,1)S(1)} %get-tuple-element.57.e_ref.ea_ref, ...), custom_call_target="tpu_custom_call" | custom-call | tf_op jit(solution)/shard_map/matrix_kernel/pallas_call | solution.py:444
  92.3 1.7 %collective-permute-done.24.far = f32[64,128]{1,0:T(8,128)S(1)} collective-permute-done((f32[64,128]{1,0:T(8,128)S(1)}, f32[64,128]{1,0:T(8,128)S(1)}, u32[]{:S(2)}, u32[]{:S(2)}) %collective-permute-start.24) | collective-permute-done | bytes 32800 | tf_op jit(solution)/shard_map/ppermute | solution.py:267
  94.2 10.5 %all_to_all.11.q_ref = bf16[16,64,128]{2,1,0:T(8,128)(2,1)S(1)} all-to-all(bf16[16,64,128]{2,1,0:T(8,128)(2,1)S(1)} %q_scale_kernel.1), channel_id=1, replica_groups=mesh['pipe'=2,'x'=4,'core'=2,'zhi'=4,'y'=4] {'x','y'}, dimensions={0} | all-to-all | bytes 524288 | tf_op jit(solution)/shard_map/all_to_all | solution.py:279
  104.7 5.1 %collective-permute-start.26 = (bf16[16,64,128]{2,1,0:T(8,128)(2,1)S(1)}, bf16[16,64,128]{2,1,0:T(8,128)(2,1)S(1)}, u32[]{:S(2)}, u32[]{:S(2)}) collective-permute-start(bf16[16,64,128]{2,1,0:T(8,128)(2,1)S(1)} %all_to_all.11.q_ref), channel_id=1, source_target_pairs={{0,16},{16,0},{1,17},{17,1},{2,18},{18,2},{3,19},{19,3},{4,20},{20... | collective-permute-start | bytes 786440 | tf_op jit(solution)/shard_map/ppermute | solution.py:271
  109.7 2.3 %error_own_kernel.1 = (bf16[512,4096]{1,0:T(8,128)(2,1)}, f32[64,512]{1,0:T(8,128)}) custom-call(bf16[128,512]{1,0:T(8,128)(2,1)S(1)} %get-tuple-element.73.ph2_ref, bf16[16,64,128]{2,1,0:T(8,128)(2,1)S(1)} %all_to_all.11.q_ref, f32[8,512,512]{2,1,0:T(8,128)S(1)} %matrix_kernel.1.m_ref), custom_call_target="tpu_custom_call" | custom-call | tf_op jit(solution)/shard_map/error_own_kernel/pallas_call | solution.py:467
  112.1 1.7 %error_sib_kernel.1 = bf16[512,4096]{1,0:T(8,128)(2,1)} custom-call(bf16[128,512]{1,0:T(8,128)(2,1)S(1)} %get-tuple-element.73.ph2_ref, bf16[16,64,128]{2,1,0:T(8,128)(2,1)S(1)} %collective-permute-done.26.q_ref, f32[8,512,512]{2,1,0:T(8,128)S(1)} %matrix_kernel.1.m_ref, bf16[512,4096]{1,0:T(8,128)(2,1)} %get-tuple-element.83._), custom_call_target="tpu_custom_call", output_to_operand_aliasing={{}: (3, {})} | custom-call | tf_op jit(solution)/shard_map/error_sib_kernel/pallas_call | solution.py:477
  (45 shorter events, 12.3 us)
Async XLA Ops:
  2.1 14.2 %collective-permute-start = (bf16[512,512]{1,0:T(8,128)(2,1)S(1)}, bf16[512,512]{1,0:T(8,128)(2,1)S(1)}, u32[]{:S(2)}, u32[]{:S(2)}) collective-permute-start(bf16[512,512]{1,0:T(8,128)(2,1)S(1)} %get-tuple-element.46), channel_id=1, source_target_pairs={{128,0},{129,1},{130,2},{131,3},{132,4},{133,5},{134,6},{135,7},{1... | collective-permute-start | bytes 1572872 | tf_op jit(solution)/shard_map/ppermute | solution.py:300
  3.4 6.0 %collective-permute-start.1 = (f32[64,512]{1,0:T(8,128)}, f32[64,512]{1,0:T(8,128)S(1)}, u32[]{:S(2)}, u32[]{:S(2)}) collective-permute-start(f32[64,512]{1,0:T(8,128)} %bitcast.24), channel_id=1, source_target_pairs={{0,32},{32,64},{64,96},{96,0},{1,33},{33,65},{65,97},{97,1},{2,34}... | collective-permute-start | bytes 393224 | tf_op jit(solution)/shard_map/ppermute | solution.py:263
  5.5 8.4 %collective-permute-start.2 = (f32[64,512]{1,0:T(8,128)}, f32[64,512]{1,0:T(8,128)S(1)}, u32[]{:S(2)}, u32[]{:S(2)}) collective-permute-start(f32[64,512]{1,0:T(8,128)} %bitcast.25), channel_id=1, source_target_pairs={{0,64},{32,96},{64,0},{96,32},{1,65},{33,97},{65,1},{97,33},{2,66}... | collective-permute-start | bytes 393224 | tf_op jit(solution)/shard_map/ppermute | solution.py:263
  7.9 5.9 %collective-permute-start.3 = (f32[64,512]{1,0:T(8,128)}, f32[64,512]{1,0:T(8,128)S(1)}, u32[]{:S(2)}, u32[]{:S(2)}) collective-permute-start(f32[64,512]{1,0:T(8,128)} %bitcast.26), channel_id=1, source_target_pairs={{0,96},{32,0},{64,32},{96,64},{1,97},{33,1},{65,33},{97,65},{2,98}... | collective-permute-start | bytes 393224 | tf_op jit(solution)/shard_map/ppermute | solution.py:263
  16.7 3.5 %collective-permute-start.4 = (f32[64,512]{1,0:T(8,128)S(1)}, f32[64,512]{1,0:T(8,128)S(1)}, u32[]{:S(2)}, u32[]{:S(2)}) collective-permute-start(f32[64,512]{1,0:T(8,128)S(1)} %get-tuple-element.51), channel_id=1, source_target_pairs={{0,16},{16,0},{1,17},{17,1},{2,18},{18,2},{3,19},{19,3},{4,20},{20... | collective-permute-start | bytes 393224 | tf_op jit(solution)/shard_map/ppermute | solution.py:271
  20.1 5.7 %collective-permute-start.8 = (bf16[4,512,512]{2,1,0:T(8,128)(2,1)S(1)}, bf16[4,512,512]{2,1,0:T(8,128)(2,1)S(1)}, u32[]{:S(2)}, u32[]{:S(2)}) collective-permute-start(bf16[4,512,512]{2,1,0:T(8,128)(2,1)S(1)} %get-tuple-element.59.eb_ref), channel_id=1, source_target_pairs={{0,16},{16,0},{1,17},{17,1},{2,18},{18,2},{3,19},{19,3},{4,20},{20... | collective-permute-start | bytes 6291464 | tf_op jit(solution)/shard_map/ppermute | solution.py:271
  20.6 7.9 %collective-permute-start.5 = (f32[64,512]{1,0:T(8,128)S(1)}, f32[64,512]{1,0:T(8,128)S(1)}, u32[]{:S(2)}, u32[]{:S(2)}) collective-permute-start(f32[64,512]{1,0:T(8,128)S(1)} %add.6.u0), channel_id=1, source_target_pairs={{0,32},{32,64},{64,96},{96,0},{1,33},{33,65},{65,97},{97,1},{2,34}... | collective-permute-start | bytes 393224 | tf_op jit(solution)/shard_map/ppermute | solution.py:263
  22.2 8.7 %collective-permute-start.6 = (f32[64,512]{1,0:T(8,128)S(1)}, f32[64,512]{1,0:T(8,128)S(1)}, u32[]{:S(2)}, u32[]{:S(2)}) collective-permute-start(f32[64,512]{1,0:T(8,128)S(1)} %add.6.u0), channel_id=1, source_target_pairs={{0,64},{32,96},{64,0},{96,32},{1,65},{33,97},{65,1},{97,33},{2,66}... | collective-permute-start | bytes 393224 | tf_op jit(solution)/shard_map/ppermute | solution.py:263
  24.7 6.3 %collective-permute-start.7 = (f32[64,512]{1,0:T(8,128)S(1)}, f32[64,512]{1,0:T(8,128)S(1)}, u32[]{:S(2)}, u32[]{:S(2)}) collective-permute-start(f32[64,512]{1,0:T(8,128)S(1)} %add.6.u0), channel_id=1, source_target_pairs={{0,96},{32,0},{64,32},{96,64},{1,97},{33,1},{65,33},{97,65},{2,98}... | collective-permute-start | bytes 393224 | tf_op jit(solution)/shard_map/ppermute | solution.py:263
  27.4 3.6 %collective-permute-start.9 = (f32[64,512]{1,0:T(8,128)S(1)}, f32[64,512]{1,0:T(8,128)S(1)}, u32[]{:S(2)}, u32[]{:S(2)}) collective-permute-start(f32[64,512]{1,0:T(8,128)S(1)} %get-tuple-element.61), channel_id=1, source_target_pairs={{0,16},{16,0},{1,17},{17,1},{2,18},{18,2},{3,19},{19,3},{4,20},{20... | collective-permute-start | bytes 393224 | tf_op jit(solution)/shard_map/ppermute | solution.py:271
  31.0 19.7 %collective-permute-start.19 = (bf16[512,512]{1,0:T(8,128)(2,1)S(1)}, bf16[512,512]{1,0:T(8,128)(2,1)S(1)}, u32[]{:S(2)}, u32[]{:S(2)}) collective-permute-start(bf16[512,512]{1,0:T(8,128)(2,1)S(1)} %get-tuple-element.68.g_ref.g0), channel_id=1, source_target_pairs={{0,32},{32,64},{64,96},{96,0},{1,33},{33,65},{65,97},{97,1},{2,34}... | collective-permute-start | bytes 1572872 | tf_op jit(solution)/shard_map/ppermute | solution.py:263
  31.5 19.1 %collective-permute-start.20 = (bf16[512,512]{1,0:T(8,128)(2,1)S(1)}, bf16[512,512]{1,0:T(8,128)(2,1)S(1)}, u32[]{:S(2)}, u32[]{:S(2)}) collective-permute-start(bf16[512,512]{1,0:T(8,128)(2,1)S(1)} %get-tuple-element.68.g_ref.g0), channel_id=1, source_target_pairs={{0,96},{32,0},{64,32},{96,64},{1,97},{33,1},{65,33},{97,65},{2,98}... | collective-permute-start | bytes 1572872 | tf_op jit(solution)/shard_map/ppermute | solution.py:263
  33.9 5.5 %collective-permute-start.10 = (f32[64,512]{1,0:T(8,128)S(1)}, f32[64,512]{1,0:T(8,128)S(1)}, u32[]{:S(2)}, u32[]{:S(2)}) collective-permute-start(f32[64,512]{1,0:T(8,128)S(1)} %p_kernel.1.a), channel_id=1, source_target_pairs={{0,1},{1,2},{2,3},{3,0},{4,5},{5,6},{6,7},{7,4},{8,9},{9,10},{10,1... | collective-permute-start | bytes 393224 | tf_op jit(solution)/shard_map/ppermute | solution.py:263
  35.3 7.1 %collective-permute-start.11 = (f32[64,512]{1,0:T(8,128)S(1)}, f32[64,512]{1,0:T(8,128)S(1)}, u32[]{:S(2)}, u32[]{:S(2)}) collective-permute-start(f32[64,512]{1,0:T(8,128)S(1)} %p_kernel.1.a), channel_id=1, source_target_pairs={{0,2},{1,3},{2,0},{3,1},{4,6},{5,7},{6,4},{7,5},{8,10},{9,11},{10,... | collective-permute-start | bytes 393224 | tf_op jit(solution)/shard_map/ppermute | solution.py:263
  37.9 5.4 %collective-permute-start.12 = (f32[64,512]{1,0:T(8,128)S(1)}, f32[64,512]{1,0:T(8,128)S(1)}, u32[]{:S(2)}, u32[]{:S(2)}) collective-permute-start(f32[64,512]{1,0:T(8,128)S(1)} %p_kernel.1.a), channel_id=1, source_target_pairs={{0,3},{1,0},{2,1},{3,2},{4,7},{5,4},{6,5},{7,6},{8,11},{9,8},{10,9... | collective-permute-start | bytes 393224 | tf_op jit(solution)/shard_map/ppermute | solution.py:263
  43.4 7.3 %collective-permute-start.13 = (f32[64,256]{1,0:T(8,128)S(1)}, f32[64,256]{1,0:T(8,128)S(1)}, u32[]{:S(2)}, u32[]{:S(2)}) collective-permute-start(f32[64,256]{1,0:T(8,128)S(1)} %get-tuple-element.62.a), channel_id=1, source_target_pairs={{0,4},{4,0},{8,12},{12,8},{1,5},{5,1},{9,13},{13,9},{2,6},{6,2},{1... | collective-permute-start | bytes 196616 | tf_op jit(solution)/shard_map/ppermute | solution.py:267
  46.4 7.1 %collective-permute-start.14 = (f32[64,256]{1,0:T(8,128)S(1)}, f32[64,256]{1,0:T(8,128)S(1)}, u32[]{:S(2)}, u32[]{:S(2)}) collective-permute-start(f32[64,256]{1,0:T(8,128)S(1)} %get-tuple-element.63.c), channel_id=1, source_target_pairs={{0,12},{4,8},{8,4},{12,0},{1,13},{5,9},{9,5},{13,1},{2,14},{6,10},... | collective-permute-start | bytes 196616 | tf_op jit(solution)/shard_map/ppermute | solution.py:267
  50.7 18.0 %collective-permute-start.21 = (bf16[256,512]{1,0:T(8,128)(2,1)S(1)}, bf16[256,512]{1,0:T(8,128)(2,1)S(1)}, u32[]{:S(2)}, u32[]{:S(2)}) collective-permute-start(bf16[256,512]{1,0:T(8,128)(2,1)S(1)} %slice.6), channel_id=1, source_target_pairs={{0,32},{32,64},{64,96},{96,0},{1,33},{33,65},{65,97},{97,1},{2,34}... | collective-permute-start | bytes 786440 | tf_op jit(solution)/shard_map/ppermute | solution.py:263
  50.8 17.9 %collective-permute-start.22 = (bf16[256,512]{1,0:T(8,128)(2,1)S(1)}, bf16[256,512]{1,0:T(8,128)(2,1)S(1)}, u32[]{:S(2)}, u32[]{:S(2)}) collective-permute-start(bf16[256,512]{1,0:T(8,128)(2,1)S(1)} %slice.7), channel_id=1, source_target_pairs={{0,96},{32,0},{64,32},{96,64},{1,97},{33,1},{65,33},{97,65},{2,98}... | collective-permute-start | bytes 786440 | tf_op jit(solution)/shard_map/ppermute | solution.py:263
  53.6 5.4 %collective-permute-start.15 = (f32[64,256]{1,0:T(8,128)S(1)}, f32[64,256]{1,0:T(8,128)S(1)}, u32[]{:S(2)}, u32[]{:S(2)}) collective-permute-start(f32[64,256]{1,0:T(8,128)S(1)} %get-tuple-element.64.lo), channel_id=1, source_target_pairs={{0,12},{4,8},{8,4},{12,0},{1,13},{5,9},{9,5},{13,1},{2,14},{6,10},... | collective-permute-start | bytes 196616 | tf_op jit(solution)/shard_map/ppermute | solution.py:267
  56.7 4.0 %collective-permute-start.16 = (f32[64,256]{1,0:T(8,128)S(1)}, f32[64,256]{1,0:T(8,128)S(1)}, u32[]{:S(2)}, u32[]{:S(2)}) collective-permute-start(f32[64,256]{1,0:T(8,128)S(1)} %get-tuple-element.65.hi), channel_id=1, source_target_pairs={{0,4},{4,0},{8,12},{12,8},{1,5},{5,1},{9,13},{13,9},{2,6},{6,2},{1... | collective-permute-start | bytes 196616 | tf_op jit(solution)/shard_map/ppermute | solution.py:267
  61.0 7.3 %collective-permute-start.17 = (f32[64,512]{1,0:T(8,128)S(1)}, f32[64,512]{1,0:T(8,128)S(1)}, u32[]{:S(2)}, u32[]{:S(2)}) collective-permute-start(f32[64,512]{1,0:T(8,128)S(1)} %get-tuple-element.66.p_ref), channel_id=1, source_target_pairs={{0,16},{16,0},{1,17},{17,1},{2,18},{18,2},{3,19},{19,3},{4,20},{20... | collective-permute-start | bytes 393224 | tf_op jit(solution)/shard_map/ppermute | solution.py:271
  67.4 1.3 %collective-permute-start.18 = (f32[64,512]{1,0:T(8,128)S(1)}, f32[64,512]{1,0:T(8,128)S(1)}, u32[]{:S(2)}, u32[]{:S(2)}) collective-permute-start(f32[64,512]{1,0:T(8,128)S(1)} %get-tuple-element.67.v_ref), channel_id=1, source_target_pairs={{0,16},{16,0},{1,17},{17,1},{2,18},{18,2},{3,19},{19,3},{4,20},{20... | collective-permute-start | bytes 393224 | tf_op jit(solution)/shard_map/ppermute | solution.py:271
  70.0 20.0 %collective-permute-start.25 = (bf16[4,512,512]{2,1,0:T(8,128)(2,1)S(1)}, bf16[4,512,512]{2,1,0:T(8,128)(2,1)S(1)}, u32[]{:S(2)}, u32[]{:S(2)}) collective-permute-start(bf16[4,512,512]{2,1,0:T(8,128)(2,1)S(1)} %get-tuple-element.79.ga_ref), channel_id=1, source_target_pairs={{0,16},{16,0},{1,17},{17,1},{2,18},{18,2},{3,19},{19,3},{4,20},{20... | collective-permute-start | bytes 6291464 | tf_op jit(solution)/shard_map/ppermute | solution.py:271
  85.3 3.8 %collective-permute-start.23 = (f32[64,128]{1,0:T(8,128)S(1)}, f32[64,128]{1,0:T(8,128)S(1)}, u32[]{:S(2)}, u32[]{:S(2)}) collective-permute-start(f32[64,128]{1,0:T(8,128)S(1)} %get-tuple-element.74), channel_id=1, source_target_pairs={{0,4},{4,0},{8,12},{12,8},{1,5},{5,1},{9,13},{13,9},{2,6},{6,2},{1... | collective-permute-start | bytes 98312 | tf_op jit(solution)/shard_map/ppermute | solution.py:267
  89.0 5.0 %collective-permute-start.24 = (f32[64,128]{1,0:T(8,128)S(1)}, f32[64,128]{1,0:T(8,128)S(1)}, u32[]{:S(2)}, u32[]{:S(2)}) collective-permute-start(f32[64,128]{1,0:T(8,128)S(1)} %add.7.near), channel_id=1, source_target_pairs={{0,12},{4,8},{8,4},{12,0},{1,13},{5,9},{9,5},{13,1},{2,14},{6,10},... | collective-permute-start | bytes 98312 | tf_op jit(solution)/shard_map/ppermute | solution.py:267
  104.7 7.4 %collective-permute-start.26 = (bf16[16,64,128]{2,1,0:T(8,128)(2,1)S(1)}, bf16[16,64,128]{2,1,0:T(8,128)(2,1)S(1)}, u32[]{:S(2)}, u32[]{:S(2)}) collective-permute-start(bf16[16,64,128]{2,1,0:T(8,128)(2,1)S(1)} %all_to_all.11.q_ref), channel_id=1, source_target_pairs={{0,16},{16,0},{1,17},{17,1},{2,18},{18,2},{3,19},{19,3},{4,20},{20... | collective-permute-start | bytes 786440 | tf_op jit(solution)/shard_map/ppermute | solution.py:271

commit v8 on v7

--- a/solution.py
+++ b/solution.py
@@ -209,8 +209,8 @@
     phat = jnp.dot(linv, p_ref[...], precision=HIGH, preferred_element_type=F32)
     phat_ref[...] = phat
     hi = phat.astype(BF)
-    ph2_ref[0:64] = hi
-    ph2_ref[64:128] = (phat - hi.astype(F32)).astype(BF)
+    lo = (phat - hi.astype(F32)).astype(BF)
+    ph2_ref[...] = -(jnp.concatenate([hi, lo], axis=0).T)
 
 
 def q_scale_kernel(near, far, linv_ref, out_ref):
@@ -228,7 +228,7 @@
 
 
 def error_half(ph2_ref, q_ref, m_ref, err_hbm, o_buf, sems, base):
-    ph = -(ph2_ref[...].T)
+    ph = ph2_ref[...]
     outs = []
     for k in range(4):
         row = block_row(base + k) * 4
@@ -321,17 +321,7 @@
         compiler_params=params(6),
         name="u_kernel",
     )(top, recv, qv)
-    grad_in = pl.pallas_call(
-        grad_in_kernel,
-        out_shape=sds((512, 512), BF),
-        in_specs=[VMEM] * 2,
-        out_specs=VMEM,
-        cost_estimate=LIGHT,
-        compiler_params=params(6),
-        name="grad_in_kernel",
-    )(grad, br)
-    other, grad_in = lax.optimization_barrier((swap(u), grad_in))
-    u = u + other
+    u = u + swap(u)
     eh, _ = lax.optimization_barrier((eh, u))
     eh_s = swap(eh)
     us = ring(u, "x")
@@ -345,6 +335,17 @@
         name="eq_kernel",
     )(qv, *qx[1:], act, err, eh_s)
     eqs = swap(eq_sib)
+    br, _ = lax.optimization_barrier((br, eq))
+    grad_in = pl.pallas_call(
+        grad_in_kernel,
+        out_shape=sds((512, 512), BF),
+        in_specs=[VMEM] * 2,
+        out_specs=VMEM,
+        cost_estimate=LIGHT,
+        compiler_params=params(6),
+        name="grad_in_kernel",
+    )(grad, br)
+    eqs, grad_in = lax.optimization_barrier((eqs, grad_in))
 
     part = pl.pallas_call(
         p_kernel,
@@ -430,7 +431,7 @@
     q_in = trade(q_part, "zhi", True)
     phat, ph2, linv = pl.pallas_call(
         factor_kernel,
-        out_shape=(sds((64, 512), F32), sds((128, 512), BF), sds((64, 64), F32)),
+        out_shape=(sds((64, 512), F32), sds((512, 128), BF), sds((64, 64), F32)),
         in_specs=[VMEM, VMEM],
         out_specs=(VMEM, VMEM, VMEM),
         cost_estimate=LIGHT,

time: 114 us -> 120 us (1.053)
  waiting for transfers between devices: 16.8 us -> 23.3 us
    ppermute x7, waiting for transfers between devices: 0.75 us -> 5.45 us  [swap(): return lax.ppermute(v, 'core', [(0, 1), (1, 0)])]
    ppermute x13, waiting for transfers between devices: 11.6 us -> 13.3 us  [shift(): return lax.ppermute(v, axis, [(i, (i + k) % n) for i in range(n)])]
  transfers between devices with their start and end apart: 27 -> 27, of which waited for: 13 -> 15; matrix products, arithmetic and copies ran while one was open for 0% -> 0% of each run, Pallas kernels for 12% -> 10%
where the time goes in v8:
time: 120 us
  starting transfers between devices  51.5 us (43%)
  blocking collectives  25.4 us (21%)
  waiting for transfers between devices  23.3 us (19%)
  Pallas kernels  18.4 us (15%)
    all_to_all x2, blocking collectives, exchange(): return lax.all_to_all(v, axes, 0, 0, tiled=True)  25.4 us
    ppermute x13, starting transfers between devices, shift(): return lax.ppermute(v, axis, [(i, (i + k) % n) for i in range(n)])  21.5 us
    ppermute x7, starting transfers between devices, swap(): return lax.ppermute(v, 'core', [(0, 1), (1, 0)])  15.2 us
    ppermute x6, starting transfers between devices, trade(): lax.ppermute(v, axis, [(i, i ^ 1 if flip else 3 - i) for i in range(4)])  13.5 us
    ppermute x13, waiting for transfers between devices, shift(): return lax.ppermute(v, axis, [(i, (i + k) % n) for i in range(n)])  13.3 us
    ppermute x7, waiting for transfers between devices, swap(): return lax.ppermute(v, 'core', [(0, 1), (1, 0)])  5.45 us
    ppermute x6, waiting for transfers between devices, trade(): lax.ppermute(v, axis, [(i, i ^ 1 if flip else 3 - i) for i in range(4)])  4.54 us
    pallas_call x1, Pallas kernels, on_device(): pl.pallas_call(factor_kernel, out_shape=(sds((64, 512), F32), sds((512, 1...  2.76 us
  transfers between devices with their start and end apart: 27, of which 15 were waited for; matrix products, arithmetic and copies ran while one was open for 0% of the time, Pallas kernels for 10%

profile of v8, /device:TPU:1, one launch (start us, length us, event | category | flops | bytes accessed | tf_op | source)
XLA Modules:
  0.0 119.6 jit_solution(17432442005631465428)
XLA Ops:
  0.6 1.4 %load_kernel.1 = (f32[64,512]{1,0:T(8,128)S(1)}, bf16[512,512]{1,0:T(8,128)(2,1)S(1)}, bf16[512,512]{1,0:T(8,128)(2,1)S(1)}, bf16[512,512]{1,0:T(8,128)(2,1)S(1)}) custom-call(f32[64,512]{1,0:T(8,128)} %bitcast.23, bf16[512,512]{1,0:T(8,128)(2,1)} %bitcast.21, bf16[512,512]{1,0:T(8,128)(2,1)} %bitcast.22), custom_call_target="tpu_custom_call" | custom-call | tf_op jit(solution)/shard_map/load_kernel/pallas_call | solution.py:289
  2.1 1.3 %collective-permute-start.3 = (bf16[512,512]{1,0:T(8,128)(2,1)S(1)}, bf16[512,512]{1,0:T(8,128)(2,1)S(1)}, u32[]{:S(2)}, u32[]{:S(2)}) collective-permute-start(bf16[512,512]{1,0:T(8,128)(2,1)S(1)} %get-tuple-element.49), channel_id=1, source_target_pairs={{128,0},{129,1},{130,2},{131,3},{132,4},{133,5},{134,6},{135,7},{1... | collective-permute-start | bytes 1572872 | tf_op jit(solution)/shard_map/ppermute | solution.py:300
  3.4 2.1 %collective-permute-start = (f32[64,512]{1,0:T(8,128)}, f32[64,512]{1,0:T(8,128)S(1)}, u32[]{:S(2)}, u32[]{:S(2)}) collective-permute-start(f32[64,512]{1,0:T(8,128)} %bitcast.24), channel_id=1, source_target_pairs={{0,32},{32,64},{64,96},{96,0},{1,33},{33,65},{65,97},{97,1},{2,34}... | collective-permute-start | bytes 393224 | tf_op jit(solution)/shard_map/ppermute | solution.py:263
  5.5 2.5 %collective-permute-start.1 = (f32[64,512]{1,0:T(8,128)}, f32[64,512]{1,0:T(8,128)S(1)}, u32[]{:S(2)}, u32[]{:S(2)}) collective-permute-start(f32[64,512]{1,0:T(8,128)} %bitcast.25), channel_id=1, source_target_pairs={{0,64},{32,96},{64,0},{96,32},{1,65},{33,97},{65,1},{97,33},{2,66}... | collective-permute-start | bytes 393224 | tf_op jit(solution)/shard_map/ppermute | solution.py:263
  9.3 4.5 %collective-permute-done.1.q2 = f32[64,512]{1,0:T(8,128)S(1)} collective-permute-done((f32[64,512]{1,0:T(8,128)}, f32[64,512]{1,0:T(8,128)S(1)}, u32[]{:S(2)}, u32[]{:S(2)}) %collective-permute-start.1) | collective-permute-done | bytes 131104 | tf_op jit(solution)/shard_map/ppermute | solution.py:263
  13.9 2.4 %load_error_kernel.1 = (bf16[4,512,512]{2,1,0:T(8,128)(2,1)S(1)}, bf16[4,512,512]{2,1,0:T(8,128)(2,1)S(1)}, bf16[512,512]{1,0:T(8,128)(2,1)S(1)}) custom-call(bf16[512,4096]{1,0:T(8,128)(2,1)} %bitcast.17, bf16[512,512]{1,0:T(8,128)(2,1)} %bitcast.19), custom_call_target="tpu_custom_call" | custom-call | tf_op jit(solution)/shard_map/load_error_kernel/pallas_call | solution.py:303
  16.7 2.5 %collective-permute-start.4 = (f32[64,512]{1,0:T(8,128)S(1)}, f32[64,512]{1,0:T(8,128)S(1)}, u32[]{:S(2)}, u32[]{:S(2)}) collective-permute-start(f32[64,512]{1,0:T(8,128)S(1)} %get-tuple-element.55), channel_id=1, source_target_pairs={{0,16},{16,0},{1,17},{17,1},{2,18},{18,2},{3,19},{19,3},{4,20},{20... | collective-permute-start | bytes 393224 | tf_op jit(solution)/shard_map/ppermute | solution.py:271
  20.6 3.8 %collective-permute-done.5.es_ref = bf16[4,512,512]{2,1,0:T(8,128)(2,1)S(1)} collective-permute-done((bf16[4,512,512]{2,1,0:T(8,128)(2,1)S(1)}, bf16[4,512,512]{2,1,0:T(8,128)(2,1)S(1)}, u32[]{:S(2)}, u32[]{:S(2)}) %collective-permute-start.5) | collective-permute-done | bytes 2097184 | tf_op jit(solution)/shard_map/ppermute | solution.py:271
  24.4 1.5 %eq_kernel.1 = (f32[64,512]{1,0:T(8,128)S(1)}, f32[64,512]{1,0:T(8,128)S(1)}, bf16[512,512]{1,0:T(8,128)(2,1)S(1)}) custom-call(f32[64,512]{1,0:T(8,128)S(1)} %get-tuple-element.46.q_ref.q0, f32[64,512]{1,0:T(8,128)S(1)} %collective-permute-done.q1, f32[64,512]{1,0:T(8,128)S(1)} %collective-permute-done.1.q2, f32[64,512]{1,0:T(8,128)S(1)} %collective-permute-done.2.q3, ...), custom_call_target="tpu_custom_call" | custom-call | tf_op jit(solution)/shard_map/eq_kernel/pallas_call | solution.py:328
  26.4 1.7 %collective-permute-start.7 = (f32[64,512]{1,0:T(8,128)S(1)}, f32[64,512]{1,0:T(8,128)S(1)}, u32[]{:S(2)}, u32[]{:S(2)}) collective-permute-start(f32[64,512]{1,0:T(8,128)S(1)} %add.6.u0), channel_id=1, source_target_pairs={{0,32},{32,64},{64,96},{96,0},{1,33},{33,65},{65,97},{97,1},{2,34}... | collective-permute-start | bytes 393224 | tf_op jit(solution)/shard_map/ppermute | solution.py:263
  28.0 2.5 %collective-permute-start.8 = (f32[64,512]{1,0:T(8,128)S(1)}, f32[64,512]{1,0:T(8,128)S(1)}, u32[]{:S(2)}, u32[]{:S(2)}) collective-permute-start(f32[64,512]{1,0:T(8,128)S(1)} %add.6.u0), channel_id=1, source_target_pairs={{0,64},{32,96},{64,0},{96,32},{1,65},{33,97},{65,1},{97,33},{2,66}... | collective-permute-start | bytes 393224 | tf_op jit(solution)/shard_map/ppermute | solution.py:263
  33.0 3.7 %collective-permute-done.8.u2 = f32[64,512]{1,0:T(8,128)S(1)} collective-permute-done((f32[64,512]{1,0:T(8,128)S(1)}, f32[64,512]{1,0:T(8,128)S(1)}, u32[]{:S(2)}, u32[]{:S(2)}) %collective-permute-start.8) | collective-permute-done | bytes 131104 | tf_op jit(solution)/shard_map/ppermute | solution.py:263
  37.3 2.2 %collective-permute-start.20 = (bf16[512,512]{1,0:T(8,128)(2,1)S(1)}, bf16[512,512]{1,0:T(8,128)(2,1)S(1)}, u32[]{:S(2)}, u32[]{:S(2)}) collective-permute-start(bf16[512,512]{1,0:T(8,128)(2,1)S(1)} %get-tuple-element.70.g_ref.g0), channel_id=1, source_target_pairs={{0,96},{32,0},{64,32},{96,64},{1,97},{33,1},{65,33},{97,65},{2,98}... | collective-permute-start | bytes 1572872 | tf_op jit(solution)/shard_map/ppermute | solution.py:263
  39.7 1.4 %collective-permute-start.10 = (f32[64,512]{1,0:T(8,128)S(1)}, f32[64,512]{1,0:T(8,128)S(1)}, u32[]{:S(2)}, u32[]{:S(2)}) collective-permute-start(f32[64,512]{1,0:T(8,128)S(1)} %p_kernel.1.a), channel_id=1, source_target_pairs={{0,1},{1,2},{2,3},{3,0},{4,5},{5,6},{6,7},{7,4},{8,9},{9,10},{10,1... | collective-permute-start | bytes 393224 | tf_op jit(solution)/shard_map/ppermute | solution.py:263
  41.1 2.6 %collective-permute-start.11 = (f32[64,512]{1,0:T(8,128)S(1)}, f32[64,512]{1,0:T(8,128)S(1)}, u32[]{:S(2)}, u32[]{:S(2)}) collective-permute-start(f32[64,512]{1,0:T(8,128)S(1)} %p_kernel.1.a), channel_id=1, source_target_pairs={{0,2},{1,3},{2,0},{3,1},{4,6},{5,7},{6,4},{7,5},{8,10},{9,11},{10,... | collective-permute-start | bytes 393224 | tf_op jit(solution)/shard_map/ppermute | solution.py:263
  45.2 3.0 %collective-permute-done.11.c = f32[64,512]{1,0:T(8,128)S(1)} collective-permute-done((f32[64,512]{1,0:T(8,128)S(1)}, f32[64,512]{1,0:T(8,128)S(1)}, u32[]{:S(2)}, u32[]{:S(2)}) %collective-permute-start.11) | collective-permute-done | bytes 131104 | tf_op jit(solution)/shard_map/ppermute | solution.py:263
  49.1 3.1 %collective-permute-start.13 = (f32[64,256]{1,0:T(8,128)S(1)}, f32[64,256]{1,0:T(8,128)S(1)}, u32[]{:S(2)}, u32[]{:S(2)}) collective-permute-start(f32[64,256]{1,0:T(8,128)S(1)} %get-tuple-element.64.a), channel_id=1, source_target_pairs={{0,4},{4,0},{8,12},{12,8},{1,5},{5,1},{9,13},{13,9},{2,6},{6,2},{1... | collective-permute-start | bytes 196616 | tf_op jit(solution)/shard_map/ppermute | solution.py:267
  52.2 4.2 %collective-permute-start.14 = (f32[64,256]{1,0:T(8,128)S(1)}, f32[64,256]{1,0:T(8,128)S(1)}, u32[]{:S(2)}, u32[]{:S(2)}) collective-permute-start(f32[64,256]{1,0:T(8,128)S(1)} %get-tuple-element.65.c), channel_id=1, source_target_pairs={{0,12},{4,8},{8,4},{12,0},{1,13},{5,9},{9,5},{13,1},{2,14},{6,10},... | collective-permute-start | bytes 196616 | tf_op jit(solution)/shard_map/ppermute | solution.py:267
  56.5 2.7 %collective-permute-start.22 = (bf16[256,512]{1,0:T(8,128)(2,1)S(1)}, bf16[256,512]{1,0:T(8,128)(2,1)S(1)}, u32[]{:S(2)}, u32[]{:S(2)}) collective-permute-start(bf16[256,512]{1,0:T(8,128)(2,1)S(1)} %slice.7), channel_id=1, source_target_pairs={{0,96},{32,0},{64,32},{96,64},{1,97},{33,1},{65,33},{97,65},{2,98}... | collective-permute-start | bytes 786440 | tf_op jit(solution)/shard_map/ppermute | solution.py:263
  59.3 3.1 %collective-permute-start.15 = (f32[64,256]{1,0:T(8,128)S(1)}, f32[64,256]{1,0:T(8,128)S(1)}, u32[]{:S(2)}, u32[]{:S(2)}) collective-permute-start(f32[64,256]{1,0:T(8,128)S(1)} %get-tuple-element.66.lo), channel_id=1, source_target_pairs={{0,12},{4,8},{8,4},{12,0},{1,13},{5,9},{9,5},{13,1},{2,14},{6,10},... | collective-permute-start | bytes 196616 | tf_op jit(solution)/shard_map/ppermute | solution.py:267
  62.4 1.7 %collective-permute-start.16 = (f32[64,256]{1,0:T(8,128)S(1)}, f32[64,256]{1,0:T(8,128)S(1)}, u32[]{:S(2)}, u32[]{:S(2)}) collective-permute-start(f32[64,256]{1,0:T(8,128)S(1)} %get-tuple-element.67.hi), channel_id=1, source_target_pairs={{0,4},{4,0},{8,12},{12,8},{1,5},{5,1},{9,13},{13,9},{2,6},{6,2},{1... | collective-permute-start | bytes 196616 | tf_op jit(solution)/shard_map/ppermute | solution.py:267
  64.7 1.7 %collective-permute-done.16.hi_far = f32[64,256]{1,0:T(8,128)S(1)} collective-permute-done((f32[64,256]{1,0:T(8,128)S(1)}, f32[64,256]{1,0:T(8,128)S(1)}, u32[]{:S(2)}, u32[]{:S(2)}) %collective-permute-start.16) | collective-permute-done | bytes 65568 | tf_op jit(solution)/shard_map/ppermute | solution.py:267
  66.8 6.3 %collective-permute-start.17 = (f32[64,512]{1,0:T(8,128)S(1)}, f32[64,512]{1,0:T(8,128)S(1)}, u32[]{:S(2)}, u32[]{:S(2)}) collective-permute-start(f32[64,512]{1,0:T(8,128)S(1)} %get-tuple-element.68.p_ref), channel_id=1, source_target_pairs={{0,16},{16,0},{1,17},{17,1},{2,18},{18,2},{3,19},{19,3},{4,20},{20... | collective-permute-start | bytes 393224 | tf_op jit(solution)/shard_map/ppermute | solution.py:271
  74.5 1.3 %q_kernel.1 = (f32[4,4,72,128]{3,2,1,0:T(8,128)S(1)}, bf16[4,512,512]{2,1,0:T(8,128)(2,1)S(1)}) custom-call(f32[64,512]{1,0:T(8,128)S(1)} %get-tuple-element.68.p_ref, f32[64,512]{1,0:T(8,128)S(1)} %get-tuple-element.69.v_ref, f32[64,512]{1,0:T(8,128)S(1)} %collective-permute-done.17.ps_ref, f32[64,512]{1,0:T(8,128)S(1)} %collective-permute-done.18.vs_ref, ...), custom_call_target="tpu_custom_call" | custom-call | tf_op jit(solution)/shard_map/q_kernel/pallas_call | solution.py:409
  76.0 15.0 %all_to_all.10.in_ref = f32[16,72,128]{2,1,0:T(8,128)S(1)} all-to-all(f32[16,72,128]{2,1,0:T(8,128)S(1)} %bitcast.16), channel_id=1, replica_groups=mesh['pipe'=2,'x'=4,'core'=2,'zhi'=4,'y'=4] {'x','y'}, dimensions={0} | all-to-all | bytes 1179648 | tf_op jit(solution)/shard_map/all_to_all | solution.py:279
  91.5 2.8 %factor_kernel.1 = (f32[64,512]{1,0:T(8,128)}, bf16[512,128]{1,0:T(8,128)(2,1)S(1)}, f32[64,64]{1,0:T(8,128)S(1)}) custom-call(f32[32,128]{1,0:T(8,128)S(1)} %get-tuple-element.74.gram_ref, f32[64,512]{1,0:T(8,128)S(1)} %get-tuple-element.68.p_ref), custom_call_target="tpu_custom_call" | custom-call | tf_op jit(solution)/shard_map/factor_kernel/pallas_call | solution.py:432
  95.8 2.3 %matrix_kernel.1.m_ref = f32[8,512,512]{2,1,0:T(8,128)S(1)} custom-call(bf16[512,512]{1,0:T(8,128)(2,1)S(1)} %get-tuple-element.80.at_ref, bf16[4,512,512]{2,1,0:T(8,128)(2,1)S(1)} %get-tuple-element.81.ga_ref, bf16[4,512,512]{2,1,0:T(8,128)(2,1)S(1)} %collective-permute-done.25.gb_ref, bf16[4,512,512]{2,1,0:T(8,128)(2,1)S(1)} %get-tuple-element.51.e_ref.ea_ref, ...), custom_call_target="tpu_custom_call" | custom-call | tf_op jit(solution)/shard_map/matrix_kernel/pallas_call | solution.py:445
  98.1 1.7 %collective-permute-done.24.far = f32[64,128]{1,0:T(8,128)S(1)} collective-permute-done((f32[64,128]{1,0:T(8,128)S(1)}, f32[64,128]{1,0:T(8,128)S(1)}, u32[]{:S(2)}, u32[]{:S(2)}) %collective-permute-start.24) | collective-permute-done | bytes 32800 | tf_op jit(solution)/shard_map/ppermute | solution.py:267
  100.0 10.5 %all_to_all.11.q_ref = bf16[16,64,128]{2,1,0:T(8,128)(2,1)S(1)} all-to-all(bf16[16,64,128]{2,1,0:T(8,128)(2,1)S(1)} %q_scale_kernel.1), channel_id=1, replica_groups=mesh['pipe'=2,'x'=4,'core'=2,'zhi'=4,'y'=4] {'x','y'}, dimensions={0} | all-to-all | bytes 524288 | tf_op jit(solution)/shard_map/all_to_all | solution.py:279
  110.4 5.1 %collective-permute-start.26 = (bf16[16,64,128]{2,1,0:T(8,128)(2,1)S(1)}, bf16[16,64,128]{2,1,0:T(8,128)(2,1)S(1)}, u32[]{:S(2)}, u32[]{:S(2)}) collective-permute-start(bf16[16,64,128]{2,1,0:T(8,128)(2,1)S(1)} %all_to_all.11.q_ref), channel_id=1, source_target_pairs={{0,16},{16,0},{1,17},{17,1},{2,18},{18,2},{3,19},{19,3},{4,20},{20... | collective-permute-start | bytes 786440 | tf_op jit(solution)/shard_map/ppermute | solution.py:271
  115.5 2.3 %error_own_kernel.1 = (bf16[512,4096]{1,0:T(8,128)(2,1)}, f32[64,512]{1,0:T(8,128)}) custom-call(bf16[512,128]{1,0:T(8,128)(2,1)S(1)} %get-tuple-element.75.ph2_ref, bf16[16,64,128]{2,1,0:T(8,128)(2,1)S(1)} %all_to_all.11.q_ref, f32[8,512,512]{2,1,0:T(8,128)S(1)} %matrix_kernel.1.m_ref), custom_call_target="tpu_custom_call" | custom-call | tf_op jit(solution)/shard_map/error_own_kernel/pallas_call | solution.py:468
  117.8 1.6 %error_sib_kernel.1 = bf16[512,4096]{1,0:T(8,128)(2,1)} custom-call(bf16[512,128]{1,0:T(8,128)(2,1)S(1)} %get-tuple-element.75.ph2_ref, bf16[16,64,128]{2,1,0:T(8,128)(2,1)S(1)} %collective-permute-done.26.q_ref, f32[8,512,512]{2,1,0:T(8,128)S(1)} %matrix_kernel.1.m_ref, bf16[512,4096]{1,0:T(8,128)(2,1)} %get-tuple-element.85._), custom_call_target="tpu_custom_call", output_to_operand_aliasing={{}: (3, {})} | custom-call | tf_op jit(solution)/shard_map/error_sib_kernel/pallas_call | solution.py:478
  (45 shorter events, 14.3 us)
Async XLA Ops:
  2.1 14.2 %collective-permute-start.3 = (bf16[512,512]{1,0:T(8,128)(2,1)S(1)}, bf16[512,512]{1,0:T(8,128)(2,1)S(1)}, u32[]{:S(2)}, u32[]{:S(2)}) collective-permute-start(bf16[512,512]{1,0:T(8,128)(2,1)S(1)} %get-tuple-element.49), channel_id=1, source_target_pairs={{128,0},{129,1},{130,2},{131,3},{132,4},{133,5},{134,6},{135,7},{1... | collective-permute-start | bytes 1572872 | tf_op jit(solution)/shard_map/ppermute | solution.py:300
  3.4 6.0 %collective-permute-start = (f32[64,512]{1,0:T(8,128)}, f32[64,512]{1,0:T(8,128)S(1)}, u32[]{:S(2)}, u32[]{:S(2)}) collective-permute-start(f32[64,512]{1,0:T(8,128)} %bitcast.24), channel_id=1, source_target_pairs={{0,32},{32,64},{64,96},{96,0},{1,33},{33,65},{65,97},{97,1},{2,34}... | collective-permute-start | bytes 393224 | tf_op jit(solution)/shard_map/ppermute | solution.py:263
  5.5 8.4 %collective-permute-start.1 = (f32[64,512]{1,0:T(8,128)}, f32[64,512]{1,0:T(8,128)S(1)}, u32[]{:S(2)}, u32[]{:S(2)}) collective-permute-start(f32[64,512]{1,0:T(8,128)} %bitcast.25), channel_id=1, source_target_pairs={{0,64},{32,96},{64,0},{96,32},{1,65},{33,97},{65,1},{97,33},{2,66}... | collective-permute-start | bytes 393224 | tf_op jit(solution)/shard_map/ppermute | solution.py:263
  7.9 5.9 %collective-permute-start.2 = (f32[64,512]{1,0:T(8,128)}, f32[64,512]{1,0:T(8,128)S(1)}, u32[]{:S(2)}, u32[]{:S(2)}) collective-permute-start(f32[64,512]{1,0:T(8,128)} %bitcast.26), channel_id=1, source_target_pairs={{0,96},{32,0},{64,32},{96,64},{1,97},{33,1},{65,33},{97,65},{2,98}... | collective-permute-start | bytes 393224 | tf_op jit(solution)/shard_map/ppermute | solution.py:263
  16.7 3.5 %collective-permute-start.4 = (f32[64,512]{1,0:T(8,128)S(1)}, f32[64,512]{1,0:T(8,128)S(1)}, u32[]{:S(2)}, u32[]{:S(2)}) collective-permute-start(f32[64,512]{1,0:T(8,128)S(1)} %get-tuple-element.55), channel_id=1, source_target_pairs={{0,16},{16,0},{1,17},{17,1},{2,18},{18,2},{3,19},{19,3},{4,20},{20... | collective-permute-start | bytes 393224 | tf_op jit(solution)/shard_map/ppermute | solution.py:271
  20.1 4.2 %collective-permute-start.5 = (bf16[4,512,512]{2,1,0:T(8,128)(2,1)S(1)}, bf16[4,512,512]{2,1,0:T(8,128)(2,1)S(1)}, u32[]{:S(2)}, u32[]{:S(2)}) collective-permute-start(bf16[4,512,512]{2,1,0:T(8,128)(2,1)S(1)} %get-tuple-element.56.eb_ref), channel_id=1, source_target_pairs={{0,16},{16,0},{1,17},{17,1},{2,18},{18,2},{3,19},{19,3},{4,20},{20... | collective-permute-start | bytes 6291464 | tf_op jit(solution)/shard_map/ppermute | solution.py:271
  25.9 6.6 %collective-permute-start.6 = (f32[64,512]{1,0:T(8,128)S(1)}, f32[64,512]{1,0:T(8,128)S(1)}, u32[]{:S(2)}, u32[]{:S(2)}) collective-permute-start(f32[64,512]{1,0:T(8,128)S(1)} %get-tuple-element.57), channel_id=1, source_target_pairs={{0,16},{16,0},{1,17},{17,1},{2,18},{18,2},{3,19},{19,3},{4,20},{20... | collective-permute-start | bytes 393224 | tf_op jit(solution)/shard_map/ppermute | solution.py:271
  26.4 6.7 %collective-permute-start.7 = (f32[64,512]{1,0:T(8,128)S(1)}, f32[64,512]{1,0:T(8,128)S(1)}, u32[]{:S(2)}, u32[]{:S(2)}) collective-permute-start(f32[64,512]{1,0:T(8,128)S(1)} %add.6.u0), channel_id=1, source_target_pairs={{0,32},{32,64},{64,96},{96,0},{1,33},{33,65},{65,97},{97,1},{2,34}... | collective-permute-start | bytes 393224 | tf_op jit(solution)/shard_map/ppermute | solution.py:263
  28.0 8.7 %collective-permute-start.8 = (f32[64,512]{1,0:T(8,128)S(1)}, f32[64,512]{1,0:T(8,128)S(1)}, u32[]{:S(2)}, u32[]{:S(2)}) collective-permute-start(f32[64,512]{1,0:T(8,128)S(1)} %add.6.u0), channel_id=1, source_target_pairs={{0,64},{32,96},{64,0},{96,32},{1,65},{33,97},{65,1},{97,33},{2,66}... | collective-permute-start | bytes 393224 | tf_op jit(solution)/shard_map/ppermute | solution.py:263
  30.5 6.3 %collective-permute-start.9 = (f32[64,512]{1,0:T(8,128)S(1)}, f32[64,512]{1,0:T(8,128)S(1)}, u32[]{:S(2)}, u32[]{:S(2)}) collective-permute-start(f32[64,512]{1,0:T(8,128)S(1)} %add.6.u0), channel_id=1, source_target_pairs={{0,96},{32,0},{64,32},{96,64},{1,97},{33,1},{65,33},{97,65},{2,98}... | collective-permute-start | bytes 393224 | tf_op jit(solution)/shard_map/ppermute | solution.py:263
  36.8 19.6 %collective-permute-start.19 = (bf16[512,512]{1,0:T(8,128)(2,1)S(1)}, bf16[512,512]{1,0:T(8,128)(2,1)S(1)}, u32[]{:S(2)}, u32[]{:S(2)}) collective-permute-start(bf16[512,512]{1,0:T(8,128)(2,1)S(1)} %get-tuple-element.70.g_ref.g0), channel_id=1, source_target_pairs={{0,32},{32,64},{64,96},{96,0},{1,33},{33,65},{65,97},{97,1},{2,34}... | collective-permute-start | bytes 1572872 | tf_op jit(solution)/shard_map/ppermute | solution.py:263
  37.3 19.1 %collective-permute-start.20 = (bf16[512,512]{1,0:T(8,128)(2,1)S(1)}, bf16[512,512]{1,0:T(8,128)(2,1)S(1)}, u32[]{:S(2)}, u32[]{:S(2)}) collective-permute-start(bf16[512,512]{1,0:T(8,128)(2,1)S(1)} %get-tuple-element.70.g_ref.g0), channel_id=1, source_target_pairs={{0,96},{32,0},{64,32},{96,64},{1,97},{33,1},{65,33},{97,65},{2,98}... | collective-permute-start | bytes 1572872 | tf_op jit(solution)/shard_map/ppermute | solution.py:263
  39.7 5.5 %collective-permute-start.10 = (f32[64,512]{1,0:T(8,128)S(1)}, f32[64,512]{1,0:T(8,128)S(1)}, u32[]{:S(2)}, u32[]{:S(2)}) collective-permute-start(f32[64,512]{1,0:T(8,128)S(1)} %p_kernel.1.a), channel_id=1, source_target_pairs={{0,1},{1,2},{2,3},{3,0},{4,5},{5,6},{6,7},{7,4},{8,9},{9,10},{10,1... | collective-permute-start | bytes 393224 | tf_op jit(solution)/shard_map/ppermute | solution.py:263
  41.1 7.1 %collective-permute-start.11 = (f32[64,512]{1,0:T(8,128)S(1)}, f32[64,512]{1,0:T(8,128)S(1)}, u32[]{:S(2)}, u32[]{:S(2)}) collective-permute-start(f32[64,512]{1,0:T(8,128)S(1)} %p_kernel.1.a), channel_id=1, source_target_pairs={{0,2},{1,3},{2,0},{3,1},{4,6},{5,7},{6,4},{7,5},{8,10},{9,11},{10,... | collective-permute-start | bytes 393224 | tf_op jit(solution)/shard_map/ppermute | solution.py:263
  43.7 5.4 %collective-permute-start.12 = (f32[64,512]{1,0:T(8,128)S(1)}, f32[64,512]{1,0:T(8,128)S(1)}, u32[]{:S(2)}, u32[]{:S(2)}) collective-permute-start(f32[64,512]{1,0:T(8,128)S(1)} %p_kernel.1.a), channel_id=1, source_target_pairs={{0,3},{1,0},{2,1},{3,2},{4,7},{5,4},{6,5},{7,6},{8,11},{9,8},{10,9... | collective-permute-start | bytes 393224 | tf_op jit(solution)/shard_map/ppermute | solution.py:263
  49.1 7.3 %collective-permute-start.13 = (f32[64,256]{1,0:T(8,128)S(1)}, f32[64,256]{1,0:T(8,128)S(1)}, u32[]{:S(2)}, u32[]{:S(2)}) collective-permute-start(f32[64,256]{1,0:T(8,128)S(1)} %get-tuple-element.64.a), channel_id=1, source_target_pairs={{0,4},{4,0},{8,12},{12,8},{1,5},{5,1},{9,13},{13,9},{2,6},{6,2},{1... | collective-permute-start | bytes 196616 | tf_op jit(solution)/shard_map/ppermute | solution.py:267
  52.2 7.1 %collective-permute-start.14 = (f32[64,256]{1,0:T(8,128)S(1)}, f32[64,256]{1,0:T(8,128)S(1)}, u32[]{:S(2)}, u32[]{:S(2)}) collective-permute-start(f32[64,256]{1,0:T(8,128)S(1)} %get-tuple-element.65.c), channel_id=1, source_target_pairs={{0,12},{4,8},{8,4},{12,0},{1,13},{5,9},{9,5},{13,1},{2,14},{6,10},... | collective-permute-start | bytes 196616 | tf_op jit(solution)/shard_map/ppermute | solution.py:267
  56.4 18.0 %collective-permute-start.21 = (bf16[256,512]{1,0:T(8,128)(2,1)S(1)}, bf16[256,512]{1,0:T(8,128)(2,1)S(1)}, u32[]{:S(2)}, u32[]{:S(2)}) collective-permute-start(bf16[256,512]{1,0:T(8,128)(2,1)S(1)} %slice.6), channel_id=1, source_target_pairs={{0,32},{32,64},{64,96},{96,0},{1,33},{33,65},{65,97},{97,1},{2,34}... | collective-permute-start | bytes 786440 | tf_op jit(solution)/shard_map/ppermute | solution.py:263
  56.5 17.9 %collective-permute-start.22 = (bf16[256,512]{1,0:T(8,128)(2,1)S(1)}, bf16[256,512]{1,0:T(8,128)(2,1)S(1)}, u32[]{:S(2)}, u32[]{:S(2)}) collective-permute-start(bf16[256,512]{1,0:T(8,128)(2,1)S(1)} %slice.7), channel_id=1, source_target_pairs={{0,96},{32,0},{64,32},{96,64},{1,97},{33,1},{65,33},{97,65},{2,98}... | collective-permute-start | bytes 786440 | tf_op jit(solution)/shard_map/ppermute | solution.py:263
  59.3 5.4 %collective-permute-start.15 = (f32[64,256]{1,0:T(8,128)S(1)}, f32[64,256]{1,0:T(8,128)S(1)}, u32[]{:S(2)}, u32[]{:S(2)}) collective-permute-start(f32[64,256]{1,0:T(8,128)S(1)} %get-tuple-element.66.lo), channel_id=1, source_target_pairs={{0,12},{4,8},{8,4},{12,0},{1,13},{5,9},{9,5},{13,1},{2,14},{6,10},... | collective-permute-start | bytes 196616 | tf_op jit(solution)/shard_map/ppermute | solution.py:267
  62.4 4.0 %collective-permute-start.16 = (f32[64,256]{1,0:T(8,128)S(1)}, f32[64,256]{1,0:T(8,128)S(1)}, u32[]{:S(2)}, u32[]{:S(2)}) collective-permute-start(f32[64,256]{1,0:T(8,128)S(1)} %get-tuple-element.67.hi), channel_id=1, source_target_pairs={{0,4},{4,0},{8,12},{12,8},{1,5},{5,1},{9,13},{13,9},{2,6},{6,2},{1... | collective-permute-start | bytes 196616 | tf_op jit(solution)/shard_map/ppermute | solution.py:267
  66.8 7.3 %collective-permute-start.17 = (f32[64,512]{1,0:T(8,128)S(1)}, f32[64,512]{1,0:T(8,128)S(1)}, u32[]{:S(2)}, u32[]{:S(2)}) collective-permute-start(f32[64,512]{1,0:T(8,128)S(1)} %get-tuple-element.68.p_ref), channel_id=1, source_target_pairs={{0,16},{16,0},{1,17},{17,1},{2,18},{18,2},{3,19},{19,3},{4,20},{20... | collective-permute-start | bytes 393224 | tf_op jit(solution)/shard_map/ppermute | solution.py:271
  73.1 1.3 %collective-permute-start.18 = (f32[64,512]{1,0:T(8,128)S(1)}, f32[64,512]{1,0:T(8,128)S(1)}, u32[]{:S(2)}, u32[]{:S(2)}) collective-permute-start(f32[64,512]{1,0:T(8,128)S(1)} %get-tuple-element.69.v_ref), channel_id=1, source_target_pairs={{0,16},{16,0},{1,17},{17,1},{2,18},{18,2},{3,19},{19,3},{4,20},{20... | collective-permute-start | bytes 393224 | tf_op jit(solution)/shard_map/ppermute | solution.py:271
  75.8 20.0 %collective-permute-start.25 = (bf16[4,512,512]{2,1,0:T(8,128)(2,1)S(1)}, bf16[4,512,512]{2,1,0:T(8,128)(2,1)S(1)}, u32[]{:S(2)}, u32[]{:S(2)}) collective-permute-start(bf16[4,512,512]{2,1,0:T(8,128)(2,1)S(1)} %get-tuple-element.81.ga_ref), channel_id=1, source_target_pairs={{0,16},{16,0},{1,17},{17,1},{2,18},{18,2},{3,19},{19,3},{4,20},{20... | collective-permute-start | bytes 6291464 | tf_op jit(solution)/shard_map/ppermute | solution.py:271
  91.1 3.8 %collective-permute-start.23 = (f32[64,128]{1,0:T(8,128)S(1)}, f32[64,128]{1,0:T(8,128)S(1)}, u32[]{:S(2)}, u32[]{:S(2)}) collective-permute-start(f32[64,128]{1,0:T(8,128)S(1)} %get-tuple-element.76), channel_id=1, source_target_pairs={{0,4},{4,0},{8,12},{12,8},{1,5},{5,1},{9,13},{13,9},{2,6},{6,2},{1... | collective-permute-start | bytes 98312 | tf_op jit(solution)/shard_map/ppermute | solution.py:267
  94.8 5.0 %collective-permute-start.24 = (f32[64,128]{1,0:T(8,128)S(1)}, f32[64,128]{1,0:T(8,128)S(1)}, u32[]{:S(2)}, u32[]{:S(2)}) collective-permute-start(f32[64,128]{1,0:T(8,128)S(1)} %add.7.near), channel_id=1, source_target_pairs={{0,12},{4,8},{8,4},{12,0},{1,13},{5,9},{9,5},{13,1},{2,14},{6,10},... | collective-permute-start | bytes 98312 | tf_op jit(solution)/shard_map/ppermute | solution.py:267
  110.4 7.4 %collective-permute-start.26 = (bf16[16,64,128]{2,1,0:T(8,128)(2,1)S(1)}, bf16[16,64,128]{2,1,0:T(8,128)(2,1)S(1)}, u32[]{:S(2)}, u32[]{:S(2)}) collective-permute-start(bf16[16,64,128]{2,1,0:T(8,128)(2,1)S(1)} %all_to_all.11.q_ref), channel_id=1, source_target_pairs={{0,16},{16,0},{1,17},{17,1},{2,18},{18,2},{3,19},{19,3},{4,20},{20... | collective-permute-start | bytes 786440 | tf_op jit(solution)/shard_map/ppermute | solution.py:271
